TPU v7x, 256 devices: a whole 4x4x8 slice. The times are simulated.
256 devices in a mesh: dp: 16 (over z, core), filter: 16 (over x, y).
Axes of the slice: x: 4, y: 4, z: 8, core: 2. Of those that a mesh axis runs over, the one named last changes fastest.
Arguments:
- patches: bfloat16 [256, 48, 2048], P('filter', 'dp'), may hold values from -6 to 6
- cotangent: bfloat16 [256, 48, 2048], P('filter', 'dp'), may hold values from -6 to 6
- first_weight: bfloat16 [27, 256, 256], P(None, 'filter'), may hold values from -0.078125 to 0.078125
- second_weight: bfloat16 [27, 256, 256], P(None, 'filter'), may hold values from -0.078125 to 0.078125
- counts: int32 [16], P('dp'), may hold values from 0 to 3, as said below
Outputs:
- output_maps: float32 [256, 48, 2048], P('filter', 'dp')
- input_grad: float32 [256, 48, 2048], P('filter', 'dp')
- first_grad: float32 [27, 256, 256], P(None, 'filter')
- second_grad: float32 [27, 256, 256], P(None, 'filter')
Inputs may be any that keep to these rules, and one draw needn't show every extreme that they name: The counts of all groups sum to 16; one group holds exactly 3 live patches. Live patches of a group occupy its first slots.
All inputs are finite; a program needn't handle non-finite values.
Results may differ from a plain program's by a relative error of at most 0.0029.
Values may be sent and summed in bfloat16 or wider, within the bound.
No kernel may reach another device: no remote copies, remote signals or barrier semaphores. Data moves between devices by JAX's collectives and lax.ppermute only.
A program may use at most 128 MiB of HBM per device.

v0:
```python
import functools

import jax
import jax.numpy as jnp
from jax import lax
from jax.experimental import pallas as pl
from jax.experimental.pallas import tpu as pltpu
from jax.sharding import PartitionSpec as P

PX = 8
PY = 16
PZ = 16
CAP = 3
CELLS = 2048
PLANE = PY * PZ
C = 256
BLK = 16
TAPS = 27
ROWS = TAPS * BLK

SIDE = 4


def axis_masks():
    cell = lax.broadcasted_iota(jnp.int32, (BLK, CELLS), 1)
    pos_y = (cell >> 4) & 15
    pos_z = cell & 15
    in_y = {-1: pos_y > 0, 0: None, 1: pos_y < PY - 1}
    in_z = {-1: pos_z > 0, 0: None, 1: pos_z < PZ - 1}
    return in_y, in_z


def shift_x(v, ox):
    if ox == 0:
        return v
    zero = jnp.zeros((v.shape[0], PLANE), v.dtype)
    if ox > 0:
        return jnp.concatenate([v[:, PLANE:], zero], axis=1)
    return jnp.concatenate([zero, v[:, :-PLANE]], axis=1)


def shift_yz(v, oy, oz, masks):
    step = oy * PZ + oz
    if step == 0:
        return v
    v = pltpu.roll(v, (-step) % CELLS, 1)
    for inside in (masks[0][oy], masks[1][oz]):
        if inside is not None:
            v = jnp.where(inside, v, 0.0)
    return v


def tap_conv(w_ref, full, sign, masks):
    proj = [
        jnp.dot(w_ref[k * 9 * BLK:(k + 1) * 9 * BLK, :], full, preferred_element_type=jnp.float32)
        for k in range(3)
    ]
    total = None
    for oy in (-1, 0, 1):
        for oz in (-1, 0, 1):
            at = (3 * (oy + 1) + oz + 1) * BLK
            part = None
            for ox in (-1, 0, 1):
                term = shift_x(proj[ox + 1][at:at + BLK, :], sign * ox)
                part = term if part is None else part + term
            part = shift_yz(part, sign * oy, sign * oz, masks)
            total = part if total is None else total + part
    return total


def tap_stack(stack_ref, v, sign, masks):
    for oy in (-1, 0, 1):
        for oz in (-1, 0, 1):
            moved = shift_yz(v, sign * oy, sign * oz, masks)
            for ox in (-1, 0, 1):
                t = 9 * (ox + 1) + 3 * (oy + 1) + (oz + 1)
                stack_ref[t * BLK:(t + 1) * BLK, :] = shift_x(moved, sign * ox).astype(jnp.bfloat16)


def place(scalars, pieces, full_ref, outer_is_x):
    x, y, sign = scalars[1], scalars[2], scalars[3]
    for outer in range(SIDE):
        for inner in range(SIDE):
            if outer_is_x:
                bx, by = x + SIDE + sign * outer, y + inner
            else:
                bx, by = x + inner, y + SIDE + sign * outer
            block = lax.rem(bx, SIDE) * SIDE + lax.rem(by, SIDE)
            at = pl.multiple_of(block * BLK, BLK)
            full_ref[pl.ds(at, BLK), :] = pieces[outer][inner, 0]


def over_cells(a, b):
    return lax.dot_general(a, b, (((1,), (1,)), ((), ())), preferred_element_type=jnp.float32)


def kernel_one(scalars, *refs):
    px, gx = refs[0:4], refs[4:8]
    w1, w2t, hid_out, del_out, keep_out, send_out, full_p, full_g, stack, grads = refs[8:]
    s = pl.program_id(0)
    core = scalars[4]

    @pl.when(s == 0)
    def _():
        grads[...] = jnp.zeros_like(grads)

    @pl.when(s >= scalars[0])
    def _():
        hid_out[...] = jnp.zeros_like(hid_out)
        del_out[...] = jnp.zeros_like(del_out)

    @pl.when(s < scalars[0])
    def _():
        masks = axis_masks()
        place(scalars, px, full_p, True)
        place(scalars, gx, full_g, False)
        first = tap_conv(w1, full_p[...], 1, masks)
        hidden_grad = tap_conv(w2t, full_g[...], -1, masks)
        sigma = 1.0 / (1.0 + jnp.exp(-first))
        hidden = (first * sigma).astype(jnp.bfloat16)
        delta = (hidden_grad * sigma * (1.0 + first * (1.0 - sigma))).astype(jnp.bfloat16)
        hid_out[0] = hidden
        del_out[0] = delta
        tap_stack(stack, delta.astype(jnp.float32), -1, masks)
        grads[0] += over_cells(full_p[...], stack[...])
        tap_stack(stack, hidden.astype(jnp.float32), 1, masks)
        grads[1] += over_cells(full_g[...], stack[...])

    @pl.when(s == pl.num_programs(0) - 1)
    def _():
        keep_out[...] = grads[core]
        send_out[...] = grads[1 - core]


def kernel_two(scalars, *refs):
    hx, dx = refs[0:4], refs[4:8]
    w2, w1t, out_ref, in_ref, full_h, full_d = refs[8:]
    s = pl.program_id(0)

    @pl.when(s >= scalars[0])
    def _():
        out_ref[...] = jnp.zeros_like(out_ref)
        in_ref[...] = jnp.zeros_like(in_ref)

    @pl.when(s < scalars[0])
    def _():
        masks = axis_masks()
        place(scalars, hx, full_h, True)
        place(scalars, dx, full_d, False)
        out_ref[0] = tap_conv(w2, full_h[...], 1, masks)
        in_ref[0] = tap_conv(w1t, full_d[...], -1, masks)


def from_near(axis, step):
    def at(x, y):
        return (x % SIDE) * SIDE + y % SIDE

    sides = [(x, y) for x in range(SIDE) for y in range(SIDE)]
    if axis == "x":
        return [(at(x + step, y), at(x, y)) for x, y in sides]
    return [(at(x, y + step), at(x, y)) for x, y in sides]


def from_mirrored(axis, step):
    pairs = []
    for d in range(BLK):
        for src, dst in from_near(axis, step if d % 2 == 0 else -step):
            pairs.append((d * BLK + src, d * BLK + dst))
    return pairs


def gather(v, inner, outer):
    near = [v] + [lax.ppermute(v, "filter", from_near(inner, k)) for k in (1, 2, 3)]
    own = jnp.stack(near)
    both = ("dp", "filter")
    ahead = lax.ppermute(own, both, from_mirrored(outer, 1))
    behind = lax.ppermute(own, both, from_mirrored(outer, 3))
    across = lax.ppermute(ahead, both, from_mirrored(outer, 1))
    return [own, ahead, across, behind]


def specs_of(count):
    piece = pl.BlockSpec((SIDE, 1, BLK, CELLS), lambda s, *_: (0, s, 0, 0))
    weight = pl.BlockSpec((ROWS, C), lambda s, *_: (0, 0))
    return [piece] * count + [weight] * 2


def slot_spec():
    return pl.BlockSpec((1, BLK, CELLS), lambda s, *_: (s, 0, 0))


def call_one(scalars, pieces, w1, w2t):
    slots = pieces[0].shape[1]
    flat = jax.ShapeDtypeStruct((slots, BLK, CELLS), jnp.bfloat16)
    return pl.pallas_call(
        kernel_one,
        name="layer_one",
        grid_spec=pltpu.PrefetchScalarGridSpec(
            num_scalar_prefetch=1,
            grid=(slots,),
            in_specs=specs_of(8),
            out_specs=[
                slot_spec(),
                slot_spec(),
                pl.BlockSpec((C, ROWS), lambda s, *_: (0, 0)),
                pl.BlockSpec((C, ROWS), lambda s, *_: (0, 0)),
            ],
            scratch_shapes=[
                pltpu.VMEM((C, CELLS), jnp.bfloat16),
                pltpu.VMEM((C, CELLS), jnp.bfloat16),
                pltpu.VMEM((ROWS, CELLS), jnp.bfloat16),
                pltpu.VMEM((2, C, ROWS), jnp.float32),
            ],
        ),
        out_shape=[flat, flat] + [jax.ShapeDtypeStruct((C, ROWS), jnp.float32)] * 2,
        compiler_params=pltpu.CompilerParams(vmem_limit_bytes=48 * 1024 * 1024),
        cost_estimate=pl.CostEstimate(
            flops=slots * 8 * ROWS * C * CELLS, transcendentals=slots * BLK * CELLS, bytes_accessed=slots * 4 * C * CELLS
        ),
    )(scalars, *pieces, w1, w2t)


def call_two(scalars, pieces, w2, w1t):
    slots = pieces[0].shape[1]
    flat = jax.ShapeDtypeStruct((slots, BLK, CELLS), jnp.float32)
    return pl.pallas_call(
        kernel_two,
        name="layer_two",
        grid_spec=pltpu.PrefetchScalarGridSpec(
            num_scalar_prefetch=1,
            grid=(slots,),
            in_specs=specs_of(8),
            out_specs=[slot_spec(), slot_spec()],
            scratch_shapes=[
                pltpu.VMEM((C, CELLS), jnp.bfloat16),
                pltpu.VMEM((C, CELLS), jnp.bfloat16),
            ],
        ),
        out_shape=[flat, flat],
        compiler_params=pltpu.CompilerParams(vmem_limit_bytes=48 * 1024 * 1024),
        cost_estimate=pl.CostEstimate(
            flops=slots * 4 * ROWS * C * CELLS, transcendentals=0, bytes_accessed=slots * 4 * C * CELLS
        ),
    )(scalars, *pieces, w2, w1t)


def kernel_split(w1, w2, out_ref):
    lane = lax.broadcasted_iota(jnp.int32, (BLK, 128), 1) >> 4
    for k, w in enumerate((w1, w2)):
        for half in range(2):
            for low in range(0, TAPS, 8):
                taps = range(low, min(low + 8, TAPS))
                tiles = [w[t, :, half * 128:(half + 1) * 128].astype(jnp.float32) for t in taps]
                for a in range(8):
                    total = None
                    for j, tile in enumerate(tiles):
                        amount = (BLK * (j - a)) % 128
                        moved = pltpu.roll(tile, amount, 1) if amount else tile
                        total = moved if total is None else jnp.where(lane == j, moved, total)
                    width = BLK * len(tiles)
                    out_ref[half * 8 + a, k, :, low * BLK:low * BLK + width] = total[:, :width].astype(jnp.bfloat16)


def split_weights(w1, w2):
    return pl.pallas_call(
        kernel_split,
        name="split_weights",
        out_shape=jax.ShapeDtypeStruct((BLK, 2, BLK, ROWS), jnp.bfloat16),
        cost_estimate=pl.CostEstimate(flops=0, transcendentals=0, bytes_accessed=4 * ROWS * C * 2),
    )(w1, w2)


def kernel_finish(scalars, own, other, first_ref, second_ref):
    @pl.when(scalars[4] == 0)
    def _():
        first_ref[...] = own[...].T
        second_ref[...] = other[...].T

    @pl.when(scalars[4] == 1)
    def _():
        first_ref[...] = other[...].T
        second_ref[...] = own[...].T


def finish(scalars, own, other):
    whole = pl.BlockSpec((C, ROWS), lambda i, *_: (0, 0))
    turned = pl.BlockSpec((ROWS, C), lambda i, *_: (0, 0))
    return pl.pallas_call(
        kernel_finish,
        name="finish_gradients",
        grid_spec=pltpu.PrefetchScalarGridSpec(
            num_scalar_prefetch=1, grid=(1,), in_specs=[whole, whole], out_specs=[turned, turned]
        ),
        out_shape=[jax.ShapeDtypeStruct((ROWS, C), jnp.float32)] * 2,
        cost_estimate=pl.CostEstimate(flops=0, transcendentals=0, bytes_accessed=16 * ROWS * C),
    )(scalars, own, other)


def sum_over_dp(scalars, keep, send):
    swap_cores = [(d, d ^ 1) for d in range(BLK)]
    by_core = [[2 * z + core for z in range(8)] for core in range(2)]
    total = keep + lax.ppermute(send, "dp", swap_cores)
    parts = lax.all_to_all(total.reshape(8, 32, ROWS), "dp", 0, 0, axis_index_groups=by_core, tiled=True)
    scale = 1.0 / jnp.sqrt(jnp.float32(lax.axis_size("dp") * CELLS))
    mine = parts.sum(axis=0) * scale

    odd = lax.axis_index("filter") % 2 == 1
    low, high = mine[:BLK], mine[BLK:]
    got = []
    for m in range(2):
        pairs = []
        for z in range(8):
            for f in range(BLK):
                j = (f + m) % 2
                pairs.append(((2 * z + 1) * BLK + f, (2 * (f // 2) + 1) * BLK + 2 * z + j))
        message = jnp.where(odd, low, high) if m else jnp.where(odd, high, low)
        got.append(lax.ppermute(message, ("dp", "filter"), pairs))
    halves = jnp.stack([jnp.where(odd, got[1], got[0]), jnp.where(odd, got[0], got[1])])
    second = halves.reshape(2, BLK, TAPS, BLK).transpose(0, 3, 2, 1).reshape(2 * BLK, ROWS)
    piece = jnp.where(scalars[4] == 0, mine, second)

    copies = jnp.broadcast_to(piece[None], (8, 2 * BLK, ROWS))
    own = lax.all_to_all(copies, "dp", 0, 0, axis_index_groups=by_core, tiled=True).reshape(C, ROWS)
    other = lax.ppermute(own, "dp", swap_cores)
    first_grad, second_grad = finish(scalars, own, other)
    return first_grad.reshape(TAPS, BLK, C), second_grad.reshape(TAPS, BLK, C)


def shards(patches, cotangent, first_weight, second_weight, counts):
    me = lax.axis_index("filter")
    core = lax.axis_index("dp") % 2
    scalars = jnp.stack([counts[0], me // SIDE, me % SIDE, 1 - 2 * core, core]).astype(jnp.int32)
    all_p = gather(patches.transpose(1, 0, 2), "y", "x")
    all_g = gather(cotangent.transpose(1, 0, 2), "x", "y")

    turned = lax.all_to_all(split_weights(first_weight, second_weight), "filter", 0, 0, tiled=True)
    w1t = turned[:, 0].reshape(C, ROWS).T
    w2t = turned[:, 1].reshape(C, ROWS).T
    w1 = first_weight.reshape(ROWS, C)
    w2 = second_weight.reshape(ROWS, C)

    hidden, delta, keep, send = call_one(scalars, all_p + all_g, w1, w2t)
    first_grad, second_grad = sum_over_dp(scalars, keep, send)

    all_h = gather(hidden, "y", "x")
    all_d = gather(delta, "x", "y")
    out, in_grad = call_two(scalars, all_h + all_d, w2, w1t)
    return (out.transpose(1, 0, 2), in_grad.transpose(1, 0, 2), first_grad, second_grad)


def solution(mesh):
    placed = (
        P("filter", "dp", None),
        P("filter", "dp", None),
        P(None, "filter", None),
        P(None, "filter", None),
        P("dp"),
    )
    return jax.shard_map(
        shards,
        mesh=mesh,
        in_specs=placed,
        out_specs=(
            P("filter", "dp", None),
            P("filter", "dp", None),
            P(None, "filter", None),
            P(None, "filter", None),
        ),
        check_vma=False,
    )
```

profile of v0, /device:TPU:1, one launch (start us, length us, event | category | flops | bytes accessed | tf_op | source)
XLA Modules:
  0.0 150.8 jit_solution(18438526566022771400)
XLA Ops:
  0.6 3.7 %collective-permute-start.7 = (bf16[3,16,2048]{2,1,0:T(8,128)(2,1)}, bf16[3,16,2048]{2,1,0:T(8,128)(2,1)S(1)}, u32[]{:S(2)}, u32[]{:S(2)}) collective-permute-start(bf16[3,16,2048]{2,1,0:T(8,128)(2,1)} %bitcast.48), channel_id=1, source_target_pairs={{8,0},{9,1},{10,2},{11,3},{12,4},{13,5},{14,6},{15,7},{0,8},{1,9},... | collective-permute-start | bytes 589832 | tf_op jit(solution)/shard_map/ppermute | solution.py:173
  4.3 0.9 collective-permute-start.6
  5.8 2.9 %collective-permute-start.1 = (bf16[3,16,2048]{2,1,0:T(8,128)(2,1)}, bf16[3,16,2048]{2,1,0:T(8,128)(2,1)S(1)}, u32[]{:S(2)}, u32[]{:S(2)}) collective-permute-start(bf16[3,16,2048]{2,1,0:T(8,128)(2,1)} %bitcast.52), channel_id=1, source_target_pairs={{2,0},{3,1},{0,2},{1,3},{6,4},{7,5},{4,6},{5,7},{10,8},{11,9},{8,1... | collective-permute-start | bytes 589832 | tf_op jit(solution)/shard_map/ppermute | solution.py:173
  8.7 0.8 collective-permute-start
  9.5 0.9 collective-permute-start.2
  10.3 3.1 %collective-permute-done.6 = bf16[3,16,2048]{2,1,0:T(8,128)(2,1)S(1)} collective-permute-done((bf16[3,16,2048]{2,1,0:T(8,128)(2,1)}, bf16[3,16,2048]{2,1,0:T(8,128)(2,1)S(1)}, u32[]{:S(2)}, u32[]{:S(2)}) %collective-permute-start.6) | collective-permute-done | bytes 196640 | tf_op jit(solution)/shard_map/ppermute | solution.py:173
  13.5 1.0 collective-permute-done.8
  14.5 1.1 pad_maximum_fusion.1.refs_4_
  16.1 1.5 %collective-permute-done = bf16[3,16,2048]{2,1,0:T(8,128)(2,1)S(1)} collective-permute-done((bf16[3,16,2048]{2,1,0:T(8,128)(2,1)}, bf16[3,16,2048]{2,1,0:T(8,128)(2,1)S(1)}, u32[]{:S(2)}, u32[]{:S(2)}) %collective-permute-start) | collective-permute-done | bytes 196640 | tf_op jit(solution)/shard_map/ppermute | solution.py:173
  18.2 3.2 %collective-permute-start.11 = (bf16[4,3,16,2048]{3,2,1,0:T(8,128)(2,1)S(1)}, bf16[4,3,16,2048]{3,2,1,0:T(8,128)(2,1)}, u32[]{:S(2)}, u32[]{:S(2)}) collective-permute-start(bf16[4,3,16,2048]{3,2,1,0:T(8,128)(2,1)S(1)} %pad_maximum_fusion.1.refs_4_), channel_id=1, source_target_pairs={{3,0},{0,1},{1,2},{2,3},{7,4},{4,5},{5,6},{6,7},{11,8},{8,9},{9,10... | collective-permute-start | bytes 2359304 | tf_op jit(solution)/shard_map/ppermute | solution.py:177
  21.4 2.4 %collective-permute-start.5 = (bf16[4,3,16,2048]{3,2,1,0:T(8,128)(2,1)S(1)}, bf16[4,3,16,2048]{3,2,1,0:T(8,128)(2,1)}, u32[]{:S(2)}, u32[]{:S(2)}) collective-permute-start(bf16[4,3,16,2048]{3,2,1,0:T(8,128)(2,1)S(1)} %pad_maximum_fusion.refs_0_), channel_id=1, source_target_pairs={{12,0},{13,1},{14,2},{15,3},{0,4},{1,5},{2,6},{3,7},{4,8},{5,9},{6... | collective-permute-start | bytes 2359304 | tf_op jit(solution)/shard_map/ppermute | solution.py:177
  23.8 5.9 %collective-permute-done.9.refs_5_ = bf16[4,3,16,2048]{3,2,1,0:T(8,128)(2,1)} collective-permute-done((bf16[4,3,16,2048]{3,2,1,0:T(8,128)(2,1)S(1)}, bf16[4,3,16,2048]{3,2,1,0:T(8,128)(2,1)}, u32[]{:S(2)}, u32[]{:S(2)}) %collective-permute-start.9) | collective-permute-done | bytes 786464 | tf_op jit(solution)/shard_map/ppermute | solution.py:176
  29.6 1.1 collective-permute-start.10
  30.7 1.9 %collective-permute-done.3.refs_1_ = bf16[4,3,16,2048]{3,2,1,0:T(8,128)(2,1)S(1)} collective-permute-done((bf16[4,3,16,2048]{3,2,1,0:T(8,128)(2,1)S(1)}, bf16[4,3,16,2048]{3,2,1,0:T(8,128)(2,1)S(1)}, u32[]{:S(2)}, u32[]{:S(2)}) %collective-permute-start.3) | collective-permute-done | bytes 786464 | tf_op jit(solution)/shard_map/ppermute | solution.py:176
  32.6 2.7 %split_weights.1 = bf16[16,2,16,432]{3,2,1,0:T(8,128)(2,1)} custom-call(bf16[27,16,256]{2,1,0:T(8,128)(2,1)} %w1.1, bf16[27,16,256]{2,1,0:T(8,128)(2,1)} %w2.1), custom_call_target="tpu_custom_call" | custom-call | bytes 884736 | tf_op jit(solution)/shard_map/split_weights/pallas_call | solution.py:265
  35.3 9.7 %all-to-all-start = ((bf16[16,2,16,432]{3,2,1,0:T(8,128)(2,1)}), bf16[16,2,16,432]{3,2,1,0:T(8,128)(2,1)S(1)}, u32[]{:S(2)}, u32[]{:S(2)}) async-start(bf16[16,2,16,432]{3,2,1,0:T(8,128)(2,1)} %split_weights.1), calls=%async_computation | async-start | bytes 1048576 | tf_op jit(solution)/shard_map/all_to_all | solution.py:336
  45.8 9.1 %all-to-all-done = bf16[16,2,16,432]{3,2,1,0:T(8,128)(2,1)S(1)} async-done(((bf16[16,2,16,432]{3,2,1,0:T(8,128)(2,1)}), bf16[16,2,16,432]{3,2,1,0:T(8,128)(2,1)S(1)}, u32[]{:S(2)}, u32[]{:S(2)}) %all-to-all-start) | async-done | bytes 442400 | tf_op jit(solution)/shard_map/all_to_all | solution.py:336
  54.9 0.7 fusion
  55.9 0.8 copy-done
  56.6 6.3 %layer_one.1 = (bf16[3,16,2048]{2,1,0:T(8,128)(2,1)S(1)}, bf16[3,16,2048]{2,1,0:T(8,128)(2,1)S(1)}, f32[256,432]{1,0:T(8,128)S(1)}, f32[256,432]{1,0:T(8,128)S(1)}) custom-call(s32[5]{0:T(128)S(1)} %stack.88.scalars, bf16[4,3,16,2048]{3,2,1,0:T(8,128)(2,1)S(1)} %pad_maximum_fusion.refs_0_, bf16[4,3,16,2048]{3,2,1,0:T(8,128)(2,1)S(1)} %collective-permute-done.3.refs_1_, ...), custom_call_target="tpu_custom_call" | custom-call | flops 5435817984 | bytes 6291456 | tf_op jit(solution)/shard_map/layer_one/pallas_call | solution.py:195
  63.0 2.5 %collective-permute-start.24 = (f32[256,432]{1,0:T(8,128)S(1)}, f32[256,432]{1,0:T(8,128)S(1)}, u32[]{:S(2)}, u32[]{:S(2)}) collective-permute-start(f32[256,432]{1,0:T(8,128)S(1)} %get-tuple-element.17), channel_id=1, source_target_pairs={{0,16},{16,0},{32,48},{48,32},{64,80},{80,64},{96,112},{112,96},{1... | collective-permute-start | bytes 1327112 | tf_op jit(solution)/shard_map/ppermute | solution.py:302
  65.4 1.5 %collective-permute-done.24 = f32[256,432]{1,0:T(8,128)S(1)} collective-permute-done((f32[256,432]{1,0:T(8,128)S(1)}, f32[256,432]{1,0:T(8,128)S(1)}, u32[]{:S(2)}, u32[]{:S(2)}) %collective-permute-start.24) | collective-permute-done | bytes 442400 | tf_op jit(solution)/shard_map/ppermute | solution.py:302
  66.9 0.9 add.16
  67.8 11.9 %all-to-all-start.1 = ((f32[8,32,432]{2,1,0:T(8,128)}), f32[8,32,432]{2,1,0:T(8,128)}, u32[]{:S(2)}, u32[]{:S(2)}) async-start(f32[8,32,432]{2,1,0:T(8,128)} %bitcast.30), calls=%async_computation.1 | async-start | bytes 1048576 | tf_op jit(solution)/shard_map/all_to_all | solution.py:303
  79.7 4.2 %collective-permute-start.19 = (bf16[3,16,2048]{2,1,0:T(8,128)(2,1)S(1)}, bf16[3,16,2048]{2,1,0:T(8,128)(2,1)S(1)}, u32[]{:S(2)}, u32[]{:S(2)}) collective-permute-start(bf16[3,16,2048]{2,1,0:T(8,128)(2,1)S(1)} %get-tuple-element.13), channel_id=1, source_target_pairs={{8,0},{9,1},{10,2},{11,3},{12,4},{13,5},{14,6},{15,7},{0,8},{1,9},... | collective-permute-start | bytes 589832 | tf_op jit(solution)/shard_map/ppermute | solution.py:173
  84.1 2.1 %collective-permute-start.13 = (bf16[3,16,2048]{2,1,0:T(8,128)(2,1)S(1)}, bf16[3,16,2048]{2,1,0:T(8,128)(2,1)S(1)}, u32[]{:S(2)}, u32[]{:S(2)}) collective-permute-start(bf16[3,16,2048]{2,1,0:T(8,128)(2,1)S(1)} %get-tuple-element.12), channel_id=1, source_target_pairs={{2,0},{3,1},{0,2},{1,3},{6,4},{7,5},{4,6},{5,7},{10,8},{11,9},{8,1... | collective-permute-start | bytes 589832 | tf_op jit(solution)/shard_map/ppermute | solution.py:173
  86.1 1.4 collective-permute-done.20
  87.5 1.0 collective-permute-start.12
  88.5 4.0 %collective-permute-done.19 = bf16[3,16,2048]{2,1,0:T(8,128)(2,1)S(1)} collective-permute-done((bf16[3,16,2048]{2,1,0:T(8,128)(2,1)S(1)}, bf16[3,16,2048]{2,1,0:T(8,128)(2,1)S(1)}, u32[]{:S(2)}, u32[]{:S(2)}) %collective-permute-start.19) | collective-permute-done | bytes 196640 | tf_op jit(solution)/shard_map/ppermute | solution.py:173
  92.9 1.2 collective-permute-done.13
  94.0 1.2 collective-permute-done.12
  95.4 1.5 collective-permute-start.15
  96.8 0.9 all-to-all-done.1
  97.7 1.1 reduce_sum.9
  98.9 2.8 %collective-permute-start.25 = (f32[16,432]{1,0:T(8,128)S(1)}, f32[16,432]{1,0:T(8,128)S(1)}, u32[]{:S(2)}, u32[]{:S(2)}) collective-permute-start(f32[16,432]{1,0:T(8,128)S(1)} %get-tuple-element.24), channel_id=1, source_target_pairs={{16,17},{17,16},{18,49},{19,48},{20,81},{21,80},{22,113},{23,112},... | collective-permute-start | bytes 82952 | tf_op jit(solution)/shard_map/ppermute | solution.py:317
  101.7 0.7 collective-permute-start.26
  102.4 2.0 %collective-permute-done.25 = f32[16,432]{1,0:T(8,128)S(1)} collective-permute-done((f32[16,432]{1,0:T(8,128)S(1)}, f32[16,432]{1,0:T(8,128)S(1)}, u32[]{:S(2)}, u32[]{:S(2)}) %collective-permute-start.25) | collective-permute-done | bytes 27680 | tf_op jit(solution)/shard_map/ppermute | solution.py:317
  105.5 0.9 broadcast_in_dim.2
  106.4 17.2 %all-to-all-start.2 = ((f32[8,32,432]{2,1,0:T(8,128)}), f32[8,32,432]{2,1,0:T(8,128)S(1)}, u32[]{:S(2)}, u32[]{:S(2)}) async-start(f32[8,32,432]{2,1,0:T(8,128)} %broadcast_in_dim.2), calls=%async_computation.2 | async-start | bytes 1048576 | tf_op jit(solution)/shard_map/all_to_all | solution.py:323
  124.2 4.5 %collective-permute-start.17 = (bf16[4,3,16,2048]{3,2,1,0:T(8,128)(2,1)S(1)}, bf16[4,3,16,2048]{3,2,1,0:T(8,128)(2,1)}, u32[]{:S(2)}, u32[]{:S(2)}) collective-permute-start(bf16[4,3,16,2048]{3,2,1,0:T(8,128)(2,1)S(1)} %pad_maximum_fusion.2.refs_0_), channel_id=1, source_target_pairs={{12,0},{13,1},{14,2},{15,3},{0,4},{1,5},{2,6},{3,7},{4,8},{5,9},{6... | collective-permute-start | bytes 2359304 | tf_op jit(solution)/shard_map/ppermute | solution.py:177
  128.7 1.2 collective-permute-start.22
  129.9 5.8 %all-to-all-done.2 = f32[8,32,432]{2,1,0:T(8,128)S(1)} async-done(((f32[8,32,432]{2,1,0:T(8,128)}), f32[8,32,432]{2,1,0:T(8,128)S(1)}, u32[]{:S(2)}, u32[]{:S(2)}) %all-to-all-start.2) | async-done | bytes 442400 | tf_op jit(solution)/shard_map/all_to_all | solution.py:323
  135.7 1.3 copy.14
  137.0 0.7 collective-permute-done.17.refs_3_
  137.7 3.2 %collective-permute-done.22.refs_6_ = bf16[4,3,16,2048]{3,2,1,0:T(8,128)(2,1)} collective-permute-done((bf16[4,3,16,2048]{3,2,1,0:T(8,128)(2,1)S(1)}, bf16[4,3,16,2048]{3,2,1,0:T(8,128)(2,1)}, u32[]{:S(2)}, u32[]{:S(2)}) %collective-permute-start.22) | collective-permute-done | bytes 786464 | tf_op jit(solution)/shard_map/ppermute | solution.py:178
  140.9 1.4 collective-permute-done.16.refs_2_
  142.3 5.4 %layer_two.1 = (f32[3,16,2048]{2,1,0:T(8,128)}, f32[3,16,2048]{2,1,0:T(8,128)}) custom-call(s32[5]{0:T(128)S(1)} %stack.88.scalars, bf16[4,3,16,2048]{3,2,1,0:T(8,128)(2,1)S(1)} %pad_maximum_fusion.2.refs_0_, bf16[4,3,16,2048]{3,2,1,0:T(8,128)(2,1)} %collective-permute-done.15.refs_1_, bf16[4,3,16,2048]{3,2,1,0:T(8,128)(2,1)} %collective-permute-done.16.refs_2_, ...), custom_call_target="tpu_custom_call" | custom-call | flops 2717908992 | bytes 6291456 | tf_op jit(solution)/shard_map/layer_two/pallas_call | solution.py:226
  147.7 3.1 %finish_gradients.1 = (f32[432,256]{1,0:T(8,128)}, f32[432,256]{1,0:T(8,128)}) custom-call(s32[5]{0:T(128)} %copy-done.2, f32[256,432]{1,0:T(8,128)} %bitcast.45, f32[256,432]{1,0:T(8,128)} %collective-permute-done.27.other), custom_call_target="tpu_custom_call" | custom-call | bytes 1769472 | tf_op jit(solution)/shard_map/finish_gradients/pallas_call | solution.py:288
  (48 shorter events, 4.4 us)
Async XLA Ops:
  0.6 8.8 %collective-permute-start.7 = (bf16[3,16,2048]{2,1,0:T(8,128)(2,1)}, bf16[3,16,2048]{2,1,0:T(8,128)(2,1)S(1)}, u32[]{:S(2)}, u32[]{:S(2)}) collective-permute-start(bf16[3,16,2048]{2,1,0:T(8,128)(2,1)} %bitcast.48), channel_id=1, source_target_pairs={{8,0},{9,1},{10,2},{11,3},{12,4},{13,5},{14,6},{15,7},{0,8},{1,9},... | collective-permute-start | bytes 589832 | tf_op jit(solution)/shard_map/ppermute | solution.py:173
  4.3 9.2 %collective-permute-start.6 = (bf16[3,16,2048]{2,1,0:T(8,128)(2,1)}, bf16[3,16,2048]{2,1,0:T(8,128)(2,1)S(1)}, u32[]{:S(2)}, u32[]{:S(2)}) collective-permute-start(bf16[3,16,2048]{2,1,0:T(8,128)(2,1)} %bitcast.49), channel_id=1, source_target_pairs={{4,0},{5,1},{6,2},{7,3},{8,4},{9,5},{10,6},{11,7},{12,8},{13,9},{1... | collective-permute-start | bytes 589832 | tf_op jit(solution)/shard_map/ppermute | solution.py:173
  5.2 9.3 %collective-permute-start.8 = (bf16[3,16,2048]{2,1,0:T(8,128)(2,1)}, bf16[3,16,2048]{2,1,0:T(8,128)(2,1)S(1)}, u32[]{:S(2)}, u32[]{:S(2)}) collective-permute-start(bf16[3,16,2048]{2,1,0:T(8,128)(2,1)} %bitcast.50), channel_id=1, source_target_pairs={{12,0},{13,1},{14,2},{15,3},{0,4},{1,5},{2,6},{3,7},{4,8},{5,9},{6... | collective-permute-start | bytes 589832 | tf_op jit(solution)/shard_map/ppermute | solution.py:173
  5.8 10.3 %collective-permute-start.1 = (bf16[3,16,2048]{2,1,0:T(8,128)(2,1)}, bf16[3,16,2048]{2,1,0:T(8,128)(2,1)S(1)}, u32[]{:S(2)}, u32[]{:S(2)}) collective-permute-start(bf16[3,16,2048]{2,1,0:T(8,128)(2,1)} %bitcast.52), channel_id=1, source_target_pairs={{2,0},{3,1},{0,2},{1,3},{6,4},{7,5},{4,6},{5,7},{10,8},{11,9},{8,1... | collective-permute-start | bytes 589832 | tf_op jit(solution)/shard_map/ppermute | solution.py:173
  8.7 8.9 %collective-permute-start = (bf16[3,16,2048]{2,1,0:T(8,128)(2,1)}, bf16[3,16,2048]{2,1,0:T(8,128)(2,1)S(1)}, u32[]{:S(2)}, u32[]{:S(2)}) collective-permute-start(bf16[3,16,2048]{2,1,0:T(8,128)(2,1)} %bitcast.53), channel_id=1, source_target_pairs={{1,0},{2,1},{3,2},{0,3},{5,4},{6,5},{7,6},{4,7},{9,8},{10,9},{11,1... | collective-permute-start | bytes 589832 | tf_op jit(solution)/shard_map/ppermute | solution.py:173
  9.5 8.1 %collective-permute-start.2 = (bf16[3,16,2048]{2,1,0:T(8,128)(2,1)}, bf16[3,16,2048]{2,1,0:T(8,128)(2,1)S(1)}, u32[]{:S(2)}, u32[]{:S(2)}) collective-permute-start(bf16[3,16,2048]{2,1,0:T(8,128)(2,1)} %bitcast.54), channel_id=1, source_target_pairs={{3,0},{0,1},{1,2},{2,3},{7,4},{4,5},{5,6},{6,7},{11,8},{8,9},{9,10... | collective-permute-start | bytes 589832 | tf_op jit(solution)/shard_map/ppermute | solution.py:173
  14.5 3.1 %copy-start.4 = (bf16[16,3,2048]{2,0,1:T(8,128)(2,1)S(1)}, bf16[16,3,2048]{2,0,1:T(8,128)(2,1)}, u32[]{:S(2)}) copy-start(bf16[16,3,2048]{2,0,1:T(8,128)(2,1)} %param.5) | copy-start | bytes 589828
  15.5 14.1 %collective-permute-start.9 = (bf16[4,3,16,2048]{3,2,1,0:T(8,128)(2,1)S(1)}, bf16[4,3,16,2048]{3,2,1,0:T(8,128)(2,1)}, u32[]{:S(2)}, u32[]{:S(2)}) collective-permute-start(bf16[4,3,16,2048]{3,2,1,0:T(8,128)(2,1)S(1)} %pad_maximum_fusion.1.refs_4_), channel_id=1, source_target_pairs={{1,0},{2,1},{3,2},{0,3},{5,4},{6,5},{7,6},{4,7},{9,8},{10,9},{11,1... | collective-permute-start | bytes 2359304 | tf_op jit(solution)/shard_map/ppermute | solution.py:176
  17.7 14.9 %collective-permute-start.3 = (bf16[4,3,16,2048]{3,2,1,0:T(8,128)(2,1)S(1)}, bf16[4,3,16,2048]{3,2,1,0:T(8,128)(2,1)S(1)}, u32[]{:S(2)}, u32[]{:S(2)}) collective-permute-start(bf16[4,3,16,2048]{3,2,1,0:T(8,128)(2,1)S(1)} %pad_maximum_fusion.refs_0_), channel_id=1, source_target_pairs={{4,0},{5,1},{6,2},{7,3},{8,4},{9,5},{10,6},{11,7},{12,8},{13,9},{1... | collective-permute-start | bytes 2359304 | tf_op jit(solution)/shard_map/ppermute | solution.py:176
  18.2 37.6 %collective-permute-start.11 = (bf16[4,3,16,2048]{3,2,1,0:T(8,128)(2,1)S(1)}, bf16[4,3,16,2048]{3,2,1,0:T(8,128)(2,1)}, u32[]{:S(2)}, u32[]{:S(2)}) collective-permute-start(bf16[4,3,16,2048]{3,2,1,0:T(8,128)(2,1)S(1)} %pad_maximum_fusion.1.refs_4_), channel_id=1, source_target_pairs={{3,0},{0,1},{1,2},{2,3},{7,4},{4,5},{5,6},{6,7},{11,8},{8,9},{9,10... | collective-permute-start | bytes 2359304 | tf_op jit(solution)/shard_map/ppermute | solution.py:177
  21.4 34.4 %collective-permute-start.5 = (bf16[4,3,16,2048]{3,2,1,0:T(8,128)(2,1)S(1)}, bf16[4,3,16,2048]{3,2,1,0:T(8,128)(2,1)}, u32[]{:S(2)}, u32[]{:S(2)}) collective-permute-start(bf16[4,3,16,2048]{3,2,1,0:T(8,128)(2,1)S(1)} %pad_maximum_fusion.refs_0_), channel_id=1, source_target_pairs={{12,0},{13,1},{14,2},{15,3},{0,4},{1,5},{2,6},{3,7},{4,8},{5,9},{6... | collective-permute-start | bytes 2359304 | tf_op jit(solution)/shard_map/ppermute | solution.py:177
  29.6 26.2 %collective-permute-start.10 = (bf16[4,3,16,2048]{3,2,1,0:T(8,128)(2,1)}, bf16[4,3,16,2048]{3,2,1,0:T(8,128)(2,1)}, u32[]{:S(2)}, u32[]{:S(2)}) collective-permute-start(bf16[4,3,16,2048]{3,2,1,0:T(8,128)(2,1)} %collective-permute-done.9.refs_5_), channel_id=1, source_target_pairs={{1,0},{2,1},{3,2},{0,3},{5,4},{6,5},{7,6},{4,7},{9,8},{10,9},{11,1... | collective-permute-start | bytes 2359304 | tf_op jit(solution)/shard_map/ppermute | solution.py:178
  32.6 23.2 %collective-permute-start.4 = (bf16[4,3,16,2048]{3,2,1,0:T(8,128)(2,1)S(1)}, bf16[4,3,16,2048]{3,2,1,0:T(8,128)(2,1)}, u32[]{:S(2)}, u32[]{:S(2)}) collective-permute-start(bf16[4,3,16,2048]{3,2,1,0:T(8,128)(2,1)S(1)} %collective-permute-done.3.refs_1_), channel_id=1, source_target_pairs={{4,0},{5,1},{6,2},{7,3},{8,4},{9,5},{10,6},{11,7},{12,8},{13,9},{1... | collective-permute-start | bytes 2359304 | tf_op jit(solution)/shard_map/ppermute | solution.py:178
  35.3 19.6 %all-to-all-start = ((bf16[16,2,16,432]{3,2,1,0:T(8,128)(2,1)}), bf16[16,2,16,432]{3,2,1,0:T(8,128)(2,1)S(1)}, u32[]{:S(2)}, u32[]{:S(2)}) async-start(bf16[16,2,16,432]{3,2,1,0:T(8,128)(2,1)} %split_weights.1), calls=%async_computation | async-start | bytes 1048576 | tf_op jit(solution)/shard_map/all_to_all | solution.py:336
  45.8 96.5 %copy-start.2 = (s32[5]{0:T(128)}, s32[5]{0:T(128)S(1)}, u32[]{:S(2)}) copy-start(s32[5]{0:T(128)S(1)} %stack.88.scalars) | copy-start | bytes 64
  55.7 0.9 copy-start
  63.0 4.0 %collective-permute-start.24 = (f32[256,432]{1,0:T(8,128)S(1)}, f32[256,432]{1,0:T(8,128)S(1)}, u32[]{:S(2)}, u32[]{:S(2)}) collective-permute-start(f32[256,432]{1,0:T(8,128)S(1)} %get-tuple-element.17), channel_id=1, source_target_pairs={{0,16},{16,0},{32,48},{48,32},{64,80},{80,64},{96,112},{112,96},{1... | collective-permute-start | bytes 1327112 | tf_op jit(solution)/shard_map/ppermute | solution.py:302
  67.8 29.9 %all-to-all-start.1 = ((f32[8,32,432]{2,1,0:T(8,128)}), f32[8,32,432]{2,1,0:T(8,128)}, u32[]{:S(2)}, u32[]{:S(2)}) async-start(f32[8,32,432]{2,1,0:T(8,128)} %bitcast.30), calls=%async_computation.1 | async-start | bytes 1048576 | tf_op jit(solution)/shard_map/all_to_all | solution.py:303
  79.7 7.8 %collective-permute-start.20 = (bf16[3,16,2048]{2,1,0:T(8,128)(2,1)S(1)}, bf16[3,16,2048]{2,1,0:T(8,128)(2,1)S(1)}, u32[]{:S(2)}, u32[]{:S(2)}) collective-permute-start(bf16[3,16,2048]{2,1,0:T(8,128)(2,1)S(1)} %get-tuple-element.13), channel_id=1, source_target_pairs={{12,0},{13,1},{14,2},{15,3},{0,4},{1,5},{2,6},{3,7},{4,8},{5,9},{6... | collective-permute-start | bytes 589832 | tf_op jit(solution)/shard_map/ppermute | solution.py:173
  79.7 12.8 %collective-permute-start.19 = (bf16[3,16,2048]{2,1,0:T(8,128)(2,1)S(1)}, bf16[3,16,2048]{2,1,0:T(8,128)(2,1)S(1)}, u32[]{:S(2)}, u32[]{:S(2)}) collective-permute-start(bf16[3,16,2048]{2,1,0:T(8,128)(2,1)S(1)} %get-tuple-element.13), channel_id=1, source_target_pairs={{8,0},{9,1},{10,2},{11,3},{12,4},{13,5},{14,6},{15,7},{0,8},{1,9},... | collective-permute-start | bytes 589832 | tf_op jit(solution)/shard_map/ppermute | solution.py:173
  83.9 8.5 %collective-permute-start.18 = (bf16[3,16,2048]{2,1,0:T(8,128)(2,1)S(1)}, bf16[3,16,2048]{2,1,0:T(8,128)(2,1)S(1)}, u32[]{:S(2)}, u32[]{:S(2)}) collective-permute-start(bf16[3,16,2048]{2,1,0:T(8,128)(2,1)S(1)} %get-tuple-element.13), channel_id=1, source_target_pairs={{4,0},{5,1},{6,2},{7,3},{8,4},{9,5},{10,6},{11,7},{12,8},{13,9},{1... | collective-permute-start | bytes 589832 | tf_op jit(solution)/shard_map/ppermute | solution.py:173
  83.9 9.0 %collective-permute-start.14 = (bf16[3,16,2048]{2,1,0:T(8,128)(2,1)S(1)}, bf16[3,16,2048]{2,1,0:T(8,128)(2,1)S(1)}, u32[]{:S(2)}, u32[]{:S(2)}) collective-permute-start(bf16[3,16,2048]{2,1,0:T(8,128)(2,1)S(1)} %get-tuple-element.12), channel_id=1, source_target_pairs={{3,0},{0,1},{1,2},{2,3},{7,4},{4,5},{5,6},{6,7},{11,8},{8,9},{9,10... | collective-permute-start | bytes 589832 | tf_op jit(solution)/shard_map/ppermute | solution.py:173
  84.1 10.0 %collective-permute-start.13 = (bf16[3,16,2048]{2,1,0:T(8,128)(2,1)S(1)}, bf16[3,16,2048]{2,1,0:T(8,128)(2,1)S(1)}, u32[]{:S(2)}, u32[]{:S(2)}) collective-permute-start(bf16[3,16,2048]{2,1,0:T(8,128)(2,1)S(1)} %get-tuple-element.12), channel_id=1, source_target_pairs={{2,0},{3,1},{0,2},{1,3},{6,4},{7,5},{4,6},{5,7},{10,8},{11,9},{8,1... | collective-permute-start | bytes 589832 | tf_op jit(solution)/shard_map/ppermute | solution.py:173
  87.5 7.8 %collective-permute-start.12 = (bf16[3,16,2048]{2,1,0:T(8,128)(2,1)S(1)}, bf16[3,16,2048]{2,1,0:T(8,128)(2,1)S(1)}, u32[]{:S(2)}, u32[]{:S(2)}) collective-permute-start(bf16[3,16,2048]{2,1,0:T(8,128)(2,1)S(1)} %get-tuple-element.12), channel_id=1, source_target_pairs={{1,0},{2,1},{3,2},{0,3},{5,4},{6,5},{7,6},{4,7},{9,8},{10,9},{11,1... | collective-permute-start | bytes 589832 | tf_op jit(solution)/shard_map/ppermute | solution.py:173
  92.6 36.1 %collective-permute-start.21 = (bf16[4,3,16,2048]{3,2,1,0:T(8,128)(2,1)S(1)}, bf16[4,3,16,2048]{3,2,1,0:T(8,128)(2,1)S(1)}, u32[]{:S(2)}, u32[]{:S(2)}) collective-permute-start(bf16[4,3,16,2048]{3,2,1,0:T(8,128)(2,1)S(1)} %pad_maximum_fusion.3.refs_4_), channel_id=1, source_target_pairs={{1,0},{2,1},{3,2},{0,3},{5,4},{6,5},{7,6},{4,7},{9,8},{10,9},{11,1... | collective-permute-start | bytes 2359304 | tf_op jit(solution)/shard_map/ppermute | solution.py:176
  95.4 34.5 %collective-permute-start.15 = (bf16[4,3,16,2048]{3,2,1,0:T(8,128)(2,1)S(1)}, bf16[4,3,16,2048]{3,2,1,0:T(8,128)(2,1)}, u32[]{:S(2)}, u32[]{:S(2)}) collective-permute-start(bf16[4,3,16,2048]{3,2,1,0:T(8,128)(2,1)S(1)} %pad_maximum_fusion.2.refs_0_), channel_id=1, source_target_pairs={{4,0},{5,1},{6,2},{7,3},{8,4},{9,5},{10,6},{11,7},{12,8},{13,9},{1... | collective-permute-start | bytes 2359304 | tf_op jit(solution)/shard_map/ppermute | solution.py:176
  98.9 5.5 %collective-permute-start.25 = (f32[16,432]{1,0:T(8,128)S(1)}, f32[16,432]{1,0:T(8,128)S(1)}, u32[]{:S(2)}, u32[]{:S(2)}) collective-permute-start(f32[16,432]{1,0:T(8,128)S(1)} %get-tuple-element.24), channel_id=1, source_target_pairs={{16,17},{17,16},{18,49},{19,48},{20,81},{21,80},{22,113},{23,112},... | collective-permute-start | bytes 82952 | tf_op jit(solution)/shard_map/ppermute | solution.py:317
  101.7 2.6 %collective-permute-start.26 = (f32[16,432]{1,0:T(8,128)S(1)}, f32[16,432]{1,0:T(8,128)S(1)}, u32[]{:S(2)}, u32[]{:S(2)}) collective-permute-start(f32[16,432]{1,0:T(8,128)S(1)} %get-tuple-element.25), channel_id=1, source_target_pairs={{16,16},{17,17},{18,48},{19,49},{20,80},{21,81},{22,112},{23,113},... | collective-permute-start | bytes 82952 | tf_op jit(solution)/shard_map/ppermute | solution.py:317
  106.4 29.3 %all-to-all-start.2 = ((f32[8,32,432]{2,1,0:T(8,128)}), f32[8,32,432]{2,1,0:T(8,128)S(1)}, u32[]{:S(2)}, u32[]{:S(2)}) async-start(f32[8,32,432]{2,1,0:T(8,128)} %broadcast_in_dim.2), calls=%async_computation.2 | async-start | bytes 1048576 | tf_op jit(solution)/shard_map/all_to_all | solution.py:323
  123.5 13.4 %collective-permute-start.23 = (bf16[4,3,16,2048]{3,2,1,0:T(8,128)(2,1)S(1)}, bf16[4,3,16,2048]{3,2,1,0:T(8,128)(2,1)}, u32[]{:S(2)}, u32[]{:S(2)}) collective-permute-start(bf16[4,3,16,2048]{3,2,1,0:T(8,128)(2,1)S(1)} %pad_maximum_fusion.3.refs_4_), channel_id=1, source_target_pairs={{3,0},{0,1},{1,2},{2,3},{7,4},{4,5},{5,6},{6,7},{11,8},{8,9},{9,10... | collective-permute-start | bytes 2359304 | tf_op jit(solution)/shard_map/ppermute | solution.py:177
  124.2 13.5 %collective-permute-start.17 = (bf16[4,3,16,2048]{3,2,1,0:T(8,128)(2,1)S(1)}, bf16[4,3,16,2048]{3,2,1,0:T(8,128)(2,1)}, u32[]{:S(2)}, u32[]{:S(2)}) collective-permute-start(bf16[4,3,16,2048]{3,2,1,0:T(8,128)(2,1)S(1)} %pad_maximum_fusion.2.refs_0_), channel_id=1, source_target_pairs={{12,0},{13,1},{14,2},{15,3},{0,4},{1,5},{2,6},{3,7},{4,8},{5,9},{6... | collective-permute-start | bytes 2359304 | tf_op jit(solution)/shard_map/ppermute | solution.py:177
  128.7 12.2 %collective-permute-start.22 = (bf16[4,3,16,2048]{3,2,1,0:T(8,128)(2,1)S(1)}, bf16[4,3,16,2048]{3,2,1,0:T(8,128)(2,1)}, u32[]{:S(2)}, u32[]{:S(2)}) collective-permute-start(bf16[4,3,16,2048]{3,2,1,0:T(8,128)(2,1)S(1)} %collective-permute-done.21.refs_5_), channel_id=1, source_target_pairs={{1,0},{2,1},{3,2},{0,3},{5,4},{6,5},{7,6},{4,7},{9,8},{10,9},{11,1... | collective-permute-start | bytes 2359304 | tf_op jit(solution)/shard_map/ppermute | solution.py:178
  129.9 12.4 %collective-permute-start.16 = (bf16[4,3,16,2048]{3,2,1,0:T(8,128)(2,1)}, bf16[4,3,16,2048]{3,2,1,0:T(8,128)(2,1)}, u32[]{:S(2)}, u32[]{:S(2)}) collective-permute-start(bf16[4,3,16,2048]{3,2,1,0:T(8,128)(2,1)} %collective-permute-done.15.refs_1_), channel_id=1, source_target_pairs={{4,0},{5,1},{6,2},{7,3},{8,4},{9,5},{10,6},{11,7},{12,8},{13,9},{1... | collective-permute-start | bytes 2359304 | tf_op jit(solution)/shard_map/ppermute | solution.py:178
  135.7 12.0 %copy-start.3 = (f32[8,32,432]{2,1,0:T(8,128)}, f32[8,32,432]{2,1,0:T(8,128)S(1)}, u32[]{:S(2)}) copy-start(f32[8,32,432]{2,1,0:T(8,128)S(1)} %all-to-all-done.2) | copy-start | bytes 1327108
  135.7 12.0 %collective-permute-start.27 = (f32[256,432]{1,0:T(8,128)S(1)}, f32[256,432]{1,0:T(8,128)}, u32[]{:S(2)}, u32[]{:S(2)}) collective-permute-start(f32[256,432]{1,0:T(8,128)S(1)} %bitcast.44), channel_id=1, source_target_pairs={{0,16},{16,0},{32,48},{48,32},{64,80},{80,64},{96,112},{112,96},{1... | collective-permute-start | bytes 1327112 | tf_op jit(solution)/shard_map/ppermute | solution.py:324
  135.7 6.6 %copy-start.1 = (bf16[27,16,256]{2,1,0:T(8,128)(2,1)S(1)}, bf16[27,16,256]{2,1,0:T(8,128)(2,1)}, u32[]{:S(2)}) copy-start(bf16[27,16,256]{2,1,0:T(8,128)(2,1)} %w2.1) | copy-start | bytes 663556
where the time goes:
time: 153 us; the launch traced here: 151 us
  starting transfers between devices  77.6 us (51%)
  waiting for transfers between devices  45.8 us (30%)
  Pallas kernels  17.6 us (12%)
  local copies, waits for them, and re-layouts  4.93 us (3%)
  other arithmetic  3.41 us (2%)
    all_to_all x1, starting transfers between devices, sum_over_dp(): lax.all_to_all(copies, 'dp', 0, 0, axis_index_groups=by_core, tiled=True)  17.2 us
    ppermute x12, starting transfers between devices, gather(): lax.ppermute(v, 'filter', from_near(inner, k))  17.1 us
    ppermute x12, waiting for transfers between devices, gather(): lax.ppermute(v, 'filter', from_near(inner, k))  13.4 us
    all_to_all x1, starting transfers between devices, sum_over_dp(): lax.all_to_all(total.reshape(8, 32, ROWS), 'dp', 0, 0, axis_index_groups=...  11.9 us
    ppermute x4, starting transfers between devices, gather(): behind = lax.ppermute(own, both, from_mirrored(outer, 3))  10.8 us
    all_to_all x1, starting transfers between devices, shards(): lax.all_to_all(split_weights(first_weight, second_weight), 'filter', 0, 0...  9.71 us
    all_to_all x1, waiting for transfers between devices, shards(): lax.all_to_all(split_weights(first_weight, second_weight), 'filter', 0, 0...  9.13 us
    ppermute x4, waiting for transfers between devices, gather(): ahead = lax.ppermute(own, both, from_mirrored(outer, 1))  7.76 us
  transfers between devices with their start and end apart: 31, of which 17 were waited for; matrix products, arithmetic and copies ran while one was open for 4% of the time, Pallas kernels for 5%

commit v1 on v0

--- a/solution.py
+++ b/solution.py
@@ -96,13 +96,8 @@
 
 def kernel_one(scalars, *refs):
     px, gx = refs[0:4], refs[4:8]
-    w1, w2t, hid_out, del_out, keep_out, send_out, full_p, full_g, stack, grads = refs[8:]
+    w1, w2t, hid_out, del_out, full_p, full_g = refs[8:]
     s = pl.program_id(0)
-    core = scalars[4]
-
-    @pl.when(s == 0)
-    def _():
-        grads[...] = jnp.zeros_like(grads)
 
     @pl.when(s >= scalars[0])
     def _():
@@ -117,14 +112,29 @@
         first = tap_conv(w1, full_p[...], 1, masks)
         hidden_grad = tap_conv(w2t, full_g[...], -1, masks)
         sigma = 1.0 / (1.0 + jnp.exp(-first))
-        hidden = (first * sigma).astype(jnp.bfloat16)
-        delta = (hidden_grad * sigma * (1.0 + first * (1.0 - sigma))).astype(jnp.bfloat16)
-        hid_out[0] = hidden
-        del_out[0] = delta
-        tap_stack(stack, delta.astype(jnp.float32), -1, masks)
-        grads[0] += over_cells(full_p[...], stack[...])
-        tap_stack(stack, hidden.astype(jnp.float32), 1, masks)
-        grads[1] += over_cells(full_g[...], stack[...])
+        hid_out[0] = (first * sigma).astype(jnp.bfloat16)
+        del_out[0] = (hidden_grad * sigma * (1.0 + first * (1.0 - sigma))).astype(jnp.bfloat16)
+
+
+def kernel_grads(scalars, *refs):
+    px, gx = refs[0:4], refs[4:8]
+    hid, dlt, keep_out, send_out, full, stack, grads = refs[8:]
+    s = pl.program_id(0)
+    core = scalars[4]
+
+    @pl.when(s == 0)
+    def _():
+        grads[...] = jnp.zeros_like(grads)
+
+    @pl.when(s < scalars[0])
+    def _():
+        masks = axis_masks()
+        place(scalars, px, full, True)
+        tap_stack(stack, dlt[0].astype(jnp.float32), -1, masks)
+        grads[0] += over_cells(full[...], stack[...])
+        place(scalars, gx, full, False)
+        tap_stack(stack, hid[0].astype(jnp.float32), 1, masks)
+        grads[1] += over_cells(full[...], stack[...])
 
     @pl.when(s == pl.num_programs(0) - 1)
     def _():
@@ -169,24 +179,39 @@
     return pairs
 
 
-def gather(v, inner, outer):
-    near = [v] + [lax.ppermute(v, "filter", from_near(inner, k)) for k in (1, 2, 3)]
-    own = jnp.stack(near)
+def gather_near(v, inner, first=None):
+    move = lambda k: lax.ppermute(v, "filter", from_near(inner, k))
+    return jnp.stack([v, move(1) if first is None else first, move(2), move(3)])
+
+
+def gather_far(own, outer):
     both = ("dp", "filter")
-    ahead = lax.ppermute(own, both, from_mirrored(outer, 1))
-    behind = lax.ppermute(own, both, from_mirrored(outer, 3))
-    across = lax.ppermute(ahead, both, from_mirrored(outer, 1))
-    return [own, ahead, across, behind]
-
-
-def specs_of(count):
-    piece = pl.BlockSpec((SIDE, 1, BLK, CELLS), lambda s, *_: (0, s, 0, 0))
-    weight = pl.BlockSpec((ROWS, C), lambda s, *_: (0, 0))
-    return [piece] * count + [weight] * 2
+    return own, lax.ppermute(own, both, from_mirrored(outer, 1)), lax.ppermute(own, both, from_mirrored(outer, 3))
+
+
+def gather_last(parts, outer):
+    own, ahead, behind = parts
+    return [own, ahead, lax.ppermute(ahead, ("dp", "filter"), from_mirrored(outer, 1)), behind]
+
+
+def live_slot(s, scalars):
+    return jnp.minimum(s, jnp.maximum(scalars[0] - 1, 0))
+
+
+def piece_specs():
+    return [pl.BlockSpec((SIDE, 1, BLK, CELLS), lambda s, sc: (0, live_slot(s, sc), 0, 0))] * 8
+
+
+def weight_specs():
+    return [pl.BlockSpec((ROWS, C), lambda s, *_: (0, 0))] * 2
 
 
 def slot_spec():
     return pl.BlockSpec((1, BLK, CELLS), lambda s, *_: (s, 0, 0))
+
+
+def params():
+    return pltpu.CompilerParams(vmem_limit_bytes=48 * 1024 * 1024)
 
 
 def call_one(scalars, pieces, w1, w2t):
@@ -198,26 +223,40 @@
         grid_spec=pltpu.PrefetchScalarGridSpec(
             num_scalar_prefetch=1,
             grid=(slots,),
-            in_specs=specs_of(8),
-            out_specs=[
-                slot_spec(),
-                slot_spec(),
-                pl.BlockSpec((C, ROWS), lambda s, *_: (0, 0)),
-                pl.BlockSpec((C, ROWS), lambda s, *_: (0, 0)),
-            ],
+            in_specs=piece_specs() + weight_specs(),
+            out_specs=[slot_spec(), slot_spec()],
+            scratch_shapes=[pltpu.VMEM((C, CELLS), jnp.bfloat16)] * 2,
+        ),
+        out_shape=[flat, flat],
+        compiler_params=params(),
+        cost_estimate=pl.CostEstimate(
+            flops=slots * 4 * ROWS * C * CELLS, transcendentals=slots * BLK * CELLS, bytes_accessed=slots * 4 * C * CELLS
+        ),
+    )(scalars, *pieces, w1, w2t)
+
+
+def call_grads(scalars, pieces, hidden, delta):
+    slots = pieces[0].shape[1]
+    return pl.pallas_call(
+        kernel_grads,
+        name="weight_grads",
+        grid_spec=pltpu.PrefetchScalarGridSpec(
+            num_scalar_prefetch=1,
+            grid=(slots,),
+            in_specs=piece_specs() + [slot_spec(), slot_spec()],
+            out_specs=[pl.BlockSpec((C, ROWS), lambda s, *_: (0, 0))] * 2,
             scratch_shapes=[
-                pltpu.VMEM((C, CELLS), jnp.bfloat16),
                 pltpu.VMEM((C, CELLS), jnp.bfloat16),
                 pltpu.VMEM((ROWS, CELLS), jnp.bfloat16),
                 pltpu.VMEM((2, C, ROWS), jnp.float32),
             ],
         ),
-        out_shape=[flat, flat] + [jax.ShapeDtypeStruct((C, ROWS), jnp.float32)] * 2,
-        compiler_params=pltpu.CompilerParams(vmem_limit_bytes=48 * 1024 * 1024),
+        out_shape=[jax.ShapeDtypeStruct((C, ROWS), jnp.float32)] * 2,
+        compiler_params=params(),
         cost_estimate=pl.CostEstimate(
-            flops=slots * 8 * ROWS * C * CELLS, transcendentals=slots * BLK * CELLS, bytes_accessed=slots * 4 * C * CELLS
-        ),
-    )(scalars, *pieces, w1, w2t)
+            flops=slots * 4 * ROWS * C * CELLS, transcendentals=0, bytes_accessed=slots * 4 * C * CELLS
+        ),
+    )(scalars, *pieces, hidden, delta)
 
 
 def call_two(scalars, pieces, w2, w1t):
@@ -229,7 +268,7 @@
         grid_spec=pltpu.PrefetchScalarGridSpec(
             num_scalar_prefetch=1,
             grid=(slots,),
-            in_specs=specs_of(8),
+            in_specs=piece_specs() + weight_specs(),
             out_specs=[slot_spec(), slot_spec()],
             scratch_shapes=[
                 pltpu.VMEM((C, CELLS), jnp.bfloat16),
@@ -237,9 +276,9 @@
             ],
         ),
         out_shape=[flat, flat],
-        compiler_params=pltpu.CompilerParams(vmem_limit_bytes=48 * 1024 * 1024),
+        compiler_params=params(),
         cost_estimate=pl.CostEstimate(
-            flops=slots * 4 * ROWS * C * CELLS, transcendentals=0, bytes_accessed=slots * 4 * C * CELLS
+            flops=slots * 160 * ROWS * C * CELLS, transcendentals=0, bytes_accessed=slots * 4 * C * CELLS
         ),
     )(scalars, *pieces, w2, w1t)
 
@@ -330,20 +369,30 @@
     me = lax.axis_index("filter")
     core = lax.axis_index("dp") % 2
     scalars = jnp.stack([counts[0], me // SIDE, me % SIDE, 1 - 2 * core, core]).astype(jnp.int32)
-    all_p = gather(patches.transpose(1, 0, 2), "y", "x")
-    all_g = gather(cotangent.transpose(1, 0, 2), "x", "y")
-
-    turned = lax.all_to_all(split_weights(first_weight, second_weight), "filter", 0, 0, tiled=True)
+    split = split_weights(first_weight, second_weight)
+    near_p = gather_near(patches.transpose(1, 0, 2), "y")
+    near_g = gather_near(cotangent.transpose(1, 0, 2), "x")
+    near_g, split = lax.optimization_barrier((near_g, split))
+    far_p = gather_far(near_p, "x")
+    far_g = gather_far(near_g, "y")
+
+    turned = lax.all_to_all(split, "filter", 0, 0, tiled=True)
+    far_p, turned = lax.optimization_barrier((far_p, turned))
+    all_p = gather_last(far_p, "x")
+    all_g = gather_last(far_g, "y")
     w1t = turned[:, 0].reshape(C, ROWS).T
     w2t = turned[:, 1].reshape(C, ROWS).T
     w1 = first_weight.reshape(ROWS, C)
     w2 = second_weight.reshape(ROWS, C)
 
-    hidden, delta, keep, send = call_one(scalars, all_p + all_g, w1, w2t)
+    hidden, delta = call_one(scalars, all_p + all_g, w1, w2t)
+    first_h = lax.ppermute(hidden, "filter", from_near("y", 1))
+    near_h = gather_near(hidden, "y", first_h)
+    near_d = gather_near(delta, "x")
+    keep, send = call_grads(scalars, all_p + all_g, hidden, delta)
+    all_h = gather_last(gather_far(near_h, "x"), "x")
+    all_d = gather_last(gather_far(near_d, "y"), "y")
     first_grad, second_grad = sum_over_dp(scalars, keep, send)
-
-    all_h = gather(hidden, "y", "x")
-    all_d = gather(delta, "x", "y")
     out, in_grad = call_two(scalars, all_h + all_d, w2, w1t)
     return (out.transpose(1, 0, 2), in_grad.transpose(1, 0, 2), first_grad, second_grad)
 

time: 153 us -> 148 us (0.967)
  starting transfers between devices: 77.6 us -> 66.6 us
  waiting for transfers between devices: 45.8 us -> 54.5 us
    ppermute x24, waiting for transfers between devices: 26.5 us -> 16.8 us  [the longest x4 10.6 us: gather_last(): lax.ppermute(ahead, ('dp', 'filter'), from_mirrored(outer, 1))]
    all_to_all x1, waiting for transfers between devices: 0.89 us -> 10.5 us  [sum_over_dp(): lax.all_to_all(total.reshape(8, 32, ROWS), 'dp', 0, 0, axis_index_groups=...]
    all_to_all x1, waiting for transfers between devices: 9.13 us -> 16.2 us  [shards(): turned = lax.all_to_all(split, 'filter', 0, 0, tiled=True)]
    all_to_all x1, starting transfers between devices: 17.2 us -> 10.5 us  [sum_over_dp(): lax.all_to_all(copies, 'dp', 0, 0, axis_index_groups=by_core, tiled=True)]
    all_to_all x1, waiting for transfers between devices: 5.8 us -> 11 us  [sum_over_dp(): lax.all_to_all(copies, 'dp', 0, 0, axis_index_groups=by_core, tiled=True)]
    pallas_call x0 -> x1, Pallas kernels: none -> 3.76 us  [call_grads(): pl.pallas_call(kernel_grads, name='weight_grads', grid_spec=pltpu.Prefetc...]
    all_to_all x1, starting transfers between devices: 9.71 us -> 6.61 us  [shards(): turned = lax.all_to_all(split, 'filter', 0, 0, tiled=True)]
    pallas_call x1, Pallas kernels: 6.34 us -> 3.57 us  [call_one(): pl.pallas_call(kernel_one, name='layer_one', grid_spec=pltpu.PrefetchScal...]
  transfers between devices with their start and end apart: 31 -> 31, of which waited for: 17 -> 11; matrix products, arithmetic and copies ran while one was open for 4% -> 4% of each run, Pallas kernels for 5% -> 5%
where the time goes in v1:
time: 148 us; the launch traced here: 147 us
  starting transfers between devices  66.6 us (45%)
  waiting for transfers between devices  54.5 us (37%)
  Pallas kernels  17.9 us (12%)
  local copies, waits for them, and re-layouts  4.03 us (3%)
  other arithmetic  2.44 us (2%)
  between operations  1.53 us (1%)
    all_to_all x1, waiting for transfers between devices, shards(): turned = lax.all_to_all(split, 'filter', 0, 0, tiled=True)  16.2 us
    ppermute x11, starting transfers between devices, gather_near(): move = lambda k: lax.ppermute(v, 'filter', from_near(inner, k))  15 us
    ppermute x4, starting transfers between devices, gather_far(): lax.ppermute(own, both, from_mirrored(outer, 3))  13 us
    all_to_all x1, starting transfers between devices, sum_over_dp(): lax.all_to_all(total.reshape(8, 32, ROWS), 'dp', 0, 0, axis_index_groups=...  12.9 us
    all_to_all x1, waiting for transfers between devices, sum_over_dp(): lax.all_to_all(copies, 'dp', 0, 0, axis_index_groups=by_core, tiled=True)  11 us
    ppermute x4, waiting for transfers between devices, gather_last(): lax.ppermute(ahead, ('dp', 'filter'), from_mirrored(outer, 1))  10.6 us
    all_to_all x1, starting transfers between devices, sum_over_dp(): lax.all_to_all(copies, 'dp', 0, 0, axis_index_groups=by_core, tiled=True)  10.5 us
    all_to_all x1, waiting for transfers between devices, sum_over_dp(): lax.all_to_all(total.reshape(8, 32, ROWS), 'dp', 0, 0, axis_index_groups=...  10.5 us
  transfers between devices with their start and end apart: 31, of which 11 were waited for; matrix products, arithmetic and copies ran while one was open for 4% of the time, Pallas kernels for 5%

profile of v1, /device:TPU:1, one launch (start us, length us, event | category | flops | bytes accessed | tf_op | source)
XLA Modules:
  0.0 147.0 jit_solution(3524770707877381174)
XLA Ops:
  0.6 3.8 %collective-permute-start.1 = (bf16[3,16,2048]{2,1,0:T(8,128)(2,1)}, bf16[3,16,2048]{2,1,0:T(8,128)(2,1)S(1)}, u32[]{:S(2)}, u32[]{:S(2)}) collective-permute-start(bf16[3,16,2048]{2,1,0:T(8,128)(2,1)} %bitcast.48), channel_id=1, source_target_pairs={{2,0},{3,1},{0,2},{1,3},{6,4},{7,5},{4,6},{5,7},{10,8},{11,9},{8,1... | collective-permute-start | bytes 589832 | tf_op jit(solution)/shard_map/ppermute | solution.py:183
  4.5 0.8 collective-permute-start
  5.2 0.7 collective-permute-start.2
  5.9 2.7 %collective-permute-start.6 = (bf16[3,16,2048]{2,1,0:T(8,128)(2,1)}, bf16[3,16,2048]{2,1,0:T(8,128)(2,1)S(1)}, u32[]{:S(2)}, u32[]{:S(2)}) collective-permute-start(bf16[3,16,2048]{2,1,0:T(8,128)(2,1)} %bitcast.52), channel_id=1, source_target_pairs={{8,0},{9,1},{10,2},{11,3},{12,4},{13,5},{14,6},{15,7},{0,8},{1,9},... | collective-permute-start | bytes 589832 | tf_op jit(solution)/shard_map/ppermute | solution.py:183
  8.7 0.9 collective-permute-start.5
  9.5 2.7 %split_weights.1 = bf16[16,2,16,432]{3,2,1,0:T(8,128)(2,1)} custom-call(bf16[27,16,256]{2,1,0:T(8,128)(2,1)} %w1.1, bf16[27,16,256]{2,1,0:T(8,128)(2,1)} %w2.1), custom_call_target="tpu_custom_call" | custom-call | bytes 884736 | tf_op jit(solution)/shard_map/split_weights/pallas_call | solution.py:304
  12.3 0.6 collective-permute-start.7
  12.9 0.9 collective-permute-done
  13.7 0.8 collective-permute-done.2
  14.6 1.8 %collective-permute-start.4 = (bf16[4,3,16,2048]{3,2,1,0:T(8,128)(2,1)S(1)}, bf16[4,3,16,2048]{3,2,1,0:T(8,128)(2,1)S(1)}, u32[]{:S(2)}, u32[]{:S(2)}) collective-permute-start(bf16[4,3,16,2048]{3,2,1,0:T(8,128)(2,1)S(1)} %pad_maximum_fusion.refs_0_), channel_id=1, source_target_pairs={{12,0},{13,1},{14,2},{15,3},{0,4},{1,5},{2,6},{3,7},{4,8},{5,9},{6... | collective-permute-start | bytes 2359304 | tf_op jit(solution)/shard_map/ppermute | solution.py:189
  16.4 1.0 collective-permute-done.5
  17.4 0.6 collective-permute-done.7
  18.1 0.5 collective-permute-start.9
  18.6 6.6 %all-to-all-start = ((bf16[16,2,16,432]{3,2,1,0:T(8,128)(2,1)}), bf16[16,2,16,432]{3,2,1,0:T(8,128)(2,1)S(1)}, u32[]{:S(2)}, u32[]{:S(2)}) async-start(bf16[16,2,16,432]{3,2,1,0:T(8,128)(2,1)} %split_weights.1), calls=%async_computation | async-start | bytes 1048576 | tf_op jit(solution)/shard_map/all_to_all | solution.py:379
  25.2 2.6 %collective-permute-start.11 = (bf16[4,3,16,2048]{3,2,1,0:T(8,128)(2,1)S(1)}, bf16[4,3,16,2048]{3,2,1,0:T(8,128)(2,1)}, u32[]{:S(2)}, u32[]{:S(2)}) collective-permute-start(bf16[4,3,16,2048]{3,2,1,0:T(8,128)(2,1)S(1)} %pad_maximum_fusion.1.refs_4_), channel_id=1, source_target_pairs={{3,0},{0,1},{1,2},{2,3},{7,4},{4,5},{5,6},{6,7},{11,8},{8,9},{9,10... | collective-permute-start | bytes 2359304 | tf_op jit(solution)/shard_map/ppermute | solution.py:189
  27.8 16.2 %all-to-all-done = bf16[16,2,16,432]{3,2,1,0:T(8,128)(2,1)S(1)} async-done(((bf16[16,2,16,432]{3,2,1,0:T(8,128)(2,1)}), bf16[16,2,16,432]{3,2,1,0:T(8,128)(2,1)S(1)}, u32[]{:S(2)}, u32[]{:S(2)}) %all-to-all-start) | async-done | bytes 442400 | tf_op jit(solution)/shard_map/all_to_all | solution.py:379
  44.0 1.5 %collective-permute-start.10 = (bf16[4,3,16,2048]{3,2,1,0:T(8,128)(2,1)}, bf16[4,3,16,2048]{3,2,1,0:T(8,128)(2,1)}, u32[]{:S(2)}, u32[]{:S(2)}) collective-permute-start(bf16[4,3,16,2048]{3,2,1,0:T(8,128)(2,1)} %collective-permute-done.9.refs_5_), channel_id=1, source_target_pairs={{1,0},{2,1},{3,2},{0,3},{5,4},{6,5},{7,6},{4,7},{9,8},{10,9},{11,1... | collective-permute-start | bytes 2359304 | tf_op jit(solution)/shard_map/ppermute | solution.py:194
  46.3 0.7 fusion
  47.2 0.1 collective-permute-done.11.refs_7_
  47.3 9.2 %collective-permute-done.10.refs_6_ = bf16[4,3,16,2048]{3,2,1,0:T(8,128)(2,1)} collective-permute-done((bf16[4,3,16,2048]{3,2,1,0:T(8,128)(2,1)}, bf16[4,3,16,2048]{3,2,1,0:T(8,128)(2,1)}, u32[]{:S(2)}, u32[]{:S(2)}) %collective-permute-start.10) | collective-permute-done | bytes 786464 | tf_op jit(solution)/shard_map/ppermute | solution.py:194
  56.5 1.4 collective-permute-done.8.refs_2_
  57.9 3.6 %layer_one.1 = (bf16[3,16,2048]{2,1,0:T(8,128)(2,1)S(1)}, bf16[3,16,2048]{2,1,0:T(8,128)(2,1)S(1)}) custom-call(s32[5]{0:T(128)S(1)} %stack.88.scalars, bf16[4,3,16,2048]{3,2,1,0:T(8,128)(2,1)S(1)} %pad_maximum_fusion.refs_0_, bf16[4,3,16,2048]{3,2,1,0:T(8,128)(2,1)} %collective-permute-done.3.refs_1_, ...), custom_call_target="tpu_custom_call" | custom-call | flops 2717908992 | bytes 6291456 | tf_op jit(solution)/shard_map/layer_one/pallas_call | solution.py:220
  61.5 3.8 %weight_grads.1 = (f32[256,432]{1,0:T(8,128)S(1)}, f32[256,432]{1,0:T(8,128)S(1)}) custom-call(s32[5]{0:T(128)S(1)} %stack.88.scalars, bf16[4,3,16,2048]{3,2,1,0:T(8,128)(2,1)S(1)} %pad_maximum_fusion.refs_0_, bf16[4,3,16,2048]{3,2,1,0:T(8,128)(2,1)} %collective-permute-done.3.refs_1_, bf16[4,3,16,2048]{3,2,1,0:T(8,128)(2,1)} %collective-permute-done.8.refs_2_, ...), custom_call_target="tpu_custom_call" | custom-call | flops 2717908992 | bytes 6291456 | tf_op jit(solution)/shard_map/weight_grads/pallas_call | solution.py:240
  65.4 1.6 %collective-permute-start.19 = (bf16[3,16,2048]{2,1,0:T(8,128)(2,1)S(1)}, bf16[3,16,2048]{2,1,0:T(8,128)(2,1)S(1)}, u32[]{:S(2)}, u32[]{:S(2)}) collective-permute-start(bf16[3,16,2048]{2,1,0:T(8,128)(2,1)S(1)} %get-tuple-element.25.refs_9_), channel_id=1, source_target_pairs={{8,0},{9,1},{10,2},{11,3},{12,4},{13,5},{14,6},{15,7},{0,8},{1,9},... | collective-permute-start | bytes 589832 | tf_op jit(solution)/shard_map/ppermute | solution.py:183
  67.1 1.0 collective-permute-start.18
  68.1 0.3 collective-permute-start.14
  68.4 2.5 %collective-permute-start.13 = (bf16[3,16,2048]{2,1,0:T(8,128)(2,1)S(1)}, bf16[3,16,2048]{2,1,0:T(8,128)(2,1)S(1)}, u32[]{:S(2)}, u32[]{:S(2)}) collective-permute-start(bf16[3,16,2048]{2,1,0:T(8,128)(2,1)S(1)} %get-tuple-element.24.refs_8_), channel_id=1, source_target_pairs={{2,0},{3,1},{0,2},{1,3},{6,4},{7,5},{4,6},{5,7},{10,8},{11,9},{8,1... | collective-permute-start | bytes 589832 | tf_op jit(solution)/shard_map/ppermute | solution.py:183
  70.8 0.9 add.16
  71.7 12.9 %all-to-all-start.1 = ((f32[8,32,432]{2,1,0:T(8,128)}), f32[8,32,432]{2,1,0:T(8,128)}, u32[]{:S(2)}, u32[]{:S(2)}) async-start(f32[8,32,432]{2,1,0:T(8,128)} %bitcast.30), calls=%async_computation.1 | async-start | bytes 1048576 | tf_op jit(solution)/shard_map/all_to_all | solution.py:342
  84.6 0.6 collective-permute-start.12
  85.4 1.0 collective-permute-start.21
  86.4 2.9 %collective-permute-done.12 = bf16[3,16,2048]{2,1,0:T(8,128)(2,1)S(1)} collective-permute-done((bf16[3,16,2048]{2,1,0:T(8,128)(2,1)S(1)}, bf16[3,16,2048]{2,1,0:T(8,128)(2,1)S(1)}, u32[]{:S(2)}, u32[]{:S(2)}) %collective-permute-start.12) | collective-permute-done | bytes 196640 | tf_op jit(solution)/shard_map/ppermute | solution.py:389
  89.3 1.0 collective-permute-start.15
  90.3 10.5 %all-to-all-done.1 = f32[8,32,432]{2,1,0:T(8,128)} async-done(((f32[8,32,432]{2,1,0:T(8,128)}), f32[8,32,432]{2,1,0:T(8,128)}, u32[]{:S(2)}, u32[]{:S(2)}) %all-to-all-start.1) | async-done | bytes 442400 | tf_op jit(solution)/shard_map/all_to_all | solution.py:342
  100.8 1.1 reduce_sum.9
  101.9 3.0 %collective-permute-start.25 = (f32[16,432]{1,0:T(8,128)S(1)}, f32[16,432]{1,0:T(8,128)S(1)}, u32[]{:S(2)}, u32[]{:S(2)}) collective-permute-start(f32[16,432]{1,0:T(8,128)S(1)} %get-tuple-element.36), channel_id=1, source_target_pairs={{16,17},{17,16},{18,49},{19,48},{20,81},{21,80},{22,113},{23,112},... | collective-permute-start | bytes 82952 | tf_op jit(solution)/shard_map/ppermute | solution.py:356
  104.9 0.7 collective-permute-start.26
  105.6 4.5 %collective-permute-start.23 = (bf16[4,3,16,2048]{3,2,1,0:T(8,128)(2,1)S(1)}, bf16[4,3,16,2048]{3,2,1,0:T(8,128)(2,1)}, u32[]{:S(2)}, u32[]{:S(2)}) collective-permute-start(bf16[4,3,16,2048]{3,2,1,0:T(8,128)(2,1)S(1)} %pad_maximum_fusion.3.refs_4_), channel_id=1, source_target_pairs={{3,0},{0,1},{1,2},{2,3},{7,4},{4,5},{5,6},{6,7},{11,8},{8,9},{9,10... | collective-permute-start | bytes 2359304 | tf_op jit(solution)/shard_map/ppermute | solution.py:189
  110.1 4.1 %collective-permute-start.17 = (bf16[4,3,16,2048]{3,2,1,0:T(8,128)(2,1)S(1)}, bf16[4,3,16,2048]{3,2,1,0:T(8,128)(2,1)}, u32[]{:S(2)}, u32[]{:S(2)}) collective-permute-start(bf16[4,3,16,2048]{3,2,1,0:T(8,128)(2,1)S(1)} %pad_maximum_fusion.2.refs_0_), channel_id=1, source_target_pairs={{12,0},{13,1},{14,2},{15,3},{0,4},{1,5},{2,6},{3,7},{4,8},{5,9},{6... | collective-permute-start | bytes 2359304 | tf_op jit(solution)/shard_map/ppermute | solution.py:189
  114.2 0.1 collective-permute-start.22
  114.7 0.6 copy.15
  115.3 0.2 reshape.45
  115.5 0.9 broadcast_in_dim.2
  116.4 10.5 %all-to-all-start.2 = ((f32[8,32,432]{2,1,0:T(8,128)}), f32[8,32,432]{2,1,0:T(8,128)S(1)}, u32[]{:S(2)}, u32[]{:S(2)}) async-start(f32[8,32,432]{2,1,0:T(8,128)} %broadcast_in_dim.2), calls=%async_computation.2 | async-start | bytes 1048576 | tf_op jit(solution)/shard_map/all_to_all | solution.py:362
  127.0 1.1 copy.14
  128.1 11.0 %all-to-all-done.2 = f32[8,32,432]{2,1,0:T(8,128)S(1)} async-done(((f32[8,32,432]{2,1,0:T(8,128)}), f32[8,32,432]{2,1,0:T(8,128)S(1)}, u32[]{:S(2)}, u32[]{:S(2)}) %all-to-all-start.2) | async-done | bytes 442400 | tf_op jit(solution)/shard_map/all_to_all | solution.py:362
  139.2 4.7 %layer_two.1 = (f32[3,16,2048]{2,1,0:T(8,128)}, f32[3,16,2048]{2,1,0:T(8,128)}) custom-call(s32[5]{0:T(128)S(1)} %stack.88.scalars, bf16[4,3,16,2048]{3,2,1,0:T(8,128)(2,1)S(1)} %pad_maximum_fusion.2.refs_0_, bf16[4,3,16,2048]{3,2,1,0:T(8,128)(2,1)} %collective-permute-done.15.refs_1_, bf16[4,3,16,2048]{3,2,1,0:T(8,128)(2,1)} %collective-permute-done.16.refs_2_, ...), custom_call_target="tpu_custom_call" | custom-call | flops 108716359680 | bytes 6291456 | tf_op jit(solution)/shard_map/layer_two/pallas_call | solution.py:265
  143.9 3.1 %finish_gradients.1 = (f32[432,256]{1,0:T(8,128)}, f32[432,256]{1,0:T(8,128)}) custom-call(s32[5]{0:T(128)} %copy-done.2, f32[256,432]{1,0:T(8,128)} %bitcast.45, f32[256,432]{1,0:T(8,128)} %collective-permute-done.27.other), custom_call_target="tpu_custom_call" | custom-call | bytes 1769472 | tf_op jit(solution)/shard_map/finish_gradients/pallas_call | solution.py:327
  (51 shorter events, 1.2 us)
Async XLA Ops:
  0.6 11.6 %collective-permute-start.1 = (bf16[3,16,2048]{2,1,0:T(8,128)(2,1)}, bf16[3,16,2048]{2,1,0:T(8,128)(2,1)S(1)}, u32[]{:S(2)}, u32[]{:S(2)}) collective-permute-start(bf16[3,16,2048]{2,1,0:T(8,128)(2,1)} %bitcast.48), channel_id=1, source_target_pairs={{2,0},{3,1},{0,2},{1,3},{6,4},{7,5},{4,6},{5,7},{10,8},{11,9},{8,1... | collective-permute-start | bytes 589832 | tf_op jit(solution)/shard_map/ppermute | solution.py:183
  4.5 9.3 %collective-permute-start = (bf16[3,16,2048]{2,1,0:T(8,128)(2,1)}, bf16[3,16,2048]{2,1,0:T(8,128)(2,1)S(1)}, u32[]{:S(2)}, u32[]{:S(2)}) collective-permute-start(bf16[3,16,2048]{2,1,0:T(8,128)(2,1)} %bitcast.49), channel_id=1, source_target_pairs={{1,0},{2,1},{3,2},{0,3},{5,4},{6,5},{7,6},{4,7},{9,8},{10,9},{11,1... | collective-permute-start | bytes 589832 | tf_op jit(solution)/shard_map/ppermute | solution.py:183
  5.2 9.2 %collective-permute-start.2 = (bf16[3,16,2048]{2,1,0:T(8,128)(2,1)}, bf16[3,16,2048]{2,1,0:T(8,128)(2,1)S(1)}, u32[]{:S(2)}, u32[]{:S(2)}) collective-permute-start(bf16[3,16,2048]{2,1,0:T(8,128)(2,1)} %bitcast.50), channel_id=1, source_target_pairs={{3,0},{0,1},{1,2},{2,3},{7,4},{4,5},{5,6},{6,7},{11,8},{8,9},{9,10... | collective-permute-start | bytes 589832 | tf_op jit(solution)/shard_map/ppermute | solution.py:183
  5.9 6.3 %copy-start.5 = (bf16[16,3,2048]{2,0,1:T(8,128)(2,1)S(1)}, bf16[16,3,2048]{2,0,1:T(8,128)(2,1)}, u32[]{:S(2)}) copy-start(bf16[16,3,2048]{2,0,1:T(8,128)(2,1)} %param.6) | copy-start | bytes 589828
  5.9 8.6 %copy-start.4 = (bf16[16,3,2048]{2,0,1:T(8,128)(2,1)S(1)}, bf16[16,3,2048]{2,0,1:T(8,128)(2,1)}, u32[]{:S(2)}) copy-start(bf16[16,3,2048]{2,0,1:T(8,128)(2,1)} %param.5) | copy-start | bytes 589828
  5.9 10.5 %collective-permute-start.6 = (bf16[3,16,2048]{2,1,0:T(8,128)(2,1)}, bf16[3,16,2048]{2,1,0:T(8,128)(2,1)S(1)}, u32[]{:S(2)}, u32[]{:S(2)}) collective-permute-start(bf16[3,16,2048]{2,1,0:T(8,128)(2,1)} %bitcast.52), channel_id=1, source_target_pairs={{8,0},{9,1},{10,2},{11,3},{12,4},{13,5},{14,6},{15,7},{0,8},{1,9},... | collective-permute-start | bytes 589832 | tf_op jit(solution)/shard_map/ppermute | solution.py:183
  8.7 8.8 %collective-permute-start.5 = (bf16[3,16,2048]{2,1,0:T(8,128)(2,1)}, bf16[3,16,2048]{2,1,0:T(8,128)(2,1)S(1)}, u32[]{:S(2)}, u32[]{:S(2)}) collective-permute-start(bf16[3,16,2048]{2,1,0:T(8,128)(2,1)} %bitcast.53), channel_id=1, source_target_pairs={{4,0},{5,1},{6,2},{7,3},{8,4},{9,5},{10,6},{11,7},{12,8},{13,9},{1... | collective-permute-start | bytes 589832 | tf_op jit(solution)/shard_map/ppermute | solution.py:183
  12.3 5.7 %collective-permute-start.7 = (bf16[3,16,2048]{2,1,0:T(8,128)(2,1)S(1)}, bf16[3,16,2048]{2,1,0:T(8,128)(2,1)S(1)}, u32[]{:S(2)}, u32[]{:S(2)}) collective-permute-start(bf16[3,16,2048]{2,1,0:T(8,128)(2,1)S(1)} %bitcast.54), channel_id=1, source_target_pairs={{12,0},{13,1},{14,2},{15,3},{0,4},{1,5},{2,6},{3,7},{4,8},{5,9},{6... | collective-permute-start | bytes 589832 | tf_op jit(solution)/shard_map/ppermute | solution.py:183
  14.6 29.4 %collective-permute-start.4 = (bf16[4,3,16,2048]{3,2,1,0:T(8,128)(2,1)S(1)}, bf16[4,3,16,2048]{3,2,1,0:T(8,128)(2,1)S(1)}, u32[]{:S(2)}, u32[]{:S(2)}) collective-permute-start(bf16[4,3,16,2048]{3,2,1,0:T(8,128)(2,1)S(1)} %pad_maximum_fusion.refs_0_), channel_id=1, source_target_pairs={{12,0},{13,1},{14,2},{15,3},{0,4},{1,5},{2,6},{3,7},{4,8},{5,9},{6... | collective-permute-start | bytes 2359304 | tf_op jit(solution)/shard_map/ppermute | solution.py:189
  16.4 27.6 %collective-permute-start.3 = (bf16[4,3,16,2048]{3,2,1,0:T(8,128)(2,1)S(1)}, bf16[4,3,16,2048]{3,2,1,0:T(8,128)(2,1)}, u32[]{:S(2)}, u32[]{:S(2)}) collective-permute-start(bf16[4,3,16,2048]{3,2,1,0:T(8,128)(2,1)S(1)} %pad_maximum_fusion.refs_0_), channel_id=1, source_target_pairs={{4,0},{5,1},{6,2},{7,3},{8,4},{9,5},{10,6},{11,7},{12,8},{13,9},{1... | collective-permute-start | bytes 2359304 | tf_op jit(solution)/shard_map/ppermute | solution.py:189
  18.1 25.9 %collective-permute-start.9 = (bf16[4,3,16,2048]{3,2,1,0:T(8,128)(2,1)S(1)}, bf16[4,3,16,2048]{3,2,1,0:T(8,128)(2,1)}, u32[]{:S(2)}, u32[]{:S(2)}) collective-permute-start(bf16[4,3,16,2048]{3,2,1,0:T(8,128)(2,1)S(1)} %pad_maximum_fusion.1.refs_4_), channel_id=1, source_target_pairs={{1,0},{2,1},{3,2},{0,3},{5,4},{6,5},{7,6},{4,7},{9,8},{10,9},{11,1... | collective-permute-start | bytes 2359304 | tf_op jit(solution)/shard_map/ppermute | solution.py:189
  18.6 25.4 %all-to-all-start = ((bf16[16,2,16,432]{3,2,1,0:T(8,128)(2,1)}), bf16[16,2,16,432]{3,2,1,0:T(8,128)(2,1)S(1)}, u32[]{:S(2)}, u32[]{:S(2)}) async-start(bf16[16,2,16,432]{3,2,1,0:T(8,128)(2,1)} %split_weights.1), calls=%async_computation | async-start | bytes 1048576 | tf_op jit(solution)/shard_map/all_to_all | solution.py:379
  25.2 22.1 %collective-permute-start.11 = (bf16[4,3,16,2048]{3,2,1,0:T(8,128)(2,1)S(1)}, bf16[4,3,16,2048]{3,2,1,0:T(8,128)(2,1)}, u32[]{:S(2)}, u32[]{:S(2)}) collective-permute-start(bf16[4,3,16,2048]{3,2,1,0:T(8,128)(2,1)S(1)} %pad_maximum_fusion.1.refs_4_), channel_id=1, source_target_pairs={{3,0},{0,1},{1,2},{2,3},{7,4},{4,5},{5,6},{6,7},{11,8},{8,9},{9,10... | collective-permute-start | bytes 2359304 | tf_op jit(solution)/shard_map/ppermute | solution.py:189
  44.0 12.4 %collective-permute-start.10 = (bf16[4,3,16,2048]{3,2,1,0:T(8,128)(2,1)}, bf16[4,3,16,2048]{3,2,1,0:T(8,128)(2,1)}, u32[]{:S(2)}, u32[]{:S(2)}) collective-permute-start(bf16[4,3,16,2048]{3,2,1,0:T(8,128)(2,1)} %collective-permute-done.9.refs_5_), channel_id=1, source_target_pairs={{1,0},{2,1},{3,2},{0,3},{5,4},{6,5},{7,6},{4,7},{9,8},{10,9},{11,1... | collective-permute-start | bytes 2359304 | tf_op jit(solution)/shard_map/ppermute | solution.py:194
  45.5 12.4 %collective-permute-start.8 = (bf16[4,3,16,2048]{3,2,1,0:T(8,128)(2,1)}, bf16[4,3,16,2048]{3,2,1,0:T(8,128)(2,1)}, u32[]{:S(2)}, u32[]{:S(2)}) collective-permute-start(bf16[4,3,16,2048]{3,2,1,0:T(8,128)(2,1)} %collective-permute-done.3.refs_1_), channel_id=1, source_target_pairs={{4,0},{5,1},{6,2},{7,3},{8,4},{9,5},{10,6},{11,7},{12,8},{13,9},{1... | collective-permute-start | bytes 2359304 | tf_op jit(solution)/shard_map/ppermute | solution.py:194
  46.3 92.9 %copy-start.2 = (s32[5]{0:T(128)}, s32[5]{0:T(128)S(1)}, u32[]{:S(2)}) copy-start(s32[5]{0:T(128)S(1)} %stack.88.scalars) | copy-start | bytes 64
  47.0 10.9 %copy-start = (bf16[27,16,256]{2,1,0:T(8,128)(2,1)S(1)}, bf16[27,16,256]{2,1,0:T(8,128)(2,1)}, u32[]{:S(2)}) copy-start(bf16[27,16,256]{2,1,0:T(8,128)(2,1)} %w1.1) | copy-start | bytes 663556
  65.2 3.1 %collective-permute-start.24 = (f32[256,432]{1,0:T(8,128)S(1)}, f32[256,432]{1,0:T(8,128)S(1)}, u32[]{:S(2)}, u32[]{:S(2)}) collective-permute-start(f32[256,432]{1,0:T(8,128)S(1)} %get-tuple-element.29), channel_id=1, source_target_pairs={{0,16},{16,0},{32,48},{48,32},{64,80},{80,64},{96,112},{112,96},{1... | collective-permute-start | bytes 1327112 | tf_op jit(solution)/shard_map/ppermute | solution.py:341
  65.3 19.3 %collective-permute-start.20 = (bf16[3,16,2048]{2,1,0:T(8,128)(2,1)S(1)}, bf16[3,16,2048]{2,1,0:T(8,128)(2,1)S(1)}, u32[]{:S(2)}, u32[]{:S(2)}) collective-permute-start(bf16[3,16,2048]{2,1,0:T(8,128)(2,1)S(1)} %get-tuple-element.25.refs_9_), channel_id=1, source_target_pairs={{12,0},{13,1},{14,2},{15,3},{0,4},{1,5},{2,6},{3,7},{4,8},{5,9},{6... | collective-permute-start | bytes 589832 | tf_op jit(solution)/shard_map/ppermute | solution.py:183
  65.4 19.8 %collective-permute-start.19 = (bf16[3,16,2048]{2,1,0:T(8,128)(2,1)S(1)}, bf16[3,16,2048]{2,1,0:T(8,128)(2,1)S(1)}, u32[]{:S(2)}, u32[]{:S(2)}) collective-permute-start(bf16[3,16,2048]{2,1,0:T(8,128)(2,1)S(1)} %get-tuple-element.25.refs_9_), channel_id=1, source_target_pairs={{8,0},{9,1},{10,2},{11,3},{12,4},{13,5},{14,6},{15,7},{0,8},{1,9},... | collective-permute-start | bytes 589832 | tf_op jit(solution)/shard_map/ppermute | solution.py:183
  67.1 18.2 %collective-permute-start.18 = (bf16[3,16,2048]{2,1,0:T(8,128)(2,1)S(1)}, bf16[3,16,2048]{2,1,0:T(8,128)(2,1)S(1)}, u32[]{:S(2)}, u32[]{:S(2)}) collective-permute-start(bf16[3,16,2048]{2,1,0:T(8,128)(2,1)S(1)} %get-tuple-element.25.refs_9_), channel_id=1, source_target_pairs={{4,0},{5,1},{6,2},{7,3},{8,4},{9,5},{10,6},{11,7},{12,8},{13,9},{1... | collective-permute-start | bytes 589832 | tf_op jit(solution)/shard_map/ppermute | solution.py:183
  68.1 18.3 %collective-permute-start.14 = (bf16[3,16,2048]{2,1,0:T(8,128)(2,1)S(1)}, bf16[3,16,2048]{2,1,0:T(8,128)(2,1)S(1)}, u32[]{:S(2)}, u32[]{:S(2)}) collective-permute-start(bf16[3,16,2048]{2,1,0:T(8,128)(2,1)S(1)} %get-tuple-element.24.refs_8_), channel_id=1, source_target_pairs={{3,0},{0,1},{1,2},{2,3},{7,4},{4,5},{5,6},{6,7},{11,8},{8,9},{9,10... | collective-permute-start | bytes 589832 | tf_op jit(solution)/shard_map/ppermute | solution.py:183
  68.4 18.0 %collective-permute-start.13 = (bf16[3,16,2048]{2,1,0:T(8,128)(2,1)S(1)}, bf16[3,16,2048]{2,1,0:T(8,128)(2,1)S(1)}, u32[]{:S(2)}, u32[]{:S(2)}) collective-permute-start(bf16[3,16,2048]{2,1,0:T(8,128)(2,1)S(1)} %get-tuple-element.24.refs_8_), channel_id=1, source_target_pairs={{2,0},{3,1},{0,2},{1,3},{6,4},{7,5},{4,6},{5,7},{10,8},{11,9},{8,1... | collective-permute-start | bytes 589832 | tf_op jit(solution)/shard_map/ppermute | solution.py:183
  71.7 29.1 %all-to-all-start.1 = ((f32[8,32,432]{2,1,0:T(8,128)}), f32[8,32,432]{2,1,0:T(8,128)}, u32[]{:S(2)}, u32[]{:S(2)}) async-start(f32[8,32,432]{2,1,0:T(8,128)} %bitcast.30), calls=%async_computation.1 | async-start | bytes 1048576 | tf_op jit(solution)/shard_map/all_to_all | solution.py:342
  84.6 4.6 %collective-permute-start.12 = (bf16[3,16,2048]{2,1,0:T(8,128)(2,1)S(1)}, bf16[3,16,2048]{2,1,0:T(8,128)(2,1)S(1)}, u32[]{:S(2)}, u32[]{:S(2)}) collective-permute-start(bf16[3,16,2048]{2,1,0:T(8,128)(2,1)S(1)} %get-tuple-element.24.refs_8_), channel_id=1, source_target_pairs={{1,0},{2,1},{3,2},{0,3},{5,4},{6,5},{7,6},{4,7},{9,8},{10,9},{11,1... | collective-permute-start | bytes 589832 | tf_op jit(solution)/shard_map/ppermute | solution.py:389
  85.4 24.8 %collective-permute-start.21 = (bf16[4,3,16,2048]{3,2,1,0:T(8,128)(2,1)S(1)}, bf16[4,3,16,2048]{3,2,1,0:T(8,128)(2,1)S(1)}, u32[]{:S(2)}, u32[]{:S(2)}) collective-permute-start(bf16[4,3,16,2048]{3,2,1,0:T(8,128)(2,1)S(1)} %pad_maximum_fusion.3.refs_4_), channel_id=1, source_target_pairs={{1,0},{2,1},{3,2},{0,3},{5,4},{6,5},{7,6},{4,7},{9,8},{10,9},{11,1... | collective-permute-start | bytes 2359304 | tf_op jit(solution)/shard_map/ppermute | solution.py:189
  89.3 24.9 %collective-permute-start.15 = (bf16[4,3,16,2048]{3,2,1,0:T(8,128)(2,1)S(1)}, bf16[4,3,16,2048]{3,2,1,0:T(8,128)(2,1)}, u32[]{:S(2)}, u32[]{:S(2)}) collective-permute-start(bf16[4,3,16,2048]{3,2,1,0:T(8,128)(2,1)S(1)} %pad_maximum_fusion.2.refs_0_), channel_id=1, source_target_pairs={{4,0},{5,1},{6,2},{7,3},{8,4},{9,5},{10,6},{11,7},{12,8},{13,9},{1... | collective-permute-start | bytes 2359304 | tf_op jit(solution)/shard_map/ppermute | solution.py:189
  101.9 12.5 %collective-permute-start.25 = (f32[16,432]{1,0:T(8,128)S(1)}, f32[16,432]{1,0:T(8,128)S(1)}, u32[]{:S(2)}, u32[]{:S(2)}) collective-permute-start(f32[16,432]{1,0:T(8,128)S(1)} %get-tuple-element.36), channel_id=1, source_target_pairs={{16,17},{17,16},{18,49},{19,48},{20,81},{21,80},{22,113},{23,112},... | collective-permute-start | bytes 82952 | tf_op jit(solution)/shard_map/ppermute | solution.py:356
  104.9 9.5 %collective-permute-start.26 = (f32[16,432]{1,0:T(8,128)S(1)}, f32[16,432]{1,0:T(8,128)S(1)}, u32[]{:S(2)}, u32[]{:S(2)}) collective-permute-start(f32[16,432]{1,0:T(8,128)S(1)} %get-tuple-element.37), channel_id=1, source_target_pairs={{16,16},{17,17},{18,48},{19,49},{20,80},{21,81},{22,112},{23,113},... | collective-permute-start | bytes 82952 | tf_op jit(solution)/shard_map/ppermute | solution.py:356
  105.6 33.5 %collective-permute-start.23 = (bf16[4,3,16,2048]{3,2,1,0:T(8,128)(2,1)S(1)}, bf16[4,3,16,2048]{3,2,1,0:T(8,128)(2,1)}, u32[]{:S(2)}, u32[]{:S(2)}) collective-permute-start(bf16[4,3,16,2048]{3,2,1,0:T(8,128)(2,1)S(1)} %pad_maximum_fusion.3.refs_4_), channel_id=1, source_target_pairs={{3,0},{0,1},{1,2},{2,3},{7,4},{4,5},{5,6},{6,7},{11,8},{8,9},{9,10... | collective-permute-start | bytes 2359304 | tf_op jit(solution)/shard_map/ppermute | solution.py:189
  110.1 29.0 %collective-permute-start.17 = (bf16[4,3,16,2048]{3,2,1,0:T(8,128)(2,1)S(1)}, bf16[4,3,16,2048]{3,2,1,0:T(8,128)(2,1)}, u32[]{:S(2)}, u32[]{:S(2)}) collective-permute-start(bf16[4,3,16,2048]{3,2,1,0:T(8,128)(2,1)S(1)} %pad_maximum_fusion.2.refs_0_), channel_id=1, source_target_pairs={{12,0},{13,1},{14,2},{15,3},{0,4},{1,5},{2,6},{3,7},{4,8},{5,9},{6... | collective-permute-start | bytes 2359304 | tf_op jit(solution)/shard_map/ppermute | solution.py:189
  114.2 24.9 %collective-permute-start.22 = (bf16[4,3,16,2048]{3,2,1,0:T(8,128)(2,1)S(1)}, bf16[4,3,16,2048]{3,2,1,0:T(8,128)(2,1)}, u32[]{:S(2)}, u32[]{:S(2)}) collective-permute-start(bf16[4,3,16,2048]{3,2,1,0:T(8,128)(2,1)S(1)} %collective-permute-done.21.refs_5_), channel_id=1, source_target_pairs={{1,0},{2,1},{3,2},{0,3},{5,4},{6,5},{7,6},{4,7},{9,8},{10,9},{11,1... | collective-permute-start | bytes 2359304 | tf_op jit(solution)/shard_map/ppermute | solution.py:194
  114.4 24.8 %collective-permute-start.16 = (bf16[4,3,16,2048]{3,2,1,0:T(8,128)(2,1)}, bf16[4,3,16,2048]{3,2,1,0:T(8,128)(2,1)}, u32[]{:S(2)}, u32[]{:S(2)}) collective-permute-start(bf16[4,3,16,2048]{3,2,1,0:T(8,128)(2,1)} %collective-permute-done.15.refs_1_), channel_id=1, source_target_pairs={{4,0},{5,1},{6,2},{7,3},{8,4},{9,5},{10,6},{11,7},{12,8},{13,9},{1... | collective-permute-start | bytes 2359304 | tf_op jit(solution)/shard_map/ppermute | solution.py:194
  116.4 22.7 %all-to-all-start.2 = ((f32[8,32,432]{2,1,0:T(8,128)}), f32[8,32,432]{2,1,0:T(8,128)S(1)}, u32[]{:S(2)}, u32[]{:S(2)}) async-start(f32[8,32,432]{2,1,0:T(8,128)} %broadcast_in_dim.2), calls=%async_computation.2 | async-start | bytes 1048576 | tf_op jit(solution)/shard_map/all_to_all | solution.py:362
  127.0 12.2 %copy-start.1 = (bf16[27,16,256]{2,1,0:T(8,128)(2,1)S(1)}, bf16[27,16,256]{2,1,0:T(8,128)(2,1)}, u32[]{:S(2)}) copy-start(bf16[27,16,256]{2,1,0:T(8,128)(2,1)} %w2.1) | copy-start | bytes 663556
  139.1 4.8 %copy-start.3 = (f32[8,32,432]{2,1,0:T(8,128)}, f32[8,32,432]{2,1,0:T(8,128)S(1)}, u32[]{:S(2)}) copy-start(f32[8,32,432]{2,1,0:T(8,128)S(1)} %all-to-all-done.2) | copy-start | bytes 1327108
  139.1 4.8 %collective-permute-start.27 = (f32[256,432]{1,0:T(8,128)S(1)}, f32[256,432]{1,0:T(8,128)}, u32[]{:S(2)}, u32[]{:S(2)}) collective-permute-start(f32[256,432]{1,0:T(8,128)S(1)} %bitcast.44), channel_id=1, source_target_pairs={{0,16},{16,0},{32,48},{48,32},{64,80},{80,64},{96,112},{112,96},{1... | collective-permute-start | bytes 1327112 | tf_op jit(solution)/shard_map/ppermute | solution.py:363

commit v2 on v1

--- a/solution.py
+++ b/solution.py
@@ -77,14 +77,13 @@
                 stack_ref[t * BLK:(t + 1) * BLK, :] = shift_x(moved, sign * ox).astype(jnp.bfloat16)
 
 
-def place(scalars, pieces, full_ref, outer_is_x):
-    x, y, sign = scalars[1], scalars[2], scalars[3]
+def place(scalars, pieces, full_ref, sign):
+    x, y, core = scalars[1], scalars[2], scalars[3]
     for outer in range(SIDE):
         for inner in range(SIDE):
-            if outer_is_x:
-                bx, by = x + SIDE + sign * outer, y + inner
-            else:
-                bx, by = x + inner, y + SIDE + sign * outer
+            far, near = SIDE + sign * outer, SIDE + inner
+            bx = x + jnp.where(core == 0, far, near)
+            by = y + jnp.where(core == 0, near, far)
             block = lax.rem(bx, SIDE) * SIDE + lax.rem(by, SIDE)
             at = pl.multiple_of(block * BLK, BLK)
             full_ref[pl.ds(at, BLK), :] = pieces[outer][inner, 0]
@@ -96,31 +95,30 @@
 
 def kernel_one(scalars, *refs):
     px, gx = refs[0:4], refs[4:8]
-    w1, w2t, hid_out, del_out, full_p, full_g = refs[8:]
+    w1, w2t, pair_out, full_p, full_g = refs[8:]
     s = pl.program_id(0)
 
     @pl.when(s >= scalars[0])
     def _():
-        hid_out[...] = jnp.zeros_like(hid_out)
-        del_out[...] = jnp.zeros_like(del_out)
+        pair_out[...] = jnp.zeros_like(pair_out)
 
     @pl.when(s < scalars[0])
     def _():
         masks = axis_masks()
-        place(scalars, px, full_p, True)
-        place(scalars, gx, full_g, False)
+        place(scalars, px, full_p, 1)
+        place(scalars, gx, full_g, -1)
         first = tap_conv(w1, full_p[...], 1, masks)
         hidden_grad = tap_conv(w2t, full_g[...], -1, masks)
         sigma = 1.0 / (1.0 + jnp.exp(-first))
-        hid_out[0] = (first * sigma).astype(jnp.bfloat16)
-        del_out[0] = (hidden_grad * sigma * (1.0 + first * (1.0 - sigma))).astype(jnp.bfloat16)
+        pair_out[0, 0] = (first * sigma).astype(jnp.bfloat16)
+        pair_out[1, 0] = (hidden_grad * sigma * (1.0 + first * (1.0 - sigma))).astype(jnp.bfloat16)
 
 
 def kernel_grads(scalars, *refs):
     px, gx = refs[0:4], refs[4:8]
-    hid, dlt, keep_out, send_out, full, stack, grads = refs[8:]
+    pair, keep_out, send_out, full, stack, grads = refs[8:]
     s = pl.program_id(0)
-    core = scalars[4]
+    core = scalars[3]
 
     @pl.when(s == 0)
     def _():
@@ -129,11 +127,11 @@
     @pl.when(s < scalars[0])
     def _():
         masks = axis_masks()
-        place(scalars, px, full, True)
-        tap_stack(stack, dlt[0].astype(jnp.float32), -1, masks)
+        place(scalars, px, full, 1)
+        tap_stack(stack, pair[1, 0].astype(jnp.float32), -1, masks)
         grads[0] += over_cells(full[...], stack[...])
-        place(scalars, gx, full, False)
-        tap_stack(stack, hid[0].astype(jnp.float32), 1, masks)
+        place(scalars, gx, full, -1)
+        tap_stack(stack, pair[0, 0].astype(jnp.float32), 1, masks)
         grads[1] += over_cells(full[...], stack[...])
 
     @pl.when(s == pl.num_programs(0) - 1)
@@ -155,43 +153,40 @@
     @pl.when(s < scalars[0])
     def _():
         masks = axis_masks()
-        place(scalars, hx, full_h, True)
-        place(scalars, dx, full_d, False)
+        place(scalars, hx, full_h, 1)
+        place(scalars, dx, full_d, -1)
         out_ref[0] = tap_conv(w2, full_h[...], 1, masks)
         in_ref[0] = tap_conv(w1t, full_d[...], -1, masks)
 
 
-def from_near(axis, step):
-    def at(x, y):
-        return (x % SIDE) * SIDE + y % SIDE
-
-    sides = [(x, y) for x in range(SIDE) for y in range(SIDE)]
-    if axis == "x":
-        return [(at(x + step, y), at(x, y)) for x, y in sides]
-    return [(at(x, y + step), at(x, y)) for x, y in sides]
-
-
-def from_mirrored(axis, step):
+def from_axis(axes, step):
     pairs = []
     for d in range(BLK):
-        for src, dst in from_near(axis, step if d % 2 == 0 else -step):
-            pairs.append((d * BLK + src, d * BLK + dst))
+        for x in range(SIDE):
+            for y in range(SIDE):
+                sx, sy = (x + step, y) if axes[d % 2] == "x" else (x, y + step)
+                pairs.append((d * BLK + (sx % SIDE) * SIDE + sy % SIDE, d * BLK + x * SIDE + y))
     return pairs
 
 
-def gather_near(v, inner, first=None):
-    move = lambda k: lax.ppermute(v, "filter", from_near(inner, k))
-    return jnp.stack([v, move(1) if first is None else first, move(2), move(3)])
-
-
-def gather_far(own, outer):
-    both = ("dp", "filter")
-    return own, lax.ppermute(own, both, from_mirrored(outer, 1)), lax.ppermute(own, both, from_mirrored(outer, 3))
-
-
-def gather_last(parts, outer):
-    own, ahead, behind = parts
-    return [own, ahead, lax.ppermute(ahead, ("dp", "filter"), from_mirrored(outer, 1)), behind]
+def turn(v, axes, step):
+    return lax.ppermute(v, ("dp", "filter"), from_axis(axes, step))
+
+
+def gather_near(pair):
+    near = [pair] + [turn(pair, "yx", k) for k in (1, 2, 3)]
+    return [jnp.stack([v[k] for v in near]) for k in range(2)]
+
+
+def gather_far(nears):
+    return [(own, turn(own, "xy", sign), turn(own, "xy", -sign)) for own, sign in zip(nears, (1, -1))]
+
+
+def gather_last(parts):
+    pieces = []
+    for (own, ahead, behind), sign in zip(parts, (1, -1)):
+        pieces += [own, ahead, turn(ahead, "xy", sign), behind]
+    return pieces
 
 
 def live_slot(s, scalars):
@@ -210,13 +205,17 @@
     return pl.BlockSpec((1, BLK, CELLS), lambda s, *_: (s, 0, 0))
 
 
+def pair_spec():
+    return pl.BlockSpec((2, 1, BLK, CELLS), lambda s, *_: (0, s, 0, 0))
+
+
 def params():
     return pltpu.CompilerParams(vmem_limit_bytes=48 * 1024 * 1024)
 
 
 def call_one(scalars, pieces, w1, w2t):
     slots = pieces[0].shape[1]
-    flat = jax.ShapeDtypeStruct((slots, BLK, CELLS), jnp.bfloat16)
+    pair = jax.ShapeDtypeStruct((2, slots, BLK, CELLS), jnp.bfloat16)
     return pl.pallas_call(
         kernel_one,
         name="layer_one",
@@ -224,10 +223,10 @@
             num_scalar_prefetch=1,
             grid=(slots,),
             in_specs=piece_specs() + weight_specs(),
-            out_specs=[slot_spec(), slot_spec()],
+            out_specs=pair_spec(),
             scratch_shapes=[pltpu.VMEM((C, CELLS), jnp.bfloat16)] * 2,
         ),
-        out_shape=[flat, flat],
+        out_shape=pair,
         compiler_params=params(),
         cost_estimate=pl.CostEstimate(
             flops=slots * 4 * ROWS * C * CELLS, transcendentals=slots * BLK * CELLS, bytes_accessed=slots * 4 * C * CELLS
@@ -235,7 +234,7 @@
     )(scalars, *pieces, w1, w2t)
 
 
-def call_grads(scalars, pieces, hidden, delta):
+def call_grads(scalars, pieces, pair):
     slots = pieces[0].shape[1]
     return pl.pallas_call(
         kernel_grads,
@@ -243,7 +242,7 @@
         grid_spec=pltpu.PrefetchScalarGridSpec(
             num_scalar_prefetch=1,
             grid=(slots,),
-            in_specs=piece_specs() + [slot_spec(), slot_spec()],
+            in_specs=piece_specs() + [pair_spec()],
             out_specs=[pl.BlockSpec((C, ROWS), lambda s, *_: (0, 0))] * 2,
             scratch_shapes=[
                 pltpu.VMEM((C, CELLS), jnp.bfloat16),
@@ -256,7 +255,7 @@
         cost_estimate=pl.CostEstimate(
             flops=slots * 4 * ROWS * C * CELLS, transcendentals=0, bytes_accessed=slots * 4 * C * CELLS
         ),
-    )(scalars, *pieces, hidden, delta)
+    )(scalars, *pieces, pair)
 
 
 def call_two(scalars, pieces, w2, w1t):
@@ -283,9 +282,10 @@
     )(scalars, *pieces, w2, w1t)
 
 
-def kernel_split(w1, w2, out_ref):
+def kernel_split(scalars, w1, w2, out_ref):
     lane = lax.broadcasted_iota(jnp.int32, (BLK, 128), 1) >> 4
-    for k, w in enumerate((w1, w2)):
+
+    def split(w):
         for half in range(2):
             for low in range(0, TAPS, 8):
                 taps = range(low, min(low + 8, TAPS))
@@ -297,25 +297,40 @@
                         moved = pltpu.roll(tile, amount, 1) if amount else tile
                         total = moved if total is None else jnp.where(lane == j, moved, total)
                     width = BLK * len(tiles)
-                    out_ref[half * 8 + a, k, :, low * BLK:low * BLK + width] = total[:, :width].astype(jnp.bfloat16)
-
-
-def split_weights(w1, w2):
+                    out_ref[half * 8 + a, :, low * BLK:low * BLK + width] = total[:, :width].astype(jnp.bfloat16)
+
+    @pl.when(scalars[3] == 0)
+    def _():
+        split(w1)
+
+    @pl.when(scalars[3] == 1)
+    def _():
+        split(w2)
+
+
+def split_weights(scalars, w1, w2):
+    whole = pl.BlockSpec((TAPS, BLK, C), lambda i, *_: (0, 0, 0))
     return pl.pallas_call(
         kernel_split,
         name="split_weights",
-        out_shape=jax.ShapeDtypeStruct((BLK, 2, BLK, ROWS), jnp.bfloat16),
+        grid_spec=pltpu.PrefetchScalarGridSpec(
+            num_scalar_prefetch=1,
+            grid=(1,),
+            in_specs=[whole, whole],
+            out_specs=pl.BlockSpec((BLK, BLK, ROWS), lambda i, *_: (0, 0, 0)),
+        ),
+        out_shape=jax.ShapeDtypeStruct((BLK, BLK, ROWS), jnp.bfloat16),
         cost_estimate=pl.CostEstimate(flops=0, transcendentals=0, bytes_accessed=4 * ROWS * C * 2),
-    )(w1, w2)
+    )(scalars, w1, w2)
 
 
 def kernel_finish(scalars, own, other, first_ref, second_ref):
-    @pl.when(scalars[4] == 0)
+    @pl.when(scalars[3] == 0)
     def _():
         first_ref[...] = own[...].T
         second_ref[...] = other[...].T
 
-    @pl.when(scalars[4] == 1)
+    @pl.when(scalars[3] == 1)
     def _():
         first_ref[...] = other[...].T
         second_ref[...] = own[...].T
@@ -335,10 +350,13 @@
     )(scalars, own, other)
 
 
+def swap_cores(v):
+    return lax.ppermute(v, "dp", [(d, d ^ 1) for d in range(BLK)])
+
+
 def sum_over_dp(scalars, keep, send):
-    swap_cores = [(d, d ^ 1) for d in range(BLK)]
     by_core = [[2 * z + core for z in range(8)] for core in range(2)]
-    total = keep + lax.ppermute(send, "dp", swap_cores)
+    total = keep + swap_cores(send)
     parts = lax.all_to_all(total.reshape(8, 32, ROWS), "dp", 0, 0, axis_index_groups=by_core, tiled=True)
     scale = 1.0 / jnp.sqrt(jnp.float32(lax.axis_size("dp") * CELLS))
     mine = parts.sum(axis=0) * scale
@@ -356,44 +374,42 @@
         got.append(lax.ppermute(message, ("dp", "filter"), pairs))
     halves = jnp.stack([jnp.where(odd, got[1], got[0]), jnp.where(odd, got[0], got[1])])
     second = halves.reshape(2, BLK, TAPS, BLK).transpose(0, 3, 2, 1).reshape(2 * BLK, ROWS)
-    piece = jnp.where(scalars[4] == 0, mine, second)
+    piece = jnp.where(scalars[3] == 0, mine, second)
 
     copies = jnp.broadcast_to(piece[None], (8, 2 * BLK, ROWS))
-    own = lax.all_to_all(copies, "dp", 0, 0, axis_index_groups=by_core, tiled=True).reshape(C, ROWS)
-    other = lax.ppermute(own, "dp", swap_cores)
-    first_grad, second_grad = finish(scalars, own, other)
+    return lax.all_to_all(copies, "dp", 0, 0, axis_index_groups=by_core, tiled=True).reshape(C, ROWS)
+
+
+def both_gradients(scalars, own):
+    first_grad, second_grad = finish(scalars, own, swap_cores(own))
     return first_grad.reshape(TAPS, BLK, C), second_grad.reshape(TAPS, BLK, C)
 
 
 def shards(patches, cotangent, first_weight, second_weight, counts):
     me = lax.axis_index("filter")
     core = lax.axis_index("dp") % 2
-    scalars = jnp.stack([counts[0], me // SIDE, me % SIDE, 1 - 2 * core, core]).astype(jnp.int32)
-    split = split_weights(first_weight, second_weight)
-    near_p = gather_near(patches.transpose(1, 0, 2), "y")
-    near_g = gather_near(cotangent.transpose(1, 0, 2), "x")
-    near_g, split = lax.optimization_barrier((near_g, split))
-    far_p = gather_far(near_p, "x")
-    far_g = gather_far(near_g, "y")
-
-    turned = lax.all_to_all(split, "filter", 0, 0, tiled=True)
-    far_p, turned = lax.optimization_barrier((far_p, turned))
-    all_p = gather_last(far_p, "x")
-    all_g = gather_last(far_g, "y")
-    w1t = turned[:, 0].reshape(C, ROWS).T
-    w2t = turned[:, 1].reshape(C, ROWS).T
+    scalars = jnp.stack([counts[0], me // SIDE, me % SIDE, core]).astype(jnp.int32)
+    split = split_weights(scalars, first_weight, second_weight)
+    nears = gather_near(jnp.stack([patches.transpose(1, 0, 2), cotangent.transpose(1, 0, 2)]))
+    nears, split = lax.optimization_barrier((nears, split))
+    fars = gather_far(nears)
+
+    turned = lax.all_to_all(split, "filter", 0, 0, tiled=True).reshape(C, ROWS)
+    fars, turned = lax.optimization_barrier((fars, turned))
+    pieces = gather_last(fars)
+    other = swap_cores(turned)
+    w1t = jnp.where(core == 0, turned, other).T
+    w2t = jnp.where(core == 0, other, turned).T
     w1 = first_weight.reshape(ROWS, C)
     w2 = second_weight.reshape(ROWS, C)
 
-    hidden, delta = call_one(scalars, all_p + all_g, w1, w2t)
-    first_h = lax.ppermute(hidden, "filter", from_near("y", 1))
-    near_h = gather_near(hidden, "y", first_h)
-    near_d = gather_near(delta, "x")
-    keep, send = call_grads(scalars, all_p + all_g, hidden, delta)
-    all_h = gather_last(gather_far(near_h, "x"), "x")
-    all_d = gather_last(gather_far(near_d, "y"), "y")
-    first_grad, second_grad = sum_over_dp(scalars, keep, send)
-    out, in_grad = call_two(scalars, all_h + all_d, w2, w1t)
+    pair = call_one(scalars, pieces, w1, w2t)
+    second_pieces = gather_last(gather_far(gather_near(pair)))
+    keep, send = call_grads(scalars, pieces, pair)
+    own = sum_over_dp(scalars, keep, send)
+    out, in_grad = call_two(scalars, second_pieces, w2, w1t)
+    out, in_grad, own = lax.optimization_barrier((out, in_grad, own))
+    first_grad, second_grad = both_gradients(scalars, own)
     return (out.transpose(1, 0, 2), in_grad.transpose(1, 0, 2), first_grad, second_grad)
 
 

time: 148 us -> 153 us (1.034); the launches traced: 147 us -> 155 us
  waiting for transfers between devices: 54.5 us -> 33.9 us
  blocking collectives: 0 us -> 18.9 us
  starting transfers between devices: 66.6 us -> 70.7 us
  local copies, waits for them, and re-layouts: 4.03 us -> 7.23 us
  other arithmetic: 2.44 us -> 4.09 us
    all_to_all x0 -> x1, blocking collectives: none -> 18.9 us  [shards(): turned = lax.all_to_all(split, 'filter', 0, 0, tiled=True).reshape(C, ROWS)]
    all_to_all x1 -> x0, waiting for transfers between devices: 16.2 us -> none  [shards(): turned = lax.all_to_all(split, 'filter', 0, 0, tiled=True)]
    all_to_all x1, starting transfers between devices: 10.5 us -> 20.1 us  [sum_over_dp(): lax.all_to_all(copies, 'dp', 0, 0, axis_index_groups=by_core, tiled=True)]
    all_to_all x1 -> x0, starting transfers between devices: 6.61 us -> none  [shards(): turned = lax.all_to_all(split, 'filter', 0, 0, tiled=True)]
    ppermute x26 -> x21, waiting for transfers between devices: 16.9 us -> 12.1 us  [the longest x18 9.1 us: turn(): return lax.ppermute(v, ('dp', 'filter'), from_axis(axes, step))]
    ppermute x2, waiting for transfers between devices: 0.01 us -> 4.39 us  [sum_over_dp(): got.append(lax.ppermute(message, ('dp', 'filter'), pairs))]
    ppermute x26 -> x21, starting transfers between devices: 32.8 us -> 36.7 us  [the longest x18 21.1 us: turn(): return lax.ppermute(v, ('dp', 'filter'), from_axis(axes, step))]
    all_to_all x1, waiting for transfers between devices: 11 us -> 7.32 us  [sum_over_dp(): lax.all_to_all(copies, 'dp', 0, 0, axis_index_groups=by_core, tiled=True)]
  transfers between devices with their start and end apart: 31 -> 25, of which waited for: 11 -> 8; matrix products, arithmetic and copies ran while one was open for 4% -> 5% of each run, Pallas kernels for 5% -> 7%
where the time goes in v2:
time: 153 us; the launch traced here: 155 us
  starting transfers between devices  70.7 us (46%)
  waiting for transfers between devices  33.9 us (22%)
  blocking collectives  18.9 us (12%)
  Pallas kernels  18.3 us (12%)
  local copies, waits for them, and re-layouts  7.23 us (5%)
  other arithmetic  4.09 us (3%)
  between operations  1.59 us (1%)
    ppermute x18, starting transfers between devices, turn(): return lax.ppermute(v, ('dp', 'filter'), from_axis(axes, step))  21.1 us
    all_to_all x1, starting transfers between devices, sum_over_dp(): lax.all_to_all(copies, 'dp', 0, 0, axis_index_groups=by_core, tiled=True)  20.1 us
    all_to_all x1, blocking collectives, shards(): turned = lax.all_to_all(split, 'filter', 0, 0, tiled=True).reshape(C, ROWS)  18.9 us
    ppermute x3, starting transfers between devices, swap_cores(): return lax.ppermute(v, 'dp', [(d, d ^ 1) for d in range(BLK)])  15.6 us
    all_to_all x1, starting transfers between devices, sum_over_dp(): lax.all_to_all(total.reshape(8, 32, ROWS), 'dp', 0, 0, axis_index_groups=...  11.3 us
    all_to_all x1, waiting for transfers between devices, sum_over_dp(): lax.all_to_all(total.reshape(8, 32, ROWS), 'dp', 0, 0, axis_index_groups=...  10 us
    ppermute x18, waiting for transfers between devices, turn(): return lax.ppermute(v, ('dp', 'filter'), from_axis(axes, step))  9.1 us
    all_to_all x1, waiting for transfers between devices, sum_over_dp(): lax.all_to_all(copies, 'dp', 0, 0, axis_index_groups=by_core, tiled=True)  7.32 us
  transfers between devices with their start and end apart: 25, of which 8 were waited for; matrix products, arithmetic and copies ran while one was open for 5% of the time, Pallas kernels for 7%

profile of v2, /device:TPU:1, one launch (start us, length us, event | category | flops | bytes accessed | tf_op | source)
XLA Modules:
  0.0 154.6 jit_solution(4908289023792566724)
XLA Ops:
  0.6 1.1 pad_maximum_fusion.4
  1.7 2.1 %collective-permute-start.2 = (bf16[2,3,16,2048]{3,2,1,0:T(8,128)(2,1)S(1)}, bf16[2,3,16,2048]{3,2,1,0:T(8,128)(2,1)S(1)}, u32[]{:S(2)}, u32[]{:S(2)}) collective-permute-start(bf16[2,3,16,2048]{3,2,1,0:T(8,128)(2,1)S(1)} %pad_maximum_fusion.4), channel_id=1, source_target_pairs={{3,0},{0,1},{1,2},{2,3},{7,4},{4,5},{5,6},{6,7},{11,8},{8,9},{9,10... | collective-permute-start | bytes 1179656 | tf_op jit(solution)/shard_map/ppermute | solution.py:173
  3.8 2.5 %collective-permute-start.1 = (bf16[2,3,16,2048]{3,2,1,0:T(8,128)(2,1)S(1)}, bf16[2,3,16,2048]{3,2,1,0:T(8,128)(2,1)S(1)}, u32[]{:S(2)}, u32[]{:S(2)}) collective-permute-start(bf16[2,3,16,2048]{3,2,1,0:T(8,128)(2,1)S(1)} %pad_maximum_fusion.4), channel_id=1, source_target_pairs={{2,0},{3,1},{0,2},{1,3},{6,4},{7,5},{4,6},{5,7},{10,8},{11,9},{8,1... | collective-permute-start | bytes 1179656 | tf_op jit(solution)/shard_map/ppermute | solution.py:173
  6.3 1.2 collective-permute-start
  8.1 0.6 pad_add_fusion.scalars
  8.7 2.9 %split_weights.1 = bf16[16,16,432]{2,1,0:T(8,128)(2,1)} custom-call(s32[4]{0:T(128)} %pad_add_fusion.scalars, bf16[27,16,256]{2,1,0:T(8,128)(2,1)} %w1.1, bf16[27,16,256]{2,1,0:T(8,128)(2,1)} %w2.1), custom_call_target="tpu_custom_call" | custom-call | bytes 884736 | tf_op jit(solution)/shard_map/split_weights/pallas_call | solution.py:313
  11.6 4.3 %collective-permute-done.1 = bf16[2,3,16,2048]{3,2,1,0:T(8,128)(2,1)S(1)} collective-permute-done((bf16[2,3,16,2048]{3,2,1,0:T(8,128)(2,1)S(1)}, bf16[2,3,16,2048]{3,2,1,0:T(8,128)(2,1)S(1)}, u32[]{:S(2)}, u32[]{:S(2)}) %collective-permute-start.1) | collective-permute-done | bytes 393248 | tf_op jit(solution)/shard_map/ppermute | solution.py:173
  16.0 0.9 copy-done.5
  17.0 0.2 pad_maximum_fusion
  17.2 1.1 collective-permute-start.4
  18.3 1.7 %collective-permute-start.3 = (bf16[4,3,16,2048]{3,2,1,0:T(8,128)(2,1)S(1)}, bf16[4,3,16,2048]{3,2,1,0:T(8,128)(2,1)}, u32[]{:S(2)}, u32[]{:S(2)}) collective-permute-start(bf16[4,3,16,2048]{3,2,1,0:T(8,128)(2,1)S(1)} %get-tuple-element.26.refs_0_), channel_id=1, source_target_pairs={{4,0},{5,1},{6,2},{7,3},{8,4},{9,5},{10,6},{11,7},{12,8},{13,9},{1... | collective-permute-start | bytes 2359304 | tf_op jit(solution)/shard_map/ppermute | solution.py:173
  19.9 1.2 collective-permute-start.6
  21.2 0.2 collective-permute-start.5
  21.4 18.9 %all_to_all.15 = bf16[16,16,432]{2,1,0:T(8,128)(2,1)S(1)} all-to-all(bf16[16,16,432]{2,1,0:T(8,128)(2,1)S(1)} %copy-done.4), channel_id=1, replica_groups=mesh['dp'=16,'filter'=16] {'filter'}, dimensions={0} | all-to-all | bytes 442368 | tf_op jit(solution)/shard_map/all_to_all | solution.py:397
  40.3 2.4 %collective-permute-start.7 = (bf16[4,3,16,2048]{3,2,1,0:T(8,128)(2,1)}, bf16[4,3,16,2048]{3,2,1,0:T(8,128)(2,1)}, u32[]{:S(2)}, u32[]{:S(2)}) collective-permute-start(bf16[4,3,16,2048]{3,2,1,0:T(8,128)(2,1)} %collective-permute-done.3.refs_1_), channel_id=1, source_target_pairs={{4,0},{5,1},{6,2},{7,3},{8,4},{9,5},{10,6},{11,7},{12,8},{13,9},{1... | collective-permute-start | bytes 2359304 | tf_op jit(solution)/shard_map/ppermute | solution.py:173
  42.7 0.1 copy.12
  42.8 6.6 %collective-permute-start.9 = (bf16[256,432]{0,1:T(8,128)(2,1)S(1)}, bf16[256,432]{0,1:T(8,128)(2,1)S(1)}, u32[]{:S(2)}, u32[]{:S(2)}) collective-permute-start(bf16[256,432]{0,1:T(8,128)(2,1)S(1)} %copy.12), channel_id=1, source_target_pairs={{0,16},{16,0},{32,48},{48,32},{64,80},{80,64},{96,112},{112,96},{1... | collective-permute-start | bytes 663560 | tf_op jit(solution)/shard_map/ppermute | solution.py:354
  49.5 1.1 collective-permute-done.9
  50.6 1.6 %collective-permute-done.7.refs_2_ = bf16[4,3,16,2048]{3,2,1,0:T(8,128)(2,1)} collective-permute-done((bf16[4,3,16,2048]{3,2,1,0:T(8,128)(2,1)}, bf16[4,3,16,2048]{3,2,1,0:T(8,128)(2,1)}, u32[]{:S(2)}, u32[]{:S(2)}) %collective-permute-start.7) | collective-permute-done | bytes 786464 | tf_op jit(solution)/shard_map/ppermute | solution.py:173
  52.2 3.2 %collective-permute-done.8.refs_6_ = bf16[4,3,16,2048]{3,2,1,0:T(8,128)(2,1)} collective-permute-done((bf16[4,3,16,2048]{3,2,1,0:T(8,128)(2,1)}, bf16[4,3,16,2048]{3,2,1,0:T(8,128)(2,1)}, u32[]{:S(2)}, u32[]{:S(2)}) %collective-permute-start.8) | collective-permute-done | bytes 786464 | tf_op jit(solution)/shard_map/ppermute | solution.py:173
  55.4 0.6 copy-done.2
  56.0 3.7 %layer_one.1.refs_8_ = bf16[2,3,16,2048]{3,2,1,0:T(8,128)(2,1)S(1)} custom-call(s32[4]{0:T(128)S(1)} %copy-done.2, bf16[4,3,16,2048]{3,2,1,0:T(8,128)(2,1)S(1)} %get-tuple-element.26.refs_0_, bf16[4,3,16,2048]{3,2,1,0:T(8,128)(2,1)} %collective-permute-done.3.refs_1_, bf16[4,3,16,2048]{3,2,1,0:T(8,128)(2,1)} %collective-permute-done.7.refs_2_, ...), custom_call_target="tpu_custom_call" | custom-call | flops 2717908992 | bytes 6291456 | tf_op jit(solution)/shard_map/layer_one/pallas_call | solution.py:219
  59.8 2.4 %collective-permute-start.11 = (bf16[2,3,16,2048]{3,2,1,0:T(8,128)(2,1)S(1)}, bf16[2,3,16,2048]{3,2,1,0:T(8,128)(2,1)S(1)}, u32[]{:S(2)}, u32[]{:S(2)}) collective-permute-start(bf16[2,3,16,2048]{3,2,1,0:T(8,128)(2,1)S(1)} %layer_one.1.refs_8_), channel_id=1, source_target_pairs={{2,0},{3,1},{0,2},{1,3},{6,4},{7,5},{4,6},{5,7},{10,8},{11,9},{8,1... | collective-permute-start | bytes 1179656 | tf_op jit(solution)/shard_map/ppermute | solution.py:173
  62.2 0.5 collective-permute-start.10
  62.7 3.8 %weight_grads.1 = (f32[256,432]{1,0:T(8,128)S(1)}, f32[256,432]{1,0:T(8,128)S(1)}) custom-call(s32[4]{0:T(128)S(1)} %copy-done.2, bf16[4,3,16,2048]{3,2,1,0:T(8,128)(2,1)S(1)} %get-tuple-element.26.refs_0_, bf16[4,3,16,2048]{3,2,1,0:T(8,128)(2,1)} %collective-permute-done.3.refs_1_, bf16[4,3,16,2048]{3,2,1,0:T(8,128)(2,1)} %collective-permute-done.7.refs_2_, ...), custom_call_target="tpu_custom_call" | custom-call | flops 2717908992 | bytes 6291456 | tf_op jit(solution)/shard_map/weight_grads/pallas_call | solution.py:239
  66.5 9.0 %collective-permute-start.19 = (f32[256,432]{1,0:T(8,128)S(1)}, f32[256,432]{1,0:T(8,128)S(1)}, u32[]{:S(2)}, u32[]{:S(2)}) collective-permute-start(f32[256,432]{1,0:T(8,128)S(1)} %get-tuple-element.36), channel_id=1, source_target_pairs={{0,16},{16,0},{32,48},{48,32},{64,80},{80,64},{96,112},{112,96},{1... | collective-permute-start | bytes 1327112 | tf_op jit(solution)/shard_map/ppermute | solution.py:354
  76.0 1.5 collective-permute-start.16
  77.5 0.9 add.16
  78.4 11.3 %all-to-all-start.1 = ((f32[8,32,432]{2,1,0:T(8,128)}), f32[8,32,432]{2,1,0:T(8,128)S(1)}, u32[]{:S(2)}, u32[]{:S(2)}) async-start(f32[8,32,432]{2,1,0:T(8,128)} %bitcast.14), calls=%async_computation.1 | async-start | bytes 1048576 | tf_op jit(solution)/shard_map/all_to_all | solution.py:360
  89.7 0.6 collective-permute-start.15
  90.3 2.1 %collective-permute-start.18 = (bf16[4,3,16,2048]{3,2,1,0:T(8,128)(2,1)S(1)}, bf16[4,3,16,2048]{3,2,1,0:T(8,128)(2,1)}, u32[]{:S(2)}, u32[]{:S(2)}) collective-permute-start(bf16[4,3,16,2048]{3,2,1,0:T(8,128)(2,1)S(1)} %pad_maximum_fusion.3.refs_4_), channel_id=1, source_target_pairs={{4,0},{5,1},{6,2},{7,3},{8,4},{9,5},{10,6},{11,7},{12,8},{13,9},{1... | collective-permute-start | bytes 2359304 | tf_op jit(solution)/shard_map/ppermute | solution.py:173
  92.4 1.4 collective-permute-start.17
  93.9 10.0 %all-to-all-done.1 = f32[8,32,432]{2,1,0:T(8,128)S(1)} async-done(((f32[8,32,432]{2,1,0:T(8,128)}), f32[8,32,432]{2,1,0:T(8,128)S(1)}, u32[]{:S(2)}, u32[]{:S(2)}) %all-to-all-start.1) | async-done | bytes 442400 | tf_op jit(solution)/shard_map/all_to_all | solution.py:360
  104.0 1.9 %collective-permute-start.20 = (f32[16,432]{1,0:T(8,128)S(1)}, f32[16,432]{1,0:T(8,128)S(1)}, u32[]{:S(2)}, u32[]{:S(2)}) collective-permute-start(f32[16,432]{1,0:T(8,128)S(1)} %get-tuple-element.60), channel_id=1, source_target_pairs={{16,17},{17,16},{18,49},{19,48},{20,81},{21,80},{22,113},{23,112},... | collective-permute-start | bytes 82952 | tf_op jit(solution)/shard_map/ppermute | solution.py:374
  105.9 4.4 %collective-permute-done.20 = f32[16,432]{1,0:T(8,128)S(1)} collective-permute-done((f32[16,432]{1,0:T(8,128)S(1)}, f32[16,432]{1,0:T(8,128)S(1)}, u32[]{:S(2)}, u32[]{:S(2)}) %collective-permute-start.20) | collective-permute-done | bytes 27680 | tf_op jit(solution)/shard_map/ppermute | solution.py:374
  110.3 0.7 collective-permute-start.21
  111.0 0.1 stack.53
  111.1 0.8 stack.54
  112.0 1.0 maximum_bitcast_fusion
  113.0 1.4 copy.15
  114.3 1.3 reshape.49
  115.6 0.9 broadcast_in_dim.2
  116.5 20.1 %all-to-all-start.2 = ((f32[8,32,432]{2,1,0:T(8,128)}), f32[8,32,432]{2,1,0:T(8,128)S(1)}, u32[]{:S(2)}, u32[]{:S(2)}) async-start(f32[8,32,432]{2,1,0:T(8,128)} %broadcast_in_dim.2), calls=%async_computation.2 | async-start | bytes 1048576 | tf_op jit(solution)/shard_map/all_to_all | solution.py:380
  136.7 4.8 %layer_two.1 = (f32[3,16,2048]{2,1,0:T(8,128)}, f32[3,16,2048]{2,1,0:T(8,128)}) custom-call(s32[4]{0:T(128)S(1)} %copy-done.2, bf16[4,3,16,2048]{3,2,1,0:T(8,128)(2,1)S(1)} %pad_maximum_fusion.2.refs_0_, bf16[4,3,16,2048]{3,2,1,0:T(8,128)(2,1)S(1)} %collective-permute-done.13.refs_1_, bf16[4,3,16,2048]{3,2,1,0:T(8,128)(2,1)} %collective-permute-done.14.refs_2_, ...), custom_call_target="tpu_custom_call" | custom-call | flops 108716359680 | bytes 6291456 | tf_op jit(solution)/shard_map/layer_two/pallas_call | solution.py:264
  141.4 7.3 %all-to-all-done.2 = f32[8,32,432]{2,1,0:T(8,128)S(1)} async-done(((f32[8,32,432]{2,1,0:T(8,128)}), f32[8,32,432]{2,1,0:T(8,128)S(1)}, u32[]{:S(2)}, u32[]{:S(2)}) %all-to-all-start.2) | async-done | bytes 442400 | tf_op jit(solution)/shard_map/all_to_all | solution.py:380
  148.8 1.9 %collective-permute-done.22.other = f32[256,432]{1,0:T(8,128)S(1)} collective-permute-done((f32[256,432]{1,0:T(8,128)S(1)}, f32[256,432]{1,0:T(8,128)S(1)}, u32[]{:S(2)}, u32[]{:S(2)}) %collective-permute-start.22) | collective-permute-done | bytes 442400 | tf_op jit(solution)/shard_map/ppermute | solution.py:354
  150.7 0.8 copy-done.7
  151.5 3.1 %finish_gradients.1 = (f32[432,256]{1,0:T(8,128)}, f32[432,256]{1,0:T(8,128)}) custom-call(s32[4]{0:T(128)} %pad_add_fusion.scalars, f32[256,432]{1,0:T(8,128)} %bitcast.27, f32[256,432]{1,0:T(8,128)} %copy-done.7), custom_call_target="tpu_custom_call" | custom-call | bytes 1769472 | tf_op jit(solution)/shard_map/finish_gradients/pallas_call | solution.py:342
  (52 shorter events, 0.9 us)
Async XLA Ops:
  1.7 9.9 %collective-permute-start.2 = (bf16[2,3,16,2048]{3,2,1,0:T(8,128)(2,1)S(1)}, bf16[2,3,16,2048]{3,2,1,0:T(8,128)(2,1)S(1)}, u32[]{:S(2)}, u32[]{:S(2)}) collective-permute-start(bf16[2,3,16,2048]{3,2,1,0:T(8,128)(2,1)S(1)} %pad_maximum_fusion.4), channel_id=1, source_target_pairs={{3,0},{0,1},{1,2},{2,3},{7,4},{4,5},{5,6},{6,7},{11,8},{8,9},{9,10... | collective-permute-start | bytes 1179656 | tf_op jit(solution)/shard_map/ppermute | solution.py:173
  3.8 12.1 %collective-permute-start.1 = (bf16[2,3,16,2048]{3,2,1,0:T(8,128)(2,1)S(1)}, bf16[2,3,16,2048]{3,2,1,0:T(8,128)(2,1)S(1)}, u32[]{:S(2)}, u32[]{:S(2)}) collective-permute-start(bf16[2,3,16,2048]{3,2,1,0:T(8,128)(2,1)S(1)} %pad_maximum_fusion.4), channel_id=1, source_target_pairs={{2,0},{3,1},{0,2},{1,3},{6,4},{7,5},{4,6},{5,7},{10,8},{11,9},{8,1... | collective-permute-start | bytes 1179656 | tf_op jit(solution)/shard_map/ppermute | solution.py:173
  6.3 9.7 %collective-permute-start = (bf16[2,3,16,2048]{3,2,1,0:T(8,128)(2,1)S(1)}, bf16[2,3,16,2048]{3,2,1,0:T(8,128)(2,1)S(1)}, u32[]{:S(2)}, u32[]{:S(2)}) collective-permute-start(bf16[2,3,16,2048]{3,2,1,0:T(8,128)(2,1)S(1)} %pad_maximum_fusion.4), channel_id=1, source_target_pairs={{1,0},{2,1},{3,2},{0,3},{5,4},{6,5},{7,6},{4,7},{9,8},{10,9},{11,1... | collective-permute-start | bytes 1179656 | tf_op jit(solution)/shard_map/ppermute | solution.py:173
  16.0 0.9 copy-start.5
  16.0 1.0 copy-start.6
  17.0 4.4 %copy-start.4 = (bf16[16,16,432]{2,1,0:T(8,128)(2,1)S(1)}, bf16[16,16,432]{2,1,0:T(8,128)(2,1)}, u32[]{:S(2)}) copy-start(bf16[16,16,432]{2,1,0:T(8,128)(2,1)} %split_weights.1) | copy-start | bytes 663556
  17.2 23.1 %collective-permute-start.4 = (bf16[4,3,16,2048]{3,2,1,0:T(8,128)(2,1)S(1)}, bf16[4,3,16,2048]{3,2,1,0:T(8,128)(2,1)S(1)}, u32[]{:S(2)}, u32[]{:S(2)}) collective-permute-start(bf16[4,3,16,2048]{3,2,1,0:T(8,128)(2,1)S(1)} %get-tuple-element.26.refs_0_), channel_id=1, source_target_pairs={{12,0},{13,1},{14,2},{15,3},{0,4},{1,5},{2,6},{3,7},{4,8},{5,9},{6... | collective-permute-start | bytes 2359304 | tf_op jit(solution)/shard_map/ppermute | solution.py:173
  18.3 22.0 %collective-permute-start.3 = (bf16[4,3,16,2048]{3,2,1,0:T(8,128)(2,1)S(1)}, bf16[4,3,16,2048]{3,2,1,0:T(8,128)(2,1)}, u32[]{:S(2)}, u32[]{:S(2)}) collective-permute-start(bf16[4,3,16,2048]{3,2,1,0:T(8,128)(2,1)S(1)} %get-tuple-element.26.refs_0_), channel_id=1, source_target_pairs={{4,0},{5,1},{6,2},{7,3},{8,4},{9,5},{10,6},{11,7},{12,8},{13,9},{1... | collective-permute-start | bytes 2359304 | tf_op jit(solution)/shard_map/ppermute | solution.py:173
  19.9 20.3 %collective-permute-start.6 = (bf16[4,3,16,2048]{3,2,1,0:T(8,128)(2,1)S(1)}, bf16[4,3,16,2048]{3,2,1,0:T(8,128)(2,1)S(1)}, u32[]{:S(2)}, u32[]{:S(2)}) collective-permute-start(bf16[4,3,16,2048]{3,2,1,0:T(8,128)(2,1)S(1)} %get-tuple-element.29.refs_4_), channel_id=1, source_target_pairs={{4,0},{5,1},{6,2},{7,3},{8,4},{9,5},{10,6},{11,7},{12,8},{13,9},{1... | collective-permute-start | bytes 2359304 | tf_op jit(solution)/shard_map/ppermute | solution.py:173
  21.2 19.1 %collective-permute-start.5 = (bf16[4,3,16,2048]{3,2,1,0:T(8,128)(2,1)S(1)}, bf16[4,3,16,2048]{3,2,1,0:T(8,128)(2,1)}, u32[]{:S(2)}, u32[]{:S(2)}) collective-permute-start(bf16[4,3,16,2048]{3,2,1,0:T(8,128)(2,1)S(1)} %get-tuple-element.29.refs_4_), channel_id=1, source_target_pairs={{12,0},{13,1},{14,2},{15,3},{0,4},{1,5},{2,6},{3,7},{4,8},{5,9},{6... | collective-permute-start | bytes 2359304 | tf_op jit(solution)/shard_map/ppermute | solution.py:173
  40.3 2.4 %copy-start.8 = (bf16[4,3,16,2048]{3,2,1,0:T(8,128)(2,1)}, bf16[4,3,16,2048]{3,2,1,0:T(8,128)(2,1)S(1)}, u32[]{:S(2)}) copy-start(bf16[4,3,16,2048]{3,2,1,0:T(8,128)(2,1)S(1)} %collective-permute-done.6.refs_7_) | copy-start | bytes 2359300
  40.3 11.9 %collective-permute-start.7 = (bf16[4,3,16,2048]{3,2,1,0:T(8,128)(2,1)}, bf16[4,3,16,2048]{3,2,1,0:T(8,128)(2,1)}, u32[]{:S(2)}, u32[]{:S(2)}) collective-permute-start(bf16[4,3,16,2048]{3,2,1,0:T(8,128)(2,1)} %collective-permute-done.3.refs_1_), channel_id=1, source_target_pairs={{4,0},{5,1},{6,2},{7,3},{8,4},{9,5},{10,6},{11,7},{12,8},{13,9},{1... | collective-permute-start | bytes 2359304 | tf_op jit(solution)/shard_map/ppermute | solution.py:173
  42.7 12.7 %collective-permute-start.8 = (bf16[4,3,16,2048]{3,2,1,0:T(8,128)(2,1)}, bf16[4,3,16,2048]{3,2,1,0:T(8,128)(2,1)}, u32[]{:S(2)}, u32[]{:S(2)}) collective-permute-start(bf16[4,3,16,2048]{3,2,1,0:T(8,128)(2,1)} %collective-permute-done.5.refs_5_), channel_id=1, source_target_pairs={{12,0},{13,1},{14,2},{15,3},{0,4},{1,5},{2,6},{3,7},{4,8},{5,9},{6... | collective-permute-start | bytes 2359304 | tf_op jit(solution)/shard_map/ppermute | solution.py:173
  42.8 7.7 %collective-permute-start.9 = (bf16[256,432]{0,1:T(8,128)(2,1)S(1)}, bf16[256,432]{0,1:T(8,128)(2,1)S(1)}, u32[]{:S(2)}, u32[]{:S(2)}) collective-permute-start(bf16[256,432]{0,1:T(8,128)(2,1)S(1)} %copy.12), channel_id=1, source_target_pairs={{0,16},{16,0},{32,48},{48,32},{64,80},{80,64},{96,112},{112,96},{1... | collective-permute-start | bytes 663560 | tf_op jit(solution)/shard_map/ppermute | solution.py:354
  49.5 5.9 %copy-start = (bf16[27,16,256]{2,1,0:T(8,128)(2,1)S(1)}, bf16[27,16,256]{2,1,0:T(8,128)(2,1)}, u32[]{:S(2)}) copy-start(bf16[27,16,256]{2,1,0:T(8,128)(2,1)} %w1.1) | copy-start | bytes 663556
  55.4 0.6 copy-start.2
  59.7 15.9 %collective-permute-start.12 = (bf16[2,3,16,2048]{3,2,1,0:T(8,128)(2,1)S(1)}, bf16[2,3,16,2048]{3,2,1,0:T(8,128)(2,1)S(1)}, u32[]{:S(2)}, u32[]{:S(2)}) collective-permute-start(bf16[2,3,16,2048]{3,2,1,0:T(8,128)(2,1)S(1)} %layer_one.1.refs_8_), channel_id=1, source_target_pairs={{3,0},{0,1},{1,2},{2,3},{7,4},{4,5},{5,6},{6,7},{11,8},{8,9},{9,10... | collective-permute-start | bytes 1179656 | tf_op jit(solution)/shard_map/ppermute | solution.py:173
  59.8 15.8 %collective-permute-start.11 = (bf16[2,3,16,2048]{3,2,1,0:T(8,128)(2,1)S(1)}, bf16[2,3,16,2048]{3,2,1,0:T(8,128)(2,1)S(1)}, u32[]{:S(2)}, u32[]{:S(2)}) collective-permute-start(bf16[2,3,16,2048]{3,2,1,0:T(8,128)(2,1)S(1)} %layer_one.1.refs_8_), channel_id=1, source_target_pairs={{2,0},{3,1},{0,2},{1,3},{6,4},{7,5},{4,6},{5,7},{10,8},{11,9},{8,1... | collective-permute-start | bytes 1179656 | tf_op jit(solution)/shard_map/ppermute | solution.py:173
  62.2 13.5 %collective-permute-start.10 = (bf16[2,3,16,2048]{3,2,1,0:T(8,128)(2,1)S(1)}, bf16[2,3,16,2048]{3,2,1,0:T(8,128)(2,1)S(1)}, u32[]{:S(2)}, u32[]{:S(2)}) collective-permute-start(bf16[2,3,16,2048]{3,2,1,0:T(8,128)(2,1)S(1)} %layer_one.1.refs_8_), channel_id=1, source_target_pairs={{1,0},{2,1},{3,2},{0,3},{5,4},{6,5},{7,6},{4,7},{9,8},{10,9},{11,1... | collective-permute-start | bytes 1179656 | tf_op jit(solution)/shard_map/ppermute | solution.py:173
  66.5 11.0 %collective-permute-start.19 = (f32[256,432]{1,0:T(8,128)S(1)}, f32[256,432]{1,0:T(8,128)S(1)}, u32[]{:S(2)}, u32[]{:S(2)}) collective-permute-start(f32[256,432]{1,0:T(8,128)S(1)} %get-tuple-element.36), channel_id=1, source_target_pairs={{0,16},{16,0},{32,48},{48,32},{64,80},{80,64},{96,112},{112,96},{1... | collective-permute-start | bytes 1327112 | tf_op jit(solution)/shard_map/ppermute | solution.py:354
  75.8 16.6 %collective-permute-start.13 = (bf16[4,3,16,2048]{3,2,1,0:T(8,128)(2,1)S(1)}, bf16[4,3,16,2048]{3,2,1,0:T(8,128)(2,1)S(1)}, u32[]{:S(2)}, u32[]{:S(2)}) collective-permute-start(bf16[4,3,16,2048]{3,2,1,0:T(8,128)(2,1)S(1)} %pad_maximum_fusion.2.refs_0_), channel_id=1, source_target_pairs={{4,0},{5,1},{6,2},{7,3},{8,4},{9,5},{10,6},{11,7},{12,8},{13,9},{1... | collective-permute-start | bytes 2359304 | tf_op jit(solution)/shard_map/ppermute | solution.py:173
  76.0 16.4 %collective-permute-start.16 = (bf16[4,3,16,2048]{3,2,1,0:T(8,128)(2,1)S(1)}, bf16[4,3,16,2048]{3,2,1,0:T(8,128)(2,1)}, u32[]{:S(2)}, u32[]{:S(2)}) collective-permute-start(bf16[4,3,16,2048]{3,2,1,0:T(8,128)(2,1)S(1)} %pad_maximum_fusion.3.refs_4_), channel_id=1, source_target_pairs={{12,0},{13,1},{14,2},{15,3},{0,4},{1,5},{2,6},{3,7},{4,8},{5,9},{6... | collective-permute-start | bytes 2359304 | tf_op jit(solution)/shard_map/ppermute | solution.py:173
  78.4 25.5 %all-to-all-start.1 = ((f32[8,32,432]{2,1,0:T(8,128)}), f32[8,32,432]{2,1,0:T(8,128)S(1)}, u32[]{:S(2)}, u32[]{:S(2)}) async-start(f32[8,32,432]{2,1,0:T(8,128)} %bitcast.14), calls=%async_computation.1 | async-start | bytes 1048576 | tf_op jit(solution)/shard_map/all_to_all | solution.py:360
  89.7 46.9 %collective-permute-start.15 = (bf16[4,3,16,2048]{3,2,1,0:T(8,128)(2,1)S(1)}, bf16[4,3,16,2048]{3,2,1,0:T(8,128)(2,1)}, u32[]{:S(2)}, u32[]{:S(2)}) collective-permute-start(bf16[4,3,16,2048]{3,2,1,0:T(8,128)(2,1)S(1)} %pad_maximum_fusion.2.refs_0_), channel_id=1, source_target_pairs={{12,0},{13,1},{14,2},{15,3},{0,4},{1,5},{2,6},{3,7},{4,8},{5,9},{6... | collective-permute-start | bytes 2359304 | tf_op jit(solution)/shard_map/ppermute | solution.py:173
  90.3 46.4 %collective-permute-start.18 = (bf16[4,3,16,2048]{3,2,1,0:T(8,128)(2,1)S(1)}, bf16[4,3,16,2048]{3,2,1,0:T(8,128)(2,1)}, u32[]{:S(2)}, u32[]{:S(2)}) collective-permute-start(bf16[4,3,16,2048]{3,2,1,0:T(8,128)(2,1)S(1)} %pad_maximum_fusion.3.refs_4_), channel_id=1, source_target_pairs={{4,0},{5,1},{6,2},{7,3},{8,4},{9,5},{10,6},{11,7},{12,8},{13,9},{1... | collective-permute-start | bytes 2359304 | tf_op jit(solution)/shard_map/ppermute | solution.py:173
  92.4 44.2 %collective-permute-start.14 = (bf16[4,3,16,2048]{3,2,1,0:T(8,128)(2,1)S(1)}, bf16[4,3,16,2048]{3,2,1,0:T(8,128)(2,1)}, u32[]{:S(2)}, u32[]{:S(2)}) collective-permute-start(bf16[4,3,16,2048]{3,2,1,0:T(8,128)(2,1)S(1)} %collective-permute-done.13.refs_1_), channel_id=1, source_target_pairs={{4,0},{5,1},{6,2},{7,3},{8,4},{9,5},{10,6},{11,7},{12,8},{13,9},{1... | collective-permute-start | bytes 2359304 | tf_op jit(solution)/shard_map/ppermute | solution.py:173
  92.4 44.2 %collective-permute-start.17 = (bf16[4,3,16,2048]{3,2,1,0:T(8,128)(2,1)}, bf16[4,3,16,2048]{3,2,1,0:T(8,128)(2,1)}, u32[]{:S(2)}, u32[]{:S(2)}) collective-permute-start(bf16[4,3,16,2048]{3,2,1,0:T(8,128)(2,1)} %collective-permute-done.16.refs_5_), channel_id=1, source_target_pairs={{12,0},{13,1},{14,2},{15,3},{0,4},{1,5},{2,6},{3,7},{4,8},{5,9},{6... | collective-permute-start | bytes 2359304 | tf_op jit(solution)/shard_map/ppermute | solution.py:173
  104.0 6.3 %collective-permute-start.20 = (f32[16,432]{1,0:T(8,128)S(1)}, f32[16,432]{1,0:T(8,128)S(1)}, u32[]{:S(2)}, u32[]{:S(2)}) collective-permute-start(f32[16,432]{1,0:T(8,128)S(1)} %get-tuple-element.60), channel_id=1, source_target_pairs={{16,17},{17,16},{18,49},{19,48},{20,81},{21,80},{22,113},{23,112},... | collective-permute-start | bytes 82952 | tf_op jit(solution)/shard_map/ppermute | solution.py:374
  110.3 0.7 collective-permute-start.21
  116.5 20.2 %copy-start.1 = (bf16[27,16,256]{2,1,0:T(8,128)(2,1)S(1)}, bf16[27,16,256]{2,1,0:T(8,128)(2,1)}, u32[]{:S(2)}) copy-start(bf16[27,16,256]{2,1,0:T(8,128)(2,1)} %w2.1) | copy-start | bytes 663556
  116.5 32.3 %all-to-all-start.2 = ((f32[8,32,432]{2,1,0:T(8,128)}), f32[8,32,432]{2,1,0:T(8,128)S(1)}, u32[]{:S(2)}, u32[]{:S(2)}) async-start(f32[8,32,432]{2,1,0:T(8,128)} %broadcast_in_dim.2), calls=%async_computation.2 | async-start | bytes 1048576 | tf_op jit(solution)/shard_map/all_to_all | solution.py:380
  148.8 1.9 %copy-start.3 = (f32[8,32,432]{2,1,0:T(8,128)}, f32[8,32,432]{2,1,0:T(8,128)S(1)}, u32[]{:S(2)}) copy-start(f32[8,32,432]{2,1,0:T(8,128)S(1)} %all-to-all-done.2) | copy-start | bytes 1327108
  148.8 1.9 %collective-permute-start.22 = (f32[256,432]{1,0:T(8,128)S(1)}, f32[256,432]{1,0:T(8,128)S(1)}, u32[]{:S(2)}, u32[]{:S(2)}) collective-permute-start(f32[256,432]{1,0:T(8,128)S(1)} %bitcast.26), channel_id=1, source_target_pairs={{0,16},{16,0},{32,48},{48,32},{64,80},{80,64},{96,112},{112,96},{1... | collective-permute-start | bytes 1327112 | tf_op jit(solution)/shard_map/ppermute | solution.py:354
  150.7 0.8 copy-start.7

commit v3 on v2

--- a/solution.py
+++ b/solution.py
@@ -19,6 +19,7 @@
 ROWS = TAPS * BLK
 
 SIDE = 4
+HALF = (8, 2, BLK, ROWS)
 
 
 def axis_masks():
@@ -136,8 +137,10 @@
 
     @pl.when(s == pl.num_programs(0) - 1)
     def _():
-        keep_out[...] = grads[core]
-        send_out[...] = grads[1 - core]
+        for z in range(8):
+            for k in range(2):
+                keep_out[z, k] = grads[k, pl.ds(pl.multiple_of((2 * z + core) * BLK, BLK), BLK), :]
+                send_out[z, k] = grads[k, pl.ds(pl.multiple_of((2 * z + 1 - core) * BLK, BLK), BLK), :]
 
 
 def kernel_two(scalars, *refs):
@@ -243,14 +246,14 @@
             num_scalar_prefetch=1,
             grid=(slots,),
             in_specs=piece_specs() + [pair_spec()],
-            out_specs=[pl.BlockSpec((C, ROWS), lambda s, *_: (0, 0))] * 2,
+            out_specs=[pl.BlockSpec(HALF, lambda s, *_: (0, 0, 0, 0))] * 2,
             scratch_shapes=[
                 pltpu.VMEM((C, CELLS), jnp.bfloat16),
                 pltpu.VMEM((ROWS, CELLS), jnp.bfloat16),
                 pltpu.VMEM((2, C, ROWS), jnp.float32),
             ],
         ),
-        out_shape=[jax.ShapeDtypeStruct((C, ROWS), jnp.float32)] * 2,
+        out_shape=[jax.ShapeDtypeStruct(HALF, jnp.float32)] * 2,
         compiler_params=params(),
         cost_estimate=pl.CostEstimate(
             flops=slots * 4 * ROWS * C * CELLS, transcendentals=0, bytes_accessed=slots * 4 * C * CELLS
@@ -277,7 +280,7 @@
         out_shape=[flat, flat],
         compiler_params=params(),
         cost_estimate=pl.CostEstimate(
-            flops=slots * 160 * ROWS * C * CELLS, transcendentals=0, bytes_accessed=slots * 4 * C * CELLS
+            flops=slots * 4 * ROWS * C * CELLS, transcendentals=0, bytes_accessed=slots * 4 * C * CELLS
         ),
     )(scalars, *pieces, w2, w1t)
 
@@ -324,26 +327,55 @@
     )(scalars, w1, w2)
 
 
-def kernel_finish(scalars, own, other, first_ref, second_ref):
-    @pl.when(scalars[3] == 0)
-    def _():
-        first_ref[...] = own[...].T
-        second_ref[...] = other[...].T
-
-    @pl.when(scalars[3] == 1)
-    def _():
-        first_ref[...] = other[...].T
-        second_ref[...] = own[...].T
+def kernel_collect(mine, got, out_ref):
+    lane = lax.broadcasted_iota(jnp.int32, (BLK, 128), 1) >> 4
+    flipped = got[...].T
+    wide = jnp.concatenate([flipped, jnp.zeros((ROWS, 128 - BLK), jnp.float32)], axis=1)
+    for z in range(8):
+        out_ref[z, 0] = mine[...]
+    for low in range(0, TAPS, 8):
+        total = None
+        count = min(8, TAPS - low)
+        for j in range(count):
+            tile = wide[(low + j) * BLK:(low + j + 1) * BLK, :]
+            moved = pltpu.roll(tile, BLK * j, 1) if j else tile
+            total = moved if total is None else jnp.where(lane == j, moved, total)
+        width = BLK * count
+        for z in range(8):
+            out_ref[z, 1, :, low * BLK:low * BLK + width] = total[:, :width]
+
+
+def collect(mine, got):
+    return pl.pallas_call(
+        kernel_collect,
+        name="collect_rows",
+        out_shape=jax.ShapeDtypeStruct(HALF, jnp.float32),
+        cost_estimate=pl.CostEstimate(flops=0, transcendentals=0, bytes_accessed=4 * ROWS * C),
+    )(mine, got)
+
+
+def kernel_finish(scalars, own, other, first_ref, second_ref, full):
+    core = scalars[3]
+    scale = 1.0 / (BLK * CELLS) ** 0.5
+    for k, out_ref in enumerate((first_ref, second_ref)):
+        for z in range(8):
+            full[pl.ds(pl.multiple_of((2 * z + core) * BLK, BLK), BLK), :] = own[z, k]
+            full[pl.ds(pl.multiple_of((2 * z + 1 - core) * BLK, BLK), BLK), :] = other[z, k]
+        out_ref[...] = full[...].T * scale
 
 
 def finish(scalars, own, other):
-    whole = pl.BlockSpec((C, ROWS), lambda i, *_: (0, 0))
+    half = pl.BlockSpec(HALF, lambda i, *_: (0, 0, 0, 0))
     turned = pl.BlockSpec((ROWS, C), lambda i, *_: (0, 0))
     return pl.pallas_call(
         kernel_finish,
         name="finish_gradients",
         grid_spec=pltpu.PrefetchScalarGridSpec(
-            num_scalar_prefetch=1, grid=(1,), in_specs=[whole, whole], out_specs=[turned, turned]
+            num_scalar_prefetch=1,
+            grid=(1,),
+            in_specs=[half, half],
+            out_specs=[turned, turned],
+            scratch_shapes=[pltpu.VMEM((C, ROWS), jnp.float32)],
         ),
         out_shape=[jax.ShapeDtypeStruct((ROWS, C), jnp.float32)] * 2,
         cost_estimate=pl.CostEstimate(flops=0, transcendentals=0, bytes_accessed=16 * ROWS * C),
@@ -354,30 +386,16 @@
     return lax.ppermute(v, "dp", [(d, d ^ 1) for d in range(BLK)])
 
 
-def sum_over_dp(scalars, keep, send):
+def over_z(v):
     by_core = [[2 * z + core for z in range(8)] for core in range(2)]
-    total = keep + swap_cores(send)
-    parts = lax.all_to_all(total.reshape(8, 32, ROWS), "dp", 0, 0, axis_index_groups=by_core, tiled=True)
-    scale = 1.0 / jnp.sqrt(jnp.float32(lax.axis_size("dp") * CELLS))
-    mine = parts.sum(axis=0) * scale
-
-    odd = lax.axis_index("filter") % 2 == 1
-    low, high = mine[:BLK], mine[BLK:]
-    got = []
-    for m in range(2):
-        pairs = []
-        for z in range(8):
-            for f in range(BLK):
-                j = (f + m) % 2
-                pairs.append(((2 * z + 1) * BLK + f, (2 * (f // 2) + 1) * BLK + 2 * z + j))
-        message = jnp.where(odd, low, high) if m else jnp.where(odd, high, low)
-        got.append(lax.ppermute(message, ("dp", "filter"), pairs))
-    halves = jnp.stack([jnp.where(odd, got[1], got[0]), jnp.where(odd, got[0], got[1])])
-    second = halves.reshape(2, BLK, TAPS, BLK).transpose(0, 3, 2, 1).reshape(2 * BLK, ROWS)
-    piece = jnp.where(scalars[3] == 0, mine, second)
-
-    copies = jnp.broadcast_to(piece[None], (8, 2 * BLK, ROWS))
-    return lax.all_to_all(copies, "dp", 0, 0, axis_index_groups=by_core, tiled=True).reshape(C, ROWS)
+    return lax.all_to_all(v, "dp", 0, 0, axis_index_groups=by_core, tiled=True)
+
+
+def sum_over_dp(keep, send):
+    mine = over_z(keep + swap_cores(send)).sum(axis=0)
+    flip = [(d * BLK + f, f * BLK + d) for d in range(BLK) for f in range(BLK)]
+    got = lax.ppermute(mine[1], ("dp", "filter"), flip)
+    return over_z(collect(mine[0], got))
 
 
 def both_gradients(scalars, own):
@@ -395,7 +413,6 @@
     fars = gather_far(nears)
 
     turned = lax.all_to_all(split, "filter", 0, 0, tiled=True).reshape(C, ROWS)
-    fars, turned = lax.optimization_barrier((fars, turned))
     pieces = gather_last(fars)
     other = swap_cores(turned)
     w1t = jnp.where(core == 0, turned, other).T
@@ -406,7 +423,7 @@
     pair = call_one(scalars, pieces, w1, w2t)
     second_pieces = gather_last(gather_far(gather_near(pair)))
     keep, send = call_grads(scalars, pieces, pair)
-    own = sum_over_dp(scalars, keep, send)
+    own = sum_over_dp(keep, send)
     out, in_grad = call_two(scalars, second_pieces, w2, w1t)
     out, in_grad, own = lax.optimization_barrier((out, in_grad, own))
     first_grad, second_grad = both_gradients(scalars, own)

time: 153 us -> 147 us (0.961); the launches traced: 155 us -> 145 us
  starting transfers between devices: 70.7 us -> 58.3 us
  waiting for transfers between devices: 33.9 us -> 43.5 us
  local copies, waits for them, and re-layouts: 7.23 us -> 4 us
  Pallas kernels: 18.3 us -> 15.8 us
    all_to_all x2, starting transfers between devices: 31.4 us -> 18.8 us  [over_z(): return lax.all_to_all(v, 'dp', 0, 0, axis_index_groups=by_core, tiled=True)]
    all_to_all x2, waiting for transfers between devices: 17.4 us -> 24.6 us  [over_z(): return lax.all_to_all(v, 'dp', 0, 0, axis_index_groups=by_core, tiled=True)]
    ppermute x18, waiting for transfers between devices: 9.1 us -> 13.7 us  [turn(): return lax.ppermute(v, ('dp', 'filter'), from_axis(axes, step))]
    ppermute x18, starting transfers between devices: 21.1 us -> 23 us  [turn(): return lax.ppermute(v, ('dp', 'filter'), from_axis(axes, step))]
    ppermute x2 -> x1, waiting for transfers between devices: 4.39 us -> 2.54 us  [sum_over_dp(): got = lax.ppermute(mine[1], ('dp', 'filter'), flip)]
    pallas_call x0 -> x1, Pallas kernels: none -> 1.81 us  [collect(): pl.pallas_call(kernel_collect, name='collect_rows', out_shape=jax.ShapeDt...]
    ppermute x3, starting transfers between devices: 15.6 us -> 13.9 us  [swap_cores(): return lax.ppermute(v, 'dp', [(d, d ^ 1) for d in range(BLK)])]
  transfers between devices with their start and end apart: 25 -> 24, of which waited for: 8 -> 9; matrix products, arithmetic and copies ran while one was open for 5% -> 2% of each run, Pallas kernels for 7% -> 7%
where the time goes in v3:
time: 147 us; the launch traced here: 145 us
  starting transfers between devices  58.3 us (40%)
  waiting for transfers between devices  43.5 us (30%)
  blocking collectives  18.8 us (13%)
  Pallas kernels  15.8 us (11%)
  local copies, waits for them, and re-layouts  4 us (3%)
  other arithmetic  3.08 us (2%)
  between operations  1.53 us (1%)
    all_to_all x2, waiting for transfers between devices, over_z(): return lax.all_to_all(v, 'dp', 0, 0, axis_index_groups=by_core, tiled=True)  24.6 us
    ppermute x18, starting transfers between devices, turn(): return lax.ppermute(v, ('dp', 'filter'), from_axis(axes, step))  23 us
    all_to_all x2, starting transfers between devices, over_z(): return lax.all_to_all(v, 'dp', 0, 0, axis_index_groups=by_core, tiled=True)  18.8 us
    all_to_all x1, blocking collectives, shards(): turned = lax.all_to_all(split, 'filter', 0, 0, tiled=True).reshape(C, ROWS)  18.8 us
    ppermute x3, starting transfers between devices, swap_cores(): return lax.ppermute(v, 'dp', [(d, d ^ 1) for d in range(BLK)])  13.9 us
    ppermute x18, waiting for transfers between devices, turn(): return lax.ppermute(v, ('dp', 'filter'), from_axis(axes, step))  13.7 us
    pallas_call x1, Pallas kernels, call_two(): pl.pallas_call(kernel_two, name='layer_two', grid_spec=pltpu.PrefetchScal...  3.39 us
    unnamed x18, local copies, waits for them, and re-layouts  3.06 us
  transfers between devices with their start and end apart: 24, of which 9 were waited for; matrix products, arithmetic and copies ran while one was open for 2% of the time, Pallas kernels for 7%

profile of v3, /device:TPU:1, one launch (start us, length us, event | category | flops | bytes accessed | tf_op | source)
XLA Modules:
  0.0 145.0 jit_solution(17386148517439184249)
XLA Ops:
  0.6 1.1 pad_maximum_fusion.4
  1.7 2.1 %collective-permute-start.2 = (bf16[2,3,16,2048]{3,2,1,0:T(8,128)(2,1)S(1)}, bf16[2,3,16,2048]{3,2,1,0:T(8,128)(2,1)S(1)}, u32[]{:S(2)}, u32[]{:S(2)}) collective-permute-start(bf16[2,3,16,2048]{3,2,1,0:T(8,128)(2,1)S(1)} %pad_maximum_fusion.4), channel_id=1, source_target_pairs={{3,0},{0,1},{1,2},{2,3},{7,4},{4,5},{5,6},{6,7},{11,8},{8,9},{9,10... | collective-permute-start | bytes 1179656 | tf_op jit(solution)/shard_map/ppermute | solution.py:176
  3.8 2.5 %collective-permute-start.1 = (bf16[2,3,16,2048]{3,2,1,0:T(8,128)(2,1)S(1)}, bf16[2,3,16,2048]{3,2,1,0:T(8,128)(2,1)S(1)}, u32[]{:S(2)}, u32[]{:S(2)}) collective-permute-start(bf16[2,3,16,2048]{3,2,1,0:T(8,128)(2,1)S(1)} %pad_maximum_fusion.4), channel_id=1, source_target_pairs={{2,0},{3,1},{0,2},{1,3},{6,4},{7,5},{4,6},{5,7},{10,8},{11,9},{8,1... | collective-permute-start | bytes 1179656 | tf_op jit(solution)/shard_map/ppermute | solution.py:176
  6.3 1.2 collective-permute-start
  8.1 0.6 pad_add_fusion.scalars
  8.7 2.9 %split_weights.1 = bf16[16,16,432]{2,1,0:T(8,128)(2,1)} custom-call(s32[4]{0:T(128)} %pad_add_fusion.scalars, bf16[27,16,256]{2,1,0:T(8,128)(2,1)} %w1.1, bf16[27,16,256]{2,1,0:T(8,128)(2,1)} %w2.1), custom_call_target="tpu_custom_call" | custom-call | bytes 884736 | tf_op jit(solution)/shard_map/split_weights/pallas_call | solution.py:316
  11.6 4.3 %collective-permute-done.1 = bf16[2,3,16,2048]{3,2,1,0:T(8,128)(2,1)S(1)} collective-permute-done((bf16[2,3,16,2048]{3,2,1,0:T(8,128)(2,1)S(1)}, bf16[2,3,16,2048]{3,2,1,0:T(8,128)(2,1)S(1)}, u32[]{:S(2)}, u32[]{:S(2)}) %collective-permute-start.1) | collective-permute-done | bytes 393248 | tf_op jit(solution)/shard_map/ppermute | solution.py:176
  16.0 0.9 copy-done.5
  16.9 0.1 copy-done.6
  17.0 0.2 pad_maximum_fusion
  17.2 2.5 %collective-permute-start.3 = (bf16[4,3,16,2048]{3,2,1,0:T(8,128)(2,1)S(1)}, bf16[4,3,16,2048]{3,2,1,0:T(8,128)(2,1)S(1)}, u32[]{:S(2)}, u32[]{:S(2)}) collective-permute-start(bf16[4,3,16,2048]{3,2,1,0:T(8,128)(2,1)S(1)} %get-tuple-element.16.refs_0_), channel_id=1, source_target_pairs={{4,0},{5,1},{6,2},{7,3},{8,4},{9,5},{10,6},{11,7},{12,8},{13,9},{1... | collective-permute-start | bytes 2359304 | tf_op jit(solution)/shard_map/ppermute | solution.py:176
  19.7 2.7 %collective-permute-start.8 = (bf16[4,3,16,2048]{3,2,1,0:T(8,128)(2,1)S(1)}, bf16[4,3,16,2048]{3,2,1,0:T(8,128)(2,1)}, u32[]{:S(2)}, u32[]{:S(2)}) collective-permute-start(bf16[4,3,16,2048]{3,2,1,0:T(8,128)(2,1)S(1)} %get-tuple-element.17.refs_4_), channel_id=1, source_target_pairs={{4,0},{5,1},{6,2},{7,3},{8,4},{9,5},{10,6},{11,7},{12,8},{13,9},{1... | collective-permute-start | bytes 2359304 | tf_op jit(solution)/shard_map/ppermute | solution.py:176
  22.4 6.2 %collective-permute-done.3.refs_1_ = bf16[4,3,16,2048]{3,2,1,0:T(8,128)(2,1)S(1)} collective-permute-done((bf16[4,3,16,2048]{3,2,1,0:T(8,128)(2,1)S(1)}, bf16[4,3,16,2048]{3,2,1,0:T(8,128)(2,1)S(1)}, u32[]{:S(2)}, u32[]{:S(2)}) %collective-permute-start.3) | collective-permute-done | bytes 786464 | tf_op jit(solution)/shard_map/ppermute | solution.py:176
  28.6 3.5 %collective-permute-start.4 = (bf16[4,3,16,2048]{3,2,1,0:T(8,128)(2,1)S(1)}, bf16[4,3,16,2048]{3,2,1,0:T(8,128)(2,1)}, u32[]{:S(2)}, u32[]{:S(2)}) collective-permute-start(bf16[4,3,16,2048]{3,2,1,0:T(8,128)(2,1)S(1)} %collective-permute-done.3.refs_1_), channel_id=1, source_target_pairs={{4,0},{5,1},{6,2},{7,3},{8,4},{9,5},{10,6},{11,7},{12,8},{13,9},{1... | collective-permute-start | bytes 2359304 | tf_op jit(solution)/shard_map/ppermute | solution.py:176
  32.2 18.8 %all_to_all.15 = bf16[16,16,432]{2,1,0:T(8,128)(2,1)S(1)} all-to-all(bf16[16,16,432]{2,1,0:T(8,128)(2,1)S(1)} %copy-done.4), channel_id=1, replica_groups=mesh['dp'=16,'filter'=16] {'filter'}, dimensions={0} | all-to-all | bytes 442368 | tf_op jit(solution)/shard_map/all_to_all | solution.py:415
  50.9 0.1 copy.10
  51.1 5.1 %collective-permute-start.9 = (bf16[256,432]{0,1:T(8,128)(2,1)S(1)}, bf16[256,432]{0,1:T(8,128)(2,1)S(1)}, u32[]{:S(2)}, u32[]{:S(2)}) collective-permute-start(bf16[256,432]{0,1:T(8,128)(2,1)S(1)} %copy.10), channel_id=1, source_target_pairs={{0,16},{16,0},{32,48},{48,32},{64,80},{80,64},{96,112},{112,96},{1... | collective-permute-start | bytes 663560 | tf_op jit(solution)/shard_map/ppermute | solution.py:386
  56.2 1.1 collective-permute-done.9
  57.4 0.6 copy-done.2
  58.0 2.3 %layer_one.1.refs_8_ = bf16[2,3,16,2048]{3,2,1,0:T(8,128)(2,1)S(1)} custom-call(s32[4]{0:T(128)S(1)} %copy-done.2, bf16[4,3,16,2048]{3,2,1,0:T(8,128)(2,1)S(1)} %get-tuple-element.16.refs_0_, bf16[4,3,16,2048]{3,2,1,0:T(8,128)(2,1)S(1)} %collective-permute-done.3.refs_1_, bf16[4,3,16,2048]{3,2,1,0:T(8,128)(2,1)} %collective-permute-done.4.refs_2_, ...), custom_call_target="tpu_custom_call" | custom-call | flops 2717908992 | bytes 6291456 | tf_op jit(solution)/shard_map/layer_one/pallas_call | solution.py:222
  60.4 0.6 collective-permute-start.11
  61.0 2.1 %collective-permute-start.10 = (bf16[2,3,16,2048]{3,2,1,0:T(8,128)(2,1)S(1)}, bf16[2,3,16,2048]{3,2,1,0:T(8,128)(2,1)S(1)}, u32[]{:S(2)}, u32[]{:S(2)}) collective-permute-start(bf16[2,3,16,2048]{3,2,1,0:T(8,128)(2,1)S(1)} %layer_one.1.refs_8_), channel_id=1, source_target_pairs={{1,0},{2,1},{3,2},{0,3},{5,4},{6,5},{7,6},{4,7},{9,8},{10,9},{11,1... | collective-permute-start | bytes 1179656 | tf_op jit(solution)/shard_map/ppermute | solution.py:176
  63.1 2.4 %weight_grads.1 = (f32[8,2,16,432]{3,2,1,0:T(8,128)S(1)}, f32[8,2,16,432]{3,2,1,0:T(8,128)S(1)}) custom-call(s32[4]{0:T(128)S(1)} %copy-done.2, bf16[4,3,16,2048]{3,2,1,0:T(8,128)(2,1)S(1)} %get-tuple-element.16.refs_0_, bf16[4,3,16,2048]{3,2,1,0:T(8,128)(2,1)S(1)} %collective-permute-done.3.refs_1_, ...), custom_call_target="tpu_custom_call" | custom-call | flops 2717908992 | bytes 6291456 | tf_op jit(solution)/shard_map/weight_grads/pallas_call | solution.py:242
  65.5 4.6 %collective-permute-start.19 = (f32[8,2,16,432]{3,2,1,0:T(8,128)S(1)}, f32[8,2,16,432]{3,2,1,0:T(8,128)S(1)}, u32[]{:S(2)}, u32[]{:S(2)}) collective-permute-start(f32[8,2,16,432]{3,2,1,0:T(8,128)S(1)} %get-tuple-element.22), channel_id=1, source_target_pairs={{0,16},{16,0},{32,48},{48,32},{64,80},{80,64},{96,112},{112,96},{1... | collective-permute-start | bytes 1327112 | tf_op jit(solution)/shard_map/ppermute | solution.py:386
  70.2 2.6 %collective-permute-done.12 = bf16[2,3,16,2048]{3,2,1,0:T(8,128)(2,1)S(1)} collective-permute-done((bf16[2,3,16,2048]{3,2,1,0:T(8,128)(2,1)S(1)}, bf16[2,3,16,2048]{3,2,1,0:T(8,128)(2,1)S(1)}, u32[]{:S(2)}, u32[]{:S(2)}) %collective-permute-start.12) | collective-permute-done | bytes 393248 | tf_op jit(solution)/shard_map/ppermute | solution.py:176
  72.8 0.5 collective-permute-done.10
  73.4 0.1 pad_maximum_fusion.2.refs_0_
  73.5 1.2 collective-permute-start.13
  74.7 0.1 pad_maximum_fusion.3.refs_4_
  74.8 0.5 collective-permute-start.16
  75.3 0.9 add.13
  76.2 10.9 %all-to-all-start.1 = ((f32[8,2,16,432]{3,2,1,0:T(8,128)}), f32[8,2,16,432]{3,2,1,0:T(8,128)S(1)}, u32[]{:S(2)}, u32[]{:S(2)}) async-start(f32[8,2,16,432]{3,2,1,0:T(8,128)} %add.13), calls=%async_computation.1 | async-start | bytes 1048576 | tf_op jit(solution)/shard_map/all_to_all | solution.py:391
  87.1 0.3 collective-permute-start.15
  87.4 2.4 %collective-permute-start.18 = (bf16[4,3,16,2048]{3,2,1,0:T(8,128)(2,1)S(1)}, bf16[4,3,16,2048]{3,2,1,0:T(8,128)(2,1)}, u32[]{:S(2)}, u32[]{:S(2)}) collective-permute-start(bf16[4,3,16,2048]{3,2,1,0:T(8,128)(2,1)S(1)} %pad_maximum_fusion.3.refs_4_), channel_id=1, source_target_pairs={{4,0},{5,1},{6,2},{7,3},{8,4},{9,5},{10,6},{11,7},{12,8},{13,9},{1... | collective-permute-start | bytes 2359304 | tf_op jit(solution)/shard_map/ppermute | solution.py:176
  89.8 1.4 collective-permute-start.14
  91.2 13.7 %all-to-all-done.1 = f32[8,2,16,432]{3,2,1,0:T(8,128)S(1)} async-done(((f32[8,2,16,432]{3,2,1,0:T(8,128)}), f32[8,2,16,432]{3,2,1,0:T(8,128)S(1)}, u32[]{:S(2)}, u32[]{:S(2)}) %all-to-all-start.1) | async-done | bytes 442400 | tf_op jit(solution)/shard_map/all_to_all | solution.py:391
  105.0 0.6 slice_bitcast_fusion
  105.6 2.7 %collective-permute-start.20 = (f32[16,432]{1,0:T(8,128)S(1)}, f32[16,432]{1,0:T(8,128)S(1)}, u32[]{:S(2)}, u32[]{:S(2)}) collective-permute-start(f32[16,432]{1,0:T(8,128)S(1)} %get-tuple-element.44), channel_id=1, source_target_pairs={{0,0},{1,16},{2,32},{3,48},{4,64},{5,80},{6,96},{7,112},{8,128},{9... | collective-permute-start | bytes 82952 | tf_op jit(solution)/shard_map/ppermute | solution.py:397
  108.3 2.5 %collective-permute-done.20.got = f32[16,432]{1,0:T(8,128)S(1)} collective-permute-done((f32[16,432]{1,0:T(8,128)S(1)}, f32[16,432]{1,0:T(8,128)S(1)}, u32[]{:S(2)}, u32[]{:S(2)}) %collective-permute-start.20) | collective-permute-done | bytes 27680 | tf_op jit(solution)/shard_map/ppermute | solution.py:397
  110.8 0.6 copy-done.8
  111.4 1.8 %collect_rows.1 = f32[8,2,16,432]{3,2,1,0:T(8,128)} custom-call(f32[16,432]{1,0:T(8,128)} %get-tuple-element.45.mine, f32[16,432]{1,0:T(8,128)} %copy-done.8), custom_call_target="tpu_custom_call" | custom-call | bytes 442368 | tf_op jit(solution)/shard_map/collect_rows/pallas_call | solution.py:349
  113.3 7.9 %all-to-all-start.2 = ((f32[8,2,16,432]{3,2,1,0:T(8,128)}), f32[8,2,16,432]{3,2,1,0:T(8,128)S(1)}, u32[]{:S(2)}, u32[]{:S(2)}) async-start(f32[8,2,16,432]{3,2,1,0:T(8,128)} %collect_rows.1), calls=%async_computation.2 | async-start | bytes 1048576 | tf_op jit(solution)/shard_map/all_to_all | solution.py:391
  121.2 3.4 %layer_two.1 = (f32[3,16,2048]{2,1,0:T(8,128)}, f32[3,16,2048]{2,1,0:T(8,128)}) custom-call(s32[4]{0:T(128)S(1)} %copy-done.2, bf16[4,3,16,2048]{3,2,1,0:T(8,128)(2,1)S(1)} %pad_maximum_fusion.2.refs_0_, bf16[4,3,16,2048]{3,2,1,0:T(8,128)(2,1)S(1)} %collective-permute-done.13.refs_1_, bf16[4,3,16,2048]{3,2,1,0:T(8,128)(2,1)} %collective-permute-done.14.refs_2_, ...), custom_call_target="tpu_custom_call" | custom-call | flops 2717908992 | bytes 6291456 | tf_op jit(solution)/shard_map/layer_two/pallas_call | solution.py:267
  124.6 10.9 %all-to-all-done.2.own = f32[8,2,16,432]{3,2,1,0:T(8,128)S(1)} async-done(((f32[8,2,16,432]{3,2,1,0:T(8,128)}), f32[8,2,16,432]{3,2,1,0:T(8,128)S(1)}, u32[]{:S(2)}, u32[]{:S(2)}) %all-to-all-start.2) | async-done | bytes 442400 | tf_op jit(solution)/shard_map/all_to_all | solution.py:391
  135.5 4.1 %collective-permute-start.21 = (f32[8,2,16,432]{3,2,1,0:T(8,128)S(1)}, f32[8,2,16,432]{3,2,1,0:T(8,128)S(1)}, u32[]{:S(2)}, u32[]{:S(2)}) collective-permute-start(f32[8,2,16,432]{3,2,1,0:T(8,128)S(1)} %all-to-all-done.2.own), channel_id=1, source_target_pairs={{0,16},{16,0},{32,48},{48,32},{64,80},{80,64},{96,112},{112,96},{1... | collective-permute-start | bytes 1327112 | tf_op jit(solution)/shard_map/ppermute | solution.py:386
  139.6 1.5 %collective-permute-done.21.other = f32[8,2,16,432]{3,2,1,0:T(8,128)S(1)} collective-permute-done((f32[8,2,16,432]{3,2,1,0:T(8,128)S(1)}, f32[8,2,16,432]{3,2,1,0:T(8,128)S(1)}, u32[]{:S(2)}, u32[]{:S(2)}) %collective-permute-start.21) | collective-permute-done | bytes 442400 | tf_op jit(solution)/shard_map/ppermute | solution.py:386
  141.1 0.8 copy-done.7
  142.0 3.0 %finish_gradients.1 = (f32[432,256]{1,0:T(8,128)}, f32[432,256]{1,0:T(8,128)}) custom-call(s32[4]{0:T(128)} %pad_add_fusion.scalars, f32[8,2,16,432]{3,2,1,0:T(8,128)} %copy-done.3, f32[8,2,16,432]{3,2,1,0:T(8,128)} %copy-done.7), custom_call_target="tpu_custom_call" | custom-call | bytes 1769472 | tf_op jit(solution)/shard_map/finish_gradients/pallas_call | solution.py:370
  (42 shorter events, 0.5 us)
Async XLA Ops:
  1.7 9.9 %collective-permute-start.2 = (bf16[2,3,16,2048]{3,2,1,0:T(8,128)(2,1)S(1)}, bf16[2,3,16,2048]{3,2,1,0:T(8,128)(2,1)S(1)}, u32[]{:S(2)}, u32[]{:S(2)}) collective-permute-start(bf16[2,3,16,2048]{3,2,1,0:T(8,128)(2,1)S(1)} %pad_maximum_fusion.4), channel_id=1, source_target_pairs={{3,0},{0,1},{1,2},{2,3},{7,4},{4,5},{5,6},{6,7},{11,8},{8,9},{9,10... | collective-permute-start | bytes 1179656 | tf_op jit(solution)/shard_map/ppermute | solution.py:176
  3.8 12.1 %collective-permute-start.1 = (bf16[2,3,16,2048]{3,2,1,0:T(8,128)(2,1)S(1)}, bf16[2,3,16,2048]{3,2,1,0:T(8,128)(2,1)S(1)}, u32[]{:S(2)}, u32[]{:S(2)}) collective-permute-start(bf16[2,3,16,2048]{3,2,1,0:T(8,128)(2,1)S(1)} %pad_maximum_fusion.4), channel_id=1, source_target_pairs={{2,0},{3,1},{0,2},{1,3},{6,4},{7,5},{4,6},{5,7},{10,8},{11,9},{8,1... | collective-permute-start | bytes 1179656 | tf_op jit(solution)/shard_map/ppermute | solution.py:176
  6.3 9.7 %collective-permute-start = (bf16[2,3,16,2048]{3,2,1,0:T(8,128)(2,1)S(1)}, bf16[2,3,16,2048]{3,2,1,0:T(8,128)(2,1)S(1)}, u32[]{:S(2)}, u32[]{:S(2)}) collective-permute-start(bf16[2,3,16,2048]{3,2,1,0:T(8,128)(2,1)S(1)} %pad_maximum_fusion.4), channel_id=1, source_target_pairs={{1,0},{2,1},{3,2},{0,3},{5,4},{6,5},{7,6},{4,7},{9,8},{10,9},{11,1... | collective-permute-start | bytes 1179656 | tf_op jit(solution)/shard_map/ppermute | solution.py:176
  16.0 0.9 copy-start.5
  16.0 1.0 copy-start.6
  17.0 15.2 %copy-start.4 = (bf16[16,16,432]{2,1,0:T(8,128)(2,1)S(1)}, bf16[16,16,432]{2,1,0:T(8,128)(2,1)}, u32[]{:S(2)}) copy-start(bf16[16,16,432]{2,1,0:T(8,128)(2,1)} %split_weights.1) | copy-start | bytes 663556
  17.2 11.5 %collective-permute-start.3 = (bf16[4,3,16,2048]{3,2,1,0:T(8,128)(2,1)S(1)}, bf16[4,3,16,2048]{3,2,1,0:T(8,128)(2,1)S(1)}, u32[]{:S(2)}, u32[]{:S(2)}) collective-permute-start(bf16[4,3,16,2048]{3,2,1,0:T(8,128)(2,1)S(1)} %get-tuple-element.16.refs_0_), channel_id=1, source_target_pairs={{4,0},{5,1},{6,2},{7,3},{8,4},{9,5},{10,6},{11,7},{12,8},{13,9},{1... | collective-permute-start | bytes 2359304 | tf_op jit(solution)/shard_map/ppermute | solution.py:176
  19.7 12.5 %collective-permute-start.6 = (bf16[4,3,16,2048]{3,2,1,0:T(8,128)(2,1)S(1)}, bf16[4,3,16,2048]{3,2,1,0:T(8,128)(2,1)}, u32[]{:S(2)}, u32[]{:S(2)}) collective-permute-start(bf16[4,3,16,2048]{3,2,1,0:T(8,128)(2,1)S(1)} %get-tuple-element.17.refs_4_), channel_id=1, source_target_pairs={{12,0},{13,1},{14,2},{15,3},{0,4},{1,5},{2,6},{3,7},{4,8},{5,9},{6... | collective-permute-start | bytes 2359304 | tf_op jit(solution)/shard_map/ppermute | solution.py:176
  19.7 37.6 %collective-permute-start.5 = (bf16[4,3,16,2048]{3,2,1,0:T(8,128)(2,1)S(1)}, bf16[4,3,16,2048]{3,2,1,0:T(8,128)(2,1)}, u32[]{:S(2)}, u32[]{:S(2)}) collective-permute-start(bf16[4,3,16,2048]{3,2,1,0:T(8,128)(2,1)S(1)} %get-tuple-element.16.refs_0_), channel_id=1, source_target_pairs={{12,0},{13,1},{14,2},{15,3},{0,4},{1,5},{2,6},{3,7},{4,8},{5,9},{6... | collective-permute-start | bytes 2359304 | tf_op jit(solution)/shard_map/ppermute | solution.py:176
  19.7 37.6 %collective-permute-start.8 = (bf16[4,3,16,2048]{3,2,1,0:T(8,128)(2,1)S(1)}, bf16[4,3,16,2048]{3,2,1,0:T(8,128)(2,1)}, u32[]{:S(2)}, u32[]{:S(2)}) collective-permute-start(bf16[4,3,16,2048]{3,2,1,0:T(8,128)(2,1)S(1)} %get-tuple-element.17.refs_4_), channel_id=1, source_target_pairs={{4,0},{5,1},{6,2},{7,3},{8,4},{9,5},{10,6},{11,7},{12,8},{13,9},{1... | collective-permute-start | bytes 2359304 | tf_op jit(solution)/shard_map/ppermute | solution.py:176
  28.6 28.7 %collective-permute-start.4 = (bf16[4,3,16,2048]{3,2,1,0:T(8,128)(2,1)S(1)}, bf16[4,3,16,2048]{3,2,1,0:T(8,128)(2,1)}, u32[]{:S(2)}, u32[]{:S(2)}) collective-permute-start(bf16[4,3,16,2048]{3,2,1,0:T(8,128)(2,1)S(1)} %collective-permute-done.3.refs_1_), channel_id=1, source_target_pairs={{4,0},{5,1},{6,2},{7,3},{8,4},{9,5},{10,6},{11,7},{12,8},{13,9},{1... | collective-permute-start | bytes 2359304 | tf_op jit(solution)/shard_map/ppermute | solution.py:176
  32.2 25.2 %collective-permute-start.7 = (bf16[4,3,16,2048]{3,2,1,0:T(8,128)(2,1)}, bf16[4,3,16,2048]{3,2,1,0:T(8,128)(2,1)}, u32[]{:S(2)}, u32[]{:S(2)}) collective-permute-start(bf16[4,3,16,2048]{3,2,1,0:T(8,128)(2,1)} %collective-permute-done.6.refs_5_), channel_id=1, source_target_pairs={{12,0},{13,1},{14,2},{15,3},{0,4},{1,5},{2,6},{3,7},{4,8},{5,9},{6... | collective-permute-start | bytes 2359304 | tf_op jit(solution)/shard_map/ppermute | solution.py:176
  51.1 6.2 %collective-permute-start.9 = (bf16[256,432]{0,1:T(8,128)(2,1)S(1)}, bf16[256,432]{0,1:T(8,128)(2,1)S(1)}, u32[]{:S(2)}, u32[]{:S(2)}) collective-permute-start(bf16[256,432]{0,1:T(8,128)(2,1)S(1)} %copy.10), channel_id=1, source_target_pairs={{0,16},{16,0},{32,48},{48,32},{64,80},{80,64},{96,112},{112,96},{1... | collective-permute-start | bytes 663560 | tf_op jit(solution)/shard_map/ppermute | solution.py:386
  56.2 1.2 copy-start
  57.4 0.7 copy-start.2
  60.3 12.4 %collective-permute-start.12 = (bf16[2,3,16,2048]{3,2,1,0:T(8,128)(2,1)S(1)}, bf16[2,3,16,2048]{3,2,1,0:T(8,128)(2,1)S(1)}, u32[]{:S(2)}, u32[]{:S(2)}) collective-permute-start(bf16[2,3,16,2048]{3,2,1,0:T(8,128)(2,1)S(1)} %layer_one.1.refs_8_), channel_id=1, source_target_pairs={{3,0},{0,1},{1,2},{2,3},{7,4},{4,5},{5,6},{6,7},{11,8},{8,9},{9,10... | collective-permute-start | bytes 1179656 | tf_op jit(solution)/shard_map/ppermute | solution.py:176
  60.4 12.4 %collective-permute-start.11 = (bf16[2,3,16,2048]{3,2,1,0:T(8,128)(2,1)S(1)}, bf16[2,3,16,2048]{3,2,1,0:T(8,128)(2,1)S(1)}, u32[]{:S(2)}, u32[]{:S(2)}) collective-permute-start(bf16[2,3,16,2048]{3,2,1,0:T(8,128)(2,1)S(1)} %layer_one.1.refs_8_), channel_id=1, source_target_pairs={{2,0},{3,1},{0,2},{1,3},{6,4},{7,5},{4,6},{5,7},{10,8},{11,9},{8,1... | collective-permute-start | bytes 1179656 | tf_op jit(solution)/shard_map/ppermute | solution.py:176
  61.0 12.4 %collective-permute-start.10 = (bf16[2,3,16,2048]{3,2,1,0:T(8,128)(2,1)S(1)}, bf16[2,3,16,2048]{3,2,1,0:T(8,128)(2,1)S(1)}, u32[]{:S(2)}, u32[]{:S(2)}) collective-permute-start(bf16[2,3,16,2048]{3,2,1,0:T(8,128)(2,1)S(1)} %layer_one.1.refs_8_), channel_id=1, source_target_pairs={{1,0},{2,1},{3,2},{0,3},{5,4},{6,5},{7,6},{4,7},{9,8},{10,9},{11,1... | collective-permute-start | bytes 1179656 | tf_op jit(solution)/shard_map/ppermute | solution.py:176
  65.5 9.7 %collective-permute-start.19 = (f32[8,2,16,432]{3,2,1,0:T(8,128)S(1)}, f32[8,2,16,432]{3,2,1,0:T(8,128)S(1)}, u32[]{:S(2)}, u32[]{:S(2)}) collective-permute-start(f32[8,2,16,432]{3,2,1,0:T(8,128)S(1)} %get-tuple-element.22), channel_id=1, source_target_pairs={{0,16},{16,0},{32,48},{48,32},{64,80},{80,64},{96,112},{112,96},{1... | collective-permute-start | bytes 1327112 | tf_op jit(solution)/shard_map/ppermute | solution.py:386
  73.5 16.2 %collective-permute-start.13 = (bf16[4,3,16,2048]{3,2,1,0:T(8,128)(2,1)S(1)}, bf16[4,3,16,2048]{3,2,1,0:T(8,128)(2,1)S(1)}, u32[]{:S(2)}, u32[]{:S(2)}) collective-permute-start(bf16[4,3,16,2048]{3,2,1,0:T(8,128)(2,1)S(1)} %pad_maximum_fusion.2.refs_0_), channel_id=1, source_target_pairs={{4,0},{5,1},{6,2},{7,3},{8,4},{9,5},{10,6},{11,7},{12,8},{13,9},{1... | collective-permute-start | bytes 2359304 | tf_op jit(solution)/shard_map/ppermute | solution.py:176
  74.8 16.3 %collective-permute-start.16 = (bf16[4,3,16,2048]{3,2,1,0:T(8,128)(2,1)S(1)}, bf16[4,3,16,2048]{3,2,1,0:T(8,128)(2,1)}, u32[]{:S(2)}, u32[]{:S(2)}) collective-permute-start(bf16[4,3,16,2048]{3,2,1,0:T(8,128)(2,1)S(1)} %pad_maximum_fusion.3.refs_4_), channel_id=1, source_target_pairs={{12,0},{13,1},{14,2},{15,3},{0,4},{1,5},{2,6},{3,7},{4,8},{5,9},{6... | collective-permute-start | bytes 2359304 | tf_op jit(solution)/shard_map/ppermute | solution.py:176
  76.2 28.8 %all-to-all-start.1 = ((f32[8,2,16,432]{3,2,1,0:T(8,128)}), f32[8,2,16,432]{3,2,1,0:T(8,128)S(1)}, u32[]{:S(2)}, u32[]{:S(2)}) async-start(f32[8,2,16,432]{3,2,1,0:T(8,128)} %add.13), calls=%async_computation.1 | async-start | bytes 1048576 | tf_op jit(solution)/shard_map/all_to_all | solution.py:391
  87.1 34.0 %collective-permute-start.15 = (bf16[4,3,16,2048]{3,2,1,0:T(8,128)(2,1)S(1)}, bf16[4,3,16,2048]{3,2,1,0:T(8,128)(2,1)}, u32[]{:S(2)}, u32[]{:S(2)}) collective-permute-start(bf16[4,3,16,2048]{3,2,1,0:T(8,128)(2,1)S(1)} %pad_maximum_fusion.2.refs_0_), channel_id=1, source_target_pairs={{12,0},{13,1},{14,2},{15,3},{0,4},{1,5},{2,6},{3,7},{4,8},{5,9},{6... | collective-permute-start | bytes 2359304 | tf_op jit(solution)/shard_map/ppermute | solution.py:176
  87.4 33.8 %collective-permute-start.18 = (bf16[4,3,16,2048]{3,2,1,0:T(8,128)(2,1)S(1)}, bf16[4,3,16,2048]{3,2,1,0:T(8,128)(2,1)}, u32[]{:S(2)}, u32[]{:S(2)}) collective-permute-start(bf16[4,3,16,2048]{3,2,1,0:T(8,128)(2,1)S(1)} %pad_maximum_fusion.3.refs_4_), channel_id=1, source_target_pairs={{4,0},{5,1},{6,2},{7,3},{8,4},{9,5},{10,6},{11,7},{12,8},{13,9},{1... | collective-permute-start | bytes 2359304 | tf_op jit(solution)/shard_map/ppermute | solution.py:176
  89.8 31.4 %collective-permute-start.14 = (bf16[4,3,16,2048]{3,2,1,0:T(8,128)(2,1)S(1)}, bf16[4,3,16,2048]{3,2,1,0:T(8,128)(2,1)}, u32[]{:S(2)}, u32[]{:S(2)}) collective-permute-start(bf16[4,3,16,2048]{3,2,1,0:T(8,128)(2,1)S(1)} %collective-permute-done.13.refs_1_), channel_id=1, source_target_pairs={{4,0},{5,1},{6,2},{7,3},{8,4},{9,5},{10,6},{11,7},{12,8},{13,9},{1... | collective-permute-start | bytes 2359304 | tf_op jit(solution)/shard_map/ppermute | solution.py:176
  91.1 30.0 %collective-permute-start.17 = (bf16[4,3,16,2048]{3,2,1,0:T(8,128)(2,1)}, bf16[4,3,16,2048]{3,2,1,0:T(8,128)(2,1)}, u32[]{:S(2)}, u32[]{:S(2)}) collective-permute-start(bf16[4,3,16,2048]{3,2,1,0:T(8,128)(2,1)} %collective-permute-done.16.refs_5_), channel_id=1, source_target_pairs={{12,0},{13,1},{14,2},{15,3},{0,4},{1,5},{2,6},{3,7},{4,8},{5,9},{6... | collective-permute-start | bytes 2359304 | tf_op jit(solution)/shard_map/ppermute | solution.py:176
  105.6 5.2 %collective-permute-start.20 = (f32[16,432]{1,0:T(8,128)S(1)}, f32[16,432]{1,0:T(8,128)S(1)}, u32[]{:S(2)}, u32[]{:S(2)}) collective-permute-start(f32[16,432]{1,0:T(8,128)S(1)} %get-tuple-element.44), channel_id=1, source_target_pairs={{0,0},{1,16},{2,32},{3,48},{4,64},{5,80},{6,96},{7,112},{8,128},{9... | collective-permute-start | bytes 82952 | tf_op jit(solution)/shard_map/ppermute | solution.py:397
  110.8 0.6 copy-start.8
  113.2 7.9 %copy-start.1 = (bf16[27,16,256]{2,1,0:T(8,128)(2,1)S(1)}, bf16[27,16,256]{2,1,0:T(8,128)(2,1)}, u32[]{:S(2)}) copy-start(bf16[27,16,256]{2,1,0:T(8,128)(2,1)} %w2.1) | copy-start | bytes 663556
  113.3 22.2 %all-to-all-start.2 = ((f32[8,2,16,432]{3,2,1,0:T(8,128)}), f32[8,2,16,432]{3,2,1,0:T(8,128)S(1)}, u32[]{:S(2)}, u32[]{:S(2)}) async-start(f32[8,2,16,432]{3,2,1,0:T(8,128)} %collect_rows.1), calls=%async_computation.2 | async-start | bytes 1048576 | tf_op jit(solution)/shard_map/all_to_all | solution.py:391
  135.5 5.7 %copy-start.3 = (f32[8,2,16,432]{3,2,1,0:T(8,128)}, f32[8,2,16,432]{3,2,1,0:T(8,128)S(1)}, u32[]{:S(2)}) copy-start(f32[8,2,16,432]{3,2,1,0:T(8,128)S(1)} %all-to-all-done.2.own) | copy-start | bytes 1327108
  135.5 5.7 %collective-permute-start.21 = (f32[8,2,16,432]{3,2,1,0:T(8,128)S(1)}, f32[8,2,16,432]{3,2,1,0:T(8,128)S(1)}, u32[]{:S(2)}, u32[]{:S(2)}) collective-permute-start(f32[8,2,16,432]{3,2,1,0:T(8,128)S(1)} %all-to-all-done.2.own), channel_id=1, source_target_pairs={{0,16},{16,0},{32,48},{48,32},{64,80},{80,64},{96,112},{112,96},{1... | collective-permute-start | bytes 1327112 | tf_op jit(solution)/shard_map/ppermute | solution.py:386
  141.1 0.8 copy-start.7

commit v4 on v3

--- a/solution.py
+++ b/solution.py
@@ -331,8 +331,7 @@
     lane = lax.broadcasted_iota(jnp.int32, (BLK, 128), 1) >> 4
     flipped = got[...].T
     wide = jnp.concatenate([flipped, jnp.zeros((ROWS, 128 - BLK), jnp.float32)], axis=1)
-    for z in range(8):
-        out_ref[z, 0] = mine[...]
+    out_ref[0] = mine[...]
     for low in range(0, TAPS, 8):
         total = None
         count = min(8, TAPS - low)
@@ -341,45 +340,34 @@
             moved = pltpu.roll(tile, BLK * j, 1) if j else tile
             total = moved if total is None else jnp.where(lane == j, moved, total)
         width = BLK * count
-        for z in range(8):
-            out_ref[z, 1, :, low * BLK:low * BLK + width] = total[:, :width]
+        out_ref[1, :, low * BLK:low * BLK + width] = total[:, :width]
 
 
 def collect(mine, got):
     return pl.pallas_call(
         kernel_collect,
         name="collect_rows",
-        out_shape=jax.ShapeDtypeStruct(HALF, jnp.float32),
-        cost_estimate=pl.CostEstimate(flops=0, transcendentals=0, bytes_accessed=4 * ROWS * C),
+        out_shape=jax.ShapeDtypeStruct((2, BLK, ROWS), jnp.float32),
+        cost_estimate=pl.CostEstimate(flops=0, transcendentals=0, bytes_accessed=16 * ROWS * BLK),
     )(mine, got)
 
 
-def kernel_finish(scalars, own, other, first_ref, second_ref, full):
-    core = scalars[3]
+def kernel_finish(rows, first_ref, second_ref, full):
     scale = 1.0 / (BLK * CELLS) ** 0.5
     for k, out_ref in enumerate((first_ref, second_ref)):
-        for z in range(8):
-            full[pl.ds(pl.multiple_of((2 * z + core) * BLK, BLK), BLK), :] = own[z, k]
-            full[pl.ds(pl.multiple_of((2 * z + 1 - core) * BLK, BLK), BLK), :] = other[z, k]
+        for d in range(BLK):
+            full[d * BLK:(d + 1) * BLK, :] = rows[d, k]
         out_ref[...] = full[...].T * scale
 
 
-def finish(scalars, own, other):
-    half = pl.BlockSpec(HALF, lambda i, *_: (0, 0, 0, 0))
-    turned = pl.BlockSpec((ROWS, C), lambda i, *_: (0, 0))
+def finish(rows):
     return pl.pallas_call(
         kernel_finish,
         name="finish_gradients",
-        grid_spec=pltpu.PrefetchScalarGridSpec(
-            num_scalar_prefetch=1,
-            grid=(1,),
-            in_specs=[half, half],
-            out_specs=[turned, turned],
-            scratch_shapes=[pltpu.VMEM((C, ROWS), jnp.float32)],
-        ),
         out_shape=[jax.ShapeDtypeStruct((ROWS, C), jnp.float32)] * 2,
+        scratch_shapes=[pltpu.VMEM((C, ROWS), jnp.float32)],
         cost_estimate=pl.CostEstimate(flops=0, transcendentals=0, bytes_accessed=16 * ROWS * C),
-    )(scalars, own, other)
+    )(rows)
 
 
 def swap_cores(v):
@@ -395,11 +383,11 @@
     mine = over_z(keep + swap_cores(send)).sum(axis=0)
     flip = [(d * BLK + f, f * BLK + d) for d in range(BLK) for f in range(BLK)]
     got = lax.ppermute(mine[1], ("dp", "filter"), flip)
-    return over_z(collect(mine[0], got))
-
-
-def both_gradients(scalars, own):
-    first_grad, second_grad = finish(scalars, own, swap_cores(own))
+    return collect(mine[0], got)
+
+
+def both_gradients(piece):
+    first_grad, second_grad = finish(lax.all_gather(piece, "dp", axis=0))
     return first_grad.reshape(TAPS, BLK, C), second_grad.reshape(TAPS, BLK, C)
 
 
@@ -421,12 +409,14 @@
     w2 = second_weight.reshape(ROWS, C)
 
     pair = call_one(scalars, pieces, w1, w2t)
-    second_pieces = gather_last(gather_far(gather_near(pair)))
+    nears = gather_near(pair)
     keep, send = call_grads(scalars, pieces, pair)
-    own = sum_over_dp(keep, send)
+    nears, keep, send = lax.optimization_barrier((nears, keep, send))
+    second_pieces = gather_last(gather_far(nears))
+    piece = sum_over_dp(keep, send)
     out, in_grad = call_two(scalars, second_pieces, w2, w1t)
-    out, in_grad, own = lax.optimization_barrier((out, in_grad, own))
-    first_grad, second_grad = both_gradients(scalars, own)
+    out, in_grad, piece = lax.optimization_barrier((out, in_grad, piece))
+    first_grad, second_grad = both_gradients(piece)
     return (out.transpose(1, 0, 2), in_grad.transpose(1, 0, 2), first_grad, second_grad)
 
 

time: 147 us -> 150 us (1.020); the launches traced: 145 us -> 151 us
  blocking collectives: 18.8 us -> 46.8 us
  starting transfers between devices: 58.3 us -> 44.5 us
  waiting for transfers between devices: 43.5 us -> 37 us
    all_gather x0 -> x1, blocking collectives: none -> 28 us  [both_gradients(): first_grad, second_grad = finish(lax.all_gather(piece, 'dp', axis=0))]
    all_to_all x2 -> x1, starting transfers between devices: 18.8 us -> 7.74 us  [over_z(): return lax.all_to_all(v, 'dp', 0, 0, axis_index_groups=by_core, tiled=True)]
    all_to_all x2 -> x1, waiting for transfers between devices: 24.6 us -> 13.8 us  [over_z(): return lax.all_to_all(v, 'dp', 0, 0, axis_index_groups=by_core, tiled=True)]
    ppermute x18, waiting for transfers between devices: 13.7 us -> 18.4 us  [turn(): return lax.ppermute(v, ('dp', 'filter'), from_axis(axes, step))]
    ppermute x3 -> x2, starting transfers between devices: 13.9 us -> 10.8 us  [swap_cores(): return lax.ppermute(v, 'dp', [(d, d ^ 1) for d in range(BLK)])]
    unnamed x18 -> x16, local copies, waits for them, and re-layouts: 3.06 us -> 2.24 us
  transfers between devices with their start and end apart: 24 -> 22, of which waited for: 9 -> 8; matrix products, arithmetic and copies ran while one was open for 2% -> 2% of each run, Pallas kernels for 7% -> 5%
where the time goes in v4:
time: 150 us; the launch traced here: 151 us
  blocking collectives  46.8 us (31%)
  starting transfers between devices  44.5 us (30%)
  waiting for transfers between devices  37 us (25%)
  Pallas kernels  14.9 us (10%)
  local copies, waits for them, and re-layouts  3.18 us (2%)
  other arithmetic  3 us (2%)
  between operations  1.54 us (1%)
    all_gather x1, blocking collectives, both_gradients(): first_grad, second_grad = finish(lax.all_gather(piece, 'dp', axis=0))  28 us
    ppermute x18, starting transfers between devices, turn(): return lax.ppermute(v, ('dp', 'filter'), from_axis(axes, step))  22.9 us
    all_to_all x1, blocking collectives, shards(): turned = lax.all_to_all(split, 'filter', 0, 0, tiled=True).reshape(C, ROWS)  18.8 us
    ppermute x18, waiting for transfers between devices, turn(): return lax.ppermute(v, ('dp', 'filter'), from_axis(axes, step))  18.4 us
    all_to_all x1, waiting for transfers between devices, over_z(): return lax.all_to_all(v, 'dp', 0, 0, axis_index_groups=by_core, tiled=True)  13.8 us
    ppermute x2, starting transfers between devices, swap_cores(): return lax.ppermute(v, 'dp', [(d, d ^ 1) for d in range(BLK)])  10.8 us
    all_to_all x1, starting transfers between devices, over_z(): return lax.all_to_all(v, 'dp', 0, 0, axis_index_groups=by_core, tiled=True)  7.74 us
    pallas_call x1, Pallas kernels, call_two(): pl.pallas_call(kernel_two, name='layer_two', grid_spec=pltpu.PrefetchScal...  3.39 us
  transfers between devices with their start and end apart: 22, of which 8 were waited for; matrix products, arithmetic and copies ran while one was open for 2% of the time, Pallas kernels for 5%

profile of v4, /device:TPU:1, one launch (start us, length us, event | category | flops | bytes accessed | tf_op | source)
XLA Modules:
  0.0 150.9 jit_solution(17333132659852274681)
XLA Ops:
  0.6 1.1 pad_maximum_fusion.4
  1.7 2.1 %collective-permute-start.2 = (bf16[2,3,16,2048]{3,2,1,0:T(8,128)(2,1)S(1)}, bf16[2,3,16,2048]{3,2,1,0:T(8,128)(2,1)S(1)}, u32[]{:S(2)}, u32[]{:S(2)}) collective-permute-start(bf16[2,3,16,2048]{3,2,1,0:T(8,128)(2,1)S(1)} %pad_maximum_fusion.4), channel_id=1, source_target_pairs={{3,0},{0,1},{1,2},{2,3},{7,4},{4,5},{5,6},{6,7},{11,8},{8,9},{9,10... | collective-permute-start | bytes 1179656 | tf_op jit(solution)/shard_map/ppermute | solution.py:176
  3.8 2.5 %collective-permute-start.1 = (bf16[2,3,16,2048]{3,2,1,0:T(8,128)(2,1)S(1)}, bf16[2,3,16,2048]{3,2,1,0:T(8,128)(2,1)S(1)}, u32[]{:S(2)}, u32[]{:S(2)}) collective-permute-start(bf16[2,3,16,2048]{3,2,1,0:T(8,128)(2,1)S(1)} %pad_maximum_fusion.4), channel_id=1, source_target_pairs={{2,0},{3,1},{0,2},{1,3},{6,4},{7,5},{4,6},{5,7},{10,8},{11,9},{8,1... | collective-permute-start | bytes 1179656 | tf_op jit(solution)/shard_map/ppermute | solution.py:176
  6.3 1.2 collective-permute-start
  8.1 0.6 pad_add_fusion.scalars
  8.7 2.9 %split_weights.1 = bf16[16,16,432]{2,1,0:T(8,128)(2,1)} custom-call(s32[4]{0:T(128)} %pad_add_fusion.scalars, bf16[27,16,256]{2,1,0:T(8,128)(2,1)} %w1.1, bf16[27,16,256]{2,1,0:T(8,128)(2,1)} %w2.1), custom_call_target="tpu_custom_call" | custom-call | bytes 884736 | tf_op jit(solution)/shard_map/split_weights/pallas_call | solution.py:316
  11.6 4.4 %collective-permute-done.1 = bf16[2,3,16,2048]{3,2,1,0:T(8,128)(2,1)S(1)} collective-permute-done((bf16[2,3,16,2048]{3,2,1,0:T(8,128)(2,1)S(1)}, bf16[2,3,16,2048]{3,2,1,0:T(8,128)(2,1)S(1)}, u32[]{:S(2)}, u32[]{:S(2)}) %collective-permute-start.1) | collective-permute-done | bytes 393248 | tf_op jit(solution)/shard_map/ppermute | solution.py:176
  16.0 0.9 copy-done.4
  16.9 0.1 copy-done.5
  17.0 0.2 pad_maximum_fusion
  17.2 2.5 %collective-permute-start.3 = (bf16[4,3,16,2048]{3,2,1,0:T(8,128)(2,1)S(1)}, bf16[4,3,16,2048]{3,2,1,0:T(8,128)(2,1)S(1)}, u32[]{:S(2)}, u32[]{:S(2)}) collective-permute-start(bf16[4,3,16,2048]{3,2,1,0:T(8,128)(2,1)S(1)} %get-tuple-element.20.refs_0_), channel_id=1, source_target_pairs={{4,0},{5,1},{6,2},{7,3},{8,4},{9,5},{10,6},{11,7},{12,8},{13,9},{1... | collective-permute-start | bytes 2359304 | tf_op jit(solution)/shard_map/ppermute | solution.py:176
  19.7 0.0 collective-permute-start.5
  19.7 2.7 %collective-permute-start.8 = (bf16[4,3,16,2048]{3,2,1,0:T(8,128)(2,1)S(1)}, bf16[4,3,16,2048]{3,2,1,0:T(8,128)(2,1)}, u32[]{:S(2)}, u32[]{:S(2)}) collective-permute-start(bf16[4,3,16,2048]{3,2,1,0:T(8,128)(2,1)S(1)} %get-tuple-element.21.refs_4_), channel_id=1, source_target_pairs={{4,0},{5,1},{6,2},{7,3},{8,4},{9,5},{10,6},{11,7},{12,8},{13,9},{1... | collective-permute-start | bytes 2359304 | tf_op jit(solution)/shard_map/ppermute | solution.py:176
  22.4 6.2 %collective-permute-done.3.refs_1_ = bf16[4,3,16,2048]{3,2,1,0:T(8,128)(2,1)S(1)} collective-permute-done((bf16[4,3,16,2048]{3,2,1,0:T(8,128)(2,1)S(1)}, bf16[4,3,16,2048]{3,2,1,0:T(8,128)(2,1)S(1)}, u32[]{:S(2)}, u32[]{:S(2)}) %collective-permute-start.3) | collective-permute-done | bytes 786464 | tf_op jit(solution)/shard_map/ppermute | solution.py:176
  28.6 3.5 %collective-permute-start.4 = (bf16[4,3,16,2048]{3,2,1,0:T(8,128)(2,1)S(1)}, bf16[4,3,16,2048]{3,2,1,0:T(8,128)(2,1)}, u32[]{:S(2)}, u32[]{:S(2)}) collective-permute-start(bf16[4,3,16,2048]{3,2,1,0:T(8,128)(2,1)S(1)} %collective-permute-done.3.refs_1_), channel_id=1, source_target_pairs={{4,0},{5,1},{6,2},{7,3},{8,4},{9,5},{10,6},{11,7},{12,8},{13,9},{1... | collective-permute-start | bytes 2359304 | tf_op jit(solution)/shard_map/ppermute | solution.py:176
  32.2 18.8 %all_to_all.10 = bf16[16,16,432]{2,1,0:T(8,128)(2,1)S(1)} all-to-all(bf16[16,16,432]{2,1,0:T(8,128)(2,1)S(1)} %copy-done.3), channel_id=1, replica_groups=mesh['dp'=16,'filter'=16] {'filter'}, dimensions={0} | all-to-all | bytes 442368 | tf_op jit(solution)/shard_map/all_to_all | solution.py:403
  50.9 0.1 copy.13
  51.1 5.1 %collective-permute-start.9 = (bf16[256,432]{0,1:T(8,128)(2,1)S(1)}, bf16[256,432]{0,1:T(8,128)(2,1)S(1)}, u32[]{:S(2)}, u32[]{:S(2)}) collective-permute-start(bf16[256,432]{0,1:T(8,128)(2,1)S(1)} %copy.13), channel_id=1, source_target_pairs={{0,16},{16,0},{32,48},{48,32},{64,80},{80,64},{96,112},{112,96},{1... | collective-permute-start | bytes 663560 | tf_op jit(solution)/shard_map/ppermute | solution.py:374
  56.2 1.1 collective-permute-done.9
  57.4 0.6 copy-done.2
  58.0 2.3 %layer_one.1.refs_8_ = bf16[2,3,16,2048]{3,2,1,0:T(8,128)(2,1)S(1)} custom-call(s32[4]{0:T(128)S(1)} %copy-done.2, bf16[4,3,16,2048]{3,2,1,0:T(8,128)(2,1)S(1)} %get-tuple-element.20.refs_0_, bf16[4,3,16,2048]{3,2,1,0:T(8,128)(2,1)S(1)} %collective-permute-done.3.refs_1_, bf16[4,3,16,2048]{3,2,1,0:T(8,128)(2,1)} %collective-permute-done.4.refs_2_, ...), custom_call_target="tpu_custom_call" | custom-call | flops 2717908992 | bytes 6291456 | tf_op jit(solution)/shard_map/layer_one/pallas_call | solution.py:222
  60.3 0.1 collective-permute-start.12
  60.4 0.6 collective-permute-start.11
  61.0 2.1 %collective-permute-start.10 = (bf16[2,3,16,2048]{3,2,1,0:T(8,128)(2,1)S(1)}, bf16[2,3,16,2048]{3,2,1,0:T(8,128)(2,1)S(1)}, u32[]{:S(2)}, u32[]{:S(2)}) collective-permute-start(bf16[2,3,16,2048]{3,2,1,0:T(8,128)(2,1)S(1)} %layer_one.1.refs_8_), channel_id=1, source_target_pairs={{1,0},{2,1},{3,2},{0,3},{5,4},{6,5},{7,6},{4,7},{9,8},{10,9},{11,1... | collective-permute-start | bytes 1179656 | tf_op jit(solution)/shard_map/ppermute | solution.py:176
  63.1 2.4 %weight_grads.1 = (f32[8,2,16,432]{3,2,1,0:T(8,128)S(1)}, f32[8,2,16,432]{3,2,1,0:T(8,128)S(1)}) custom-call(s32[4]{0:T(128)S(1)} %copy-done.2, bf16[4,3,16,2048]{3,2,1,0:T(8,128)(2,1)S(1)} %get-tuple-element.20.refs_0_, bf16[4,3,16,2048]{3,2,1,0:T(8,128)(2,1)S(1)} %collective-permute-done.3.refs_1_, ...), custom_call_target="tpu_custom_call" | custom-call | flops 2717908992 | bytes 6291456 | tf_op jit(solution)/shard_map/weight_grads/pallas_call | solution.py:242
  65.6 7.2 %collective-permute-done.12 = bf16[2,3,16,2048]{3,2,1,0:T(8,128)(2,1)S(1)} collective-permute-done((bf16[2,3,16,2048]{3,2,1,0:T(8,128)(2,1)S(1)}, bf16[2,3,16,2048]{3,2,1,0:T(8,128)(2,1)S(1)}, u32[]{:S(2)}, u32[]{:S(2)}) %collective-permute-start.12) | collective-permute-done | bytes 393248 | tf_op jit(solution)/shard_map/ppermute | solution.py:176
  72.8 0.5 collective-permute-done.10
  73.4 0.1 pad_maximum_fusion.3.refs_4_
  73.5 0.1 pad_maximum_fusion.2.refs_0_
  73.6 1.2 collective-permute-start.13
  74.8 0.4 collective-permute-start.16
  75.2 5.7 %collective-permute-start.19 = (f32[8,2,16,432]{3,2,1,0:T(8,128)S(1)}, f32[8,2,16,432]{3,2,1,0:T(8,128)S(1)}, u32[]{:S(2)}, u32[]{:S(2)}) collective-permute-start(f32[8,2,16,432]{3,2,1,0:T(8,128)S(1)} %get-tuple-element.30), channel_id=1, source_target_pairs={{0,16},{16,0},{32,48},{48,32},{64,80},{80,64},{96,112},{112,96},{1... | collective-permute-start | bytes 1327112 | tf_op jit(solution)/shard_map/ppermute | solution.py:374
  80.8 1.5 %collective-permute-done.19 = f32[8,2,16,432]{3,2,1,0:T(8,128)S(1)} collective-permute-done((f32[8,2,16,432]{3,2,1,0:T(8,128)S(1)}, f32[8,2,16,432]{3,2,1,0:T(8,128)S(1)}, u32[]{:S(2)}, u32[]{:S(2)}) %collective-permute-start.19) | collective-permute-done | bytes 442400 | tf_op jit(solution)/shard_map/ppermute | solution.py:374
  82.4 0.9 add.13
  83.3 7.7 %all-to-all-start.1 = ((f32[8,2,16,432]{3,2,1,0:T(8,128)}), f32[8,2,16,432]{3,2,1,0:T(8,128)S(1)}, u32[]{:S(2)}, u32[]{:S(2)}) async-start(f32[8,2,16,432]{3,2,1,0:T(8,128)} %add.13), calls=%async_computation.1 | async-start | bytes 1048576 | tf_op jit(solution)/shard_map/all_to_all | solution.py:379
  91.0 0.8 collective-permute-start.15
  91.8 1.9 %collective-permute-start.18 = (bf16[4,3,16,2048]{3,2,1,0:T(8,128)(2,1)S(1)}, bf16[4,3,16,2048]{3,2,1,0:T(8,128)(2,1)}, u32[]{:S(2)}, u32[]{:S(2)}) collective-permute-start(bf16[4,3,16,2048]{3,2,1,0:T(8,128)(2,1)S(1)} %pad_maximum_fusion.3.refs_4_), channel_id=1, source_target_pairs={{4,0},{5,1},{6,2},{7,3},{8,4},{9,5},{10,6},{11,7},{12,8},{13,9},{1... | collective-permute-start | bytes 2359304 | tf_op jit(solution)/shard_map/ppermute | solution.py:176
  93.7 1.2 collective-permute-start.14
  94.9 0.3 collective-permute-start.17
  95.1 13.8 %all-to-all-done.1 = f32[8,2,16,432]{3,2,1,0:T(8,128)S(1)} async-done(((f32[8,2,16,432]{3,2,1,0:T(8,128)}), f32[8,2,16,432]{3,2,1,0:T(8,128)S(1)}, u32[]{:S(2)}, u32[]{:S(2)}) %all-to-all-start.1) | async-done | bytes 442400 | tf_op jit(solution)/shard_map/all_to_all | solution.py:379
  109.0 0.6 slice_bitcast_fusion
  109.6 3.0 %collective-permute-start.20 = (f32[16,432]{1,0:T(8,128)S(1)}, f32[16,432]{1,0:T(8,128)S(1)}, u32[]{:S(2)}, u32[]{:S(2)}) collective-permute-start(f32[16,432]{1,0:T(8,128)S(1)} %get-tuple-element.52), channel_id=1, source_target_pairs={{0,0},{1,16},{2,32},{3,48},{4,64},{5,80},{6,96},{7,112},{8,128},{9... | collective-permute-start | bytes 82952 | tf_op jit(solution)/shard_map/ppermute | solution.py:385
  112.7 2.2 %collective-permute-done.20.got = f32[16,432]{1,0:T(8,128)S(1)} collective-permute-done((f32[16,432]{1,0:T(8,128)S(1)}, f32[16,432]{1,0:T(8,128)S(1)}, u32[]{:S(2)}, u32[]{:S(2)}) %collective-permute-start.20) | collective-permute-done | bytes 27680 | tf_op jit(solution)/shard_map/ppermute | solution.py:385
  114.8 0.6 copy-done.7
  115.5 1.6 %collect_rows.1 = f32[2,16,432]{2,1,0:T(8,128)} custom-call(f32[16,432]{1,0:T(8,128)} %get-tuple-element.53.mine, f32[16,432]{1,0:T(8,128)} %copy-done.7), custom_call_target="tpu_custom_call" | custom-call | bytes 110592 | tf_op jit(solution)/shard_map/collect_rows/pallas_call | solution.py:347
  117.1 3.4 %layer_two.1 = (f32[3,16,2048]{2,1,0:T(8,128)}, f32[3,16,2048]{2,1,0:T(8,128)}) custom-call(s32[4]{0:T(128)S(1)} %copy-done.2, bf16[4,3,16,2048]{3,2,1,0:T(8,128)(2,1)S(1)} %pad_maximum_fusion.2.refs_0_, bf16[4,3,16,2048]{3,2,1,0:T(8,128)(2,1)S(1)} %collective-permute-done.13.refs_1_, bf16[4,3,16,2048]{3,2,1,0:T(8,128)(2,1)} %collective-permute-done.14.refs_2_, ...), custom_call_target="tpu_custom_call" | custom-call | flops 2717908992 | bytes 6291456 | tf_op jit(solution)/shard_map/layer_two/pallas_call | solution.py:267
  120.5 28.0 %all-gather = f32[32,16,432]{2,1,0:T(8,128)} all-gather(f32[2,16,432]{2,1,0:T(8,128)S(1)} %copy-done.6), channel_id=2, replica_groups=mesh['dp'=16,'filter'=16] {'dp'}, dimensions={0}, use_global_device_ids=true | all-gather | bytes 940032 | tf_op jit(solution)/shard_map/all_gather | solution.py:390
  148.5 2.3 %finish_gradients.1 = (f32[432,256]{1,0:T(8,128)}, f32[432,256]{1,0:T(8,128)}) custom-call(f32[16,2,16,432]{3,2,1,0:T(8,128)} %bitcast.27), custom_call_target="tpu_custom_call" | custom-call | bytes 1769472 | tf_op jit(solution)/shard_map/finish_gradients/pallas_call | solution.py:364
  (37 shorter events, 0.3 us)
Async XLA Ops:
  1.7 9.9 %collective-permute-start.2 = (bf16[2,3,16,2048]{3,2,1,0:T(8,128)(2,1)S(1)}, bf16[2,3,16,2048]{3,2,1,0:T(8,128)(2,1)S(1)}, u32[]{:S(2)}, u32[]{:S(2)}) collective-permute-start(bf16[2,3,16,2048]{3,2,1,0:T(8,128)(2,1)S(1)} %pad_maximum_fusion.4), channel_id=1, source_target_pairs={{3,0},{0,1},{1,2},{2,3},{7,4},{4,5},{5,6},{6,7},{11,8},{8,9},{9,10... | collective-permute-start | bytes 1179656 | tf_op jit(solution)/shard_map/ppermute | solution.py:176
  3.8 12.1 %collective-permute-start.1 = (bf16[2,3,16,2048]{3,2,1,0:T(8,128)(2,1)S(1)}, bf16[2,3,16,2048]{3,2,1,0:T(8,128)(2,1)S(1)}, u32[]{:S(2)}, u32[]{:S(2)}) collective-permute-start(bf16[2,3,16,2048]{3,2,1,0:T(8,128)(2,1)S(1)} %pad_maximum_fusion.4), channel_id=1, source_target_pairs={{2,0},{3,1},{0,2},{1,3},{6,4},{7,5},{4,6},{5,7},{10,8},{11,9},{8,1... | collective-permute-start | bytes 1179656 | tf_op jit(solution)/shard_map/ppermute | solution.py:176
  6.3 9.7 %collective-permute-start = (bf16[2,3,16,2048]{3,2,1,0:T(8,128)(2,1)S(1)}, bf16[2,3,16,2048]{3,2,1,0:T(8,128)(2,1)S(1)}, u32[]{:S(2)}, u32[]{:S(2)}) collective-permute-start(bf16[2,3,16,2048]{3,2,1,0:T(8,128)(2,1)S(1)} %pad_maximum_fusion.4), channel_id=1, source_target_pairs={{1,0},{2,1},{3,2},{0,3},{5,4},{6,5},{7,6},{4,7},{9,8},{10,9},{11,1... | collective-permute-start | bytes 1179656 | tf_op jit(solution)/shard_map/ppermute | solution.py:176
  16.0 0.9 copy-start.4
  16.0 1.0 copy-start.5
  17.0 15.2 %copy-start.3 = (bf16[16,16,432]{2,1,0:T(8,128)(2,1)S(1)}, bf16[16,16,432]{2,1,0:T(8,128)(2,1)}, u32[]{:S(2)}) copy-start(bf16[16,16,432]{2,1,0:T(8,128)(2,1)} %split_weights.1) | copy-start | bytes 663556
  17.2 11.5 %collective-permute-start.3 = (bf16[4,3,16,2048]{3,2,1,0:T(8,128)(2,1)S(1)}, bf16[4,3,16,2048]{3,2,1,0:T(8,128)(2,1)S(1)}, u32[]{:S(2)}, u32[]{:S(2)}) collective-permute-start(bf16[4,3,16,2048]{3,2,1,0:T(8,128)(2,1)S(1)} %get-tuple-element.20.refs_0_), channel_id=1, source_target_pairs={{4,0},{5,1},{6,2},{7,3},{8,4},{9,5},{10,6},{11,7},{12,8},{13,9},{1... | collective-permute-start | bytes 2359304 | tf_op jit(solution)/shard_map/ppermute | solution.py:176
  19.7 12.5 %collective-permute-start.6 = (bf16[4,3,16,2048]{3,2,1,0:T(8,128)(2,1)S(1)}, bf16[4,3,16,2048]{3,2,1,0:T(8,128)(2,1)}, u32[]{:S(2)}, u32[]{:S(2)}) collective-permute-start(bf16[4,3,16,2048]{3,2,1,0:T(8,128)(2,1)S(1)} %get-tuple-element.21.refs_4_), channel_id=1, source_target_pairs={{12,0},{13,1},{14,2},{15,3},{0,4},{1,5},{2,6},{3,7},{4,8},{5,9},{6... | collective-permute-start | bytes 2359304 | tf_op jit(solution)/shard_map/ppermute | solution.py:176
  19.7 37.6 %collective-permute-start.5 = (bf16[4,3,16,2048]{3,2,1,0:T(8,128)(2,1)S(1)}, bf16[4,3,16,2048]{3,2,1,0:T(8,128)(2,1)}, u32[]{:S(2)}, u32[]{:S(2)}) collective-permute-start(bf16[4,3,16,2048]{3,2,1,0:T(8,128)(2,1)S(1)} %get-tuple-element.20.refs_0_), channel_id=1, source_target_pairs={{12,0},{13,1},{14,2},{15,3},{0,4},{1,5},{2,6},{3,7},{4,8},{5,9},{6... | collective-permute-start | bytes 2359304 | tf_op jit(solution)/shard_map/ppermute | solution.py:176
  19.7 37.6 %collective-permute-start.8 = (bf16[4,3,16,2048]{3,2,1,0:T(8,128)(2,1)S(1)}, bf16[4,3,16,2048]{3,2,1,0:T(8,128)(2,1)}, u32[]{:S(2)}, u32[]{:S(2)}) collective-permute-start(bf16[4,3,16,2048]{3,2,1,0:T(8,128)(2,1)S(1)} %get-tuple-element.21.refs_4_), channel_id=1, source_target_pairs={{4,0},{5,1},{6,2},{7,3},{8,4},{9,5},{10,6},{11,7},{12,8},{13,9},{1... | collective-permute-start | bytes 2359304 | tf_op jit(solution)/shard_map/ppermute | solution.py:176
  28.6 28.7 %collective-permute-start.4 = (bf16[4,3,16,2048]{3,2,1,0:T(8,128)(2,1)S(1)}, bf16[4,3,16,2048]{3,2,1,0:T(8,128)(2,1)}, u32[]{:S(2)}, u32[]{:S(2)}) collective-permute-start(bf16[4,3,16,2048]{3,2,1,0:T(8,128)(2,1)S(1)} %collective-permute-done.3.refs_1_), channel_id=1, source_target_pairs={{4,0},{5,1},{6,2},{7,3},{8,4},{9,5},{10,6},{11,7},{12,8},{13,9},{1... | collective-permute-start | bytes 2359304 | tf_op jit(solution)/shard_map/ppermute | solution.py:176
  32.2 25.2 %collective-permute-start.7 = (bf16[4,3,16,2048]{3,2,1,0:T(8,128)(2,1)}, bf16[4,3,16,2048]{3,2,1,0:T(8,128)(2,1)}, u32[]{:S(2)}, u32[]{:S(2)}) collective-permute-start(bf16[4,3,16,2048]{3,2,1,0:T(8,128)(2,1)} %collective-permute-done.6.refs_5_), channel_id=1, source_target_pairs={{12,0},{13,1},{14,2},{15,3},{0,4},{1,5},{2,6},{3,7},{4,8},{5,9},{6... | collective-permute-start | bytes 2359304 | tf_op jit(solution)/shard_map/ppermute | solution.py:176
  51.1 6.2 %collective-permute-start.9 = (bf16[256,432]{0,1:T(8,128)(2,1)S(1)}, bf16[256,432]{0,1:T(8,128)(2,1)S(1)}, u32[]{:S(2)}, u32[]{:S(2)}) collective-permute-start(bf16[256,432]{0,1:T(8,128)(2,1)S(1)} %copy.13), channel_id=1, source_target_pairs={{0,16},{16,0},{32,48},{48,32},{64,80},{80,64},{96,112},{112,96},{1... | collective-permute-start | bytes 663560 | tf_op jit(solution)/shard_map/ppermute | solution.py:374
  56.2 1.2 copy-start
  57.4 0.7 copy-start.2
  60.3 12.4 %collective-permute-start.12 = (bf16[2,3,16,2048]{3,2,1,0:T(8,128)(2,1)S(1)}, bf16[2,3,16,2048]{3,2,1,0:T(8,128)(2,1)S(1)}, u32[]{:S(2)}, u32[]{:S(2)}) collective-permute-start(bf16[2,3,16,2048]{3,2,1,0:T(8,128)(2,1)S(1)} %layer_one.1.refs_8_), channel_id=1, source_target_pairs={{3,0},{0,1},{1,2},{2,3},{7,4},{4,5},{5,6},{6,7},{11,8},{8,9},{9,10... | collective-permute-start | bytes 1179656 | tf_op jit(solution)/shard_map/ppermute | solution.py:176
  60.4 12.4 %collective-permute-start.11 = (bf16[2,3,16,2048]{3,2,1,0:T(8,128)(2,1)S(1)}, bf16[2,3,16,2048]{3,2,1,0:T(8,128)(2,1)S(1)}, u32[]{:S(2)}, u32[]{:S(2)}) collective-permute-start(bf16[2,3,16,2048]{3,2,1,0:T(8,128)(2,1)S(1)} %layer_one.1.refs_8_), channel_id=1, source_target_pairs={{2,0},{3,1},{0,2},{1,3},{6,4},{7,5},{4,6},{5,7},{10,8},{11,9},{8,1... | collective-permute-start | bytes 1179656 | tf_op jit(solution)/shard_map/ppermute | solution.py:176
  61.0 12.4 %collective-permute-start.10 = (bf16[2,3,16,2048]{3,2,1,0:T(8,128)(2,1)S(1)}, bf16[2,3,16,2048]{3,2,1,0:T(8,128)(2,1)S(1)}, u32[]{:S(2)}, u32[]{:S(2)}) collective-permute-start(bf16[2,3,16,2048]{3,2,1,0:T(8,128)(2,1)S(1)} %layer_one.1.refs_8_), channel_id=1, source_target_pairs={{1,0},{2,1},{3,2},{0,3},{5,4},{6,5},{7,6},{4,7},{9,8},{10,9},{11,1... | collective-permute-start | bytes 1179656 | tf_op jit(solution)/shard_map/ppermute | solution.py:176
  73.6 20.0 %collective-permute-start.13 = (bf16[4,3,16,2048]{3,2,1,0:T(8,128)(2,1)S(1)}, bf16[4,3,16,2048]{3,2,1,0:T(8,128)(2,1)S(1)}, u32[]{:S(2)}, u32[]{:S(2)}) collective-permute-start(bf16[4,3,16,2048]{3,2,1,0:T(8,128)(2,1)S(1)} %pad_maximum_fusion.2.refs_0_), channel_id=1, source_target_pairs={{4,0},{5,1},{6,2},{7,3},{8,4},{9,5},{10,6},{11,7},{12,8},{13,9},{1... | collective-permute-start | bytes 2359304 | tf_op jit(solution)/shard_map/ppermute | solution.py:176
  74.8 20.1 %collective-permute-start.16 = (bf16[4,3,16,2048]{3,2,1,0:T(8,128)(2,1)S(1)}, bf16[4,3,16,2048]{3,2,1,0:T(8,128)(2,1)}, u32[]{:S(2)}, u32[]{:S(2)}) collective-permute-start(bf16[4,3,16,2048]{3,2,1,0:T(8,128)(2,1)S(1)} %pad_maximum_fusion.3.refs_4_), channel_id=1, source_target_pairs={{12,0},{13,1},{14,2},{15,3},{0,4},{1,5},{2,6},{3,7},{4,8},{5,9},{6... | collective-permute-start | bytes 2359304 | tf_op jit(solution)/shard_map/ppermute | solution.py:176
  75.2 7.2 %collective-permute-start.19 = (f32[8,2,16,432]{3,2,1,0:T(8,128)S(1)}, f32[8,2,16,432]{3,2,1,0:T(8,128)S(1)}, u32[]{:S(2)}, u32[]{:S(2)}) collective-permute-start(f32[8,2,16,432]{3,2,1,0:T(8,128)S(1)} %get-tuple-element.30), channel_id=1, source_target_pairs={{0,16},{16,0},{32,48},{48,32},{64,80},{80,64},{96,112},{112,96},{1... | collective-permute-start | bytes 1327112 | tf_op jit(solution)/shard_map/ppermute | solution.py:374
  83.3 25.7 %all-to-all-start.1 = ((f32[8,2,16,432]{3,2,1,0:T(8,128)}), f32[8,2,16,432]{3,2,1,0:T(8,128)S(1)}, u32[]{:S(2)}, u32[]{:S(2)}) async-start(f32[8,2,16,432]{3,2,1,0:T(8,128)} %add.13), calls=%async_computation.1 | async-start | bytes 1048576 | tf_op jit(solution)/shard_map/all_to_all | solution.py:379
  91.0 26.1 %collective-permute-start.15 = (bf16[4,3,16,2048]{3,2,1,0:T(8,128)(2,1)S(1)}, bf16[4,3,16,2048]{3,2,1,0:T(8,128)(2,1)}, u32[]{:S(2)}, u32[]{:S(2)}) collective-permute-start(bf16[4,3,16,2048]{3,2,1,0:T(8,128)(2,1)S(1)} %pad_maximum_fusion.2.refs_0_), channel_id=1, source_target_pairs={{12,0},{13,1},{14,2},{15,3},{0,4},{1,5},{2,6},{3,7},{4,8},{5,9},{6... | collective-permute-start | bytes 2359304 | tf_op jit(solution)/shard_map/ppermute | solution.py:176
  91.8 25.3 %collective-permute-start.18 = (bf16[4,3,16,2048]{3,2,1,0:T(8,128)(2,1)S(1)}, bf16[4,3,16,2048]{3,2,1,0:T(8,128)(2,1)}, u32[]{:S(2)}, u32[]{:S(2)}) collective-permute-start(bf16[4,3,16,2048]{3,2,1,0:T(8,128)(2,1)S(1)} %pad_maximum_fusion.3.refs_4_), channel_id=1, source_target_pairs={{4,0},{5,1},{6,2},{7,3},{8,4},{9,5},{10,6},{11,7},{12,8},{13,9},{1... | collective-permute-start | bytes 2359304 | tf_op jit(solution)/shard_map/ppermute | solution.py:176
  93.7 23.4 %collective-permute-start.14 = (bf16[4,3,16,2048]{3,2,1,0:T(8,128)(2,1)S(1)}, bf16[4,3,16,2048]{3,2,1,0:T(8,128)(2,1)}, u32[]{:S(2)}, u32[]{:S(2)}) collective-permute-start(bf16[4,3,16,2048]{3,2,1,0:T(8,128)(2,1)S(1)} %collective-permute-done.13.refs_1_), channel_id=1, source_target_pairs={{4,0},{5,1},{6,2},{7,3},{8,4},{9,5},{10,6},{11,7},{12,8},{13,9},{1... | collective-permute-start | bytes 2359304 | tf_op jit(solution)/shard_map/ppermute | solution.py:176
  94.9 22.2 %collective-permute-start.17 = (bf16[4,3,16,2048]{3,2,1,0:T(8,128)(2,1)}, bf16[4,3,16,2048]{3,2,1,0:T(8,128)(2,1)}, u32[]{:S(2)}, u32[]{:S(2)}) collective-permute-start(bf16[4,3,16,2048]{3,2,1,0:T(8,128)(2,1)} %collective-permute-done.16.refs_5_), channel_id=1, source_target_pairs={{12,0},{13,1},{14,2},{15,3},{0,4},{1,5},{2,6},{3,7},{4,8},{5,9},{6... | collective-permute-start | bytes 2359304 | tf_op jit(solution)/shard_map/ppermute | solution.py:176
  109.0 8.1 %copy-start.1 = (bf16[27,16,256]{2,1,0:T(8,128)(2,1)S(1)}, bf16[27,16,256]{2,1,0:T(8,128)(2,1)}, u32[]{:S(2)}) copy-start(bf16[27,16,256]{2,1,0:T(8,128)(2,1)} %w2.1) | copy-start | bytes 663556
  109.6 5.2 %collective-permute-start.20 = (f32[16,432]{1,0:T(8,128)S(1)}, f32[16,432]{1,0:T(8,128)S(1)}, u32[]{:S(2)}, u32[]{:S(2)}) collective-permute-start(f32[16,432]{1,0:T(8,128)S(1)} %get-tuple-element.52), channel_id=1, source_target_pairs={{0,0},{1,16},{2,32},{3,48},{4,64},{5,80},{6,96},{7,112},{8,128},{9... | collective-permute-start | bytes 82952 | tf_op jit(solution)/shard_map/ppermute | solution.py:385
  114.8 0.6 copy-start.7
  117.1 3.4 %copy-start.6 = (f32[2,16,432]{2,1,0:T(8,128)S(1)}, f32[2,16,432]{2,1,0:T(8,128)}, u32[]{:S(2)}) copy-start(f32[2,16,432]{2,1,0:T(8,128)} %collect_rows.1) | copy-start | bytes 165892

commit v5 on v4

--- a/solution.py
+++ b/solution.py
@@ -379,11 +379,12 @@
     return lax.all_to_all(v, "dp", 0, 0, axis_index_groups=by_core, tiled=True)
 
 
-def sum_over_dp(keep, send):
-    mine = over_z(keep + swap_cores(send)).sum(axis=0)
+def sum_over_dp(parts, done):
+    mine = parts.astype(jnp.float32).sum(axis=0)
     flip = [(d * BLK + f, f * BLK + d) for d in range(BLK) for f in range(BLK)]
     got = lax.ppermute(mine[1], ("dp", "filter"), flip)
-    return collect(mine[0], got)
+    got, done = lax.optimization_barrier((got, done))
+    return collect(mine[0], got), done
 
 
 def both_gradients(piece):
@@ -411,11 +412,14 @@
     pair = call_one(scalars, pieces, w1, w2t)
     nears = gather_near(pair)
     keep, send = call_grads(scalars, pieces, pair)
-    nears, keep, send = lax.optimization_barrier((nears, keep, send))
-    second_pieces = gather_last(gather_far(nears))
-    piece = sum_over_dp(keep, send)
+    pair_sum = (keep + swap_cores(send)).astype(jnp.bfloat16)
+    nears, pair_sum = lax.optimization_barrier((nears, pair_sum))
+    fars = gather_far(nears)
+    parts = over_z(pair_sum)
+    fars[0], parts = lax.optimization_barrier((fars[0], parts))
+    second_pieces = gather_last(fars)
     out, in_grad = call_two(scalars, second_pieces, w2, w1t)
-    out, in_grad, piece = lax.optimization_barrier((out, in_grad, piece))
+    piece, (out, in_grad) = sum_over_dp(parts, (out, in_grad))
     first_grad, second_grad = both_gradients(piece)
     return (out.transpose(1, 0, 2), in_grad.transpose(1, 0, 2), first_grad, second_grad)
 

time: 150 us -> 149 us (level); the launches traced: 151 us -> 147 us
  waiting for transfers between devices: 37 us -> 29.1 us
  Pallas kernels: 14.9 us -> 19 us
  starting transfers between devices: 44.5 us -> 48.2 us
  blocking collectives: 46.8 us -> 43.1 us
    all_to_all x1, waiting for transfers between devices: 13.8 us -> 6.44 us  [over_z(): return lax.all_to_all(v, 'dp', 0, 0, axis_index_groups=by_core, tiled=True)]
    ppermute x2, starting transfers between devices: 10.8 us -> 6.84 us  [swap_cores(): return lax.ppermute(v, 'dp', [(d, d ^ 1) for d in range(BLK)])]
    all_gather x1, blocking collectives: 28 us -> 24.4 us  [both_gradients(): first_grad, second_grad = finish(lax.all_gather(piece, 'dp', axis=0))]
    ppermute x18, waiting for transfers between devices: 18.4 us -> 21.5 us  [turn(): return lax.ppermute(v, ('dp', 'filter'), from_axis(axes, step))]
    ppermute x18, starting transfers between devices: 22.9 us -> 25.8 us  [turn(): return lax.ppermute(v, ('dp', 'filter'), from_axis(axes, step))]
    ppermute x1, starting transfers between devices: 3.04 us -> 5.54 us  [sum_over_dp(): got = lax.ppermute(mine[1], ('dp', 'filter'), flip)]
    all_to_all x1, starting transfers between devices: 7.74 us -> 9.93 us  [over_z(): return lax.all_to_all(v, 'dp', 0, 0, axis_index_groups=by_core, tiled=True)]
    ppermute x1, waiting for transfers between devices: 2.17 us -> 0.01 us  [sum_over_dp(): got = lax.ppermute(mine[1], ('dp', 'filter'), flip)]
  transfers between devices with their start and end apart: 22 -> 22, of which waited for: 8 -> 8; matrix products, arithmetic and copies ran while one was open for 2% -> 1% of each run, Pallas kernels for 5% -> 8%
where the time goes in v5:
time: 149 us; the launch traced here: 147 us
  starting transfers between devices  48.2 us (32%)
  blocking collectives  43.1 us (29%)
  waiting for transfers between devices  29.1 us (20%)
  Pallas kernels  19 us (13%)
  local copies, waits for them, and re-layouts  3.16 us (2%)
  other arithmetic  2.91 us (2%)
  between operations  1.53 us (1%)
    ppermute x18, starting transfers between devices, turn(): return lax.ppermute(v, ('dp', 'filter'), from_axis(axes, step))  25.8 us
    all_gather x1, blocking collectives, both_gradients(): first_grad, second_grad = finish(lax.all_gather(piece, 'dp', axis=0))  24.4 us
    ppermute x18, waiting for transfers between devices, turn(): return lax.ppermute(v, ('dp', 'filter'), from_axis(axes, step))  21.5 us
    all_to_all x1, blocking collectives, shards(): turned = lax.all_to_all(split, 'filter', 0, 0, tiled=True).reshape(C, ROWS)  18.8 us
    all_to_all x1, starting transfers between devices, over_z(): return lax.all_to_all(v, 'dp', 0, 0, axis_index_groups=by_core, tiled=True)  9.93 us
    ppermute x2, starting transfers between devices, swap_cores(): return lax.ppermute(v, 'dp', [(d, d ^ 1) for d in range(BLK)])  6.84 us
    all_to_all x1, waiting for transfers between devices, over_z(): return lax.all_to_all(v, 'dp', 0, 0, axis_index_groups=by_core, tiled=True)  6.44 us
    ppermute x1, starting transfers between devices, sum_over_dp(): got = lax.ppermute(mine[1], ('dp', 'filter'), flip)  5.54 us
  transfers between devices with their start and end apart: 22, of which 8 were waited for; matrix products, arithmetic and copies ran while one was open for 1% of the time, Pallas kernels for 8%

profile of v5, /device:TPU:1, one launch (start us, length us, event | category | flops | bytes accessed | tf_op | source)
XLA Modules:
  0.0 147.0 jit_solution(8700947121518777598)
XLA Ops:
  0.6 1.1 pad_maximum_fusion.4
  1.7 2.1 %collective-permute-start.2 = (bf16[2,3,16,2048]{3,2,1,0:T(8,128)(2,1)S(1)}, bf16[2,3,16,2048]{3,2,1,0:T(8,128)(2,1)S(1)}, u32[]{:S(2)}, u32[]{:S(2)}) collective-permute-start(bf16[2,3,16,2048]{3,2,1,0:T(8,128)(2,1)S(1)} %pad_maximum_fusion.4), channel_id=1, source_target_pairs={{3,0},{0,1},{1,2},{2,3},{7,4},{4,5},{5,6},{6,7},{11,8},{8,9},{9,10... | collective-permute-start | bytes 1179656 | tf_op jit(solution)/shard_map/ppermute | solution.py:176
  3.8 2.5 %collective-permute-start.1 = (bf16[2,3,16,2048]{3,2,1,0:T(8,128)(2,1)S(1)}, bf16[2,3,16,2048]{3,2,1,0:T(8,128)(2,1)S(1)}, u32[]{:S(2)}, u32[]{:S(2)}) collective-permute-start(bf16[2,3,16,2048]{3,2,1,0:T(8,128)(2,1)S(1)} %pad_maximum_fusion.4), channel_id=1, source_target_pairs={{2,0},{3,1},{0,2},{1,3},{6,4},{7,5},{4,6},{5,7},{10,8},{11,9},{8,1... | collective-permute-start | bytes 1179656 | tf_op jit(solution)/shard_map/ppermute | solution.py:176
  6.3 1.2 collective-permute-start
  8.1 0.6 pad_add_fusion.scalars
  8.7 2.9 %split_weights.1 = bf16[16,16,432]{2,1,0:T(8,128)(2,1)} custom-call(s32[4]{0:T(128)} %pad_add_fusion.scalars, bf16[27,16,256]{2,1,0:T(8,128)(2,1)} %w1.1, bf16[27,16,256]{2,1,0:T(8,128)(2,1)} %w2.1), custom_call_target="tpu_custom_call" | custom-call | bytes 884736 | tf_op jit(solution)/shard_map/split_weights/pallas_call | solution.py:316
  11.6 4.4 %collective-permute-done.1 = bf16[2,3,16,2048]{3,2,1,0:T(8,128)(2,1)S(1)} collective-permute-done((bf16[2,3,16,2048]{3,2,1,0:T(8,128)(2,1)S(1)}, bf16[2,3,16,2048]{3,2,1,0:T(8,128)(2,1)S(1)}, u32[]{:S(2)}, u32[]{:S(2)}) %collective-permute-start.1) | collective-permute-done | bytes 393248 | tf_op jit(solution)/shard_map/ppermute | solution.py:176
  16.0 0.0 copy-start.4
  16.0 0.0 copy-start.5
  16.0 0.9 copy-done.4
  16.9 0.1 copy-done.5
  17.0 0.2 pad_maximum_fusion
  17.2 2.5 %collective-permute-start.3 = (bf16[4,3,16,2048]{3,2,1,0:T(8,128)(2,1)S(1)}, bf16[4,3,16,2048]{3,2,1,0:T(8,128)(2,1)S(1)}, u32[]{:S(2)}, u32[]{:S(2)}) collective-permute-start(bf16[4,3,16,2048]{3,2,1,0:T(8,128)(2,1)S(1)} %get-tuple-element.23.refs_0_), channel_id=1, source_target_pairs={{4,0},{5,1},{6,2},{7,3},{8,4},{9,5},{10,6},{11,7},{12,8},{13,9},{1... | collective-permute-start | bytes 2359304 | tf_op jit(solution)/shard_map/ppermute | solution.py:176
  19.7 0.0 collective-permute-start.5
  19.7 2.7 %collective-permute-start.8 = (bf16[4,3,16,2048]{3,2,1,0:T(8,128)(2,1)S(1)}, bf16[4,3,16,2048]{3,2,1,0:T(8,128)(2,1)}, u32[]{:S(2)}, u32[]{:S(2)}) collective-permute-start(bf16[4,3,16,2048]{3,2,1,0:T(8,128)(2,1)S(1)} %get-tuple-element.24.refs_4_), channel_id=1, source_target_pairs={{4,0},{5,1},{6,2},{7,3},{8,4},{9,5},{10,6},{11,7},{12,8},{13,9},{1... | collective-permute-start | bytes 2359304 | tf_op jit(solution)/shard_map/ppermute | solution.py:176
  22.4 6.2 %collective-permute-done.3.refs_1_ = bf16[4,3,16,2048]{3,2,1,0:T(8,128)(2,1)S(1)} collective-permute-done((bf16[4,3,16,2048]{3,2,1,0:T(8,128)(2,1)S(1)}, bf16[4,3,16,2048]{3,2,1,0:T(8,128)(2,1)S(1)}, u32[]{:S(2)}, u32[]{:S(2)}) %collective-permute-start.3) | collective-permute-done | bytes 786464 | tf_op jit(solution)/shard_map/ppermute | solution.py:176
  28.6 3.5 %collective-permute-start.4 = (bf16[4,3,16,2048]{3,2,1,0:T(8,128)(2,1)S(1)}, bf16[4,3,16,2048]{3,2,1,0:T(8,128)(2,1)}, u32[]{:S(2)}, u32[]{:S(2)}) collective-permute-start(bf16[4,3,16,2048]{3,2,1,0:T(8,128)(2,1)S(1)} %collective-permute-done.3.refs_1_), channel_id=1, source_target_pairs={{4,0},{5,1},{6,2},{7,3},{8,4},{9,5},{10,6},{11,7},{12,8},{13,9},{1... | collective-permute-start | bytes 2359304 | tf_op jit(solution)/shard_map/ppermute | solution.py:176
  32.2 18.8 %all_to_all.10 = bf16[16,16,432]{2,1,0:T(8,128)(2,1)S(1)} all-to-all(bf16[16,16,432]{2,1,0:T(8,128)(2,1)S(1)} %copy-done.3), channel_id=1, replica_groups=mesh['dp'=16,'filter'=16] {'filter'}, dimensions={0} | all-to-all | bytes 442368 | tf_op jit(solution)/shard_map/all_to_all | solution.py:404
  50.9 0.1 copy.13
  51.1 5.1 %collective-permute-start.9 = (bf16[256,432]{0,1:T(8,128)(2,1)S(1)}, bf16[256,432]{0,1:T(8,128)(2,1)S(1)}, u32[]{:S(2)}, u32[]{:S(2)}) collective-permute-start(bf16[256,432]{0,1:T(8,128)(2,1)S(1)} %copy.13), channel_id=1, source_target_pairs={{0,16},{16,0},{32,48},{48,32},{64,80},{80,64},{96,112},{112,96},{1... | collective-permute-start | bytes 663560 | tf_op jit(solution)/shard_map/ppermute | solution.py:374
  56.2 1.1 collective-permute-done.9
  57.4 0.0 copy-start.2
  57.4 0.6 copy-done.2
  58.0 3.7 %layer_one.1.refs_8_ = bf16[2,3,16,2048]{3,2,1,0:T(8,128)(2,1)S(1)} custom-call(s32[4]{0:T(128)S(1)} %copy-done.2, bf16[4,3,16,2048]{3,2,1,0:T(8,128)(2,1)S(1)} %get-tuple-element.23.refs_0_, bf16[4,3,16,2048]{3,2,1,0:T(8,128)(2,1)S(1)} %collective-permute-done.3.refs_1_, bf16[4,3,16,2048]{3,2,1,0:T(8,128)(2,1)} %collective-permute-done.4.refs_2_, ...), custom_call_target="tpu_custom_call" | custom-call | flops 2717908992 | bytes 6291456 | tf_op jit(solution)/shard_map/layer_one/pallas_call | solution.py:222
  61.8 0.1 collective-permute-start.12
  61.9 0.6 collective-permute-start.11
  62.5 2.1 %collective-permute-start.10 = (bf16[2,3,16,2048]{3,2,1,0:T(8,128)(2,1)S(1)}, bf16[2,3,16,2048]{3,2,1,0:T(8,128)(2,1)S(1)}, u32[]{:S(2)}, u32[]{:S(2)}) collective-permute-start(bf16[2,3,16,2048]{3,2,1,0:T(8,128)(2,1)S(1)} %layer_one.1.refs_8_), channel_id=1, source_target_pairs={{1,0},{2,1},{3,2},{0,3},{5,4},{6,5},{7,6},{4,7},{9,8},{10,9},{11,1... | collective-permute-start | bytes 1179656 | tf_op jit(solution)/shard_map/ppermute | solution.py:176
  64.5 3.9 %weight_grads.1 = (f32[8,2,16,432]{3,2,1,0:T(8,128)S(1)}, f32[8,2,16,432]{3,2,1,0:T(8,128)S(1)}) custom-call(s32[4]{0:T(128)S(1)} %copy-done.2, bf16[4,3,16,2048]{3,2,1,0:T(8,128)(2,1)S(1)} %get-tuple-element.23.refs_0_, bf16[4,3,16,2048]{3,2,1,0:T(8,128)(2,1)S(1)} %collective-permute-done.3.refs_1_, ...), custom_call_target="tpu_custom_call" | custom-call | flops 2717908992 | bytes 6291456 | tf_op jit(solution)/shard_map/weight_grads/pallas_call | solution.py:242
  68.4 1.7 %collective-permute-start.13 = (f32[8,2,16,432]{3,2,1,0:T(8,128)S(1)}, f32[8,2,16,432]{3,2,1,0:T(8,128)S(1)}, u32[]{:S(2)}, u32[]{:S(2)}) collective-permute-start(f32[8,2,16,432]{3,2,1,0:T(8,128)S(1)} %get-tuple-element.27), channel_id=1, source_target_pairs={{0,16},{16,0},{32,48},{48,32},{64,80},{80,64},{96,112},{112,96},{1... | collective-permute-start | bytes 1327112 | tf_op jit(solution)/shard_map/ppermute | solution.py:374
  70.2 4.0 %collective-permute-done.12 = bf16[2,3,16,2048]{3,2,1,0:T(8,128)(2,1)S(1)} collective-permute-done((bf16[2,3,16,2048]{3,2,1,0:T(8,128)(2,1)S(1)}, bf16[2,3,16,2048]{3,2,1,0:T(8,128)(2,1)S(1)}, u32[]{:S(2)}, u32[]{:S(2)}) %collective-permute-start.12) | collective-permute-done | bytes 393248 | tf_op jit(solution)/shard_map/ppermute | solution.py:176
  74.3 0.5 collective-permute-done.10
  74.9 0.1 pad_maximum_fusion.3.refs_4_
  75.0 0.1 pad_maximum_fusion.2.refs_0_
  75.1 0.8 add_convert_fusion
  75.9 2.7 %collective-permute-start.14 = (bf16[4,3,16,2048]{3,2,1,0:T(8,128)(2,1)S(1)}, bf16[4,3,16,2048]{3,2,1,0:T(8,128)(2,1)}, u32[]{:S(2)}, u32[]{:S(2)}) collective-permute-start(bf16[4,3,16,2048]{3,2,1,0:T(8,128)(2,1)S(1)} %pad_maximum_fusion.2.refs_0_), channel_id=1, source_target_pairs={{4,0},{5,1},{6,2},{7,3},{8,4},{9,5},{10,6},{11,7},{12,8},{13,9},{1... | collective-permute-start | bytes 2359304 | tf_op jit(solution)/shard_map/ppermute | solution.py:176
  78.5 9.9 %all-to-all-start.1 = ((bf16[8,2,16,432]{3,2,1,0:T(8,128)(2,1)}), bf16[8,2,16,432]{3,2,1,0:T(8,128)(2,1)S(1)}, u32[]{:S(2)}, u32[]{:S(2)}) async-start(bf16[8,2,16,432]{3,2,1,0:T(8,128)(2,1)} %add_convert_fusion), calls=%async_computation.1 | async-start | bytes 524288 | tf_op jit(solution)/shard_map/all_to_all | solution.py:379
  88.5 2.8 %collective-permute-start.20 = (bf16[4,3,16,2048]{3,2,1,0:T(8,128)(2,1)S(1)}, bf16[4,3,16,2048]{3,2,1,0:T(8,128)(2,1)}, u32[]{:S(2)}, u32[]{:S(2)}) collective-permute-start(bf16[4,3,16,2048]{3,2,1,0:T(8,128)(2,1)S(1)} %pad_maximum_fusion.3.refs_4_), channel_id=1, source_target_pairs={{4,0},{5,1},{6,2},{7,3},{8,4},{9,5},{10,6},{11,7},{12,8},{13,9},{1... | collective-permute-start | bytes 2359304 | tf_op jit(solution)/shard_map/ppermute | solution.py:176
  91.2 6.4 %all-to-all-done.1 = bf16[8,2,16,432]{3,2,1,0:T(8,128)(2,1)S(1)} async-done(((bf16[8,2,16,432]{3,2,1,0:T(8,128)(2,1)}), bf16[8,2,16,432]{3,2,1,0:T(8,128)(2,1)S(1)}, u32[]{:S(2)}, u32[]{:S(2)}) %all-to-all-start.1) | async-done | bytes 221216 | tf_op jit(solution)/shard_map/all_to_all | solution.py:379
  97.7 3.2 %collective-permute-start.17 = (bf16[4,3,16,2048]{3,2,1,0:T(8,128)(2,1)}, bf16[4,3,16,2048]{3,2,1,0:T(8,128)(2,1)S(1)}, u32[]{:S(2)}, u32[]{:S(2)}) collective-permute-start(bf16[4,3,16,2048]{3,2,1,0:T(8,128)(2,1)} %collective-permute-done.14.refs_1_), channel_id=1, source_target_pairs={{4,0},{5,1},{6,2},{7,3},{8,4},{9,5},{10,6},{11,7},{12,8},{13,9},{1... | collective-permute-start | bytes 2359304 | tf_op jit(solution)/shard_map/ppermute | solution.py:176
  100.9 0.6 slice_bitcast_fusion
  101.5 5.5 %collective-permute-start.16 = (f32[16,432]{1,0:T(8,128)S(1)}, f32[16,432]{1,0:T(8,128)S(1)}, u32[]{:S(2)}, u32[]{:S(2)}) collective-permute-start(f32[16,432]{1,0:T(8,128)S(1)} %get-tuple-element.59), channel_id=1, source_target_pairs={{0,0},{1,16},{2,32},{3,48},{4,64},{5,80},{6,96},{7,112},{8,128},{9... | collective-permute-start | bytes 82952 | tf_op jit(solution)/shard_map/ppermute | solution.py:385
  107.1 3.4 %collective-permute-done.17.refs_2_ = bf16[4,3,16,2048]{3,2,1,0:T(8,128)(2,1)S(1)} collective-permute-done((bf16[4,3,16,2048]{3,2,1,0:T(8,128)(2,1)}, bf16[4,3,16,2048]{3,2,1,0:T(8,128)(2,1)S(1)}, u32[]{:S(2)}, u32[]{:S(2)}) %collective-permute-start.17) | collective-permute-done | bytes 786464 | tf_op jit(solution)/shard_map/ppermute | solution.py:176
  110.5 3.0 %collective-permute-done.19.refs_6_ = bf16[4,3,16,2048]{3,2,1,0:T(8,128)(2,1)S(1)} collective-permute-done((bf16[4,3,16,2048]{3,2,1,0:T(8,128)(2,1)}, bf16[4,3,16,2048]{3,2,1,0:T(8,128)(2,1)S(1)}, u32[]{:S(2)}, u32[]{:S(2)}) %collective-permute-start.19) | collective-permute-done | bytes 786464 | tf_op jit(solution)/shard_map/ppermute | solution.py:176
  113.4 4.6 %layer_two.1 = (f32[3,16,2048]{2,1,0:T(8,128)}, f32[3,16,2048]{2,1,0:T(8,128)}) custom-call(s32[4]{0:T(128)S(1)} %copy-done.2, bf16[4,3,16,2048]{3,2,1,0:T(8,128)(2,1)S(1)} %pad_maximum_fusion.2.refs_0_, bf16[4,3,16,2048]{3,2,1,0:T(8,128)(2,1)} %collective-permute-done.14.refs_1_, bf16[4,3,16,2048]{3,2,1,0:T(8,128)(2,1)S(1)} %collective-permute-done.17.refs_2_, ...), custom_call_target="tpu_custom_call" | custom-call | flops 2717908992 | bytes 6291456 | tf_op jit(solution)/shard_map/layer_two/pallas_call | solution.py:267
  118.0 0.6 copy-done.6
  118.6 1.6 %collect_rows.1 = f32[2,16,432]{2,1,0:T(8,128)} custom-call(f32[16,432]{1,0:T(8,128)} %get-tuple-element.58.mine, f32[16,432]{1,0:T(8,128)} %copy-done.6), custom_call_target="tpu_custom_call" | custom-call | bytes 110592 | tf_op jit(solution)/shard_map/collect_rows/pallas_call | solution.py:347
  120.3 24.4 %all-gather = f32[32,16,432]{2,1,0:T(8,128)} all-gather(f32[2,16,432]{2,1,0:T(8,128)} %collect_rows.1), channel_id=2, replica_groups=mesh['dp'=16,'filter'=16] {'dp'}, dimensions={0}, use_global_device_ids=true | all-gather | bytes 940032 | tf_op jit(solution)/shard_map/all_gather | solution.py:391
  144.6 2.3 %finish_gradients.1 = (f32[432,256]{1,0:T(8,128)}, f32[432,256]{1,0:T(8,128)}) custom-call(f32[16,2,16,432]{3,2,1,0:T(8,128)} %bitcast.27), custom_call_target="tpu_custom_call" | custom-call | bytes 1769472 | tf_op jit(solution)/shard_map/finish_gradients/pallas_call | solution.py:364
  (35 shorter events, 0.3 us)
Async XLA Ops:
  1.7 9.9 %collective-permute-start.2 = (bf16[2,3,16,2048]{3,2,1,0:T(8,128)(2,1)S(1)}, bf16[2,3,16,2048]{3,2,1,0:T(8,128)(2,1)S(1)}, u32[]{:S(2)}, u32[]{:S(2)}) collective-permute-start(bf16[2,3,16,2048]{3,2,1,0:T(8,128)(2,1)S(1)} %pad_maximum_fusion.4), channel_id=1, source_target_pairs={{3,0},{0,1},{1,2},{2,3},{7,4},{4,5},{5,6},{6,7},{11,8},{8,9},{9,10... | collective-permute-start | bytes 1179656 | tf_op jit(solution)/shard_map/ppermute | solution.py:176
  3.8 12.1 %collective-permute-start.1 = (bf16[2,3,16,2048]{3,2,1,0:T(8,128)(2,1)S(1)}, bf16[2,3,16,2048]{3,2,1,0:T(8,128)(2,1)S(1)}, u32[]{:S(2)}, u32[]{:S(2)}) collective-permute-start(bf16[2,3,16,2048]{3,2,1,0:T(8,128)(2,1)S(1)} %pad_maximum_fusion.4), channel_id=1, source_target_pairs={{2,0},{3,1},{0,2},{1,3},{6,4},{7,5},{4,6},{5,7},{10,8},{11,9},{8,1... | collective-permute-start | bytes 1179656 | tf_op jit(solution)/shard_map/ppermute | solution.py:176
  6.3 9.7 %collective-permute-start = (bf16[2,3,16,2048]{3,2,1,0:T(8,128)(2,1)S(1)}, bf16[2,3,16,2048]{3,2,1,0:T(8,128)(2,1)S(1)}, u32[]{:S(2)}, u32[]{:S(2)}) collective-permute-start(bf16[2,3,16,2048]{3,2,1,0:T(8,128)(2,1)S(1)} %pad_maximum_fusion.4), channel_id=1, source_target_pairs={{1,0},{2,1},{3,2},{0,3},{5,4},{6,5},{7,6},{4,7},{9,8},{10,9},{11,1... | collective-permute-start | bytes 1179656 | tf_op jit(solution)/shard_map/ppermute | solution.py:176
  16.0 0.9 copy-start.4
  16.0 1.0 copy-start.5
  17.0 15.2 %copy-start.3 = (bf16[16,16,432]{2,1,0:T(8,128)(2,1)S(1)}, bf16[16,16,432]{2,1,0:T(8,128)(2,1)}, u32[]{:S(2)}) copy-start(bf16[16,16,432]{2,1,0:T(8,128)(2,1)} %split_weights.1) | copy-start | bytes 663556
  17.2 11.5 %collective-permute-start.3 = (bf16[4,3,16,2048]{3,2,1,0:T(8,128)(2,1)S(1)}, bf16[4,3,16,2048]{3,2,1,0:T(8,128)(2,1)S(1)}, u32[]{:S(2)}, u32[]{:S(2)}) collective-permute-start(bf16[4,3,16,2048]{3,2,1,0:T(8,128)(2,1)S(1)} %get-tuple-element.23.refs_0_), channel_id=1, source_target_pairs={{4,0},{5,1},{6,2},{7,3},{8,4},{9,5},{10,6},{11,7},{12,8},{13,9},{1... | collective-permute-start | bytes 2359304 | tf_op jit(solution)/shard_map/ppermute | solution.py:176
  19.7 12.5 %collective-permute-start.6 = (bf16[4,3,16,2048]{3,2,1,0:T(8,128)(2,1)S(1)}, bf16[4,3,16,2048]{3,2,1,0:T(8,128)(2,1)}, u32[]{:S(2)}, u32[]{:S(2)}) collective-permute-start(bf16[4,3,16,2048]{3,2,1,0:T(8,128)(2,1)S(1)} %get-tuple-element.24.refs_4_), channel_id=1, source_target_pairs={{12,0},{13,1},{14,2},{15,3},{0,4},{1,5},{2,6},{3,7},{4,8},{5,9},{6... | collective-permute-start | bytes 2359304 | tf_op jit(solution)/shard_map/ppermute | solution.py:176
  19.7 37.6 %collective-permute-start.5 = (bf16[4,3,16,2048]{3,2,1,0:T(8,128)(2,1)S(1)}, bf16[4,3,16,2048]{3,2,1,0:T(8,128)(2,1)}, u32[]{:S(2)}, u32[]{:S(2)}) collective-permute-start(bf16[4,3,16,2048]{3,2,1,0:T(8,128)(2,1)S(1)} %get-tuple-element.23.refs_0_), channel_id=1, source_target_pairs={{12,0},{13,1},{14,2},{15,3},{0,4},{1,5},{2,6},{3,7},{4,8},{5,9},{6... | collective-permute-start | bytes 2359304 | tf_op jit(solution)/shard_map/ppermute | solution.py:176
  19.7 37.6 %collective-permute-start.8 = (bf16[4,3,16,2048]{3,2,1,0:T(8,128)(2,1)S(1)}, bf16[4,3,16,2048]{3,2,1,0:T(8,128)(2,1)}, u32[]{:S(2)}, u32[]{:S(2)}) collective-permute-start(bf16[4,3,16,2048]{3,2,1,0:T(8,128)(2,1)S(1)} %get-tuple-element.24.refs_4_), channel_id=1, source_target_pairs={{4,0},{5,1},{6,2},{7,3},{8,4},{9,5},{10,6},{11,7},{12,8},{13,9},{1... | collective-permute-start | bytes 2359304 | tf_op jit(solution)/shard_map/ppermute | solution.py:176
  28.6 28.7 %collective-permute-start.4 = (bf16[4,3,16,2048]{3,2,1,0:T(8,128)(2,1)S(1)}, bf16[4,3,16,2048]{3,2,1,0:T(8,128)(2,1)}, u32[]{:S(2)}, u32[]{:S(2)}) collective-permute-start(bf16[4,3,16,2048]{3,2,1,0:T(8,128)(2,1)S(1)} %collective-permute-done.3.refs_1_), channel_id=1, source_target_pairs={{4,0},{5,1},{6,2},{7,3},{8,4},{9,5},{10,6},{11,7},{12,8},{13,9},{1... | collective-permute-start | bytes 2359304 | tf_op jit(solution)/shard_map/ppermute | solution.py:176
  32.2 25.2 %collective-permute-start.7 = (bf16[4,3,16,2048]{3,2,1,0:T(8,128)(2,1)}, bf16[4,3,16,2048]{3,2,1,0:T(8,128)(2,1)}, u32[]{:S(2)}, u32[]{:S(2)}) collective-permute-start(bf16[4,3,16,2048]{3,2,1,0:T(8,128)(2,1)} %collective-permute-done.6.refs_5_), channel_id=1, source_target_pairs={{12,0},{13,1},{14,2},{15,3},{0,4},{1,5},{2,6},{3,7},{4,8},{5,9},{6... | collective-permute-start | bytes 2359304 | tf_op jit(solution)/shard_map/ppermute | solution.py:176
  51.1 6.2 %collective-permute-start.9 = (bf16[256,432]{0,1:T(8,128)(2,1)S(1)}, bf16[256,432]{0,1:T(8,128)(2,1)S(1)}, u32[]{:S(2)}, u32[]{:S(2)}) collective-permute-start(bf16[256,432]{0,1:T(8,128)(2,1)S(1)} %copy.13), channel_id=1, source_target_pairs={{0,16},{16,0},{32,48},{48,32},{64,80},{80,64},{96,112},{112,96},{1... | collective-permute-start | bytes 663560 | tf_op jit(solution)/shard_map/ppermute | solution.py:374
  56.2 1.2 copy-start
  57.4 0.7 copy-start.2
  61.8 12.4 %collective-permute-start.12 = (bf16[2,3,16,2048]{3,2,1,0:T(8,128)(2,1)S(1)}, bf16[2,3,16,2048]{3,2,1,0:T(8,128)(2,1)S(1)}, u32[]{:S(2)}, u32[]{:S(2)}) collective-permute-start(bf16[2,3,16,2048]{3,2,1,0:T(8,128)(2,1)S(1)} %layer_one.1.refs_8_), channel_id=1, source_target_pairs={{3,0},{0,1},{1,2},{2,3},{7,4},{4,5},{5,6},{6,7},{11,8},{8,9},{9,10... | collective-permute-start | bytes 1179656 | tf_op jit(solution)/shard_map/ppermute | solution.py:176
  61.9 12.4 %collective-permute-start.11 = (bf16[2,3,16,2048]{3,2,1,0:T(8,128)(2,1)S(1)}, bf16[2,3,16,2048]{3,2,1,0:T(8,128)(2,1)S(1)}, u32[]{:S(2)}, u32[]{:S(2)}) collective-permute-start(bf16[2,3,16,2048]{3,2,1,0:T(8,128)(2,1)S(1)} %layer_one.1.refs_8_), channel_id=1, source_target_pairs={{2,0},{3,1},{0,2},{1,3},{6,4},{7,5},{4,6},{5,7},{10,8},{11,9},{8,1... | collective-permute-start | bytes 1179656 | tf_op jit(solution)/shard_map/ppermute | solution.py:176
  62.5 12.4 %collective-permute-start.10 = (bf16[2,3,16,2048]{3,2,1,0:T(8,128)(2,1)S(1)}, bf16[2,3,16,2048]{3,2,1,0:T(8,128)(2,1)S(1)}, u32[]{:S(2)}, u32[]{:S(2)}) collective-permute-start(bf16[2,3,16,2048]{3,2,1,0:T(8,128)(2,1)S(1)} %layer_one.1.refs_8_), channel_id=1, source_target_pairs={{1,0},{2,1},{3,2},{0,3},{5,4},{6,5},{7,6},{4,7},{9,8},{10,9},{11,1... | collective-permute-start | bytes 1179656 | tf_op jit(solution)/shard_map/ppermute | solution.py:176
  68.4 6.7 %collective-permute-start.13 = (f32[8,2,16,432]{3,2,1,0:T(8,128)S(1)}, f32[8,2,16,432]{3,2,1,0:T(8,128)S(1)}, u32[]{:S(2)}, u32[]{:S(2)}) collective-permute-start(f32[8,2,16,432]{3,2,1,0:T(8,128)S(1)} %get-tuple-element.27), channel_id=1, source_target_pairs={{0,16},{16,0},{32,48},{48,32},{64,80},{80,64},{96,112},{112,96},{1... | collective-permute-start | bytes 1327112 | tf_op jit(solution)/shard_map/ppermute | solution.py:374
  75.9 21.8 %collective-permute-start.15 = (bf16[4,3,16,2048]{3,2,1,0:T(8,128)(2,1)S(1)}, bf16[4,3,16,2048]{3,2,1,0:T(8,128)(2,1)S(1)}, u32[]{:S(2)}, u32[]{:S(2)}) collective-permute-start(bf16[4,3,16,2048]{3,2,1,0:T(8,128)(2,1)S(1)} %pad_maximum_fusion.2.refs_0_), channel_id=1, source_target_pairs={{12,0},{13,1},{14,2},{15,3},{0,4},{1,5},{2,6},{3,7},{4,8},{5,9},{6... | collective-permute-start | bytes 2359304 | tf_op jit(solution)/shard_map/ppermute | solution.py:176
  75.9 21.8 %collective-permute-start.14 = (bf16[4,3,16,2048]{3,2,1,0:T(8,128)(2,1)S(1)}, bf16[4,3,16,2048]{3,2,1,0:T(8,128)(2,1)}, u32[]{:S(2)}, u32[]{:S(2)}) collective-permute-start(bf16[4,3,16,2048]{3,2,1,0:T(8,128)(2,1)S(1)} %pad_maximum_fusion.2.refs_0_), channel_id=1, source_target_pairs={{4,0},{5,1},{6,2},{7,3},{8,4},{9,5},{10,6},{11,7},{12,8},{13,9},{1... | collective-permute-start | bytes 2359304 | tf_op jit(solution)/shard_map/ppermute | solution.py:176
  78.5 22.3 %collective-permute-start.18 = (bf16[4,3,16,2048]{3,2,1,0:T(8,128)(2,1)S(1)}, bf16[4,3,16,2048]{3,2,1,0:T(8,128)(2,1)}, u32[]{:S(2)}, u32[]{:S(2)}) collective-permute-start(bf16[4,3,16,2048]{3,2,1,0:T(8,128)(2,1)S(1)} %pad_maximum_fusion.3.refs_4_), channel_id=1, source_target_pairs={{12,0},{13,1},{14,2},{15,3},{0,4},{1,5},{2,6},{3,7},{4,8},{5,9},{6... | collective-permute-start | bytes 2359304 | tf_op jit(solution)/shard_map/ppermute | solution.py:176
  78.5 19.1 %all-to-all-start.1 = ((bf16[8,2,16,432]{3,2,1,0:T(8,128)(2,1)}), bf16[8,2,16,432]{3,2,1,0:T(8,128)(2,1)S(1)}, u32[]{:S(2)}, u32[]{:S(2)}) async-start(bf16[8,2,16,432]{3,2,1,0:T(8,128)(2,1)} %add_convert_fusion), calls=%async_computation.1 | async-start | bytes 524288 | tf_op jit(solution)/shard_map/all_to_all | solution.py:379
  88.5 24.9 %copy-start.1 = (bf16[27,16,256]{2,1,0:T(8,128)(2,1)S(1)}, bf16[27,16,256]{2,1,0:T(8,128)(2,1)}, u32[]{:S(2)}) copy-start(bf16[27,16,256]{2,1,0:T(8,128)(2,1)} %w2.1) | copy-start | bytes 663556
  88.5 18.6 %collective-permute-start.20 = (bf16[4,3,16,2048]{3,2,1,0:T(8,128)(2,1)S(1)}, bf16[4,3,16,2048]{3,2,1,0:T(8,128)(2,1)}, u32[]{:S(2)}, u32[]{:S(2)}) collective-permute-start(bf16[4,3,16,2048]{3,2,1,0:T(8,128)(2,1)S(1)} %pad_maximum_fusion.3.refs_4_), channel_id=1, source_target_pairs={{4,0},{5,1},{6,2},{7,3},{8,4},{9,5},{10,6},{11,7},{12,8},{13,9},{1... | collective-permute-start | bytes 2359304 | tf_op jit(solution)/shard_map/ppermute | solution.py:176
  97.7 12.8 %collective-permute-start.17 = (bf16[4,3,16,2048]{3,2,1,0:T(8,128)(2,1)}, bf16[4,3,16,2048]{3,2,1,0:T(8,128)(2,1)S(1)}, u32[]{:S(2)}, u32[]{:S(2)}) collective-permute-start(bf16[4,3,16,2048]{3,2,1,0:T(8,128)(2,1)} %collective-permute-done.14.refs_1_), channel_id=1, source_target_pairs={{4,0},{5,1},{6,2},{7,3},{8,4},{9,5},{10,6},{11,7},{12,8},{13,9},{1... | collective-permute-start | bytes 2359304 | tf_op jit(solution)/shard_map/ppermute | solution.py:176
  100.9 12.6 %collective-permute-start.19 = (bf16[4,3,16,2048]{3,2,1,0:T(8,128)(2,1)}, bf16[4,3,16,2048]{3,2,1,0:T(8,128)(2,1)S(1)}, u32[]{:S(2)}, u32[]{:S(2)}) collective-permute-start(bf16[4,3,16,2048]{3,2,1,0:T(8,128)(2,1)} %collective-permute-done.18.refs_5_), channel_id=1, source_target_pairs={{12,0},{13,1},{14,2},{15,3},{0,4},{1,5},{2,6},{3,7},{4,8},{5,9},{6... | collective-permute-start | bytes 2359304 | tf_op jit(solution)/shard_map/ppermute | solution.py:176
  101.5 16.5 %collective-permute-start.16 = (f32[16,432]{1,0:T(8,128)S(1)}, f32[16,432]{1,0:T(8,128)S(1)}, u32[]{:S(2)}, u32[]{:S(2)}) collective-permute-start(f32[16,432]{1,0:T(8,128)S(1)} %get-tuple-element.59), channel_id=1, source_target_pairs={{0,0},{1,16},{2,32},{3,48},{4,64},{5,80},{6,96},{7,112},{8,128},{9... | collective-permute-start | bytes 82952 | tf_op jit(solution)/shard_map/ppermute | solution.py:385
  118.0 0.6 copy-start.6

commit v6 on v3

--- a/solution.py
+++ b/solution.py
@@ -391,8 +391,8 @@
     return lax.all_to_all(v, "dp", 0, 0, axis_index_groups=by_core, tiled=True)
 
 
-def sum_over_dp(keep, send):
-    mine = over_z(keep + swap_cores(send)).sum(axis=0)
+def sum_over_dp(parts):
+    mine = parts.astype(jnp.float32).sum(axis=0)
     flip = [(d * BLK + f, f * BLK + d) for d in range(BLK) for f in range(BLK)]
     got = lax.ppermute(mine[1], ("dp", "filter"), flip)
     return over_z(collect(mine[0], got))
@@ -421,9 +421,15 @@
     w2 = second_weight.reshape(ROWS, C)
 
     pair = call_one(scalars, pieces, w1, w2t)
-    second_pieces = gather_last(gather_far(gather_near(pair)))
+    nears = gather_near(pair)
     keep, send = call_grads(scalars, pieces, pair)
-    own = sum_over_dp(keep, send)
+    pair_sum = (keep + swap_cores(send)).astype(jnp.bfloat16)
+    nears, pair_sum = lax.optimization_barrier((nears, pair_sum))
+    fars = gather_far(nears)
+    parts = over_z(pair_sum)
+    fars[0], parts = lax.optimization_barrier((fars[0], parts))
+    second_pieces = gather_last(fars)
+    own = sum_over_dp(parts)
     out, in_grad = call_two(scalars, second_pieces, w2, w1t)
     out, in_grad, own = lax.optimization_barrier((out, in_grad, own))
     first_grad, second_grad = both_gradients(scalars, own)

time: 147 us -> 147 us (level)
  waiting for transfers between devices: 43.5 us -> 37.9 us
  Pallas kernels: 15.8 us -> 20 us
  starting transfers between devices: 58.3 us -> 60.2 us
    all_to_all x2, waiting for transfers between devices: 24.6 us -> 16.6 us  [over_z(): return lax.all_to_all(v, 'dp', 0, 0, axis_index_groups=by_core, tiled=True)]
    ppermute x3, starting transfers between devices: 13.9 us -> 9.05 us  [swap_cores(): return lax.ppermute(v, 'dp', [(d, d ^ 1) for d in range(BLK)])]
    ppermute x1, starting transfers between devices: 2.67 us -> 6.59 us  [sum_over_dp(): got = lax.ppermute(mine[1], ('dp', 'filter'), flip)]
    ppermute x18, waiting for transfers between devices: 13.7 us -> 16.5 us  [turn(): return lax.ppermute(v, ('dp', 'filter'), from_axis(axes, step))]
    ppermute x18, starting transfers between devices: 23 us -> 25.3 us  [turn(): return lax.ppermute(v, ('dp', 'filter'), from_axis(axes, step))]
  transfers between devices with their start and end apart: 24 -> 24, of which waited for: 9 -> 9; matrix products, arithmetic and copies ran while one was open for 2% -> 1% of each run, Pallas kernels for 7% -> 9%
where the time goes in v6:
time: 147 us; the launch traced here: 145 us
  starting transfers between devices  60.2 us (41%)
  waiting for transfers between devices  37.9 us (26%)
  Pallas kernels  20 us (14%)
  blocking collectives  18.8 us (13%)
  local copies, waits for them, and re-layouts  4 us (3%)
  other arithmetic  2.96 us (2%)
  between operations  1.55 us (1%)
    ppermute x18, starting transfers between devices, turn(): return lax.ppermute(v, ('dp', 'filter'), from_axis(axes, step))  25.3 us
    all_to_all x2, starting transfers between devices, over_z(): return lax.all_to_all(v, 'dp', 0, 0, axis_index_groups=by_core, tiled=True)  19.3 us
    all_to_all x1, blocking collectives, shards(): turned = lax.all_to_all(split, 'filter', 0, 0, tiled=True).reshape(C, ROWS)  18.8 us
    all_to_all x2, waiting for transfers between devices, over_z(): return lax.all_to_all(v, 'dp', 0, 0, axis_index_groups=by_core, tiled=True)  16.6 us
    ppermute x18, waiting for transfers between devices, turn(): return lax.ppermute(v, ('dp', 'filter'), from_axis(axes, step))  16.5 us
    ppermute x3, starting transfers between devices, swap_cores(): return lax.ppermute(v, 'dp', [(d, d ^ 1) for d in range(BLK)])  9.05 us
    ppermute x1, starting transfers between devices, sum_over_dp(): got = lax.ppermute(mine[1], ('dp', 'filter'), flip)  6.59 us
    pallas_call x1, Pallas kernels, call_two(): pl.pallas_call(kernel_two, name='layer_two', grid_spec=pltpu.PrefetchScal...  4.75 us
  transfers between devices with their start and end apart: 24, of which 9 were waited for; matrix products, arithmetic and copies ran while one was open for 1% of the time, Pallas kernels for 9%

profile of v6, /device:TPU:1, one launch (start us, length us, event | category | flops | bytes accessed | tf_op | source)
XLA Modules:
  0.0 145.4 jit_solution(14063318324229876589)
XLA Ops:
  0.6 1.1 pad_maximum_fusion.4
  1.7 2.1 %collective-permute-start.2 = (bf16[2,3,16,2048]{3,2,1,0:T(8,128)(2,1)S(1)}, bf16[2,3,16,2048]{3,2,1,0:T(8,128)(2,1)S(1)}, u32[]{:S(2)}, u32[]{:S(2)}) collective-permute-start(bf16[2,3,16,2048]{3,2,1,0:T(8,128)(2,1)S(1)} %pad_maximum_fusion.4), channel_id=1, source_target_pairs={{3,0},{0,1},{1,2},{2,3},{7,4},{4,5},{5,6},{6,7},{11,8},{8,9},{9,10... | collective-permute-start | bytes 1179656 | tf_op jit(solution)/shard_map/ppermute | solution.py:176
  3.8 2.5 %collective-permute-start.1 = (bf16[2,3,16,2048]{3,2,1,0:T(8,128)(2,1)S(1)}, bf16[2,3,16,2048]{3,2,1,0:T(8,128)(2,1)S(1)}, u32[]{:S(2)}, u32[]{:S(2)}) collective-permute-start(bf16[2,3,16,2048]{3,2,1,0:T(8,128)(2,1)S(1)} %pad_maximum_fusion.4), channel_id=1, source_target_pairs={{2,0},{3,1},{0,2},{1,3},{6,4},{7,5},{4,6},{5,7},{10,8},{11,9},{8,1... | collective-permute-start | bytes 1179656 | tf_op jit(solution)/shard_map/ppermute | solution.py:176
  6.3 1.2 collective-permute-start
  8.1 0.6 pad_add_fusion.scalars
  8.7 2.9 %split_weights.1 = bf16[16,16,432]{2,1,0:T(8,128)(2,1)} custom-call(s32[4]{0:T(128)} %pad_add_fusion.scalars, bf16[27,16,256]{2,1,0:T(8,128)(2,1)} %w1.1, bf16[27,16,256]{2,1,0:T(8,128)(2,1)} %w2.1), custom_call_target="tpu_custom_call" | custom-call | bytes 884736 | tf_op jit(solution)/shard_map/split_weights/pallas_call | solution.py:316
  11.6 4.3 %collective-permute-done.1 = bf16[2,3,16,2048]{3,2,1,0:T(8,128)(2,1)S(1)} collective-permute-done((bf16[2,3,16,2048]{3,2,1,0:T(8,128)(2,1)S(1)}, bf16[2,3,16,2048]{3,2,1,0:T(8,128)(2,1)S(1)}, u32[]{:S(2)}, u32[]{:S(2)}) %collective-permute-start.1) | collective-permute-done | bytes 393248 | tf_op jit(solution)/shard_map/ppermute | solution.py:176
  16.0 0.9 copy-done.5
  16.9 0.1 copy-done.6
  17.0 0.2 pad_maximum_fusion
  17.2 2.5 %collective-permute-start.3 = (bf16[4,3,16,2048]{3,2,1,0:T(8,128)(2,1)S(1)}, bf16[4,3,16,2048]{3,2,1,0:T(8,128)(2,1)S(1)}, u32[]{:S(2)}, u32[]{:S(2)}) collective-permute-start(bf16[4,3,16,2048]{3,2,1,0:T(8,128)(2,1)S(1)} %get-tuple-element.23.refs_0_), channel_id=1, source_target_pairs={{4,0},{5,1},{6,2},{7,3},{8,4},{9,5},{10,6},{11,7},{12,8},{13,9},{1... | collective-permute-start | bytes 2359304 | tf_op jit(solution)/shard_map/ppermute | solution.py:176
  19.7 2.7 %collective-permute-start.8 = (bf16[4,3,16,2048]{3,2,1,0:T(8,128)(2,1)S(1)}, bf16[4,3,16,2048]{3,2,1,0:T(8,128)(2,1)}, u32[]{:S(2)}, u32[]{:S(2)}) collective-permute-start(bf16[4,3,16,2048]{3,2,1,0:T(8,128)(2,1)S(1)} %get-tuple-element.24.refs_4_), channel_id=1, source_target_pairs={{4,0},{5,1},{6,2},{7,3},{8,4},{9,5},{10,6},{11,7},{12,8},{13,9},{1... | collective-permute-start | bytes 2359304 | tf_op jit(solution)/shard_map/ppermute | solution.py:176
  22.4 6.2 %collective-permute-done.3.refs_1_ = bf16[4,3,16,2048]{3,2,1,0:T(8,128)(2,1)S(1)} collective-permute-done((bf16[4,3,16,2048]{3,2,1,0:T(8,128)(2,1)S(1)}, bf16[4,3,16,2048]{3,2,1,0:T(8,128)(2,1)S(1)}, u32[]{:S(2)}, u32[]{:S(2)}) %collective-permute-start.3) | collective-permute-done | bytes 786464 | tf_op jit(solution)/shard_map/ppermute | solution.py:176
  28.6 3.5 %collective-permute-start.4 = (bf16[4,3,16,2048]{3,2,1,0:T(8,128)(2,1)S(1)}, bf16[4,3,16,2048]{3,2,1,0:T(8,128)(2,1)}, u32[]{:S(2)}, u32[]{:S(2)}) collective-permute-start(bf16[4,3,16,2048]{3,2,1,0:T(8,128)(2,1)S(1)} %collective-permute-done.3.refs_1_), channel_id=1, source_target_pairs={{4,0},{5,1},{6,2},{7,3},{8,4},{9,5},{10,6},{11,7},{12,8},{13,9},{1... | collective-permute-start | bytes 2359304 | tf_op jit(solution)/shard_map/ppermute | solution.py:176
  32.2 18.8 %all_to_all.15 = bf16[16,16,432]{2,1,0:T(8,128)(2,1)S(1)} all-to-all(bf16[16,16,432]{2,1,0:T(8,128)(2,1)S(1)} %copy-done.4), channel_id=1, replica_groups=mesh['dp'=16,'filter'=16] {'filter'}, dimensions={0} | all-to-all | bytes 442368 | tf_op jit(solution)/shard_map/all_to_all | solution.py:415
  50.9 0.1 copy.10
  51.1 5.1 %collective-permute-start.9 = (bf16[256,432]{0,1:T(8,128)(2,1)S(1)}, bf16[256,432]{0,1:T(8,128)(2,1)S(1)}, u32[]{:S(2)}, u32[]{:S(2)}) collective-permute-start(bf16[256,432]{0,1:T(8,128)(2,1)S(1)} %copy.10), channel_id=1, source_target_pairs={{0,16},{16,0},{32,48},{48,32},{64,80},{80,64},{96,112},{112,96},{1... | collective-permute-start | bytes 663560 | tf_op jit(solution)/shard_map/ppermute | solution.py:386
  56.2 1.1 collective-permute-done.9
  57.4 0.6 copy-done.2
  58.0 3.7 %layer_one.1.refs_8_ = bf16[2,3,16,2048]{3,2,1,0:T(8,128)(2,1)S(1)} custom-call(s32[4]{0:T(128)S(1)} %copy-done.2, bf16[4,3,16,2048]{3,2,1,0:T(8,128)(2,1)S(1)} %get-tuple-element.23.refs_0_, bf16[4,3,16,2048]{3,2,1,0:T(8,128)(2,1)S(1)} %collective-permute-done.3.refs_1_, bf16[4,3,16,2048]{3,2,1,0:T(8,128)(2,1)} %collective-permute-done.4.refs_2_, ...), custom_call_target="tpu_custom_call" | custom-call | flops 2717908992 | bytes 6291456 | tf_op jit(solution)/shard_map/layer_one/pallas_call | solution.py:222
  61.8 0.1 collective-permute-start.12
  61.9 0.6 collective-permute-start.11
  62.5 2.1 %collective-permute-start.10 = (bf16[2,3,16,2048]{3,2,1,0:T(8,128)(2,1)S(1)}, bf16[2,3,16,2048]{3,2,1,0:T(8,128)(2,1)S(1)}, u32[]{:S(2)}, u32[]{:S(2)}) collective-permute-start(bf16[2,3,16,2048]{3,2,1,0:T(8,128)(2,1)S(1)} %layer_one.1.refs_8_), channel_id=1, source_target_pairs={{1,0},{2,1},{3,2},{0,3},{5,4},{6,5},{7,6},{4,7},{9,8},{10,9},{11,1... | collective-permute-start | bytes 1179656 | tf_op jit(solution)/shard_map/ppermute | solution.py:176
  64.5 3.9 %weight_grads.1 = (f32[8,2,16,432]{3,2,1,0:T(8,128)S(1)}, f32[8,2,16,432]{3,2,1,0:T(8,128)S(1)}) custom-call(s32[4]{0:T(128)S(1)} %copy-done.2, bf16[4,3,16,2048]{3,2,1,0:T(8,128)(2,1)S(1)} %get-tuple-element.23.refs_0_, bf16[4,3,16,2048]{3,2,1,0:T(8,128)(2,1)S(1)} %collective-permute-done.3.refs_1_, ...), custom_call_target="tpu_custom_call" | custom-call | flops 2717908992 | bytes 6291456 | tf_op jit(solution)/shard_map/weight_grads/pallas_call | solution.py:242
  68.4 0.1 collective-permute-start.13
  68.5 5.4 %collective-permute-done.12 = bf16[2,3,16,2048]{3,2,1,0:T(8,128)(2,1)S(1)} collective-permute-done((bf16[2,3,16,2048]{3,2,1,0:T(8,128)(2,1)S(1)}, bf16[2,3,16,2048]{3,2,1,0:T(8,128)(2,1)S(1)}, u32[]{:S(2)}, u32[]{:S(2)}) %collective-permute-start.12) | collective-permute-done | bytes 393248 | tf_op jit(solution)/shard_map/ppermute | solution.py:176
  74.0 0.5 collective-permute-done.10
  74.6 0.1 pad_maximum_fusion.3.refs_4_
  74.7 0.1 pad_maximum_fusion.2.refs_0_
  74.8 0.8 add_convert_fusion
  75.6 0.3 collective-permute-start.15
  75.9 2.4 %collective-permute-start.14 = (bf16[4,3,16,2048]{3,2,1,0:T(8,128)(2,1)S(1)}, bf16[4,3,16,2048]{3,2,1,0:T(8,128)(2,1)}, u32[]{:S(2)}, u32[]{:S(2)}) collective-permute-start(bf16[4,3,16,2048]{3,2,1,0:T(8,128)(2,1)S(1)} %pad_maximum_fusion.2.refs_0_), channel_id=1, source_target_pairs={{4,0},{5,1},{6,2},{7,3},{8,4},{9,5},{10,6},{11,7},{12,8},{13,9},{1... | collective-permute-start | bytes 2359304 | tf_op jit(solution)/shard_map/ppermute | solution.py:176
  78.2 9.6 %all-to-all-start.1 = ((bf16[8,2,16,432]{3,2,1,0:T(8,128)(2,1)}), bf16[8,2,16,432]{3,2,1,0:T(8,128)(2,1)S(1)}, u32[]{:S(2)}, u32[]{:S(2)}) async-start(bf16[8,2,16,432]{3,2,1,0:T(8,128)(2,1)} %add_convert_fusion), calls=%async_computation.1 | async-start | bytes 524288 | tf_op jit(solution)/shard_map/all_to_all | solution.py:391
  87.9 2.7 %collective-permute-start.19 = (bf16[4,3,16,2048]{3,2,1,0:T(8,128)(2,1)S(1)}, bf16[4,3,16,2048]{3,2,1,0:T(8,128)(2,1)}, u32[]{:S(2)}, u32[]{:S(2)}) collective-permute-start(bf16[4,3,16,2048]{3,2,1,0:T(8,128)(2,1)S(1)} %pad_maximum_fusion.3.refs_4_), channel_id=1, source_target_pairs={{4,0},{5,1},{6,2},{7,3},{8,4},{9,5},{10,6},{11,7},{12,8},{13,9},{1... | collective-permute-start | bytes 2359304 | tf_op jit(solution)/shard_map/ppermute | solution.py:176
  90.5 6.7 %all-to-all-done.1 = bf16[8,2,16,432]{3,2,1,0:T(8,128)(2,1)S(1)} async-done(((bf16[8,2,16,432]{3,2,1,0:T(8,128)(2,1)}), bf16[8,2,16,432]{3,2,1,0:T(8,128)(2,1)S(1)}, u32[]{:S(2)}, u32[]{:S(2)}) %all-to-all-start.1) | async-done | bytes 221216 | tf_op jit(solution)/shard_map/all_to_all | solution.py:391
  97.3 2.7 %collective-permute-start.16 = (bf16[4,3,16,2048]{3,2,1,0:T(8,128)(2,1)}, bf16[4,3,16,2048]{3,2,1,0:T(8,128)(2,1)}, u32[]{:S(2)}, u32[]{:S(2)}) collective-permute-start(bf16[4,3,16,2048]{3,2,1,0:T(8,128)(2,1)} %collective-permute-done.14.refs_1_), channel_id=1, source_target_pairs={{4,0},{5,1},{6,2},{7,3},{8,4},{9,5},{10,6},{11,7},{12,8},{13,9},{1... | collective-permute-start | bytes 2359304 | tf_op jit(solution)/shard_map/ppermute | solution.py:176
  100.0 0.6 slice_bitcast_fusion
  100.6 6.6 %collective-permute-start.20 = (f32[16,432]{1,0:T(8,128)S(1)}, f32[16,432]{1,0:T(8,128)S(1)}, u32[]{:S(2)}, u32[]{:S(2)}) collective-permute-start(f32[16,432]{1,0:T(8,128)S(1)} %get-tuple-element.58), channel_id=1, source_target_pairs={{0,0},{1,16},{2,32},{3,48},{4,64},{5,80},{6,96},{7,112},{8,128},{9... | collective-permute-start | bytes 82952 | tf_op jit(solution)/shard_map/ppermute | solution.py:397
  107.2 2.2 %collective-permute-done.20.got = f32[16,432]{1,0:T(8,128)S(1)} collective-permute-done((f32[16,432]{1,0:T(8,128)S(1)}, f32[16,432]{1,0:T(8,128)S(1)}, u32[]{:S(2)}, u32[]{:S(2)}) %collective-permute-start.20) | collective-permute-done | bytes 27680 | tf_op jit(solution)/shard_map/ppermute | solution.py:397
  109.5 0.6 copy-done.8
  110.1 1.8 %collect_rows.1 = f32[8,2,16,432]{3,2,1,0:T(8,128)} custom-call(f32[16,432]{1,0:T(8,128)} %get-tuple-element.59.mine, f32[16,432]{1,0:T(8,128)} %copy-done.8), custom_call_target="tpu_custom_call" | custom-call | bytes 442368 | tf_op jit(solution)/shard_map/collect_rows/pallas_call | solution.py:349
  111.9 9.7 %all-to-all-start.2 = ((f32[8,2,16,432]{3,2,1,0:T(8,128)}), f32[8,2,16,432]{3,2,1,0:T(8,128)S(1)}, u32[]{:S(2)}, u32[]{:S(2)}) async-start(f32[8,2,16,432]{3,2,1,0:T(8,128)} %collect_rows.1), calls=%async_computation.2 | async-start | bytes 1048576 | tf_op jit(solution)/shard_map/all_to_all | solution.py:391
  121.6 4.8 %layer_two.1 = (f32[3,16,2048]{2,1,0:T(8,128)}, f32[3,16,2048]{2,1,0:T(8,128)}) custom-call(s32[4]{0:T(128)S(1)} %copy-done.2, bf16[4,3,16,2048]{3,2,1,0:T(8,128)(2,1)S(1)} %pad_maximum_fusion.2.refs_0_, bf16[4,3,16,2048]{3,2,1,0:T(8,128)(2,1)} %collective-permute-done.14.refs_1_, bf16[4,3,16,2048]{3,2,1,0:T(8,128)(2,1)} %collective-permute-done.16.refs_2_, ...), custom_call_target="tpu_custom_call" | custom-call | flops 2717908992 | bytes 6291456 | tf_op jit(solution)/shard_map/layer_two/pallas_call | solution.py:267
  126.4 9.8 %all-to-all-done.2.own = f32[8,2,16,432]{3,2,1,0:T(8,128)S(1)} async-done(((f32[8,2,16,432]{3,2,1,0:T(8,128)}), f32[8,2,16,432]{3,2,1,0:T(8,128)S(1)}, u32[]{:S(2)}, u32[]{:S(2)}) %all-to-all-start.2) | async-done | bytes 442400 | tf_op jit(solution)/shard_map/all_to_all | solution.py:391
  136.2 3.8 %collective-permute-start.21 = (f32[8,2,16,432]{3,2,1,0:T(8,128)S(1)}, f32[8,2,16,432]{3,2,1,0:T(8,128)S(1)}, u32[]{:S(2)}, u32[]{:S(2)}) collective-permute-start(f32[8,2,16,432]{3,2,1,0:T(8,128)S(1)} %all-to-all-done.2.own), channel_id=1, source_target_pairs={{0,16},{16,0},{32,48},{48,32},{64,80},{80,64},{96,112},{112,96},{1... | collective-permute-start | bytes 1327112 | tf_op jit(solution)/shard_map/ppermute | solution.py:386
  140.0 1.5 %collective-permute-done.21.other = f32[8,2,16,432]{3,2,1,0:T(8,128)S(1)} collective-permute-done((f32[8,2,16,432]{3,2,1,0:T(8,128)S(1)}, f32[8,2,16,432]{3,2,1,0:T(8,128)S(1)}, u32[]{:S(2)}, u32[]{:S(2)}) %collective-permute-start.21) | collective-permute-done | bytes 442400 | tf_op jit(solution)/shard_map/ppermute | solution.py:386
  141.6 0.8 copy-done.7
  142.4 3.0 %finish_gradients.1 = (f32[432,256]{1,0:T(8,128)}, f32[432,256]{1,0:T(8,128)}) custom-call(s32[4]{0:T(128)} %pad_add_fusion.scalars, f32[8,2,16,432]{3,2,1,0:T(8,128)} %copy-done.3, f32[8,2,16,432]{3,2,1,0:T(8,128)} %copy-done.7), custom_call_target="tpu_custom_call" | custom-call | bytes 1769472 | tf_op jit(solution)/shard_map/finish_gradients/pallas_call | solution.py:370
  (42 shorter events, 0.4 us)
Async XLA Ops:
  1.7 9.9 %collective-permute-start.2 = (bf16[2,3,16,2048]{3,2,1,0:T(8,128)(2,1)S(1)}, bf16[2,3,16,2048]{3,2,1,0:T(8,128)(2,1)S(1)}, u32[]{:S(2)}, u32[]{:S(2)}) collective-permute-start(bf16[2,3,16,2048]{3,2,1,0:T(8,128)(2,1)S(1)} %pad_maximum_fusion.4), channel_id=1, source_target_pairs={{3,0},{0,1},{1,2},{2,3},{7,4},{4,5},{5,6},{6,7},{11,8},{8,9},{9,10... | collective-permute-start | bytes 1179656 | tf_op jit(solution)/shard_map/ppermute | solution.py:176
  3.8 12.1 %collective-permute-start.1 = (bf16[2,3,16,2048]{3,2,1,0:T(8,128)(2,1)S(1)}, bf16[2,3,16,2048]{3,2,1,0:T(8,128)(2,1)S(1)}, u32[]{:S(2)}, u32[]{:S(2)}) collective-permute-start(bf16[2,3,16,2048]{3,2,1,0:T(8,128)(2,1)S(1)} %pad_maximum_fusion.4), channel_id=1, source_target_pairs={{2,0},{3,1},{0,2},{1,3},{6,4},{7,5},{4,6},{5,7},{10,8},{11,9},{8,1... | collective-permute-start | bytes 1179656 | tf_op jit(solution)/shard_map/ppermute | solution.py:176
  6.3 9.7 %collective-permute-start = (bf16[2,3,16,2048]{3,2,1,0:T(8,128)(2,1)S(1)}, bf16[2,3,16,2048]{3,2,1,0:T(8,128)(2,1)S(1)}, u32[]{:S(2)}, u32[]{:S(2)}) collective-permute-start(bf16[2,3,16,2048]{3,2,1,0:T(8,128)(2,1)S(1)} %pad_maximum_fusion.4), channel_id=1, source_target_pairs={{1,0},{2,1},{3,2},{0,3},{5,4},{6,5},{7,6},{4,7},{9,8},{10,9},{11,1... | collective-permute-start | bytes 1179656 | tf_op jit(solution)/shard_map/ppermute | solution.py:176
  16.0 0.9 copy-start.5
  16.0 1.0 copy-start.6
  17.0 15.2 %copy-start.4 = (bf16[16,16,432]{2,1,0:T(8,128)(2,1)S(1)}, bf16[16,16,432]{2,1,0:T(8,128)(2,1)}, u32[]{:S(2)}) copy-start(bf16[16,16,432]{2,1,0:T(8,128)(2,1)} %split_weights.1) | copy-start | bytes 663556
  17.2 11.5 %collective-permute-start.3 = (bf16[4,3,16,2048]{3,2,1,0:T(8,128)(2,1)S(1)}, bf16[4,3,16,2048]{3,2,1,0:T(8,128)(2,1)S(1)}, u32[]{:S(2)}, u32[]{:S(2)}) collective-permute-start(bf16[4,3,16,2048]{3,2,1,0:T(8,128)(2,1)S(1)} %get-tuple-element.23.refs_0_), channel_id=1, source_target_pairs={{4,0},{5,1},{6,2},{7,3},{8,4},{9,5},{10,6},{11,7},{12,8},{13,9},{1... | collective-permute-start | bytes 2359304 | tf_op jit(solution)/shard_map/ppermute | solution.py:176
  19.7 12.5 %collective-permute-start.6 = (bf16[4,3,16,2048]{3,2,1,0:T(8,128)(2,1)S(1)}, bf16[4,3,16,2048]{3,2,1,0:T(8,128)(2,1)}, u32[]{:S(2)}, u32[]{:S(2)}) collective-permute-start(bf16[4,3,16,2048]{3,2,1,0:T(8,128)(2,1)S(1)} %get-tuple-element.24.refs_4_), channel_id=1, source_target_pairs={{12,0},{13,1},{14,2},{15,3},{0,4},{1,5},{2,6},{3,7},{4,8},{5,9},{6... | collective-permute-start | bytes 2359304 | tf_op jit(solution)/shard_map/ppermute | solution.py:176
  19.7 37.6 %collective-permute-start.5 = (bf16[4,3,16,2048]{3,2,1,0:T(8,128)(2,1)S(1)}, bf16[4,3,16,2048]{3,2,1,0:T(8,128)(2,1)}, u32[]{:S(2)}, u32[]{:S(2)}) collective-permute-start(bf16[4,3,16,2048]{3,2,1,0:T(8,128)(2,1)S(1)} %get-tuple-element.23.refs_0_), channel_id=1, source_target_pairs={{12,0},{13,1},{14,2},{15,3},{0,4},{1,5},{2,6},{3,7},{4,8},{5,9},{6... | collective-permute-start | bytes 2359304 | tf_op jit(solution)/shard_map/ppermute | solution.py:176
  19.7 37.6 %collective-permute-start.8 = (bf16[4,3,16,2048]{3,2,1,0:T(8,128)(2,1)S(1)}, bf16[4,3,16,2048]{3,2,1,0:T(8,128)(2,1)}, u32[]{:S(2)}, u32[]{:S(2)}) collective-permute-start(bf16[4,3,16,2048]{3,2,1,0:T(8,128)(2,1)S(1)} %get-tuple-element.24.refs_4_), channel_id=1, source_target_pairs={{4,0},{5,1},{6,2},{7,3},{8,4},{9,5},{10,6},{11,7},{12,8},{13,9},{1... | collective-permute-start | bytes 2359304 | tf_op jit(solution)/shard_map/ppermute | solution.py:176
  28.6 28.7 %collective-permute-start.4 = (bf16[4,3,16,2048]{3,2,1,0:T(8,128)(2,1)S(1)}, bf16[4,3,16,2048]{3,2,1,0:T(8,128)(2,1)}, u32[]{:S(2)}, u32[]{:S(2)}) collective-permute-start(bf16[4,3,16,2048]{3,2,1,0:T(8,128)(2,1)S(1)} %collective-permute-done.3.refs_1_), channel_id=1, source_target_pairs={{4,0},{5,1},{6,2},{7,3},{8,4},{9,5},{10,6},{11,7},{12,8},{13,9},{1... | collective-permute-start | bytes 2359304 | tf_op jit(solution)/shard_map/ppermute | solution.py:176
  32.2 25.2 %collective-permute-start.7 = (bf16[4,3,16,2048]{3,2,1,0:T(8,128)(2,1)}, bf16[4,3,16,2048]{3,2,1,0:T(8,128)(2,1)}, u32[]{:S(2)}, u32[]{:S(2)}) collective-permute-start(bf16[4,3,16,2048]{3,2,1,0:T(8,128)(2,1)} %collective-permute-done.6.refs_5_), channel_id=1, source_target_pairs={{12,0},{13,1},{14,2},{15,3},{0,4},{1,5},{2,6},{3,7},{4,8},{5,9},{6... | collective-permute-start | bytes 2359304 | tf_op jit(solution)/shard_map/ppermute | solution.py:176
  51.1 6.2 %collective-permute-start.9 = (bf16[256,432]{0,1:T(8,128)(2,1)S(1)}, bf16[256,432]{0,1:T(8,128)(2,1)S(1)}, u32[]{:S(2)}, u32[]{:S(2)}) collective-permute-start(bf16[256,432]{0,1:T(8,128)(2,1)S(1)} %copy.10), channel_id=1, source_target_pairs={{0,16},{16,0},{32,48},{48,32},{64,80},{80,64},{96,112},{112,96},{1... | collective-permute-start | bytes 663560 | tf_op jit(solution)/shard_map/ppermute | solution.py:386
  56.2 1.2 copy-start
  57.4 0.7 copy-start.2
  61.8 12.1 %collective-permute-start.12 = (bf16[2,3,16,2048]{3,2,1,0:T(8,128)(2,1)S(1)}, bf16[2,3,16,2048]{3,2,1,0:T(8,128)(2,1)S(1)}, u32[]{:S(2)}, u32[]{:S(2)}) collective-permute-start(bf16[2,3,16,2048]{3,2,1,0:T(8,128)(2,1)S(1)} %layer_one.1.refs_8_), channel_id=1, source_target_pairs={{3,0},{0,1},{1,2},{2,3},{7,4},{4,5},{5,6},{6,7},{11,8},{8,9},{9,10... | collective-permute-start | bytes 1179656 | tf_op jit(solution)/shard_map/ppermute | solution.py:176
  61.9 12.1 %collective-permute-start.11 = (bf16[2,3,16,2048]{3,2,1,0:T(8,128)(2,1)S(1)}, bf16[2,3,16,2048]{3,2,1,0:T(8,128)(2,1)S(1)}, u32[]{:S(2)}, u32[]{:S(2)}) collective-permute-start(bf16[2,3,16,2048]{3,2,1,0:T(8,128)(2,1)S(1)} %layer_one.1.refs_8_), channel_id=1, source_target_pairs={{2,0},{3,1},{0,2},{1,3},{6,4},{7,5},{4,6},{5,7},{10,8},{11,9},{8,1... | collective-permute-start | bytes 1179656 | tf_op jit(solution)/shard_map/ppermute | solution.py:176
  62.5 12.1 %collective-permute-start.10 = (bf16[2,3,16,2048]{3,2,1,0:T(8,128)(2,1)S(1)}, bf16[2,3,16,2048]{3,2,1,0:T(8,128)(2,1)S(1)}, u32[]{:S(2)}, u32[]{:S(2)}) collective-permute-start(bf16[2,3,16,2048]{3,2,1,0:T(8,128)(2,1)S(1)} %layer_one.1.refs_8_), channel_id=1, source_target_pairs={{1,0},{2,1},{3,2},{0,3},{5,4},{6,5},{7,6},{4,7},{9,8},{10,9},{11,1... | collective-permute-start | bytes 1179656 | tf_op jit(solution)/shard_map/ppermute | solution.py:176
  68.4 6.4 %collective-permute-start.13 = (f32[8,2,16,432]{3,2,1,0:T(8,128)S(1)}, f32[8,2,16,432]{3,2,1,0:T(8,128)S(1)}, u32[]{:S(2)}, u32[]{:S(2)}) collective-permute-start(f32[8,2,16,432]{3,2,1,0:T(8,128)S(1)} %get-tuple-element.27), channel_id=1, source_target_pairs={{0,16},{16,0},{32,48},{48,32},{64,80},{80,64},{96,112},{112,96},{1... | collective-permute-start | bytes 1327112 | tf_op jit(solution)/shard_map/ppermute | solution.py:386
  75.6 21.7 %collective-permute-start.15 = (bf16[4,3,16,2048]{3,2,1,0:T(8,128)(2,1)S(1)}, bf16[4,3,16,2048]{3,2,1,0:T(8,128)(2,1)S(1)}, u32[]{:S(2)}, u32[]{:S(2)}) collective-permute-start(bf16[4,3,16,2048]{3,2,1,0:T(8,128)(2,1)S(1)} %pad_maximum_fusion.2.refs_0_), channel_id=1, source_target_pairs={{12,0},{13,1},{14,2},{15,3},{0,4},{1,5},{2,6},{3,7},{4,8},{5,9},{6... | collective-permute-start | bytes 2359304 | tf_op jit(solution)/shard_map/ppermute | solution.py:176
  75.9 21.4 %collective-permute-start.14 = (bf16[4,3,16,2048]{3,2,1,0:T(8,128)(2,1)S(1)}, bf16[4,3,16,2048]{3,2,1,0:T(8,128)(2,1)}, u32[]{:S(2)}, u32[]{:S(2)}) collective-permute-start(bf16[4,3,16,2048]{3,2,1,0:T(8,128)(2,1)S(1)} %pad_maximum_fusion.2.refs_0_), channel_id=1, source_target_pairs={{4,0},{5,1},{6,2},{7,3},{8,4},{9,5},{10,6},{11,7},{12,8},{13,9},{1... | collective-permute-start | bytes 2359304 | tf_op jit(solution)/shard_map/ppermute | solution.py:176
  78.2 21.7 %collective-permute-start.17 = (bf16[4,3,16,2048]{3,2,1,0:T(8,128)(2,1)S(1)}, bf16[4,3,16,2048]{3,2,1,0:T(8,128)(2,1)}, u32[]{:S(2)}, u32[]{:S(2)}) collective-permute-start(bf16[4,3,16,2048]{3,2,1,0:T(8,128)(2,1)S(1)} %pad_maximum_fusion.3.refs_4_), channel_id=1, source_target_pairs={{12,0},{13,1},{14,2},{15,3},{0,4},{1,5},{2,6},{3,7},{4,8},{5,9},{6... | collective-permute-start | bytes 2359304 | tf_op jit(solution)/shard_map/ppermute | solution.py:176
  78.2 19.0 %all-to-all-start.1 = ((bf16[8,2,16,432]{3,2,1,0:T(8,128)(2,1)}), bf16[8,2,16,432]{3,2,1,0:T(8,128)(2,1)S(1)}, u32[]{:S(2)}, u32[]{:S(2)}) async-start(bf16[8,2,16,432]{3,2,1,0:T(8,128)(2,1)} %add_convert_fusion), calls=%async_computation.1 | async-start | bytes 524288 | tf_op jit(solution)/shard_map/all_to_all | solution.py:391
  87.9 33.7 %collective-permute-start.19 = (bf16[4,3,16,2048]{3,2,1,0:T(8,128)(2,1)S(1)}, bf16[4,3,16,2048]{3,2,1,0:T(8,128)(2,1)}, u32[]{:S(2)}, u32[]{:S(2)}) collective-permute-start(bf16[4,3,16,2048]{3,2,1,0:T(8,128)(2,1)S(1)} %pad_maximum_fusion.3.refs_4_), channel_id=1, source_target_pairs={{4,0},{5,1},{6,2},{7,3},{8,4},{9,5},{10,6},{11,7},{12,8},{13,9},{1... | collective-permute-start | bytes 2359304 | tf_op jit(solution)/shard_map/ppermute | solution.py:176
  97.3 24.3 %collective-permute-start.16 = (bf16[4,3,16,2048]{3,2,1,0:T(8,128)(2,1)}, bf16[4,3,16,2048]{3,2,1,0:T(8,128)(2,1)}, u32[]{:S(2)}, u32[]{:S(2)}) collective-permute-start(bf16[4,3,16,2048]{3,2,1,0:T(8,128)(2,1)} %collective-permute-done.14.refs_1_), channel_id=1, source_target_pairs={{4,0},{5,1},{6,2},{7,3},{8,4},{9,5},{10,6},{11,7},{12,8},{13,9},{1... | collective-permute-start | bytes 2359304 | tf_op jit(solution)/shard_map/ppermute | solution.py:176
  100.0 21.6 %collective-permute-start.18 = (bf16[4,3,16,2048]{3,2,1,0:T(8,128)(2,1)}, bf16[4,3,16,2048]{3,2,1,0:T(8,128)(2,1)}, u32[]{:S(2)}, u32[]{:S(2)}) collective-permute-start(bf16[4,3,16,2048]{3,2,1,0:T(8,128)(2,1)} %collective-permute-done.17.refs_5_), channel_id=1, source_target_pairs={{12,0},{13,1},{14,2},{15,3},{0,4},{1,5},{2,6},{3,7},{4,8},{5,9},{6... | collective-permute-start | bytes 2359304 | tf_op jit(solution)/shard_map/ppermute | solution.py:176
  100.6 8.8 %collective-permute-start.20 = (f32[16,432]{1,0:T(8,128)S(1)}, f32[16,432]{1,0:T(8,128)S(1)}, u32[]{:S(2)}, u32[]{:S(2)}) collective-permute-start(f32[16,432]{1,0:T(8,128)S(1)} %get-tuple-element.58), channel_id=1, source_target_pairs={{0,0},{1,16},{2,32},{3,48},{4,64},{5,80},{6,96},{7,112},{8,128},{9... | collective-permute-start | bytes 82952 | tf_op jit(solution)/shard_map/ppermute | solution.py:397
  109.5 0.6 copy-start.8
  111.9 9.7 %copy-start.1 = (bf16[27,16,256]{2,1,0:T(8,128)(2,1)S(1)}, bf16[27,16,256]{2,1,0:T(8,128)(2,1)}, u32[]{:S(2)}) copy-start(bf16[27,16,256]{2,1,0:T(8,128)(2,1)} %w2.1) | copy-start | bytes 663556
  111.9 24.3 %all-to-all-start.2 = ((f32[8,2,16,432]{3,2,1,0:T(8,128)}), f32[8,2,16,432]{3,2,1,0:T(8,128)S(1)}, u32[]{:S(2)}, u32[]{:S(2)}) async-start(f32[8,2,16,432]{3,2,1,0:T(8,128)} %collect_rows.1), calls=%async_computation.2 | async-start | bytes 1048576 | tf_op jit(solution)/shard_map/all_to_all | solution.py:391
  136.2 5.4 %copy-start.3 = (f32[8,2,16,432]{3,2,1,0:T(8,128)}, f32[8,2,16,432]{3,2,1,0:T(8,128)S(1)}, u32[]{:S(2)}) copy-start(f32[8,2,16,432]{3,2,1,0:T(8,128)S(1)} %all-to-all-done.2.own) | copy-start | bytes 1327108
  136.2 5.4 %collective-permute-start.21 = (f32[8,2,16,432]{3,2,1,0:T(8,128)S(1)}, f32[8,2,16,432]{3,2,1,0:T(8,128)S(1)}, u32[]{:S(2)}, u32[]{:S(2)}) collective-permute-start(f32[8,2,16,432]{3,2,1,0:T(8,128)S(1)} %all-to-all-done.2.own), channel_id=1, source_target_pairs={{0,16},{16,0},{32,48},{48,32},{64,80},{80,64},{96,112},{112,96},{1... | collective-permute-start | bytes 1327112 | tf_op jit(solution)/shard_map/ppermute | solution.py:386
  141.6 0.8 copy-start.7

commit v7 on v6

--- a/solution.py
+++ b/solution.py
@@ -96,51 +96,72 @@
 
 def kernel_one(scalars, *refs):
     px, gx = refs[0:4], refs[4:8]
-    w1, w2t, pair_out, full_p, full_g = refs[8:]
+    w1, first_out, second_out, full, stack = refs[8:]
     s = pl.program_id(0)
 
+    @pl.when(s == 0)
+    def _():
+        second_out[...] = jnp.zeros_like(second_out)
+
     @pl.when(s >= scalars[0])
     def _():
+        first_out[...] = jnp.zeros_like(first_out)
+
+    @pl.when(s < scalars[0])
+    def _():
+        masks = axis_masks()
+        place(scalars, px, full, 1)
+        first = tap_conv(w1, full[...], 1, masks)
+        first_out[0] = first
+        hidden = (first * (1.0 / (1.0 + jnp.exp(-first)))).astype(jnp.bfloat16)
+        place(scalars, gx, full, -1)
+        tap_stack(stack, hidden.astype(jnp.float32), 1, masks)
+        second_out[...] += over_cells(full[...], stack[...])
+
+
+def kernel_delta(scalars, *refs):
+    gx = refs[0:4]
+    w2t, first_in, pair_out, full = refs[4:]
+    s = pl.program_id(0)
+
+    @pl.when(s >= scalars[0])
+    def _():
         pair_out[...] = jnp.zeros_like(pair_out)
 
     @pl.when(s < scalars[0])
     def _():
         masks = axis_masks()
-        place(scalars, px, full_p, 1)
-        place(scalars, gx, full_g, -1)
-        first = tap_conv(w1, full_p[...], 1, masks)
-        hidden_grad = tap_conv(w2t, full_g[...], -1, masks)
+        place(scalars, gx, full, -1)
+        hidden_grad = tap_conv(w2t, full[...], -1, masks)
+        first = first_in[0]
         sigma = 1.0 / (1.0 + jnp.exp(-first))
         pair_out[0, 0] = (first * sigma).astype(jnp.bfloat16)
         pair_out[1, 0] = (hidden_grad * sigma * (1.0 + first * (1.0 - sigma))).astype(jnp.bfloat16)
 
 
 def kernel_grads(scalars, *refs):
-    px, gx = refs[0:4], refs[4:8]
-    pair, keep_out, send_out, full, stack, grads = refs[8:]
+    px = refs[0:4]
+    pair, second, keep_out, send_out, full, stack, first_sum = refs[4:]
     s = pl.program_id(0)
     core = scalars[3]
 
     @pl.when(s == 0)
     def _():
-        grads[...] = jnp.zeros_like(grads)
+        first_sum[...] = jnp.zeros_like(first_sum)
 
     @pl.when(s < scalars[0])
     def _():
         masks = axis_masks()
         place(scalars, px, full, 1)
         tap_stack(stack, pair[1, 0].astype(jnp.float32), -1, masks)
-        grads[0] += over_cells(full[...], stack[...])
-        place(scalars, gx, full, -1)
-        tap_stack(stack, pair[0, 0].astype(jnp.float32), 1, masks)
-        grads[1] += over_cells(full[...], stack[...])
+        first_sum[...] += over_cells(full[...], stack[...])
 
     @pl.when(s == pl.num_programs(0) - 1)
     def _():
         for z in range(8):
-            for k in range(2):
-                keep_out[z, k] = grads[k, pl.ds(pl.multiple_of((2 * z + core) * BLK, BLK), BLK), :]
-                send_out[z, k] = grads[k, pl.ds(pl.multiple_of((2 * z + 1 - core) * BLK, BLK), BLK), :]
+            for k, total in enumerate((first_sum, second)):
+                keep_out[z, k] = total[pl.ds(pl.multiple_of((2 * z + core) * BLK, BLK), BLK), :]
+                send_out[z, k] = total[pl.ds(pl.multiple_of((2 * z + 1 - core) * BLK, BLK), BLK), :]
 
 
 def kernel_two(scalars, *refs):
@@ -196,12 +217,16 @@
     return jnp.minimum(s, jnp.maximum(scalars[0] - 1, 0))
 
 
-def piece_specs():
-    return [pl.BlockSpec((SIDE, 1, BLK, CELLS), lambda s, sc: (0, live_slot(s, sc), 0, 0))] * 8
-
-
-def weight_specs():
-    return [pl.BlockSpec((ROWS, C), lambda s, *_: (0, 0))] * 2
+def piece_specs(count):
+    return [pl.BlockSpec((SIDE, 1, BLK, CELLS), lambda s, sc: (0, live_slot(s, sc), 0, 0))] * count
+
+
+def weight_specs(count):
+    return [pl.BlockSpec((ROWS, C), lambda s, *_: (0, 0))] * count
+
+
+def sum_spec():
+    return pl.BlockSpec((C, ROWS), lambda s, *_: (0, 0))
 
 
 def slot_spec():
@@ -216,28 +241,52 @@
     return pltpu.CompilerParams(vmem_limit_bytes=48 * 1024 * 1024)
 
 
-def call_one(scalars, pieces, w1, w2t):
+def cost_of(slots, convs):
+    return pl.CostEstimate(
+        flops=slots * convs * 2 * ROWS * C * CELLS, transcendentals=slots * BLK * CELLS, bytes_accessed=slots * convs * 2 * C * CELLS
+    )
+
+
+def call_one(scalars, pieces, w1):
     slots = pieces[0].shape[1]
-    pair = jax.ShapeDtypeStruct((2, slots, BLK, CELLS), jnp.bfloat16)
     return pl.pallas_call(
         kernel_one,
         name="layer_one",
         grid_spec=pltpu.PrefetchScalarGridSpec(
             num_scalar_prefetch=1,
             grid=(slots,),
-            in_specs=piece_specs() + weight_specs(),
+            in_specs=piece_specs(8) + weight_specs(1),
+            out_specs=[slot_spec(), sum_spec()],
+            scratch_shapes=[pltpu.VMEM((C, CELLS), jnp.bfloat16), pltpu.VMEM((ROWS, CELLS), jnp.bfloat16)],
+        ),
+        out_shape=[
+            jax.ShapeDtypeStruct((slots, BLK, CELLS), jnp.float32),
+            jax.ShapeDtypeStruct((C, ROWS), jnp.float32),
+        ],
+        compiler_params=params(),
+        cost_estimate=cost_of(slots, 2),
+    )(scalars, *pieces, w1)
+
+
+def call_delta(scalars, pieces, w2t, first):
+    slots = pieces[0].shape[1]
+    return pl.pallas_call(
+        kernel_delta,
+        name="layer_one_delta",
+        grid_spec=pltpu.PrefetchScalarGridSpec(
+            num_scalar_prefetch=1,
+            grid=(slots,),
+            in_specs=piece_specs(4) + weight_specs(1) + [slot_spec()],
             out_specs=pair_spec(),
-            scratch_shapes=[pltpu.VMEM((C, CELLS), jnp.bfloat16)] * 2,
-        ),
-        out_shape=pair,
+            scratch_shapes=[pltpu.VMEM((C, CELLS), jnp.bfloat16)],
+        ),
+        out_shape=jax.ShapeDtypeStruct((2, slots, BLK, CELLS), jnp.bfloat16),
         compiler_params=params(),
-        cost_estimate=pl.CostEstimate(
-            flops=slots * 4 * ROWS * C * CELLS, transcendentals=slots * BLK * CELLS, bytes_accessed=slots * 4 * C * CELLS
-        ),
-    )(scalars, *pieces, w1, w2t)
-
-
-def call_grads(scalars, pieces, pair):
+        cost_estimate=cost_of(slots, 1),
+    )(scalars, *pieces, w2t, first)
+
+
+def call_grads(scalars, pieces, pair, second):
     slots = pieces[0].shape[1]
     return pl.pallas_call(
         kernel_grads,
@@ -245,20 +294,18 @@
         grid_spec=pltpu.PrefetchScalarGridSpec(
             num_scalar_prefetch=1,
             grid=(slots,),
-            in_specs=piece_specs() + [pair_spec()],
+            in_specs=piece_specs(4) + [pair_spec(), sum_spec()],
             out_specs=[pl.BlockSpec(HALF, lambda s, *_: (0, 0, 0, 0))] * 2,
             scratch_shapes=[
                 pltpu.VMEM((C, CELLS), jnp.bfloat16),
                 pltpu.VMEM((ROWS, CELLS), jnp.bfloat16),
-                pltpu.VMEM((2, C, ROWS), jnp.float32),
+                pltpu.VMEM((C, ROWS), jnp.float32),
             ],
         ),
         out_shape=[jax.ShapeDtypeStruct(HALF, jnp.float32)] * 2,
         compiler_params=params(),
-        cost_estimate=pl.CostEstimate(
-            flops=slots * 4 * ROWS * C * CELLS, transcendentals=0, bytes_accessed=slots * 4 * C * CELLS
-        ),
-    )(scalars, *pieces, pair)
+        cost_estimate=cost_of(slots, 1),
+    )(scalars, *pieces, pair, second)
 
 
 def call_two(scalars, pieces, w2, w1t):
@@ -270,7 +317,7 @@
         grid_spec=pltpu.PrefetchScalarGridSpec(
             num_scalar_prefetch=1,
             grid=(slots,),
-            in_specs=piece_specs() + weight_specs(),
+            in_specs=piece_specs(8) + weight_specs(2),
             out_specs=[slot_spec(), slot_spec()],
             scratch_shapes=[
                 pltpu.VMEM((C, CELLS), jnp.bfloat16),
@@ -414,15 +461,17 @@
 
     turned = lax.all_to_all(split, "filter", 0, 0, tiled=True).reshape(C, ROWS)
     pieces = gather_last(fars)
+    w1 = first_weight.reshape(ROWS, C)
+    w2 = second_weight.reshape(ROWS, C)
+
+    first, second = call_one(scalars, pieces, w1)
+    turned, first = lax.optimization_barrier((turned, first))
     other = swap_cores(turned)
     w1t = jnp.where(core == 0, turned, other).T
     w2t = jnp.where(core == 0, other, turned).T
-    w1 = first_weight.reshape(ROWS, C)
-    w2 = second_weight.reshape(ROWS, C)
-
-    pair = call_one(scalars, pieces, w1, w2t)
+    pair = call_delta(scalars, pieces[4:], w2t, first)
     nears = gather_near(pair)
-    keep, send = call_grads(scalars, pieces, pair)
+    keep, send = call_grads(scalars, pieces[:4], pair, second)
     pair_sum = (keep + swap_cores(send)).astype(jnp.bfloat16)
     nears, pair_sum = lax.optimization_barrier((nears, pair_sum))
     fars = gather_far(nears)

time: 147 us -> 147 us (level)
  blocking collectives: 18.8 us -> 0 us
  waiting for transfers between devices: 37.9 us -> 51.8 us
  starting transfers between devices: 60.2 us -> 62.7 us
  Pallas kernels: 20 us -> 22.2 us
    all_to_all x1 -> x0, blocking collectives: 18.8 us -> none  [shards(): turned = lax.all_to_all(split, 'filter', 0, 0, tiled=True).reshape(C, ROWS)]
    ppermute x18, waiting for transfers between devices: 16.5 us -> 31.2 us  [turn(): return lax.ppermute(v, ('dp', 'filter'), from_axis(axes, step))]
    all_to_all x0 -> x1, starting transfers between devices: none -> 3.53 us  [shards(): turned = lax.all_to_all(split, 'filter', 0, 0, tiled=True).reshape(C, ROWS)]
    pallas_call x0 -> x1, Pallas kernels: none -> 2.85 us  [call_delta(): pl.pallas_call(kernel_delta, name='layer_one_delta', grid_spec=pltpu.Pref...]
    unnamed x18 -> x22, local copies, waits for them, and re-layouts: 3.06 us -> 3.17 us
  transfers between devices with their start and end apart: 24 -> 25, of which waited for: 9 -> 12; matrix products, arithmetic and copies ran while one was open for 1% -> 1% of each run, Pallas kernels for 9% -> 11%
where the time goes in v7:
time: 147 us; the launch traced here: 146 us
  starting transfers between devices  62.7 us (43%)
  waiting for transfers between devices  51.8 us (35%)
  Pallas kernels  22.2 us (15%)
  local copies, waits for them, and re-layouts  4.11 us (3%)
  other arithmetic  3.83 us (3%)
  between operations  1.54 us (1%)
    ppermute x18, waiting for transfers between devices, turn(): return lax.ppermute(v, ('dp', 'filter'), from_axis(axes, step))  31.2 us
    ppermute x18, starting transfers between devices, turn(): return lax.ppermute(v, ('dp', 'filter'), from_axis(axes, step))  25.6 us
    all_to_all x2, starting transfers between devices, over_z(): return lax.all_to_all(v, 'dp', 0, 0, axis_index_groups=by_core, tiled=True)  18.6 us
    all_to_all x2, waiting for transfers between devices, over_z(): return lax.all_to_all(v, 'dp', 0, 0, axis_index_groups=by_core, tiled=True)  16 us
    ppermute x3, starting transfers between devices, swap_cores(): return lax.ppermute(v, 'dp', [(d, d ^ 1) for d in range(BLK)])  8.09 us
    ppermute x1, starting transfers between devices, sum_over_dp(): got = lax.ppermute(mine[1], ('dp', 'filter'), flip)  6.91 us
    pallas_call x1, Pallas kernels, call_two(): pl.pallas_call(kernel_two, name='layer_two', grid_spec=pltpu.PrefetchScal...  4.79 us
    pallas_call x1, Pallas kernels, call_one(): pl.pallas_call(kernel_one, name='layer_one', grid_spec=pltpu.PrefetchScal...  4.04 us
  transfers between devices with their start and end apart: 25, of which 12 were waited for; matrix products, arithmetic and copies ran while one was open for 1% of the time, Pallas kernels for 11%

profile of v7, /device:TPU:1, one launch (start us, length us, event | category | flops | bytes accessed | tf_op | source)
XLA Modules:
  0.0 146.2 jit_solution(2917064254206180225)
XLA Ops:
  0.6 1.1 pad_maximum_fusion.4
  1.7 2.1 %collective-permute-start.2 = (bf16[2,3,16,2048]{3,2,1,0:T(8,128)(2,1)S(1)}, bf16[2,3,16,2048]{3,2,1,0:T(8,128)(2,1)S(1)}, u32[]{:S(2)}, u32[]{:S(2)}) collective-permute-start(bf16[2,3,16,2048]{3,2,1,0:T(8,128)(2,1)S(1)} %pad_maximum_fusion.4), channel_id=1, source_target_pairs={{3,0},{0,1},{1,2},{2,3},{7,4},{4,5},{5,6},{6,7},{11,8},{8,9},{9,10... | collective-permute-start | bytes 1179656 | tf_op jit(solution)/shard_map/ppermute | solution.py:197
  3.8 2.5 %collective-permute-start.1 = (bf16[2,3,16,2048]{3,2,1,0:T(8,128)(2,1)S(1)}, bf16[2,3,16,2048]{3,2,1,0:T(8,128)(2,1)S(1)}, u32[]{:S(2)}, u32[]{:S(2)}) collective-permute-start(bf16[2,3,16,2048]{3,2,1,0:T(8,128)(2,1)S(1)} %pad_maximum_fusion.4), channel_id=1, source_target_pairs={{2,0},{3,1},{0,2},{1,3},{6,4},{7,5},{4,6},{5,7},{10,8},{11,9},{8,1... | collective-permute-start | bytes 1179656 | tf_op jit(solution)/shard_map/ppermute | solution.py:197
  6.3 1.2 collective-permute-start
  8.1 0.6 pad_add_fusion.scalars
  8.7 2.9 %split_weights.1 = bf16[16,16,432]{2,1,0:T(8,128)(2,1)} custom-call(s32[4]{0:T(128)} %pad_add_fusion.scalars, bf16[27,16,256]{2,1,0:T(8,128)(2,1)} %w1.1, bf16[27,16,256]{2,1,0:T(8,128)(2,1)} %w2.1), custom_call_target="tpu_custom_call" | custom-call | bytes 884736 | tf_op jit(solution)/shard_map/split_weights/pallas_call | solution.py:363
  11.6 4.4 %collective-permute-done.1 = bf16[2,3,16,2048]{3,2,1,0:T(8,128)(2,1)S(1)} collective-permute-done((bf16[2,3,16,2048]{3,2,1,0:T(8,128)(2,1)S(1)}, bf16[2,3,16,2048]{3,2,1,0:T(8,128)(2,1)S(1)}, u32[]{:S(2)}, u32[]{:S(2)}) %collective-permute-start.1) | collective-permute-done | bytes 393248 | tf_op jit(solution)/shard_map/ppermute | solution.py:197
  16.0 0.9 copy-done.7
  17.2 1.1 collective-permute-start.3
  18.3 1.7 %collective-permute-start.6 = (bf16[4,3,16,2048]{3,2,1,0:T(8,128)(2,1)S(1)}, bf16[4,3,16,2048]{3,2,1,0:T(8,128)(2,1)S(1)}, u32[]{:S(2)}, u32[]{:S(2)}) collective-permute-start(bf16[4,3,16,2048]{3,2,1,0:T(8,128)(2,1)S(1)} %get-tuple-element.29.refs_0_), channel_id=1, source_target_pairs={{4,0},{5,1},{6,2},{7,3},{8,4},{9,5},{10,6},{11,7},{12,8},{13,9},{1... | collective-permute-start | bytes 2359304 | tf_op jit(solution)/shard_map/ppermute | solution.py:197
  20.0 1.2 collective-permute-start.5
  21.2 0.2 collective-permute-start.8
  21.4 8.3 %collective-permute-done.3.refs_5_.refs_1_ = bf16[4,3,16,2048]{3,2,1,0:T(8,128)(2,1)} collective-permute-done((bf16[4,3,16,2048]{3,2,1,0:T(8,128)(2,1)S(1)}, bf16[4,3,16,2048]{3,2,1,0:T(8,128)(2,1)}, u32[]{:S(2)}, u32[]{:S(2)}) %collective-permute-start.3) | collective-permute-done | bytes 786464 | tf_op jit(solution)/shard_map/ppermute | solution.py:197
  29.7 2.7 %collective-permute-start.7 = (bf16[4,3,16,2048]{3,2,1,0:T(8,128)(2,1)S(1)}, bf16[4,3,16,2048]{3,2,1,0:T(8,128)(2,1)}, u32[]{:S(2)}, u32[]{:S(2)}) collective-permute-start(bf16[4,3,16,2048]{3,2,1,0:T(8,128)(2,1)S(1)} %collective-permute-done.6.refs_1_), channel_id=1, source_target_pairs={{4,0},{5,1},{6,2},{7,3},{8,4},{9,5},{10,6},{11,7},{12,8},{13,9},{1... | collective-permute-start | bytes 2359304 | tf_op jit(solution)/shard_map/ppermute | solution.py:197
  32.4 3.5 %all-to-all-start = ((bf16[16,16,432]{2,1,0:T(8,128)(2,1)}), bf16[16,16,432]{2,1,0:T(8,128)(2,1)S(1)}, u32[]{:S(2)}, u32[]{:S(2)}) async-start(bf16[16,16,432]{2,1,0:T(8,128)(2,1)} %split_weights.1), calls=%async_computation | async-start | bytes 524288 | tf_op jit(solution)/shard_map/all_to_all | solution.py:462
  36.0 2.0 %collective-permute-done.5.refs_7_.refs_3_ = bf16[4,3,16,2048]{3,2,1,0:T(8,128)(2,1)} collective-permute-done((bf16[4,3,16,2048]{3,2,1,0:T(8,128)(2,1)S(1)}, bf16[4,3,16,2048]{3,2,1,0:T(8,128)(2,1)}, u32[]{:S(2)}, u32[]{:S(2)}) %collective-permute-start.5) | collective-permute-done | bytes 786464 | tf_op jit(solution)/shard_map/ppermute | solution.py:197
  37.9 0.2 collective-permute-done.8.refs_3_
  38.2 9.8 %collective-permute-done.4.refs_6_.refs_2_ = bf16[4,3,16,2048]{3,2,1,0:T(8,128)(2,1)} collective-permute-done((bf16[4,3,16,2048]{3,2,1,0:T(8,128)(2,1)}, bf16[4,3,16,2048]{3,2,1,0:T(8,128)(2,1)}, u32[]{:S(2)}, u32[]{:S(2)}) %collective-permute-start.4) | collective-permute-done | bytes 786464 | tf_op jit(solution)/shard_map/ppermute | solution.py:197
  48.0 4.0 %layer_one.1 = (f32[3,16,2048]{2,1,0:T(8,128)S(1)}, f32[256,432]{1,0:T(8,128)S(1)}) custom-call(s32[4]{0:T(128)S(1)} %copy-done.2, bf16[4,3,16,2048]{3,2,1,0:T(8,128)(2,1)S(1)} %get-tuple-element.29.refs_0_, bf16[4,3,16,2048]{3,2,1,0:T(8,128)(2,1)S(1)} %collective-permute-done.6.refs_1_, bf16[4,3,16,2048]{3,2,1,0:T(8,128)(2,1)} %collective-permute-done.7.refs_2_, ...), custom_call_target="tpu_custom_call" | custom-call | flops 2717908992 | bytes 6291456 | tf_op jit(solution)/shard_map/layer_one/pallas_call | solution.py:252
  52.1 0.7 copy-done.3
  53.0 3.4 %collective-permute-start.9 = (bf16[256,432]{0,1:T(8,128)(2,1)S(1)}, bf16[256,432]{0,1:T(8,128)(2,1)S(1)}, u32[]{:S(2)}, u32[]{:S(2)}) collective-permute-start(bf16[256,432]{0,1:T(8,128)(2,1)S(1)} %copy.10), channel_id=1, source_target_pairs={{0,16},{16,0},{32,48},{48,32},{64,80},{80,64},{96,112},{112,96},{1... | collective-permute-start | bytes 663560 | tf_op jit(solution)/shard_map/ppermute | solution.py:433
  56.4 1.1 collective-permute-done.9
  57.5 1.0 select_bitcast_fusion
  58.5 2.8 %layer_one_delta.1.refs_4_ = bf16[2,3,16,2048]{3,2,1,0:T(8,128)(2,1)S(1)} custom-call(s32[4]{0:T(128)S(1)} %copy-done.2, bf16[4,3,16,2048]{3,2,1,0:T(8,128)(2,1)S(1)} %get-tuple-element.27.refs_4_.refs_0_, bf16[4,3,16,2048]{3,2,1,0:T(8,128)(2,1)} %collective-permute-done.3.refs_5_.refs_1_, bf16[4,3,16,2048]{3,2,1,0:T(8,128)(2,1)} %collective-permute-done.4.refs_6_.refs_2_, ...), custom_call_target="tpu_custom_call" | custom-call | flops 1358954496 | bytes 3145728 | tf_op jit(solution)/shard_map/layer_one_delta/pallas_call | solution.py:273
  61.3 1.0 collective-permute-start.12
  62.4 3.9 %collective-permute-start.11 = (bf16[2,3,16,2048]{3,2,1,0:T(8,128)(2,1)S(1)}, bf16[2,3,16,2048]{3,2,1,0:T(8,128)(2,1)S(1)}, u32[]{:S(2)}, u32[]{:S(2)}) collective-permute-start(bf16[2,3,16,2048]{3,2,1,0:T(8,128)(2,1)S(1)} %layer_one_delta.1.refs_4_), channel_id=1, source_target_pairs={{2,0},{3,1},{0,2},{1,3},{6,4},{7,5},{4,6},{5,7},{10,8},{11,9},{8,1... | collective-permute-start | bytes 1179656 | tf_op jit(solution)/shard_map/ppermute | solution.py:197
  66.2 2.8 %weight_grads.1 = (f32[8,2,16,432]{3,2,1,0:T(8,128)S(1)}, f32[8,2,16,432]{3,2,1,0:T(8,128)S(1)}) custom-call(s32[4]{0:T(128)S(1)} %copy-done.2, bf16[4,3,16,2048]{3,2,1,0:T(8,128)(2,1)S(1)} %get-tuple-element.29.refs_0_, bf16[4,3,16,2048]{3,2,1,0:T(8,128)(2,1)S(1)} %collective-permute-done.6.refs_1_, ...), custom_call_target="tpu_custom_call" | custom-call | flops 1358954496 | bytes 3145728 | tf_op jit(solution)/shard_map/weight_grads/pallas_call | solution.py:291
  69.1 0.3 collective-permute-start.13
  69.4 1.1 collective-permute-done.12
  70.6 5.4 %collective-permute-done.11 = bf16[2,3,16,2048]{3,2,1,0:T(8,128)(2,1)S(1)} collective-permute-done((bf16[2,3,16,2048]{3,2,1,0:T(8,128)(2,1)S(1)}, bf16[2,3,16,2048]{3,2,1,0:T(8,128)(2,1)S(1)}, u32[]{:S(2)}, u32[]{:S(2)}) %collective-permute-start.11) | collective-permute-done | bytes 393248 | tf_op jit(solution)/shard_map/ppermute | solution.py:197
  76.2 0.8 add_convert_fusion
  77.1 2.6 %collective-permute-start.14 = (bf16[4,3,16,2048]{3,2,1,0:T(8,128)(2,1)S(1)}, bf16[4,3,16,2048]{3,2,1,0:T(8,128)(2,1)}, u32[]{:S(2)}, u32[]{:S(2)}) collective-permute-start(bf16[4,3,16,2048]{3,2,1,0:T(8,128)(2,1)S(1)} %pad_maximum_fusion.2.refs_0_), channel_id=1, source_target_pairs={{4,0},{5,1},{6,2},{7,3},{8,4},{9,5},{10,6},{11,7},{12,8},{13,9},{1... | collective-permute-start | bytes 2359304 | tf_op jit(solution)/shard_map/ppermute | solution.py:197
  79.7 8.8 %all-to-all-start.1 = ((bf16[8,2,16,432]{3,2,1,0:T(8,128)(2,1)}), bf16[8,2,16,432]{3,2,1,0:T(8,128)(2,1)S(1)}, u32[]{:S(2)}, u32[]{:S(2)}) async-start(bf16[8,2,16,432]{3,2,1,0:T(8,128)(2,1)} %add_convert_fusion), calls=%async_computation.1 | async-start | bytes 524288 | tf_op jit(solution)/shard_map/all_to_all | solution.py:438
  88.5 2.7 %collective-permute-start.19 = (bf16[4,3,16,2048]{3,2,1,0:T(8,128)(2,1)S(1)}, bf16[4,3,16,2048]{3,2,1,0:T(8,128)(2,1)}, u32[]{:S(2)}, u32[]{:S(2)}) collective-permute-start(bf16[4,3,16,2048]{3,2,1,0:T(8,128)(2,1)S(1)} %pad_maximum_fusion.3.refs_4_), channel_id=1, source_target_pairs={{4,0},{5,1},{6,2},{7,3},{8,4},{9,5},{10,6},{11,7},{12,8},{13,9},{1... | collective-permute-start | bytes 2359304 | tf_op jit(solution)/shard_map/ppermute | solution.py:197
  91.2 6.7 %all-to-all-done.1 = bf16[8,2,16,432]{3,2,1,0:T(8,128)(2,1)S(1)} async-done(((bf16[8,2,16,432]{3,2,1,0:T(8,128)(2,1)}), bf16[8,2,16,432]{3,2,1,0:T(8,128)(2,1)S(1)}, u32[]{:S(2)}, u32[]{:S(2)}) %all-to-all-start.1) | async-done | bytes 221216 | tf_op jit(solution)/shard_map/all_to_all | solution.py:438
  97.9 2.7 %collective-permute-start.16 = (bf16[4,3,16,2048]{3,2,1,0:T(8,128)(2,1)}, bf16[4,3,16,2048]{3,2,1,0:T(8,128)(2,1)}, u32[]{:S(2)}, u32[]{:S(2)}) collective-permute-start(bf16[4,3,16,2048]{3,2,1,0:T(8,128)(2,1)} %collective-permute-done.14.refs_1_), channel_id=1, source_target_pairs={{4,0},{5,1},{6,2},{7,3},{8,4},{9,5},{10,6},{11,7},{12,8},{13,9},{1... | collective-permute-start | bytes 2359304 | tf_op jit(solution)/shard_map/ppermute | solution.py:197
  100.7 0.6 slice_bitcast_fusion
  101.3 6.9 %collective-permute-start.20 = (f32[16,432]{1,0:T(8,128)S(1)}, f32[16,432]{1,0:T(8,128)S(1)}, u32[]{:S(2)}, u32[]{:S(2)}) collective-permute-start(f32[16,432]{1,0:T(8,128)S(1)} %get-tuple-element.66), channel_id=1, source_target_pairs={{0,0},{1,16},{2,32},{3,48},{4,64},{5,80},{6,96},{7,112},{8,128},{9... | collective-permute-start | bytes 82952 | tf_op jit(solution)/shard_map/ppermute | solution.py:444
  108.2 2.0 %collective-permute-done.20.got = f32[16,432]{1,0:T(8,128)S(1)} collective-permute-done((f32[16,432]{1,0:T(8,128)S(1)}, f32[16,432]{1,0:T(8,128)S(1)}, u32[]{:S(2)}, u32[]{:S(2)}) %collective-permute-start.20) | collective-permute-done | bytes 27680 | tf_op jit(solution)/shard_map/ppermute | solution.py:444
  110.2 0.6 copy-done.10
  110.8 1.8 %collect_rows.1 = f32[8,2,16,432]{3,2,1,0:T(8,128)} custom-call(f32[16,432]{1,0:T(8,128)} %get-tuple-element.67.mine, f32[16,432]{1,0:T(8,128)} %copy-done.10), custom_call_target="tpu_custom_call" | custom-call | bytes 442368 | tf_op jit(solution)/shard_map/collect_rows/pallas_call | solution.py:396
  112.6 9.8 %all-to-all-start.2 = ((f32[8,2,16,432]{3,2,1,0:T(8,128)}), f32[8,2,16,432]{3,2,1,0:T(8,128)S(1)}, u32[]{:S(2)}, u32[]{:S(2)}) async-start(f32[8,2,16,432]{3,2,1,0:T(8,128)} %collect_rows.1), calls=%async_computation.2 | async-start | bytes 1048576 | tf_op jit(solution)/shard_map/all_to_all | solution.py:438
  122.4 4.8 %layer_two.1 = (f32[3,16,2048]{2,1,0:T(8,128)}, f32[3,16,2048]{2,1,0:T(8,128)}) custom-call(s32[4]{0:T(128)S(1)} %copy-done.2, bf16[4,3,16,2048]{3,2,1,0:T(8,128)(2,1)S(1)} %pad_maximum_fusion.2.refs_0_, bf16[4,3,16,2048]{3,2,1,0:T(8,128)(2,1)} %collective-permute-done.14.refs_1_, bf16[4,3,16,2048]{3,2,1,0:T(8,128)(2,1)} %collective-permute-done.16.refs_2_, ...), custom_call_target="tpu_custom_call" | custom-call | flops 2717908992 | bytes 6291456 | tf_op jit(solution)/shard_map/layer_two/pallas_call | solution.py:314
  127.2 9.2 %all-to-all-done.2.own = f32[8,2,16,432]{3,2,1,0:T(8,128)S(1)} async-done(((f32[8,2,16,432]{3,2,1,0:T(8,128)}), f32[8,2,16,432]{3,2,1,0:T(8,128)S(1)}, u32[]{:S(2)}, u32[]{:S(2)}) %all-to-all-start.2) | async-done | bytes 442400 | tf_op jit(solution)/shard_map/all_to_all | solution.py:438
  136.5 4.4 %collective-permute-start.21 = (f32[8,2,16,432]{3,2,1,0:T(8,128)S(1)}, f32[8,2,16,432]{3,2,1,0:T(8,128)S(1)}, u32[]{:S(2)}, u32[]{:S(2)}) collective-permute-start(f32[8,2,16,432]{3,2,1,0:T(8,128)S(1)} %all-to-all-done.2.own), channel_id=1, source_target_pairs={{0,16},{16,0},{32,48},{48,32},{64,80},{80,64},{96,112},{112,96},{1... | collective-permute-start | bytes 1327112 | tf_op jit(solution)/shard_map/ppermute | solution.py:433
  140.9 1.5 %collective-permute-done.21.other = f32[8,2,16,432]{3,2,1,0:T(8,128)S(1)} collective-permute-done((f32[8,2,16,432]{3,2,1,0:T(8,128)S(1)}, f32[8,2,16,432]{3,2,1,0:T(8,128)S(1)}, u32[]{:S(2)}, u32[]{:S(2)}) %collective-permute-start.21) | collective-permute-done | bytes 442400 | tf_op jit(solution)/shard_map/ppermute | solution.py:433
  142.4 0.8 copy-done.9
  143.2 3.0 %finish_gradients.1 = (f32[432,256]{1,0:T(8,128)}, f32[432,256]{1,0:T(8,128)}) custom-call(s32[4]{0:T(128)} %pad_add_fusion.scalars, f32[8,2,16,432]{3,2,1,0:T(8,128)} %copy-done.5, f32[8,2,16,432]{3,2,1,0:T(8,128)} %copy-done.9), custom_call_target="tpu_custom_call" | custom-call | bytes 1769472 | tf_op jit(solution)/shard_map/finish_gradients/pallas_call | solution.py:417
  (48 shorter events, 1.0 us)
Async XLA Ops:
  1.7 9.8 %collective-permute-start.2 = (bf16[2,3,16,2048]{3,2,1,0:T(8,128)(2,1)S(1)}, bf16[2,3,16,2048]{3,2,1,0:T(8,128)(2,1)S(1)}, u32[]{:S(2)}, u32[]{:S(2)}) collective-permute-start(bf16[2,3,16,2048]{3,2,1,0:T(8,128)(2,1)S(1)} %pad_maximum_fusion.4), channel_id=1, source_target_pairs={{3,0},{0,1},{1,2},{2,3},{7,4},{4,5},{5,6},{6,7},{11,8},{8,9},{9,10... | collective-permute-start | bytes 1179656 | tf_op jit(solution)/shard_map/ppermute | solution.py:197
  3.8 12.1 %collective-permute-start.1 = (bf16[2,3,16,2048]{3,2,1,0:T(8,128)(2,1)S(1)}, bf16[2,3,16,2048]{3,2,1,0:T(8,128)(2,1)S(1)}, u32[]{:S(2)}, u32[]{:S(2)}) collective-permute-start(bf16[2,3,16,2048]{3,2,1,0:T(8,128)(2,1)S(1)} %pad_maximum_fusion.4), channel_id=1, source_target_pairs={{2,0},{3,1},{0,2},{1,3},{6,4},{7,5},{4,6},{5,7},{10,8},{11,9},{8,1... | collective-permute-start | bytes 1179656 | tf_op jit(solution)/shard_map/ppermute | solution.py:197
  6.3 9.7 %collective-permute-start = (bf16[2,3,16,2048]{3,2,1,0:T(8,128)(2,1)S(1)}, bf16[2,3,16,2048]{3,2,1,0:T(8,128)(2,1)S(1)}, u32[]{:S(2)}, u32[]{:S(2)}) collective-permute-start(bf16[2,3,16,2048]{3,2,1,0:T(8,128)(2,1)S(1)} %pad_maximum_fusion.4), channel_id=1, source_target_pairs={{1,0},{2,1},{3,2},{0,3},{5,4},{6,5},{7,6},{4,7},{9,8},{10,9},{11,1... | collective-permute-start | bytes 1179656 | tf_op jit(solution)/shard_map/ppermute | solution.py:197
  16.0 0.9 copy-start.7
  16.0 1.0 copy-start.8
  17.2 30.8 %copy-start = (bf16[27,16,256]{2,1,0:T(8,128)(2,1)S(1)}, bf16[27,16,256]{2,1,0:T(8,128)(2,1)}, u32[]{:S(2)}) copy-start(bf16[27,16,256]{2,1,0:T(8,128)(2,1)} %w1.1) | copy-start | bytes 663556
  17.2 12.5 %collective-permute-start.3 = (bf16[4,3,16,2048]{3,2,1,0:T(8,128)(2,1)S(1)}, bf16[4,3,16,2048]{3,2,1,0:T(8,128)(2,1)}, u32[]{:S(2)}, u32[]{:S(2)}) collective-permute-start(bf16[4,3,16,2048]{3,2,1,0:T(8,128)(2,1)S(1)} %get-tuple-element.27.refs_4_.refs_0_), channel_id=1, source_target_pairs={{12,0},{13,1},{14,2},{15,3},{0,4},{1,5},{2,6},{3,7},{4,8},{5,9},{6... | collective-permute-start | bytes 2359304 | tf_op jit(solution)/shard_map/ppermute | solution.py:197
  18.3 11.5 %collective-permute-start.6 = (bf16[4,3,16,2048]{3,2,1,0:T(8,128)(2,1)S(1)}, bf16[4,3,16,2048]{3,2,1,0:T(8,128)(2,1)S(1)}, u32[]{:S(2)}, u32[]{:S(2)}) collective-permute-start(bf16[4,3,16,2048]{3,2,1,0:T(8,128)(2,1)S(1)} %get-tuple-element.29.refs_0_), channel_id=1, source_target_pairs={{4,0},{5,1},{6,2},{7,3},{8,4},{9,5},{10,6},{11,7},{12,8},{13,9},{1... | collective-permute-start | bytes 2359304 | tf_op jit(solution)/shard_map/ppermute | solution.py:197
  20.0 18.0 %collective-permute-start.5 = (bf16[4,3,16,2048]{3,2,1,0:T(8,128)(2,1)S(1)}, bf16[4,3,16,2048]{3,2,1,0:T(8,128)(2,1)}, u32[]{:S(2)}, u32[]{:S(2)}) collective-permute-start(bf16[4,3,16,2048]{3,2,1,0:T(8,128)(2,1)S(1)} %get-tuple-element.27.refs_4_.refs_0_), channel_id=1, source_target_pairs={{4,0},{5,1},{6,2},{7,3},{8,4},{9,5},{10,6},{11,7},{12,8},{13,9},{1... | collective-permute-start | bytes 2359304 | tf_op jit(solution)/shard_map/ppermute | solution.py:197
  21.2 17.0 %collective-permute-start.8 = (bf16[4,3,16,2048]{3,2,1,0:T(8,128)(2,1)S(1)}, bf16[4,3,16,2048]{3,2,1,0:T(8,128)(2,1)}, u32[]{:S(2)}, u32[]{:S(2)}) collective-permute-start(bf16[4,3,16,2048]{3,2,1,0:T(8,128)(2,1)S(1)} %get-tuple-element.29.refs_0_), channel_id=1, source_target_pairs={{12,0},{13,1},{14,2},{15,3},{0,4},{1,5},{2,6},{3,7},{4,8},{5,9},{6... | collective-permute-start | bytes 2359304 | tf_op jit(solution)/shard_map/ppermute | solution.py:197
  29.7 18.3 %collective-permute-start.4 = (bf16[4,3,16,2048]{3,2,1,0:T(8,128)(2,1)}, bf16[4,3,16,2048]{3,2,1,0:T(8,128)(2,1)}, u32[]{:S(2)}, u32[]{:S(2)}) collective-permute-start(bf16[4,3,16,2048]{3,2,1,0:T(8,128)(2,1)} %collective-permute-done.3.refs_5_.refs_1_), channel_id=1, source_target_pairs={{12,0},{13,1},{14,2},{15,3},{0,4},{1,5},{2,6},{3,7},{4,8},{5,9},{6... | collective-permute-start | bytes 2359304 | tf_op jit(solution)/shard_map/ppermute | solution.py:197
  29.7 18.3 %collective-permute-start.7 = (bf16[4,3,16,2048]{3,2,1,0:T(8,128)(2,1)S(1)}, bf16[4,3,16,2048]{3,2,1,0:T(8,128)(2,1)}, u32[]{:S(2)}, u32[]{:S(2)}) collective-permute-start(bf16[4,3,16,2048]{3,2,1,0:T(8,128)(2,1)S(1)} %collective-permute-done.6.refs_1_), channel_id=1, source_target_pairs={{4,0},{5,1},{6,2},{7,3},{8,4},{9,5},{10,6},{11,7},{12,8},{13,9},{1... | collective-permute-start | bytes 2359304 | tf_op jit(solution)/shard_map/ppermute | solution.py:197
  32.4 20.4 %all-to-all-start = ((bf16[16,16,432]{2,1,0:T(8,128)(2,1)}), bf16[16,16,432]{2,1,0:T(8,128)(2,1)S(1)}, u32[]{:S(2)}, u32[]{:S(2)}) async-start(bf16[16,16,432]{2,1,0:T(8,128)(2,1)} %split_weights.1), calls=%async_computation | async-start | bytes 524288 | tf_op jit(solution)/shard_map/all_to_all | solution.py:462
  36.0 12.0 %copy-start.2 = (s32[4]{0:T(128)S(1)}, s32[4]{0:T(128)}, u32[]{:S(2)}) copy-start(s32[4]{0:T(128)} %pad_add_fusion.scalars) | copy-start | bytes 52
  52.0 0.7 copy-start.3
  52.9 3.4 %copy-start.6 = (bf16[256,432]{0,1:T(8,128)(2,1)}, bf16[256,432]{0,1:T(8,128)(2,1)S(1)}, u32[]{:S(2)}) copy-start(bf16[256,432]{0,1:T(8,128)(2,1)S(1)} %copy.10) | copy-start | bytes 663556
  53.0 4.5 %collective-permute-start.9 = (bf16[256,432]{0,1:T(8,128)(2,1)S(1)}, bf16[256,432]{0,1:T(8,128)(2,1)S(1)}, u32[]{:S(2)}, u32[]{:S(2)}) collective-permute-start(bf16[256,432]{0,1:T(8,128)(2,1)S(1)} %copy.10), channel_id=1, source_target_pairs={{0,16},{16,0},{32,48},{48,32},{64,80},{80,64},{96,112},{112,96},{1... | collective-permute-start | bytes 663560 | tf_op jit(solution)/shard_map/ppermute | solution.py:433
  56.4 2.1 %copy-start.4 = (f32[3,16,2048]{2,1,0:T(8,128)S(1)}, f32[3,16,2048]{2,1,0:T(8,128)}, u32[]{:S(2)}) copy-start(f32[3,16,2048]{2,1,0:T(8,128)} %copy-done.3) | copy-start | bytes 1179652
  61.3 9.2 %collective-permute-start.12 = (bf16[2,3,16,2048]{3,2,1,0:T(8,128)(2,1)S(1)}, bf16[2,3,16,2048]{3,2,1,0:T(8,128)(2,1)S(1)}, u32[]{:S(2)}, u32[]{:S(2)}) collective-permute-start(bf16[2,3,16,2048]{3,2,1,0:T(8,128)(2,1)S(1)} %layer_one_delta.1.refs_4_), channel_id=1, source_target_pairs={{3,0},{0,1},{1,2},{2,3},{7,4},{4,5},{5,6},{6,7},{11,8},{8,9},{9,10... | collective-permute-start | bytes 1179656 | tf_op jit(solution)/shard_map/ppermute | solution.py:197
  62.4 13.6 %collective-permute-start.11 = (bf16[2,3,16,2048]{3,2,1,0:T(8,128)(2,1)S(1)}, bf16[2,3,16,2048]{3,2,1,0:T(8,128)(2,1)S(1)}, u32[]{:S(2)}, u32[]{:S(2)}) collective-permute-start(bf16[2,3,16,2048]{3,2,1,0:T(8,128)(2,1)S(1)} %layer_one_delta.1.refs_4_), channel_id=1, source_target_pairs={{2,0},{3,1},{0,2},{1,3},{6,4},{7,5},{4,6},{5,7},{10,8},{11,9},{8,1... | collective-permute-start | bytes 1179656 | tf_op jit(solution)/shard_map/ppermute | solution.py:197
  66.2 9.7 %collective-permute-start.10 = (bf16[2,3,16,2048]{3,2,1,0:T(8,128)(2,1)S(1)}, bf16[2,3,16,2048]{3,2,1,0:T(8,128)(2,1)S(1)}, u32[]{:S(2)}, u32[]{:S(2)}) collective-permute-start(bf16[2,3,16,2048]{3,2,1,0:T(8,128)(2,1)S(1)} %layer_one_delta.1.refs_4_), channel_id=1, source_target_pairs={{1,0},{2,1},{3,2},{0,3},{5,4},{6,5},{7,6},{4,7},{9,8},{10,9},{11,1... | collective-permute-start | bytes 1179656 | tf_op jit(solution)/shard_map/ppermute | solution.py:197
  69.1 7.1 %collective-permute-start.13 = (f32[8,2,16,432]{3,2,1,0:T(8,128)S(1)}, f32[8,2,16,432]{3,2,1,0:T(8,128)S(1)}, u32[]{:S(2)}, u32[]{:S(2)}) collective-permute-start(f32[8,2,16,432]{3,2,1,0:T(8,128)S(1)} %get-tuple-element.35), channel_id=1, source_target_pairs={{0,16},{16,0},{32,48},{48,32},{64,80},{80,64},{96,112},{112,96},{1... | collective-permute-start | bytes 1327112 | tf_op jit(solution)/shard_map/ppermute | solution.py:433
  77.0 20.9 %collective-permute-start.15 = (bf16[4,3,16,2048]{3,2,1,0:T(8,128)(2,1)S(1)}, bf16[4,3,16,2048]{3,2,1,0:T(8,128)(2,1)S(1)}, u32[]{:S(2)}, u32[]{:S(2)}) collective-permute-start(bf16[4,3,16,2048]{3,2,1,0:T(8,128)(2,1)S(1)} %pad_maximum_fusion.2.refs_0_), channel_id=1, source_target_pairs={{12,0},{13,1},{14,2},{15,3},{0,4},{1,5},{2,6},{3,7},{4,8},{5,9},{6... | collective-permute-start | bytes 2359304 | tf_op jit(solution)/shard_map/ppermute | solution.py:197
  77.1 20.8 %collective-permute-start.14 = (bf16[4,3,16,2048]{3,2,1,0:T(8,128)(2,1)S(1)}, bf16[4,3,16,2048]{3,2,1,0:T(8,128)(2,1)}, u32[]{:S(2)}, u32[]{:S(2)}) collective-permute-start(bf16[4,3,16,2048]{3,2,1,0:T(8,128)(2,1)S(1)} %pad_maximum_fusion.2.refs_0_), channel_id=1, source_target_pairs={{4,0},{5,1},{6,2},{7,3},{8,4},{9,5},{10,6},{11,7},{12,8},{13,9},{1... | collective-permute-start | bytes 2359304 | tf_op jit(solution)/shard_map/ppermute | solution.py:197
  79.7 20.9 %collective-permute-start.17 = (bf16[4,3,16,2048]{3,2,1,0:T(8,128)(2,1)S(1)}, bf16[4,3,16,2048]{3,2,1,0:T(8,128)(2,1)}, u32[]{:S(2)}, u32[]{:S(2)}) collective-permute-start(bf16[4,3,16,2048]{3,2,1,0:T(8,128)(2,1)S(1)} %pad_maximum_fusion.3.refs_4_), channel_id=1, source_target_pairs={{12,0},{13,1},{14,2},{15,3},{0,4},{1,5},{2,6},{3,7},{4,8},{5,9},{6... | collective-permute-start | bytes 2359304 | tf_op jit(solution)/shard_map/ppermute | solution.py:197
  79.7 18.2 %all-to-all-start.1 = ((bf16[8,2,16,432]{3,2,1,0:T(8,128)(2,1)}), bf16[8,2,16,432]{3,2,1,0:T(8,128)(2,1)S(1)}, u32[]{:S(2)}, u32[]{:S(2)}) async-start(bf16[8,2,16,432]{3,2,1,0:T(8,128)(2,1)} %add_convert_fusion), calls=%async_computation.1 | async-start | bytes 524288 | tf_op jit(solution)/shard_map/all_to_all | solution.py:438
  88.5 33.9 %collective-permute-start.19 = (bf16[4,3,16,2048]{3,2,1,0:T(8,128)(2,1)S(1)}, bf16[4,3,16,2048]{3,2,1,0:T(8,128)(2,1)}, u32[]{:S(2)}, u32[]{:S(2)}) collective-permute-start(bf16[4,3,16,2048]{3,2,1,0:T(8,128)(2,1)S(1)} %pad_maximum_fusion.3.refs_4_), channel_id=1, source_target_pairs={{4,0},{5,1},{6,2},{7,3},{8,4},{9,5},{10,6},{11,7},{12,8},{13,9},{1... | collective-permute-start | bytes 2359304 | tf_op jit(solution)/shard_map/ppermute | solution.py:197
  97.9 24.5 %collective-permute-start.16 = (bf16[4,3,16,2048]{3,2,1,0:T(8,128)(2,1)}, bf16[4,3,16,2048]{3,2,1,0:T(8,128)(2,1)}, u32[]{:S(2)}, u32[]{:S(2)}) collective-permute-start(bf16[4,3,16,2048]{3,2,1,0:T(8,128)(2,1)} %collective-permute-done.14.refs_1_), channel_id=1, source_target_pairs={{4,0},{5,1},{6,2},{7,3},{8,4},{9,5},{10,6},{11,7},{12,8},{13,9},{1... | collective-permute-start | bytes 2359304 | tf_op jit(solution)/shard_map/ppermute | solution.py:197
  100.6 21.8 %collective-permute-start.18 = (bf16[4,3,16,2048]{3,2,1,0:T(8,128)(2,1)}, bf16[4,3,16,2048]{3,2,1,0:T(8,128)(2,1)}, u32[]{:S(2)}, u32[]{:S(2)}) collective-permute-start(bf16[4,3,16,2048]{3,2,1,0:T(8,128)(2,1)} %collective-permute-done.17.refs_5_), channel_id=1, source_target_pairs={{12,0},{13,1},{14,2},{15,3},{0,4},{1,5},{2,6},{3,7},{4,8},{5,9},{6... | collective-permute-start | bytes 2359304 | tf_op jit(solution)/shard_map/ppermute | solution.py:197
  101.3 8.9 %collective-permute-start.20 = (f32[16,432]{1,0:T(8,128)S(1)}, f32[16,432]{1,0:T(8,128)S(1)}, u32[]{:S(2)}, u32[]{:S(2)}) collective-permute-start(f32[16,432]{1,0:T(8,128)S(1)} %get-tuple-element.66), channel_id=1, source_target_pairs={{0,0},{1,16},{2,32},{3,48},{4,64},{5,80},{6,96},{7,112},{8,128},{9... | collective-permute-start | bytes 82952 | tf_op jit(solution)/shard_map/ppermute | solution.py:444
  110.2 0.6 copy-start.10
  112.6 9.8 %copy-start.1 = (bf16[27,16,256]{2,1,0:T(8,128)(2,1)S(1)}, bf16[27,16,256]{2,1,0:T(8,128)(2,1)}, u32[]{:S(2)}) copy-start(bf16[27,16,256]{2,1,0:T(8,128)(2,1)} %w2.1) | copy-start | bytes 663556
  112.6 23.8 %all-to-all-start.2 = ((f32[8,2,16,432]{3,2,1,0:T(8,128)}), f32[8,2,16,432]{3,2,1,0:T(8,128)S(1)}, u32[]{:S(2)}, u32[]{:S(2)}) async-start(f32[8,2,16,432]{3,2,1,0:T(8,128)} %collect_rows.1), calls=%async_computation.2 | async-start | bytes 1048576 | tf_op jit(solution)/shard_map/all_to_all | solution.py:438
  136.5 5.9 %copy-start.5 = (f32[8,2,16,432]{3,2,1,0:T(8,128)}, f32[8,2,16,432]{3,2,1,0:T(8,128)S(1)}, u32[]{:S(2)}) copy-start(f32[8,2,16,432]{3,2,1,0:T(8,128)S(1)} %all-to-all-done.2.own) | copy-start | bytes 1327108
  136.5 5.9 %collective-permute-start.21 = (f32[8,2,16,432]{3,2,1,0:T(8,128)S(1)}, f32[8,2,16,432]{3,2,1,0:T(8,128)S(1)}, u32[]{:S(2)}, u32[]{:S(2)}) collective-permute-start(f32[8,2,16,432]{3,2,1,0:T(8,128)S(1)} %all-to-all-done.2.own), channel_id=1, source_target_pairs={{0,16},{16,0},{32,48},{48,32},{64,80},{80,64},{96,112},{112,96},{1... | collective-permute-start | bytes 1327112 | tf_op jit(solution)/shard_map/ppermute | solution.py:433
  142.4 0.8 copy-start.9

commit v8 on v6

--- a/solution.py
+++ b/solution.py
@@ -391,11 +391,10 @@
     return lax.all_to_all(v, "dp", 0, 0, axis_index_groups=by_core, tiled=True)
 
 
-def sum_over_dp(parts):
+def reduce_rows(parts):
     mine = parts.astype(jnp.float32).sum(axis=0)
     flip = [(d * BLK + f, f * BLK + d) for d in range(BLK) for f in range(BLK)]
-    got = lax.ppermute(mine[1], ("dp", "filter"), flip)
-    return over_z(collect(mine[0], got))
+    return mine[0], lax.ppermute(mine[1], ("dp", "filter"), flip)
 
 
 def both_gradients(scalars, own):
@@ -424,12 +423,13 @@
     nears = gather_near(pair)
     keep, send = call_grads(scalars, pieces, pair)
     pair_sum = (keep + swap_cores(send)).astype(jnp.bfloat16)
-    nears, pair_sum = lax.optimization_barrier((nears, pair_sum))
-    fars = gather_far(nears)
     parts = over_z(pair_sum)
-    fars[0], parts = lax.optimization_barrier((fars[0], parts))
-    second_pieces = gather_last(fars)
-    own = sum_over_dp(parts)
+    last, parts = lax.optimization_barrier((nears[1], parts))
+    fars = gather_far([nears[0], last])
+    mine, got = reduce_rows(parts)
+    last, got = lax.optimization_barrier((fars[1], got))
+    second_pieces = gather_last([fars[0], last])
+    own = over_z(collect(mine, got))
     out, in_grad = call_two(scalars, second_pieces, w2, w1t)
     out, in_grad, own = lax.optimization_barrier((out, in_grad, own))
     first_grad, second_grad = both_gradients(scalars, own)

time: 147 us -> 141 us (0.959)
  starting transfers between devices: 60.2 us -> 52 us
  Pallas kernels: 20 us -> 23.9 us
  waiting for transfers between devices: 37.9 us -> 35.9 us
    ppermute x18, waiting for transfers between devices: 16.5 us -> 25.2 us  [turn(): return lax.ppermute(v, ('dp', 'filter'), from_axis(axes, step))]
    all_to_all x2, waiting for transfers between devices: 16.6 us -> 8.11 us  [over_z(): return lax.all_to_all(v, 'dp', 0, 0, axis_index_groups=by_core, tiled=True)]
    all_to_all x2, starting transfers between devices: 19.3 us -> 12.8 us  [over_z(): return lax.all_to_all(v, 'dp', 0, 0, axis_index_groups=by_core, tiled=True)]
    ppermute x18, starting transfers between devices: 25.3 us -> 22.6 us  [turn(): return lax.ppermute(v, ('dp', 'filter'), from_axis(axes, step))]
    ppermute x1, waiting for transfers between devices: 2.23 us -> 0.01 us  [reduce_rows(): return (mine[0], lax.ppermute(mine[1], ('dp', 'filter'), flip))]
    unnamed x18 -> x22, local copies, waits for them, and re-layouts: 3.06 us -> 2.43 us
  transfers between devices with their start and end apart: 24 -> 24, of which waited for: 9 -> 10; matrix products, arithmetic and copies ran while one was open for 1% -> 2% of each run, Pallas kernels for 9% -> 11%
where the time goes in v8:
time: 141 us; the launch traced here: 139 us
  starting transfers between devices  52 us (37%)
  waiting for transfers between devices  35.9 us (25%)
  Pallas kernels  23.9 us (17%)
  blocking collectives  18.8 us (13%)
  local copies, waits for them, and re-layouts  4.04 us (3%)
  other arithmetic  2.94 us (2%)
  between operations  1.55 us (1%)
    ppermute x18, waiting for transfers between devices, turn(): return lax.ppermute(v, ('dp', 'filter'), from_axis(axes, step))  25.2 us
    ppermute x18, starting transfers between devices, turn(): return lax.ppermute(v, ('dp', 'filter'), from_axis(axes, step))  22.6 us
    all_to_all x1, blocking collectives, shards(): turned = lax.all_to_all(split, 'filter', 0, 0, tiled=True).reshape(C, ROWS)  18.8 us
    all_to_all x2, starting transfers between devices, over_z(): return lax.all_to_all(v, 'dp', 0, 0, axis_index_groups=by_core, tiled=True)  12.8 us
    ppermute x3, starting transfers between devices, swap_cores(): return lax.ppermute(v, 'dp', [(d, d ^ 1) for d in range(BLK)])  9.24 us
    all_to_all x2, waiting for transfers between devices, over_z(): return lax.all_to_all(v, 'dp', 0, 0, axis_index_groups=by_core, tiled=True)  8.11 us
    ppermute x1, starting transfers between devices, reduce_rows(): return (mine[0], lax.ppermute(mine[1], ('dp', 'filter'), flip))  7.39 us
    pallas_call x1, Pallas kernels, call_two(): pl.pallas_call(kernel_two, name='layer_two', grid_spec=pltpu.PrefetchScal...  5.74 us
  transfers between devices with their start and end apart: 24, of which 10 were waited for; matrix products, arithmetic and copies ran while one was open for 2% of the time, Pallas kernels for 11%

profile of v8, /device:TPU:1, one launch (start us, length us, event | category | flops | bytes accessed | tf_op | source)
XLA Modules:
  0.0 139.2 jit_solution(9511809044697172378)
XLA Ops:
  0.6 1.1 pad_maximum_fusion.4
  1.7 2.1 %collective-permute-start.2 = (bf16[2,3,16,2048]{3,2,1,0:T(8,128)(2,1)S(1)}, bf16[2,3,16,2048]{3,2,1,0:T(8,128)(2,1)S(1)}, u32[]{:S(2)}, u32[]{:S(2)}) collective-permute-start(bf16[2,3,16,2048]{3,2,1,0:T(8,128)(2,1)S(1)} %pad_maximum_fusion.4), channel_id=1, source_target_pairs={{3,0},{0,1},{1,2},{2,3},{7,4},{4,5},{5,6},{6,7},{11,8},{8,9},{9,10... | collective-permute-start | bytes 1179656 | tf_op jit(solution)/shard_map/ppermute | solution.py:176
  3.8 2.5 %collective-permute-start.1 = (bf16[2,3,16,2048]{3,2,1,0:T(8,128)(2,1)S(1)}, bf16[2,3,16,2048]{3,2,1,0:T(8,128)(2,1)S(1)}, u32[]{:S(2)}, u32[]{:S(2)}) collective-permute-start(bf16[2,3,16,2048]{3,2,1,0:T(8,128)(2,1)S(1)} %pad_maximum_fusion.4), channel_id=1, source_target_pairs={{2,0},{3,1},{0,2},{1,3},{6,4},{7,5},{4,6},{5,7},{10,8},{11,9},{8,1... | collective-permute-start | bytes 1179656 | tf_op jit(solution)/shard_map/ppermute | solution.py:176
  6.3 1.2 collective-permute-start
  8.1 0.6 pad_add_fusion.scalars
  8.7 2.9 %split_weights.1 = bf16[16,16,432]{2,1,0:T(8,128)(2,1)} custom-call(s32[4]{0:T(128)} %pad_add_fusion.scalars, bf16[27,16,256]{2,1,0:T(8,128)(2,1)} %w1.1, bf16[27,16,256]{2,1,0:T(8,128)(2,1)} %w2.1), custom_call_target="tpu_custom_call" | custom-call | bytes 884736 | tf_op jit(solution)/shard_map/split_weights/pallas_call | solution.py:316
  11.6 4.3 %collective-permute-done.1 = bf16[2,3,16,2048]{3,2,1,0:T(8,128)(2,1)S(1)} collective-permute-done((bf16[2,3,16,2048]{3,2,1,0:T(8,128)(2,1)S(1)}, bf16[2,3,16,2048]{3,2,1,0:T(8,128)(2,1)S(1)}, u32[]{:S(2)}, u32[]{:S(2)}) %collective-permute-start.1) | collective-permute-done | bytes 393248 | tf_op jit(solution)/shard_map/ppermute | solution.py:176
  16.0 0.9 copy-done.5
  16.9 0.1 copy-done.6
  17.0 0.2 pad_maximum_fusion
  17.2 2.5 %collective-permute-start.3 = (bf16[4,3,16,2048]{3,2,1,0:T(8,128)(2,1)S(1)}, bf16[4,3,16,2048]{3,2,1,0:T(8,128)(2,1)S(1)}, u32[]{:S(2)}, u32[]{:S(2)}) collective-permute-start(bf16[4,3,16,2048]{3,2,1,0:T(8,128)(2,1)S(1)} %get-tuple-element.22.refs_0_), channel_id=1, source_target_pairs={{4,0},{5,1},{6,2},{7,3},{8,4},{9,5},{10,6},{11,7},{12,8},{13,9},{1... | collective-permute-start | bytes 2359304 | tf_op jit(solution)/shard_map/ppermute | solution.py:176
  19.7 2.7 %collective-permute-start.8 = (bf16[4,3,16,2048]{3,2,1,0:T(8,128)(2,1)S(1)}, bf16[4,3,16,2048]{3,2,1,0:T(8,128)(2,1)}, u32[]{:S(2)}, u32[]{:S(2)}) collective-permute-start(bf16[4,3,16,2048]{3,2,1,0:T(8,128)(2,1)S(1)} %get-tuple-element.23.refs_4_), channel_id=1, source_target_pairs={{4,0},{5,1},{6,2},{7,3},{8,4},{9,5},{10,6},{11,7},{12,8},{13,9},{1... | collective-permute-start | bytes 2359304 | tf_op jit(solution)/shard_map/ppermute | solution.py:176
  22.4 6.2 %collective-permute-done.3.refs_1_ = bf16[4,3,16,2048]{3,2,1,0:T(8,128)(2,1)S(1)} collective-permute-done((bf16[4,3,16,2048]{3,2,1,0:T(8,128)(2,1)S(1)}, bf16[4,3,16,2048]{3,2,1,0:T(8,128)(2,1)S(1)}, u32[]{:S(2)}, u32[]{:S(2)}) %collective-permute-start.3) | collective-permute-done | bytes 786464 | tf_op jit(solution)/shard_map/ppermute | solution.py:176
  28.6 3.5 %collective-permute-start.4 = (bf16[4,3,16,2048]{3,2,1,0:T(8,128)(2,1)S(1)}, bf16[4,3,16,2048]{3,2,1,0:T(8,128)(2,1)}, u32[]{:S(2)}, u32[]{:S(2)}) collective-permute-start(bf16[4,3,16,2048]{3,2,1,0:T(8,128)(2,1)S(1)} %collective-permute-done.3.refs_1_), channel_id=1, source_target_pairs={{4,0},{5,1},{6,2},{7,3},{8,4},{9,5},{10,6},{11,7},{12,8},{13,9},{1... | collective-permute-start | bytes 2359304 | tf_op jit(solution)/shard_map/ppermute | solution.py:176
  32.2 18.8 %all_to_all.15 = bf16[16,16,432]{2,1,0:T(8,128)(2,1)S(1)} all-to-all(bf16[16,16,432]{2,1,0:T(8,128)(2,1)S(1)} %copy-done.4), channel_id=1, replica_groups=mesh['dp'=16,'filter'=16] {'filter'}, dimensions={0} | all-to-all | bytes 442368 | tf_op jit(solution)/shard_map/all_to_all | solution.py:414
  50.9 0.1 copy.10
  51.1 5.1 %collective-permute-start.9 = (bf16[256,432]{0,1:T(8,128)(2,1)S(1)}, bf16[256,432]{0,1:T(8,128)(2,1)S(1)}, u32[]{:S(2)}, u32[]{:S(2)}) collective-permute-start(bf16[256,432]{0,1:T(8,128)(2,1)S(1)} %copy.10), channel_id=1, source_target_pairs={{0,16},{16,0},{32,48},{48,32},{64,80},{80,64},{96,112},{112,96},{1... | collective-permute-start | bytes 663560 | tf_op jit(solution)/shard_map/ppermute | solution.py:386
  56.2 1.1 collective-permute-done.9
  57.4 0.6 copy-done.2
  58.0 5.2 %layer_one.1.refs_8_ = bf16[2,3,16,2048]{3,2,1,0:T(8,128)(2,1)S(1)} custom-call(s32[4]{0:T(128)S(1)} %copy-done.2, bf16[4,3,16,2048]{3,2,1,0:T(8,128)(2,1)S(1)} %get-tuple-element.22.refs_0_, bf16[4,3,16,2048]{3,2,1,0:T(8,128)(2,1)S(1)} %collective-permute-done.3.refs_1_, bf16[4,3,16,2048]{3,2,1,0:T(8,128)(2,1)} %collective-permute-done.4.refs_2_, ...), custom_call_target="tpu_custom_call" | custom-call | flops 2717908992 | bytes 6291456 | tf_op jit(solution)/shard_map/layer_one/pallas_call | solution.py:222
  63.3 0.6 collective-permute-start.11
  63.9 2.1 %collective-permute-start.10 = (bf16[2,3,16,2048]{3,2,1,0:T(8,128)(2,1)S(1)}, bf16[2,3,16,2048]{3,2,1,0:T(8,128)(2,1)S(1)}, u32[]{:S(2)}, u32[]{:S(2)}) collective-permute-start(bf16[2,3,16,2048]{3,2,1,0:T(8,128)(2,1)S(1)} %layer_one.1.refs_8_), channel_id=1, source_target_pairs={{1,0},{2,1},{3,2},{0,3},{5,4},{6,5},{7,6},{4,7},{9,8},{10,9},{11,1... | collective-permute-start | bytes 1179656 | tf_op jit(solution)/shard_map/ppermute | solution.py:176
  65.9 5.3 %weight_grads.1 = (f32[8,2,16,432]{3,2,1,0:T(8,128)S(1)}, f32[8,2,16,432]{3,2,1,0:T(8,128)S(1)}) custom-call(s32[4]{0:T(128)S(1)} %copy-done.2, bf16[4,3,16,2048]{3,2,1,0:T(8,128)(2,1)S(1)} %get-tuple-element.22.refs_0_, bf16[4,3,16,2048]{3,2,1,0:T(8,128)(2,1)S(1)} %collective-permute-done.3.refs_1_, ...), custom_call_target="tpu_custom_call" | custom-call | flops 2717908992 | bytes 6291456 | tf_op jit(solution)/shard_map/weight_grads/pallas_call | solution.py:242
  71.2 0.1 collective-permute-start.16
  71.4 3.9 %collective-permute-done.12 = bf16[2,3,16,2048]{3,2,1,0:T(8,128)(2,1)S(1)} collective-permute-done((bf16[2,3,16,2048]{3,2,1,0:T(8,128)(2,1)S(1)}, bf16[2,3,16,2048]{3,2,1,0:T(8,128)(2,1)S(1)}, u32[]{:S(2)}, u32[]{:S(2)}) %collective-permute-start.12) | collective-permute-done | bytes 393248 | tf_op jit(solution)/shard_map/ppermute | solution.py:176
  75.4 0.5 collective-permute-done.10
  75.9 0.7 fusion.1
  76.6 0.8 add_convert_fusion
  77.4 6.6 %all-to-all-start.1 = ((bf16[8,2,16,432]{3,2,1,0:T(8,128)(2,1)}), bf16[8,2,16,432]{3,2,1,0:T(8,128)(2,1)S(1)}, u32[]{:S(2)}, u32[]{:S(2)}) async-start(bf16[8,2,16,432]{3,2,1,0:T(8,128)(2,1)} %add_convert_fusion), calls=%async_computation.1 | async-start | bytes 524288 | tf_op jit(solution)/shard_map/all_to_all | solution.py:391
  84.0 0.1 pad_maximum_fusion.2.refs_0_
  84.1 1.2 collective-permute-start.13
  85.3 0.1 pad_maximum_fusion.3.refs_4_
  85.4 8.1 %all-to-all-done.1 = bf16[8,2,16,432]{3,2,1,0:T(8,128)(2,1)S(1)} async-done(((bf16[8,2,16,432]{3,2,1,0:T(8,128)(2,1)}), bf16[8,2,16,432]{3,2,1,0:T(8,128)(2,1)S(1)}, u32[]{:S(2)}, u32[]{:S(2)}) %all-to-all-start.1) | async-done | bytes 221216 | tf_op jit(solution)/shard_map/all_to_all | solution.py:391
  93.5 0.9 collective-permute-start.18
  94.5 0.5 collective-permute-start.17
  95.0 0.6 slice_bitcast_fusion
  95.6 7.4 %collective-permute-start.19 = (f32[16,432]{1,0:T(8,128)S(1)}, f32[16,432]{1,0:T(8,128)S(1)}, u32[]{:S(2)}, u32[]{:S(2)}) collective-permute-start(f32[16,432]{1,0:T(8,128)S(1)} %get-tuple-element.57), channel_id=1, source_target_pairs={{0,0},{1,16},{2,32},{3,48},{4,64},{5,80},{6,96},{7,112},{8,128},{9... | collective-permute-start | bytes 82952 | tf_op jit(solution)/shard_map/ppermute | solution.py:397
  103.1 2.7 %collective-permute-start.14 = (bf16[4,3,16,2048]{3,2,1,0:T(8,128)(2,1)S(1)}, bf16[4,3,16,2048]{3,2,1,0:T(8,128)(2,1)}, u32[]{:S(2)}, u32[]{:S(2)}) collective-permute-start(bf16[4,3,16,2048]{3,2,1,0:T(8,128)(2,1)S(1)} %collective-permute-done.13.refs_1_), channel_id=1, source_target_pairs={{4,0},{5,1},{6,2},{7,3},{8,4},{9,5},{10,6},{11,7},{12,8},{13,9},{1... | collective-permute-start | bytes 2359304 | tf_op jit(solution)/shard_map/ppermute | solution.py:176
  105.8 1.1 collective-permute-done.17.refs_5_
  106.9 1.8 %collect_rows.1 = f32[8,2,16,432]{3,2,1,0:T(8,128)} custom-call(f32[16,432]{1,0:T(8,128)} %get-tuple-element.56.mine, f32[16,432]{1,0:T(8,128)} %copy-done.9), custom_call_target="tpu_custom_call" | custom-call | bytes 442368 | tf_op jit(solution)/shard_map/collect_rows/pallas_call | solution.py:349
  108.7 6.2 %all-to-all-start.2 = ((f32[8,2,16,432]{3,2,1,0:T(8,128)}), f32[8,2,16,432]{3,2,1,0:T(8,128)S(1)}, u32[]{:S(2)}, u32[]{:S(2)}) async-start(f32[8,2,16,432]{3,2,1,0:T(8,128)} %collect_rows.1), calls=%async_computation.2 | async-start | bytes 1048576 | tf_op jit(solution)/shard_map/all_to_all | solution.py:391
  114.9 0.6 collective-permute-done.15.refs_3_
  115.6 8.4 %collective-permute-done.20.refs_6_ = bf16[4,3,16,2048]{3,2,1,0:T(8,128)(2,1)} collective-permute-done((bf16[4,3,16,2048]{3,2,1,0:T(8,128)(2,1)}, bf16[4,3,16,2048]{3,2,1,0:T(8,128)(2,1)}, u32[]{:S(2)}, u32[]{:S(2)}) %collective-permute-start.20) | collective-permute-done | bytes 786464 | tf_op jit(solution)/shard_map/ppermute | solution.py:176
  124.0 5.7 %layer_two.1 = (f32[3,16,2048]{2,1,0:T(8,128)}, f32[3,16,2048]{2,1,0:T(8,128)}) custom-call(s32[4]{0:T(128)S(1)} %copy-done.2, bf16[4,3,16,2048]{3,2,1,0:T(8,128)(2,1)S(1)} %pad_maximum_fusion.2.refs_0_, bf16[4,3,16,2048]{3,2,1,0:T(8,128)(2,1)S(1)} %collective-permute-done.13.refs_1_, bf16[4,3,16,2048]{3,2,1,0:T(8,128)(2,1)} %collective-permute-done.14.refs_2_, ...), custom_call_target="tpu_custom_call" | custom-call | flops 2717908992 | bytes 6291456 | tf_op jit(solution)/shard_map/layer_two/pallas_call | solution.py:267
  129.7 4.0 %collective-permute-start.21 = (f32[8,2,16,432]{3,2,1,0:T(8,128)S(1)}, f32[8,2,16,432]{3,2,1,0:T(8,128)S(1)}, u32[]{:S(2)}, u32[]{:S(2)}) collective-permute-start(f32[8,2,16,432]{3,2,1,0:T(8,128)S(1)} %all-to-all-done.2.own), channel_id=1, source_target_pairs={{0,16},{16,0},{32,48},{48,32},{64,80},{80,64},{96,112},{112,96},{1... | collective-permute-start | bytes 1327112 | tf_op jit(solution)/shard_map/ppermute | solution.py:386
  133.8 1.5 %collective-permute-done.21.other = f32[8,2,16,432]{3,2,1,0:T(8,128)S(1)} collective-permute-done((f32[8,2,16,432]{3,2,1,0:T(8,128)S(1)}, f32[8,2,16,432]{3,2,1,0:T(8,128)S(1)}, u32[]{:S(2)}, u32[]{:S(2)}) %collective-permute-start.21) | collective-permute-done | bytes 442400 | tf_op jit(solution)/shard_map/ppermute | solution.py:386
  135.3 0.8 copy-done.8
  136.1 3.0 %finish_gradients.1 = (f32[432,256]{1,0:T(8,128)}, f32[432,256]{1,0:T(8,128)}) custom-call(s32[4]{0:T(128)} %pad_add_fusion.scalars, f32[8,2,16,432]{3,2,1,0:T(8,128)} %copy-done.3, f32[8,2,16,432]{3,2,1,0:T(8,128)} %copy-done.8), custom_call_target="tpu_custom_call" | custom-call | bytes 1769472 | tf_op jit(solution)/shard_map/finish_gradients/pallas_call | solution.py:370
  (46 shorter events, 0.5 us)
Async XLA Ops:
  1.7 9.9 %collective-permute-start.2 = (bf16[2,3,16,2048]{3,2,1,0:T(8,128)(2,1)S(1)}, bf16[2,3,16,2048]{3,2,1,0:T(8,128)(2,1)S(1)}, u32[]{:S(2)}, u32[]{:S(2)}) collective-permute-start(bf16[2,3,16,2048]{3,2,1,0:T(8,128)(2,1)S(1)} %pad_maximum_fusion.4), channel_id=1, source_target_pairs={{3,0},{0,1},{1,2},{2,3},{7,4},{4,5},{5,6},{6,7},{11,8},{8,9},{9,10... | collective-permute-start | bytes 1179656 | tf_op jit(solution)/shard_map/ppermute | solution.py:176
  3.8 12.1 %collective-permute-start.1 = (bf16[2,3,16,2048]{3,2,1,0:T(8,128)(2,1)S(1)}, bf16[2,3,16,2048]{3,2,1,0:T(8,128)(2,1)S(1)}, u32[]{:S(2)}, u32[]{:S(2)}) collective-permute-start(bf16[2,3,16,2048]{3,2,1,0:T(8,128)(2,1)S(1)} %pad_maximum_fusion.4), channel_id=1, source_target_pairs={{2,0},{3,1},{0,2},{1,3},{6,4},{7,5},{4,6},{5,7},{10,8},{11,9},{8,1... | collective-permute-start | bytes 1179656 | tf_op jit(solution)/shard_map/ppermute | solution.py:176
  6.3 9.7 %collective-permute-start = (bf16[2,3,16,2048]{3,2,1,0:T(8,128)(2,1)S(1)}, bf16[2,3,16,2048]{3,2,1,0:T(8,128)(2,1)S(1)}, u32[]{:S(2)}, u32[]{:S(2)}) collective-permute-start(bf16[2,3,16,2048]{3,2,1,0:T(8,128)(2,1)S(1)} %pad_maximum_fusion.4), channel_id=1, source_target_pairs={{1,0},{2,1},{3,2},{0,3},{5,4},{6,5},{7,6},{4,7},{9,8},{10,9},{11,1... | collective-permute-start | bytes 1179656 | tf_op jit(solution)/shard_map/ppermute | solution.py:176
  16.0 0.9 copy-start.5
  16.0 1.0 copy-start.6
  17.0 15.2 %copy-start.4 = (bf16[16,16,432]{2,1,0:T(8,128)(2,1)S(1)}, bf16[16,16,432]{2,1,0:T(8,128)(2,1)}, u32[]{:S(2)}) copy-start(bf16[16,16,432]{2,1,0:T(8,128)(2,1)} %split_weights.1) | copy-start | bytes 663556
  17.2 11.5 %collective-permute-start.3 = (bf16[4,3,16,2048]{3,2,1,0:T(8,128)(2,1)S(1)}, bf16[4,3,16,2048]{3,2,1,0:T(8,128)(2,1)S(1)}, u32[]{:S(2)}, u32[]{:S(2)}) collective-permute-start(bf16[4,3,16,2048]{3,2,1,0:T(8,128)(2,1)S(1)} %get-tuple-element.22.refs_0_), channel_id=1, source_target_pairs={{4,0},{5,1},{6,2},{7,3},{8,4},{9,5},{10,6},{11,7},{12,8},{13,9},{1... | collective-permute-start | bytes 2359304 | tf_op jit(solution)/shard_map/ppermute | solution.py:176
  19.7 12.5 %collective-permute-start.6 = (bf16[4,3,16,2048]{3,2,1,0:T(8,128)(2,1)S(1)}, bf16[4,3,16,2048]{3,2,1,0:T(8,128)(2,1)}, u32[]{:S(2)}, u32[]{:S(2)}) collective-permute-start(bf16[4,3,16,2048]{3,2,1,0:T(8,128)(2,1)S(1)} %get-tuple-element.23.refs_4_), channel_id=1, source_target_pairs={{12,0},{13,1},{14,2},{15,3},{0,4},{1,5},{2,6},{3,7},{4,8},{5,9},{6... | collective-permute-start | bytes 2359304 | tf_op jit(solution)/shard_map/ppermute | solution.py:176
  19.7 37.6 %collective-permute-start.5 = (bf16[4,3,16,2048]{3,2,1,0:T(8,128)(2,1)S(1)}, bf16[4,3,16,2048]{3,2,1,0:T(8,128)(2,1)}, u32[]{:S(2)}, u32[]{:S(2)}) collective-permute-start(bf16[4,3,16,2048]{3,2,1,0:T(8,128)(2,1)S(1)} %get-tuple-element.22.refs_0_), channel_id=1, source_target_pairs={{12,0},{13,1},{14,2},{15,3},{0,4},{1,5},{2,6},{3,7},{4,8},{5,9},{6... | collective-permute-start | bytes 2359304 | tf_op jit(solution)/shard_map/ppermute | solution.py:176
  19.7 37.6 %collective-permute-start.8 = (bf16[4,3,16,2048]{3,2,1,0:T(8,128)(2,1)S(1)}, bf16[4,3,16,2048]{3,2,1,0:T(8,128)(2,1)}, u32[]{:S(2)}, u32[]{:S(2)}) collective-permute-start(bf16[4,3,16,2048]{3,2,1,0:T(8,128)(2,1)S(1)} %get-tuple-element.23.refs_4_), channel_id=1, source_target_pairs={{4,0},{5,1},{6,2},{7,3},{8,4},{9,5},{10,6},{11,7},{12,8},{13,9},{1... | collective-permute-start | bytes 2359304 | tf_op jit(solution)/shard_map/ppermute | solution.py:176
  28.6 28.7 %collective-permute-start.4 = (bf16[4,3,16,2048]{3,2,1,0:T(8,128)(2,1)S(1)}, bf16[4,3,16,2048]{3,2,1,0:T(8,128)(2,1)}, u32[]{:S(2)}, u32[]{:S(2)}) collective-permute-start(bf16[4,3,16,2048]{3,2,1,0:T(8,128)(2,1)S(1)} %collective-permute-done.3.refs_1_), channel_id=1, source_target_pairs={{4,0},{5,1},{6,2},{7,3},{8,4},{9,5},{10,6},{11,7},{12,8},{13,9},{1... | collective-permute-start | bytes 2359304 | tf_op jit(solution)/shard_map/ppermute | solution.py:176
  32.2 25.2 %collective-permute-start.7 = (bf16[4,3,16,2048]{3,2,1,0:T(8,128)(2,1)}, bf16[4,3,16,2048]{3,2,1,0:T(8,128)(2,1)}, u32[]{:S(2)}, u32[]{:S(2)}) collective-permute-start(bf16[4,3,16,2048]{3,2,1,0:T(8,128)(2,1)} %collective-permute-done.6.refs_5_), channel_id=1, source_target_pairs={{12,0},{13,1},{14,2},{15,3},{0,4},{1,5},{2,6},{3,7},{4,8},{5,9},{6... | collective-permute-start | bytes 2359304 | tf_op jit(solution)/shard_map/ppermute | solution.py:176
  51.1 6.2 %collective-permute-start.9 = (bf16[256,432]{0,1:T(8,128)(2,1)S(1)}, bf16[256,432]{0,1:T(8,128)(2,1)S(1)}, u32[]{:S(2)}, u32[]{:S(2)}) collective-permute-start(bf16[256,432]{0,1:T(8,128)(2,1)S(1)} %copy.10), channel_id=1, source_target_pairs={{0,16},{16,0},{32,48},{48,32},{64,80},{80,64},{96,112},{112,96},{1... | collective-permute-start | bytes 663560 | tf_op jit(solution)/shard_map/ppermute | solution.py:386
  56.2 1.2 copy-start
  57.4 0.6 copy-start.2
  63.2 12.1 %collective-permute-start.12 = (bf16[2,3,16,2048]{3,2,1,0:T(8,128)(2,1)S(1)}, bf16[2,3,16,2048]{3,2,1,0:T(8,128)(2,1)S(1)}, u32[]{:S(2)}, u32[]{:S(2)}) collective-permute-start(bf16[2,3,16,2048]{3,2,1,0:T(8,128)(2,1)S(1)} %layer_one.1.refs_8_), channel_id=1, source_target_pairs={{3,0},{0,1},{1,2},{2,3},{7,4},{4,5},{5,6},{6,7},{11,8},{8,9},{9,10... | collective-permute-start | bytes 1179656 | tf_op jit(solution)/shard_map/ppermute | solution.py:176
  63.3 12.1 %collective-permute-start.11 = (bf16[2,3,16,2048]{3,2,1,0:T(8,128)(2,1)S(1)}, bf16[2,3,16,2048]{3,2,1,0:T(8,128)(2,1)S(1)}, u32[]{:S(2)}, u32[]{:S(2)}) collective-permute-start(bf16[2,3,16,2048]{3,2,1,0:T(8,128)(2,1)S(1)} %layer_one.1.refs_8_), channel_id=1, source_target_pairs={{2,0},{3,1},{0,2},{1,3},{6,4},{7,5},{4,6},{5,7},{10,8},{11,9},{8,1... | collective-permute-start | bytes 1179656 | tf_op jit(solution)/shard_map/ppermute | solution.py:176
  63.9 12.1 %collective-permute-start.10 = (bf16[2,3,16,2048]{3,2,1,0:T(8,128)(2,1)S(1)}, bf16[2,3,16,2048]{3,2,1,0:T(8,128)(2,1)S(1)}, u32[]{:S(2)}, u32[]{:S(2)}) collective-permute-start(bf16[2,3,16,2048]{3,2,1,0:T(8,128)(2,1)S(1)} %layer_one.1.refs_8_), channel_id=1, source_target_pairs={{1,0},{2,1},{3,2},{0,3},{5,4},{6,5},{7,6},{4,7},{9,8},{10,9},{11,1... | collective-permute-start | bytes 1179656 | tf_op jit(solution)/shard_map/ppermute | solution.py:176
  71.2 5.4 %collective-permute-start.16 = (f32[8,2,16,432]{3,2,1,0:T(8,128)S(1)}, f32[8,2,16,432]{3,2,1,0:T(8,128)S(1)}, u32[]{:S(2)}, u32[]{:S(2)}) collective-permute-start(f32[8,2,16,432]{3,2,1,0:T(8,128)S(1)} %get-tuple-element.26), channel_id=1, source_target_pairs={{0,16},{16,0},{32,48},{48,32},{64,80},{80,64},{96,112},{112,96},{1... | collective-permute-start | bytes 1327112 | tf_op jit(solution)/shard_map/ppermute | solution.py:386
  77.4 16.1 %all-to-all-start.1 = ((bf16[8,2,16,432]{3,2,1,0:T(8,128)(2,1)}), bf16[8,2,16,432]{3,2,1,0:T(8,128)(2,1)S(1)}, u32[]{:S(2)}, u32[]{:S(2)}) async-start(bf16[8,2,16,432]{3,2,1,0:T(8,128)(2,1)} %add_convert_fusion), calls=%async_computation.1 | async-start | bytes 524288 | tf_op jit(solution)/shard_map/all_to_all | solution.py:391
  84.0 1.3 copy-start.7
  84.1 19.0 %collective-permute-start.13 = (bf16[4,3,16,2048]{3,2,1,0:T(8,128)(2,1)S(1)}, bf16[4,3,16,2048]{3,2,1,0:T(8,128)(2,1)S(1)}, u32[]{:S(2)}, u32[]{:S(2)}) collective-permute-start(bf16[4,3,16,2048]{3,2,1,0:T(8,128)(2,1)S(1)} %pad_maximum_fusion.2.refs_0_), channel_id=1, source_target_pairs={{4,0},{5,1},{6,2},{7,3},{8,4},{9,5},{10,6},{11,7},{12,8},{13,9},{1... | collective-permute-start | bytes 2359304 | tf_op jit(solution)/shard_map/ppermute | solution.py:176
  93.5 12.3 %collective-permute-start.18 = (bf16[4,3,16,2048]{3,2,1,0:T(8,128)(2,1)S(1)}, bf16[4,3,16,2048]{3,2,1,0:T(8,128)(2,1)S(1)}, u32[]{:S(2)}, u32[]{:S(2)}) collective-permute-start(bf16[4,3,16,2048]{3,2,1,0:T(8,128)(2,1)S(1)} %pad_maximum_fusion.3.refs_4_), channel_id=1, source_target_pairs={{4,0},{5,1},{6,2},{7,3},{8,4},{9,5},{10,6},{11,7},{12,8},{13,9},{1... | collective-permute-start | bytes 2359304 | tf_op jit(solution)/shard_map/ppermute | solution.py:176
  94.5 12.5 %collective-permute-start.17 = (bf16[4,3,16,2048]{3,2,1,0:T(8,128)(2,1)S(1)}, bf16[4,3,16,2048]{3,2,1,0:T(8,128)(2,1)}, u32[]{:S(2)}, u32[]{:S(2)}) collective-permute-start(bf16[4,3,16,2048]{3,2,1,0:T(8,128)(2,1)S(1)} %pad_maximum_fusion.3.refs_4_), channel_id=1, source_target_pairs={{12,0},{13,1},{14,2},{15,3},{0,4},{1,5},{2,6},{3,7},{4,8},{5,9},{6... | collective-permute-start | bytes 2359304 | tf_op jit(solution)/shard_map/ppermute | solution.py:176
  95.6 10.2 %collective-permute-start.19 = (f32[16,432]{1,0:T(8,128)S(1)}, f32[16,432]{1,0:T(8,128)S(1)}, u32[]{:S(2)}, u32[]{:S(2)}) collective-permute-start(f32[16,432]{1,0:T(8,128)S(1)} %get-tuple-element.57), channel_id=1, source_target_pairs={{0,0},{1,16},{2,32},{3,48},{4,64},{5,80},{6,96},{7,112},{8,128},{9... | collective-permute-start | bytes 82952 | tf_op jit(solution)/shard_map/ppermute | solution.py:397
  103.0 12.5 %collective-permute-start.15 = (bf16[4,3,16,2048]{3,2,1,0:T(8,128)(2,1)S(1)}, bf16[4,3,16,2048]{3,2,1,0:T(8,128)(2,1)}, u32[]{:S(2)}, u32[]{:S(2)}) collective-permute-start(bf16[4,3,16,2048]{3,2,1,0:T(8,128)(2,1)S(1)} %pad_maximum_fusion.2.refs_0_), channel_id=1, source_target_pairs={{12,0},{13,1},{14,2},{15,3},{0,4},{1,5},{2,6},{3,7},{4,8},{5,9},{6... | collective-permute-start | bytes 2359304 | tf_op jit(solution)/shard_map/ppermute | solution.py:176
  103.1 12.4 %collective-permute-start.14 = (bf16[4,3,16,2048]{3,2,1,0:T(8,128)(2,1)S(1)}, bf16[4,3,16,2048]{3,2,1,0:T(8,128)(2,1)}, u32[]{:S(2)}, u32[]{:S(2)}) collective-permute-start(bf16[4,3,16,2048]{3,2,1,0:T(8,128)(2,1)S(1)} %collective-permute-done.13.refs_1_), channel_id=1, source_target_pairs={{4,0},{5,1},{6,2},{7,3},{8,4},{9,5},{10,6},{11,7},{12,8},{13,9},{1... | collective-permute-start | bytes 2359304 | tf_op jit(solution)/shard_map/ppermute | solution.py:176
  105.8 1.1 copy-start.9
  105.8 1.1 copy-start.10
  106.9 17.1 %collective-permute-start.20 = (bf16[4,3,16,2048]{3,2,1,0:T(8,128)(2,1)}, bf16[4,3,16,2048]{3,2,1,0:T(8,128)(2,1)}, u32[]{:S(2)}, u32[]{:S(2)}) collective-permute-start(bf16[4,3,16,2048]{3,2,1,0:T(8,128)(2,1)} %collective-permute-done.17.refs_5_), channel_id=1, source_target_pairs={{12,0},{13,1},{14,2},{15,3},{0,4},{1,5},{2,6},{3,7},{4,8},{5,9},{6... | collective-permute-start | bytes 2359304 | tf_op jit(solution)/shard_map/ppermute | solution.py:176
  108.7 15.3 %copy-start.1 = (bf16[27,16,256]{2,1,0:T(8,128)(2,1)S(1)}, bf16[27,16,256]{2,1,0:T(8,128)(2,1)}, u32[]{:S(2)}) copy-start(bf16[27,16,256]{2,1,0:T(8,128)(2,1)} %w2.1) | copy-start | bytes 663556
  108.7 21.0 %all-to-all-start.2 = ((f32[8,2,16,432]{3,2,1,0:T(8,128)}), f32[8,2,16,432]{3,2,1,0:T(8,128)S(1)}, u32[]{:S(2)}, u32[]{:S(2)}) async-start(f32[8,2,16,432]{3,2,1,0:T(8,128)} %collect_rows.1), calls=%async_computation.2 | async-start | bytes 1048576 | tf_op jit(solution)/shard_map/all_to_all | solution.py:391
  129.7 5.6 %copy-start.3 = (f32[8,2,16,432]{3,2,1,0:T(8,128)}, f32[8,2,16,432]{3,2,1,0:T(8,128)S(1)}, u32[]{:S(2)}) copy-start(f32[8,2,16,432]{3,2,1,0:T(8,128)S(1)} %all-to-all-done.2.own) | copy-start | bytes 1327108
  129.7 5.6 %collective-permute-start.21 = (f32[8,2,16,432]{3,2,1,0:T(8,128)S(1)}, f32[8,2,16,432]{3,2,1,0:T(8,128)S(1)}, u32[]{:S(2)}, u32[]{:S(2)}) collective-permute-start(f32[8,2,16,432]{3,2,1,0:T(8,128)S(1)} %all-to-all-done.2.own), channel_id=1, source_target_pairs={{0,16},{16,0},{32,48},{48,32},{64,80},{80,64},{96,112},{112,96},{1... | collective-permute-start | bytes 1327112 | tf_op jit(solution)/shard_map/ppermute | solution.py:386
  135.3 0.8 copy-start.8
